TPU v7x, 768 devices: a whole 4x8x12 slice. The times are simulated.
768 devices in a mesh: ctx: 48 (over x, z_lo, core), tp: 16 (over y, z_hi).
Axes of the slice: x: 4, y: 8, z: 12 (z_hi: 2, z_lo: 6; z = z_hi * 6 + z_lo), core: 2. Of those that a mesh axis runs over, the one named last changes fastest.
Arguments:
- queries: bfloat16 [18432, 2048], P('ctx', 'tp'), may hold values from -8 to 8
- key_rows: bfloat16 [18432, 2048], P('ctx', 'tp'), may hold values from -8 to 8
- values: bfloat16 [18432, 2048], P('ctx', 'tp'), may hold values from -6 to 6
- cotangent: bfloat16 [18432, 4096], P('ctx', 'tp'), may hold values from -1.5 to 1.5
- w_flat: bfloat16 [16, 4128, 128], P('tp', 'ctx'), may hold values from -0.125 to 0.125
- block_keys: int32 [144, 6], P('ctx'), may hold values from 0 to 143, as said below
Outputs:
- query_grad: float32 [18432, 2048], P('ctx', 'tp')
- key_grad: float32 [18432, 2048], P('ctx', 'tp')
- value_grad: float32 [18432, 2048], P('ctx', 'tp')
- weight_grad: float32 [16, 4128, 128], P('tp', 'ctx')
Inputs may be any that keep to these rules, and one draw needn't show every extreme that they name: `block_keys`: row b lists b, then b - 1 and b + 1 modulo 144, then for k = 1, 2, 3 a block c whose c - c % 3 equals (b - b % 3 + k * 36) modulo 144.
All inputs are finite; a program needn't handle non-finite values.
Results may differ from a plain program's by a relative error of at most 0.034.
Values may be sent and summed in bfloat16 or wider, within the bound.
No kernel may reach another device: no remote copies, remote signals or barrier semaphores. Data moves between devices by JAX's collectives and lax.ppermute only.
A program may use at most 32 MiB of HBM per device.

v0:
```python
import jax
import jax.numpy as jnp
from jax import lax
from jax.sharding import PartitionSpec as P

DH = 128
BLK = 128


def shifted(value, axis, steps):
    count = lax.axis_size(axis)
    pairs = [(source, (source + steps) % count) for source in range(count)]
    return lax.ppermute(value, axis, pairs)


def on_device(queries, key_rows, values, cotangent, w_flat, block_keys):
    n_ctx = lax.axis_size("ctx")
    quarter = n_ctx // 4
    tok_rows, feat_width = queries.shape
    blocks = tok_rows // BLK
    heads_local = feat_width // DH
    score_scale = DH ** (-0.5)
    stacked = jnp.stack([key_rows, values])
    picked = block_keys[:, 3:] % blocks
    fetched = []
    for offset in [1, -1, -quarter, -2 * quarter, -3 * quarter]:
        fetched.append(shifted(stacked, "ctx", offset))
    extended = jnp.concatenate(
        [fetched[0][:, tok_rows - BLK :], stacked, fetched[1][:, :BLK]], axis=1
    )
    distant = jnp.stack(fetched[2:])
    ext_blocks = extended.reshape(2, blocks + 2, BLK, feat_width)
    band_keys = jnp.stack(
        [ext_blocks[:, slot_index : slot_index + blocks] for slot_index in range(3)], axis=2
    )
    far_all = jnp.moveaxis(distant.reshape(3, 2, blocks, BLK, feat_width), 0, 1)
    far_picked = far_all[:, jnp.arange(3)[None, :], picked]
    selected = jnp.concatenate([band_keys, far_picked], axis=2).reshape(
        2, blocks, 6 * BLK, heads_local, DH
    )
    key_sel = selected[0]
    val_sel = selected[1]
    q_blocks = queries.reshape(blocks, BLK, heads_local, DH)
    scores = (
        jnp.einsum("jqhd,jkhd->jhqk", q_blocks, key_sel, preferred_element_type=jnp.float32)
        * score_scale
    )
    row_max = jnp.max(scores, axis=-1, keepdims=True)
    exp_terms = jnp.exp(scores - row_max)
    row_total = jnp.sum(exp_terms, axis=-1, keepdims=True)
    probs = exp_terms / row_total
    probs_low = probs.astype(jnp.bfloat16)
    attended = jnp.einsum(
        "jhqk,jkhd->jqhd", probs_low, val_sel, preferred_element_type=jnp.float32
    ).astype(jnp.bfloat16)
    attn_rows = attended.reshape(tok_rows, feat_width)
    full_cot = lax.all_gather(cotangent, "tp", axis=1, tiled=True)
    gathered_w = lax.all_gather(w_flat, "ctx", axis=1, tiled=True)
    model_width = full_cot.shape[1]
    flat_rows = feat_width * model_width // 128
    weight = gathered_w[0, :flat_rows].reshape(feat_width, model_width)
    out_grad = lax.dot_general(
        full_cot, weight, (((1,), (1,)), ((), ())), preferred_element_type=jnp.float32
    ).astype(jnp.bfloat16)
    weight_term = lax.dot_general(
        attn_rows, full_cot, (((0,), (0,)), ((), ())), preferred_element_type=jnp.float32
    )
    padded = (
        jnp.zeros((1, gathered_w.shape[1], 128), jnp.float32)
        .at[0, :flat_rows]
        .set(weight_term.reshape(flat_rows, 128))
    )
    weight_grad = lax.psum_scatter(padded, "ctx", scatter_dimension=1, tiled=True)
    grad_blocks = out_grad.reshape(blocks, BLK, heads_local, DH)
    delta_rows = jnp.sum(grad_blocks.astype(jnp.float32) * attended.astype(jnp.float32), axis=-1)
    delta_rows = jnp.transpose(delta_rows, (0, 2, 1))[..., None]
    prob_grad = jnp.einsum(
        "jqhd,jkhd->jhqk", grad_blocks, val_sel, preferred_element_type=jnp.float32
    )
    score_grad = (probs * (prob_grad - delta_rows)).astype(jnp.bfloat16)
    query_grad = (
        jnp.einsum("jhqk,jkhd->jqhd", score_grad, key_sel, preferred_element_type=jnp.float32)
        * score_scale
    )
    used_grad, used_probs, kept_slots = (score_grad, probs_low, 6)
    key_part = (
        jnp.einsum("jhqk,jqhd->jkhd", used_grad, q_blocks, preferred_element_type=jnp.float32)
        * score_scale
    )
    value_part = jnp.einsum(
        "jhqk,jqhd->jkhd", used_probs, grad_blocks, preferred_element_type=jnp.float32
    )
    slot_parts = jnp.stack([key_part, value_part]).reshape(2, blocks, kept_slots, BLK, feat_width)
    ext_grad = jnp.zeros((2, blocks + 2, BLK, feat_width), jnp.float32)
    for slot_index in range(3):
        ext_grad = ext_grad.at[:, slot_index : slot_index + blocks].add(
            slot_parts[:, :, slot_index]
        )
    grad_total = ext_grad[:, 1 : blocks + 1].reshape(2, tok_rows, feat_width)
    left_piece = (
        jnp.zeros((2, tok_rows, feat_width), jnp.float32)
        .at[:, tok_rows - BLK :]
        .set(ext_grad[:, 0])
    )
    right_piece = (
        jnp.zeros((2, tok_rows, feat_width), jnp.float32).at[:, :BLK].set(ext_grad[:, blocks + 1])
    )
    for buffer, offset in zip([left_piece, right_piece], [-1, 1]):
        grad_total = grad_total + shifted(buffer.astype(jnp.bfloat16), "ctx", offset).astype(
            buffer.dtype
        )
    for stride_index in range(3):
        far_piece = (
            jnp.zeros((2, blocks, BLK, feat_width), jnp.float32)
            .at[:, picked[:, stride_index]]
            .add(slot_parts[:, :, 3 + stride_index])
        )
        grad_total = grad_total + shifted(
            far_piece.reshape(2, tok_rows, feat_width).astype(jnp.bfloat16),
            "ctx",
            (stride_index + 1) * quarter,
        ).astype(jnp.float32)
    return (query_grad.reshape(tok_rows, feat_width), grad_total[0], grad_total[1], weight_grad)


def solution(mesh):
    in_specs = (
        P("ctx", "tp"),
        P("ctx", "tp"),
        P("ctx", "tp"),
        P("ctx", "tp"),
        P("tp", "ctx", None),
        P("ctx", None),
    )
    out_specs = (P("ctx", "tp"), P("ctx", "tp"), P("ctx", "tp"), P("tp", "ctx", None))
    return jax.shard_map(
        on_device, mesh=mesh, in_specs=in_specs, out_specs=out_specs, check_vma=False
    )
```

profile of v0, /device:TPU:1, one launch (start us, length us, event | category | flops | bytes accessed | tf_op | source)
XLA Modules:
  0.0 828.9 jit_solution(12590664789950442286)
XLA Ops:
  7.2 0.0 copy-start
  7.2 0.0 all-gather.5.cloned.1.call-start
  7.2 1.4 copy.76
  8.6 0.0 all-gather.5.cloned.1.call-update
  8.6 0.0 all-gather.3.cloned.1.call-start
  8.7 0.7 all-gather.3.cloned.1.call-update
  9.4 0.0 all-reduce.7.cloned.1.call-start
  9.4 1.0 pad_maximum_fusion.3
  10.4 5.5 collective-permute-start.3
  15.9 2.8 collective-permute-start.2
  18.7 2.5 collective-permute-start.4
  21.2 9.4 %collective-permute-start.1 = (bf16[2,384,128]{2,1,0:T(8,128)(2,1)S(1)}, bf16[2,384,128]{2,1,0:T(8,128)(2,1)S(1)}, u32[]{:S(2)}, u32[]{:S(2)}) collective-permute-start(bf16[2,384,128]{2,1,0:T(8,128)(2,1)S(1)} %pad_maximum_fusion.3), channel_id=1, source_target_pairs={{0,752},{16,0},{32,16},{48,32},{64,48},{80,64},{96,80},{112,96},{1... | collective-permute-start | bytes 589832 | tf_op jit(solution)/shard_map/ppermute | solution.py:13
  30.6 1.9 collective-permute-start
  32.5 0.8 fusion.29
  33.3 0.8 add_select_fusion
  34.1 0.1 reshape.353
  34.2 1.3 dynamic-slice.39
  36.1 0.2 fusion.30
  36.3 0.1 maximum_bitcast_fusion
  36.4 0.0 copy-start.8
  36.4 0.7 gather_fusion
  37.2 1.5 collective-permute-done
  38.8 0.1 slice_bitcast_fusion.4
  38.9 0.1 pad_maximum_fusion
  39.0 0.9 fusion.37
  39.9 1.6 fusion.38
  41.5 74.6 %all-gather.5.cloned.1.call-done = bf16[1,4128,128]{2,0,1:T(2,128)(2,1)} async-done(((bf16[1,86,128]{2,0,1:T(2,128)(2,1)}), bf16[1,4128,128]{2,0,1:T(2,128)(2,1)}) %all-gather.5.cloned.1.call-update) | async-done | bytes 1056784 | tf_op jit(solution)/shard_map/all_gather | solution.py:58
  116.1 18.5 %slice_reduce_fusion = bf16[4096,128]{1,0:T(8,128)(2,1)S(1)} fusion(bf16[1,4128,128]{2,0,1:T(2,128)(2,1)} %all-gather.5.cloned.1.call-done), kind=kLoop, calls=%fused_computation.15 | loop fusion | bytes 2097152 | tf_op jit(solution)/shard_map/slice | solution.py:61
  134.6 0.5 reshape_squeeze.3
  135.1 129.7 %all-gather.3.cloned.1.call-done = bf16[384,4096]{1,0:T(8,128)(2,1)} async-done(((bf16[384,256]{1,0:T(8,128)(2,1)}), bf16[384,4096]{1,0:T(8,128)(2,1)}) %all-gather.3.cloned.1.call-update) | async-done | bytes 3145744 | tf_op jit(solution)/shard_map/all_gather | solution.py:57
  264.8 2.9 convolution_convert_fusion.1
  267.7 2.3 fusion.23
  270.0 2.1 fusion.39
  272.1 1.7 reshape.351
  273.8 3.3 scatter.14
  277.1 0.0 all-reduce.7.cloned.1.call-update
  277.1 1.0 copy-done.7
  278.2 0.4 copy-done.10
  278.6 0.3 fusion.5
  278.9 0.3 convolution_multiply_fusion
  279.2 2.8 convolution_bitcast_fusion
  282.0 1.6 copy.82
  283.7 1.2 fusion.15
  284.8 0.8 copy.88
  285.6 1.8 scatter_fusion
  287.4 0.7 convert_element_type.83
  288.1 3.1 collective-permute-start.7
  291.2 1.0 copy.107
  292.3 0.1 fusion.18
  292.4 0.1 fusion.13
  292.7 0.7 scatter.11
  293.4 7.1 collective-permute-start.6
  300.5 2.2 collective-permute-start.5
  302.8 1.0 scatter_fusion.2
  303.8 0.7 convert_element_type.89
  304.5 3.4 collective-permute-start.9
  308.0 1.0 scatter_fusion.1
  309.0 3.4 collective-permute-start.8
  312.4 1.0 convolution_multiply_fusion.2
  313.5 3.4 collective-permute-done.8
  316.9 0.1 fusion.22
  317.1 0.8 slice_bitcast_fusion
  317.8 503.2 %all-reduce.7.cloned.1.call-done = f32[1,4128,128]{2,0,1:T(1,128)} async-done(((f32[1,4128,128]{2,0,1:T(1,128)}), f32[1,4128,128]{2,0,1:T(1,128)}) %all-reduce.7.cloned.1.call-update) | async-done | bytes 2113552
  821.0 1.4 constant_dynamic-slice_fusion
  (43 shorter events, 0.5 us)
Async XLA Ops:
  7.2 32.8 %copy-start = (bf16[384,128]{1,0:T(8,128)(2,1)S(1)}, bf16[384,128]{1,0:T(8,128)(2,1)}, u32[]{:S(2)}) copy-start(bf16[384,128]{1,0:T(8,128)(2,1)} %param.18) | copy-start | bytes 294916
  7.2 108.9 %all-gather.5.cloned.1.call-start = ((), (), s32[]{:S(2)}) async-start(), calls=%async_computation.1 | async-start | bytes 2157568 | tf_op jit(solution)/shard_map/all_gather | solution.py:58
  8.6 256.2 %all-gather.3.cloned.1.call-start = ((), (), s32[]{:S(2)}) async-start(), calls=%async_computation | async-start | bytes 3342336 | tf_op jit(solution)/shard_map/all_gather | solution.py:57
  9.4 811.6 %all-reduce.7.cloned.1.call-start = ((), (), s32[]{:S(2)}) async-start(), calls=%async_computation.2 | async-start | bytes 4227072
  10.4 25.9 %collective-permute-start.3 = (bf16[2,384,128]{2,1,0:T(8,128)(2,1)S(1)}, bf16[2,384,128]{2,1,0:T(8,128)(2,1)S(1)}, u32[]{:S(2)}, u32[]{:S(2)}) collective-permute-start(bf16[2,384,128]{2,1,0:T(8,128)(2,1)S(1)} %pad_maximum_fusion.3), channel_id=1, source_target_pairs={{0,384},{16,400},{32,416},{48,432},{64,448},{80,464},{96,480},{112... | collective-permute-start | bytes 589832 | tf_op jit(solution)/shard_map/ppermute | solution.py:13
  15.9 20.4 %collective-permute-start.2 = (bf16[2,384,128]{2,1,0:T(8,128)(2,1)S(1)}, bf16[2,384,128]{2,1,0:T(8,128)(2,1)S(1)}, u32[]{:S(2)}, u32[]{:S(2)}) collective-permute-start(bf16[2,384,128]{2,1,0:T(8,128)(2,1)S(1)} %pad_maximum_fusion.3), channel_id=1, source_target_pairs={{0,576},{16,592},{32,608},{48,624},{64,640},{80,656},{96,672},{112... | collective-permute-start | bytes 589832 | tf_op jit(solution)/shard_map/ppermute | solution.py:13
  18.7 17.6 %collective-permute-start.4 = (bf16[2,384,128]{2,1,0:T(8,128)(2,1)S(1)}, bf16[2,384,128]{2,1,0:T(8,128)(2,1)S(1)}, u32[]{:S(2)}, u32[]{:S(2)}) collective-permute-start(bf16[2,384,128]{2,1,0:T(8,128)(2,1)S(1)} %pad_maximum_fusion.3), channel_id=1, source_target_pairs={{0,192},{16,208},{32,224},{48,240},{64,256},{80,272},{96,288},{112... | collective-permute-start | bytes 589832 | tf_op jit(solution)/shard_map/ppermute | solution.py:13
  21.2 16.0 %collective-permute-start.1 = (bf16[2,384,128]{2,1,0:T(8,128)(2,1)S(1)}, bf16[2,384,128]{2,1,0:T(8,128)(2,1)S(1)}, u32[]{:S(2)}, u32[]{:S(2)}) collective-permute-start(bf16[2,384,128]{2,1,0:T(8,128)(2,1)S(1)} %pad_maximum_fusion.3), channel_id=1, source_target_pairs={{0,752},{16,0},{32,16},{48,32},{64,48},{80,64},{96,80},{112,96},{1... | collective-permute-start | bytes 589832 | tf_op jit(solution)/shard_map/ppermute | solution.py:13
  30.6 8.1 collective-permute-start
  36.4 2.3 copy-start.8
  36.4 2.3 copy-start.9
  39.9 1.6 copy-start.2
  267.7 2.3 copy-start.1
  277.1 1.1 copy-start.7
  277.1 1.5 copy-start.10
  287.4 4.9 copy-start.6
  288.1 25.3 %collective-permute-start.7 = (bf16[2,384,128]{2,1,0:T(8,128)(2,1)}, bf16[2,384,128]{2,1,0:T(8,128)(2,1)S(1)}, u32[]{:S(2)}, u32[]{:S(2)}) collective-permute-start(bf16[2,384,128]{2,1,0:T(8,128)(2,1)} %bitcast.41), channel_id=1, source_target_pairs={{0,192},{16,208},{32,224},{48,240},{64,256},{80,272},{96,288},{112... | collective-permute-start | bytes 589832 | tf_op jit(solution)/shard_map/ppermute | solution.py:13
  292.5 10.2 %copy-start.5 = (f32[3,2,128,128]{3,2,0,1:T(8,128)S(1)}, f32[3,2,128,128]{3,2,0,1:T(8,128)}, u32[]{:S(2)}) copy-start(f32[3,2,128,128]{3,2,0,1:T(8,128)} %get-tuple-element.82) | copy-start | bytes 1179652
  293.4 20.1 %collective-permute-start.6 = (bf16[2,384,128]{2,1,0:T(8,128)(2,1)}, bf16[2,384,128]{2,1,0:T(8,128)(2,1)S(1)}, u32[]{:S(2)}, u32[]{:S(2)}) collective-permute-start(bf16[2,384,128]{2,1,0:T(8,128)(2,1)} %scatter.11), channel_id=1, source_target_pairs={{0,16},{16,32},{32,48},{48,64},{64,80},{80,96},{96,112},{112,128},... | collective-permute-start | bytes 589832 | tf_op jit(solution)/shard_map/ppermute | solution.py:13
  300.5 13.0 %collective-permute-start.5 = (bf16[2,384,128]{2,1,0:T(8,128)(2,1)S(1)}, bf16[2,384,128]{2,1,0:T(8,128)(2,1)S(1)}, u32[]{:S(2)}, u32[]{:S(2)}) collective-permute-start(bf16[2,384,128]{2,1,0:T(8,128)(2,1)S(1)} %scatter.10), channel_id=1, source_target_pairs={{0,752},{16,0},{32,16},{48,32},{64,48},{80,64},{96,80},{112,96},{1... | collective-permute-start | bytes 589832 | tf_op jit(solution)/shard_map/ppermute | solution.py:13
  302.8 5.1 copy-start.4
  304.5 9.0 %collective-permute-start.9 = (bf16[2,384,128]{2,1,0:T(8,128)(2,1)}, bf16[2,384,128]{2,1,0:T(8,128)(2,1)S(1)}, u32[]{:S(2)}, u32[]{:S(2)}) collective-permute-start(bf16[2,384,128]{2,1,0:T(8,128)(2,1)} %bitcast.47), channel_id=1, source_target_pairs={{0,576},{16,592},{32,608},{48,624},{64,640},{80,656},{96,672},{112... | collective-permute-start | bytes 589832 | tf_op jit(solution)/shard_map/ppermute | solution.py:13
  307.9 4.5 copy-start.3
  309.0 7.9 collective-permute-start.8
Sparse Core Ops, SparseCore 0:
  11.1 104.9 all-gather.4
  119.7 145.0 all-gather.2
  277.3 543.6 all-reduce.6
where the time goes:
time: 830 us; the launch traced here: 829 us
  waiting for transfers between devices  713 us (86%)
  starting transfers between devices  41.4 us (5%)
  local copies, waits for them, and re-layouts  36.7 us (4%)
  between operations  14.9 us (2%)
  matrix products  13.3 us (2%)
  other arithmetic  9.53 us (1%)
    unnamed x4, waiting for transfers between devices  504 us
    all_gather x1, waiting for transfers between devices, on_device(): full_cot = lax.all_gather(cotangent, 'tp', axis=1, tiled=True)  130 us
    all_gather x1, waiting for transfers between devices, on_device(): gathered_w = lax.all_gather(w_flat, 'ctx', axis=1, tiled=True)  74.6 us
    ppermute x10, starting transfers between devices, shifted(): return lax.ppermute(value, axis, pairs)  41.3 us
    slice x1, local copies, waits for them, and re-layouts, on_device(): weight = gathered_w[0, :flat_rows].reshape(feat_width, model_width)  18.5 us
  transfers between devices with their start and end apart: 13, of which 5 were waited for; matrix products, arithmetic and copies ran while one was open for 5% of the time, Pallas kernels for 0%

commit v1 on v0

v1 whole, which is shorter than its diff:
```python
import jax
import jax.numpy as jnp
from jax import lax
from jax.experimental import pallas as pl
from jax.experimental.pallas import tpu as pltpu
from jax.sharding import PartitionSpec as P

DH = 128
BLK = 128
F32 = jnp.float32
BF16 = jnp.bfloat16

NX, NZ, NY = 4, 6, 8
N_CTX = NX * NZ * 2
N_TP = NY * 2
CHIPS = NX * NZ
SHARD = 86
SHARD_PAD = 88
FLAT_ROWS = 4096
WCOL = 256
SAME_CORE = [[2 * i + core for i in range(CHIPS)] for core in range(2)]
X_GROUPS = [[x * NZ * 2 + rest for x in range(NX)] for rest in range(NZ * 2)]
Y_GROUPS = [[2 * y + z for y in range(NY)] for z in range(2)]
SMEM = pl.BlockSpec(memory_space=pltpu.SMEM)
VMEM = pl.BlockSpec(memory_space=pltpu.VMEM)
PARAMS = pltpu.CompilerParams(vmem_limit_bytes=48 * 1024 * 1024)

M_X, M_CORE, M_Y, M_Z = 9, 10, 11, 12


def dot(a, b, ca, cb):
    return lax.dot_general(a, b, (((ca,), (cb,)), ((), ())), preferred_element_type=F32)


def ctx_shift(value, steps):
    return lax.ppermute(value, "ctx", [(s, (s + steps) % N_CTX) for s in range(N_CTX)])


def core_swap(value):
    return lax.ppermute(value, "ctx", [(s, s ^ 1) for s in range(N_CTX)])


def twin_swap(value):
    return lax.ppermute(value, "tp", [(s, s ^ 1) for s in range(N_TP)])


def y_shift(value, steps):
    pairs = [(2 * y + z, 2 * ((y + steps) % NY) + z) for y in range(NY) for z in range(2)]
    return lax.ppermute(value, "tp", pairs)


def select(meta, j, which, kv, prev, nxt, far):
    parts = [kv[which, j * BLK : (j + 1) * BLK]]
    parts.append(prev[which] if j == 0 else kv[which, (j - 1) * BLK : j * BLK])
    parts.append(nxt[which] if j == 2 else kv[which, (j + 1) * BLK : (j + 2) * BLK])
    for k in range(3):
        source = (meta[M_X] + k + 1) % NX
        row = pl.multiple_of(meta[3 * j + k] * BLK, BLK)
        parts.append(far[source, which, pl.ds(row, BLK)])
    return jnp.concatenate(parts, axis=0)


def forward_kernel(meta, q, kv, prev, nxt, far, probs_out, att_out):
    for j in range(3):
        rows = slice(j * BLK, (j + 1) * BLK)
        keys = select(meta, j, 0, kv, prev, nxt, far)
        vals = select(meta, j, 1, kv, prev, nxt, far)
        scores = dot(q[rows], keys, 1, 1) * (DH**-0.5)
        terms = jnp.exp(scores - jnp.max(scores, axis=-1, keepdims=True))
        probs = terms / jnp.sum(terms, axis=-1, keepdims=True)
        probs_out[j] = probs
        att_out[rows] = dot(probs.astype(BF16), vals, 1, 0).astype(BF16)


def weight_kernel(meta, own, other, w_out, flat):
    first = meta[M_CORE] == 0
    for i in range(CHIPS):
        a = own[i].astype(F32)
        b = other[i].astype(F32)
        even = jnp.where(first, a, b)
        odd = jnp.where(first, b, a)
        flat[2 * i * SHARD : 2 * i * SHARD + SHARD_PAD] = even
        flat[(2 * i + 1) * SHARD : (2 * i + 1) * SHARD + SHARD_PAD] = odd
    for t in range(N_TP):
        for e in range(2):
            rows = flat[pl.ds(2 * t + e, DH, stride=32)]
            w_out[t, :, e * 128 : (e + 1) * 128] = rows.astype(BF16)


def pieces_of(meta, near, ring):
    y, z = meta[M_Y], meta[M_Z]
    for i in range(NY):
        yield 2 * i + z, lambda i=i: near[i * 384 : (i + 1) * 384]
    for ref, step in ring:
        yield 2 * ((y + step + NY) % NY) + 1 - z, lambda ref=ref: ref[...]


RING = (0, -1, 1, -2, 2, -3, 3, -4)


def weight_grad_kernel(meta, att, near, *refs):
    ring = list(zip(refs[:NY], RING))
    keep, give, cols, flat = refs[NY:]
    att_now = att[...]
    for col, load in pieces_of(meta, near, ring):
        cols[col] = dot(att_now, load(), 0, 0)
    for t in range(N_TP):
        for e in range(2):
            flat[pl.ds(2 * t + e, DH, stride=32)] = cols[t, :, e * 128 : (e + 1) * 128]
    flat[FLAT_ROWS:] = jnp.zeros((flat.shape[0] - FLAT_ROWS, 128), F32)
    first = meta[M_CORE] == 0
    for i in range(CHIPS):
        a = flat[2 * i * SHARD : 2 * i * SHARD + SHARD_PAD]
        b = flat[(2 * i + 1) * SHARD : (2 * i + 1) * SHARD + SHARD_PAD]
        keep[i] = jnp.where(first, a, b)
        give[i] = jnp.where(first, b, a)


def backward_kernel(meta, q, kv, prev, nxt, far, probs, att, w, near, *refs):
    ring = list(zip(refs[:NY], RING))
    dq, dkv, dprev, dnext, dfar, acc = refs[NY:]
    total = jnp.zeros((384, DH), F32)
    for col, load in pieces_of(meta, near, ring):
        total = total + dot(load(), w[col], 1, 1)
    grad_all = total.astype(BF16)
    acc[...] = jnp.zeros(acc.shape, F32)
    dkv[...] = jnp.zeros(dkv.shape, F32)
    scale = DH**-0.5
    for j in range(3):
        rows = slice(j * BLK, (j + 1) * BLK)
        grad = grad_all[rows]
        keys = select(meta, j, 0, kv, prev, nxt, far)
        vals = select(meta, j, 1, kv, prev, nxt, far)
        delta = jnp.sum(grad.astype(F32) * att[rows].astype(F32), axis=-1, keepdims=True)
        p = probs[j]
        ds = (p * (dot(grad, vals, 1, 1) - delta)).astype(BF16)
        dq[rows] = dot(ds, keys, 1, 0) * scale
        parts = (dot(ds, q[rows], 0, 0) * scale, dot(p.astype(BF16), grad, 0, 0))
        for which in range(2):
            part = parts[which]
            dkv[which, rows] += part[:BLK]
            if j == 0:
                dprev[which] = part[BLK : 2 * BLK].astype(BF16)
            else:
                dkv[which, (j - 1) * BLK : j * BLK] += part[BLK : 2 * BLK]
            if j == 2:
                dnext[which] = part[2 * BLK : 3 * BLK].astype(BF16)
            else:
                dkv[which, (j + 1) * BLK : (j + 2) * BLK] += part[2 * BLK : 3 * BLK]
            for k in range(3):
                row = pl.multiple_of(meta[3 * j + k] * BLK, BLK)
                acc[k, which, pl.ds(row, BLK)] += part[(3 + k) * BLK : (4 + k) * BLK]
    dfar[meta[M_X]] = jnp.zeros(dfar.shape[1:], BF16)
    for k in range(3):
        dfar[(meta[M_X] + k + 1) % NX] = acc[k].astype(BF16)


def on_device(queries, key_rows, values, cotangent, w_flat, block_keys):
    ctx = lax.axis_index("ctx")
    tp = lax.axis_index("tp")
    picked = (block_keys[:, 3:] % 3).reshape(9)
    place = jnp.stack([ctx // (2 * NZ), ctx % 2, tp // 2, tp % 2]).astype(jnp.int32)
    meta = jnp.concatenate([picked, place])

    near = lax.all_gather(cotangent, "tp", axis=0, tiled=True, axis_index_groups=Y_GROUPS)
    twin = twin_swap(cotangent)
    kv = jnp.stack([key_rows, values])
    prev = ctx_shift(kv[:, 2 * BLK :], 1)
    nxt = ctx_shift(kv[:, :BLK], -1)
    far = lax.all_to_all(
        jnp.broadcast_to(kv[None], (NX,) + kv.shape),
        "ctx", 0, 0, tiled=True, axis_index_groups=X_GROUPS,
    )
    up, down = twin, twin
    ring = [twin]
    for step in range(1, 4):
        up = y_shift(up, 1)
        down = y_shift(down, -1)
        ring += [up, down]
    ring.append(y_shift(up, 1))

    w_pad = jnp.concatenate([w_flat[0], twin[:2, :128]], axis=0)
    w_own = lax.all_to_all(
        jnp.broadcast_to(w_pad[None], (CHIPS, SHARD_PAD, 128)),
        "ctx", 0, 0, tiled=True, axis_index_groups=SAME_CORE,
    )
    w_other = core_swap(w_own)
    flat_alloc = N_CTX * SHARD + 8
    weight = pl.pallas_call(
        weight_kernel,
        out_shape=jax.ShapeDtypeStruct((N_TP, DH, WCOL), BF16),
        in_specs=[SMEM, VMEM, VMEM],
        out_specs=VMEM,
        scratch_shapes=[pltpu.VMEM((flat_alloc, 128), F32)],
        compiler_params=PARAMS,
        name="weight_rows",
    )(meta, w_own, w_other)

    probs, att = pl.pallas_call(
        forward_kernel,
        out_shape=(
            jax.ShapeDtypeStruct((3, BLK, 6 * BLK), F32),
            jax.ShapeDtypeStruct((384, DH), BF16),
        ),
        in_specs=[SMEM] + [VMEM] * 5,
        out_specs=(VMEM, VMEM),
        compiler_params=PARAMS,
        name="attention_forward",
    )(meta, queries, kv, prev, nxt, far)

    chunk = jax.ShapeDtypeStruct((CHIPS, SHARD_PAD, 128), F32)
    keep, give = pl.pallas_call(
        weight_grad_kernel,
        out_shape=(chunk, chunk),
        in_specs=[SMEM] + [VMEM] * (2 + NY),
        out_specs=(VMEM, VMEM),
        scratch_shapes=[pltpu.VMEM((N_TP, DH, WCOL), F32), pltpu.VMEM((flat_alloc, 128), F32)],
        compiler_params=PARAMS,
        name="weight_grad",
    )(meta, att, near, *ring)
    pair_sum = (keep + core_swap(give)).astype(BF16)
    spread = lax.all_to_all(
        pair_sum, "ctx", 0, 0, tiled=True, axis_index_groups=SAME_CORE
    )
    weight_grad = jnp.sum(spread.astype(F32), axis=0)[None, :SHARD]

    two = (2, 384, DH)
    dq, dkv, dprev, dnext, dfar = pl.pallas_call(
        backward_kernel,
        out_shape=(
            jax.ShapeDtypeStruct((384, DH), F32),
            jax.ShapeDtypeStruct(two, F32),
            jax.ShapeDtypeStruct((2, BLK, DH), BF16),
            jax.ShapeDtypeStruct((2, BLK, DH), BF16),
            jax.ShapeDtypeStruct((NX,) + two, BF16),
        ),
        in_specs=[SMEM] + [VMEM] * (9 + NY),
        out_specs=(VMEM,) * 5,
        scratch_shapes=[pltpu.VMEM((3,) + two, F32)],
        compiler_params=PARAMS,
        name="attention_backward",
    )(meta, queries, kv, prev, nxt, far, probs, att, weight, near, *ring)
    from_far = lax.all_to_all(dfar, "ctx", 0, 0, tiled=True, axis_index_groups=X_GROUPS)
    from_next = ctx_shift(dprev, -1)
    from_prev = ctx_shift(dnext, 1)
    total = dkv + jnp.sum(from_far.astype(F32), axis=0)
    total = total.at[:, 2 * BLK :].add(from_next.astype(F32))
    total = total.at[:, :BLK].add(from_prev.astype(F32))
    return dq, total[0], total[1], weight_grad


def solution(mesh):
    in_specs = (
        P("ctx", "tp"),
        P("ctx", "tp"),
        P("ctx", "tp"),
        P("ctx", "tp"),
        P("tp", "ctx", None),
        P("ctx", None),
    )
    out_specs = (P("ctx", "tp"), P("ctx", "tp"), P("ctx", "tp"), P("tp", "ctx", None))
    return jax.shard_map(
        on_device, mesh=mesh, in_specs=in_specs, out_specs=out_specs, check_vma=False
    )
```

time: 830 us -> 180 us (0.22)
  waiting for transfers between devices: 713 us -> 37.7 us
  starting transfers between devices: 41.4 us -> 94.6 us
  local copies, waits for them, and re-layouts: 36.7 us -> 12.3 us
  Pallas kernels: 0 us -> 14.5 us
  matrix products: 13.3 us -> 0 us
    unnamed x4 -> x1, waiting for transfers between devices: 504 us -> 0.68 us
    all_gather x2 -> x1, waiting for transfers between devices: 204 us -> 0.01 us  [on_device(): lax.all_gather(cotangent, 'tp', axis=0, tiled=True, axis_index_groups=Y_G...]
    all_to_all x0 -> x4, starting transfers between devices: none -> 31.4 us  [the longest x1 17 us: on_device(): lax.all_to_all(jnp.broadcast_to(w_pad[None], (CHIPS, SHARD_PAD, 128)), 'c...]
    ppermute x10 -> x14, starting transfers between devices: 41.3 us -> 63.1 us  [the longest x7 22.2 us: y_shift(): return lax.ppermute(value, 'tp', pairs)]
    slice x6 -> x1, local copies, waits for them, and re-layouts: 19.5 us -> 0.01 us  [on_device(): w_pad = jnp.concatenate([w_flat[0], twin[:2, :128]], axis=0)]
    all_to_all x0 -> x4, waiting for transfers between devices: none -> 17 us  [the longest x1 10.1 us: on_device(): lax.all_to_all(dfar, 'ctx', 0, 0, tiled=True, axis_index_groups=X_GROUPS)]
    ppermute x10 -> x14, waiting for transfers between devices: 4.98 us -> 20.1 us  [the longest x7 6.76 us: y_shift(): return lax.ppermute(value, 'tp', pairs)]
    pallas_call x0 -> x4, Pallas kernels: none -> 14.5 us  [the longest x1 5.64 us: on_device(): pl.pallas_call(backward_kernel, out_shape=(jax.ShapeDtypeStruct((384, DH)...]
  transfers between devices with their start and end apart: 13 -> 19, of which waited for: 5 -> 9; matrix products, arithmetic and copies ran while one was open for 5% -> 4% of each run, Pallas kernels for 0% -> 8%
where the time goes in v1:
time: 180 us; the launch traced here: 178 us
  starting transfers between devices  94.6 us (53%)
  waiting for transfers between devices  37.7 us (21%)
  Pallas kernels  14.5 us (8%)
  between operations  14.5 us (8%)
  local copies, waits for them, and re-layouts  12.3 us (7%)
  other arithmetic  4.15 us (2%)
    ppermute x7, starting transfers between devices, y_shift(): return lax.ppermute(value, 'tp', pairs)  22.2 us
    all_to_all x1, starting transfers between devices, on_device(): lax.all_to_all(jnp.broadcast_to(w_pad[None], (CHIPS, SHARD_PAD, 128)), 'c...  17 us
    ppermute x1, starting transfers between devices, twin_swap(): return lax.ppermute(value, 'tp', [(s, s ^ 1) for s in range(N_TP)])  15 us
    ppermute x4, starting transfers between devices, ctx_shift(): lax.ppermute(value, 'ctx', [(s, (s + steps) % N_CTX) for s in range(N_CTX)])  14.4 us
    ppermute x2, starting transfers between devices, core_swap(): return lax.ppermute(value, 'ctx', [(s, s ^ 1) for s in range(N_CTX)])  11.6 us
    all_to_all x1, waiting for transfers between devices, on_device(): lax.all_to_all(dfar, 'ctx', 0, 0, tiled=True, axis_index_groups=X_GROUPS)  10.1 us
    unnamed x52, local copies, waits for them, and re-layouts  8.87 us
    all_to_all x1, waiting for transfers between devices, on_device(): lax.all_to_all(pair_sum, 'ctx', 0, 0, tiled=True, axis_index_groups=SAME_...  6.89 us
  transfers between devices with their start and end apart: 19, of which 9 were waited for; matrix products, arithmetic and copies ran while one was open for 4% of the time, Pallas kernels for 8%

profile of v1, /device:TPU:1, one launch (start us, length us, event | category | flops | bytes accessed | tf_op | source)
XLA Modules:
  0.0 177.8 jit_solution(3338380507182525419)
XLA Ops:
  7.2 0.0 all-gather.2.cloned.1.call-start
  7.2 0.7 all-gather.2.cloned.1.call-update
  7.9 1.0 pad_maximum_fusion.kv
  8.9 0.0 copy-start.23
  8.9 0.0 copy-start.24
  8.9 1.0 broadcast_in_dim.6
  9.9 4.8 %all-to-all-start = ((bf16[4,2,384,128]{3,2,1,0:T(8,128)(2,1)}), bf16[4,2,384,128]{3,2,1,0:T(8,128)(2,1)S(1)}, u32[]{:S(2)}, u32[]{:S(2)}) async-start(bf16[4,2,384,128]{3,2,1,0:T(8,128)(2,1)} %broadcast_in_dim.6), calls=%async_computation | async-start | bytes 1572864 | tf_op jit(solution)/shard_map/all_to_all | solution.py:170
  14.7 0.0 copy-start.25
  14.8 0.0 copy-start.14
  14.8 15.0 %collective-permute-start.2 = (bf16[384,256]{1,0:T(8,128)(2,1)S(1)}, bf16[384,256]{1,0:T(8,128)(2,1)S(1)}, u32[]{:S(2)}, u32[]{:S(2)}) collective-permute-start(bf16[384,256]{1,0:T(8,128)(2,1)S(1)} %copy-done.23), channel_id=1, source_target_pairs={{0,1},{1,0},{2,3},{3,2},{4,5},{5,4},{6,7},{7,6},{8,9},{9,8},{10,11... | collective-permute-start | bytes 589832 | tf_op jit(solution)/shard_map/ppermute | solution.py:44
  29.8 5.5 %collective-permute-done.2.refs_0_ = bf16[384,256]{1,0:T(8,128)(2,1)S(1)} collective-permute-done((bf16[384,256]{1,0:T(8,128)(2,1)S(1)}, bf16[384,256]{1,0:T(8,128)(2,1)S(1)}, u32[]{:S(2)}, u32[]{:S(2)}) %collective-permute-start.2) | collective-permute-done | bytes 196640 | tf_op jit(solution)/shard_map/ppermute | solution.py:44
  35.3 0.9 broadcast_in_dim.7
  36.2 17.0 %all-to-all-start.1 = ((bf16[24,88,128]{2,1,0:T(8,128)(2,1)}), bf16[24,88,128]{2,1,0:T(8,128)(2,1)S(1)}, u32[]{:S(2)}, u32[]{:S(2)}) async-start(bf16[24,88,128]{2,1,0:T(8,128)(2,1)} %broadcast_in_dim.7), calls=%async_computation.1 | async-start | bytes 1081344 | tf_op jit(solution)/shard_map/all_to_all | solution.py:183
  53.2 3.2 %collective-permute-start.4 = (bf16[384,256]{1,0:T(8,128)(2,1)S(1)}, bf16[384,256]{1,0:T(8,128)(2,1)S(1)}, u32[]{:S(2)}, u32[]{:S(2)}) collective-permute-start(bf16[384,256]{1,0:T(8,128)(2,1)S(1)} %collective-permute-done.2.refs_0_), channel_id=1, source_target_pairs={{0,2},{1,3},{2,4},{3,5},{4,6},{5,7},{6,8},{7,9},{8,10},{9,11},{10,... | collective-permute-start | bytes 589832 | tf_op jit(solution)/shard_map/ppermute | solution.py:49
  56.4 3.8 %collective-permute-start.5 = (bf16[384,256]{1,0:T(8,128)(2,1)S(1)}, bf16[384,256]{1,0:T(8,128)(2,1)S(1)}, u32[]{:S(2)}, u32[]{:S(2)}) collective-permute-start(bf16[384,256]{1,0:T(8,128)(2,1)S(1)} %collective-permute-done.2.refs_0_), channel_id=1, source_target_pairs={{0,14},{1,15},{2,0},{3,1},{4,2},{5,3},{6,4},{7,5},{8,6},{9,7},{10,... | collective-permute-start | bytes 589832 | tf_op jit(solution)/shard_map/ppermute | solution.py:49
  60.2 3.4 %collective-permute-done.4.refs_1_ = bf16[384,256]{1,0:T(8,128)(2,1)S(1)} collective-permute-done((bf16[384,256]{1,0:T(8,128)(2,1)S(1)}, bf16[384,256]{1,0:T(8,128)(2,1)S(1)}, u32[]{:S(2)}, u32[]{:S(2)}) %collective-permute-start.4) | collective-permute-done | bytes 196640 | tf_op jit(solution)/shard_map/ppermute | solution.py:49
  63.6 1.9 %collective-permute-start.6 = (bf16[384,256]{1,0:T(8,128)(2,1)S(1)}, bf16[384,256]{1,0:T(8,128)(2,1)S(1)}, u32[]{:S(2)}, u32[]{:S(2)}) collective-permute-start(bf16[384,256]{1,0:T(8,128)(2,1)S(1)} %collective-permute-done.4.refs_1_), channel_id=1, source_target_pairs={{0,2},{1,3},{2,4},{3,5},{4,6},{5,7},{6,8},{7,9},{8,10},{9,11},{10,... | collective-permute-start | bytes 589832 | tf_op jit(solution)/shard_map/ppermute | solution.py:49
  65.5 4.6 %collective-permute-start.7 = (bf16[384,256]{1,0:T(8,128)(2,1)S(1)}, bf16[384,256]{1,0:T(8,128)(2,1)S(1)}, u32[]{:S(2)}, u32[]{:S(2)}) collective-permute-start(bf16[384,256]{1,0:T(8,128)(2,1)S(1)} %collective-permute-done.5.refs_2_), channel_id=1, source_target_pairs={{0,14},{1,15},{2,0},{3,1},{4,2},{5,3},{6,4},{7,5},{8,6},{9,7},{10,... | collective-permute-start | bytes 589832 | tf_op jit(solution)/shard_map/ppermute | solution.py:49
  70.1 1.6 collective-permute-done.6.refs_3_
  71.7 1.9 %collective-permute-start.8 = (bf16[384,256]{1,0:T(8,128)(2,1)S(1)}, bf16[384,256]{1,0:T(8,128)(2,1)S(1)}, u32[]{:S(2)}, u32[]{:S(2)}) collective-permute-start(bf16[384,256]{1,0:T(8,128)(2,1)S(1)} %collective-permute-done.6.refs_3_), channel_id=1, source_target_pairs={{0,2},{1,3},{2,4},{3,5},{4,6},{5,7},{6,8},{7,9},{8,10},{9,11},{10,... | collective-permute-start | bytes 589832 | tf_op jit(solution)/shard_map/ppermute | solution.py:49
  73.6 0.6 fusion.3
  74.3 4.2 %collective-permute-start.1 = (bf16[2,128,128]{2,1,0:T(8,128)(2,1)}, bf16[2,128,128]{2,1,0:T(8,128)(2,1)S(1)}, u32[]{:S(2)}, u32[]{:S(2)}) collective-permute-start(bf16[2,128,128]{2,1,0:T(8,128)(2,1)} %get-tuple-element.48), channel_id=1, source_target_pairs={{0,752},{16,0},{32,16},{48,32},{64,48},{80,64},{96,80},{112,96},{1... | collective-permute-start | bytes 196616 | tf_op jit(solution)/shard_map/ppermute | solution.py:36
  78.5 3.0 %collective-permute-start = (bf16[2,128,128]{2,1,0:T(8,128)(2,1)S(1)}, bf16[2,128,128]{2,1,0:T(8,128)(2,1)S(1)}, u32[]{:S(2)}, u32[]{:S(2)}) collective-permute-start(bf16[2,128,128]{2,1,0:T(8,128)(2,1)S(1)} %get-tuple-element.49), channel_id=1, source_target_pairs={{0,16},{16,32},{32,48},{48,64},{64,80},{80,96},{96,112},{112,128},... | collective-permute-start | bytes 196616 | tf_op jit(solution)/shard_map/ppermute | solution.py:36
  81.6 0.0 copy-start.2
  81.6 4.9 %collective-permute-start.9 = (bf16[384,256]{1,0:T(8,128)(2,1)S(1)}, bf16[384,256]{1,0:T(8,128)(2,1)S(1)}, u32[]{:S(2)}, u32[]{:S(2)}) collective-permute-start(bf16[384,256]{1,0:T(8,128)(2,1)S(1)} %collective-permute-done.7.refs_4_), channel_id=1, source_target_pairs={{0,14},{1,15},{2,0},{3,1},{4,2},{5,3},{6,4},{7,5},{8,6},{9,7},{10,... | collective-permute-start | bytes 589832 | tf_op jit(solution)/shard_map/ppermute | solution.py:49
  86.5 0.0 copy-start.5
  86.5 1.9 %collective-permute-start.10 = (bf16[384,256]{1,0:T(8,128)(2,1)S(1)}, bf16[384,256]{1,0:T(8,128)(2,1)S(1)}, u32[]{:S(2)}, u32[]{:S(2)}) collective-permute-start(bf16[384,256]{1,0:T(8,128)(2,1)S(1)} %collective-permute-done.8.refs_5_), channel_id=1, source_target_pairs={{0,2},{1,3},{2,4},{3,5},{4,6},{5,7},{6,8},{7,9},{8,10},{9,11},{10,... | collective-permute-start | bytes 589832 | tf_op jit(solution)/shard_map/ppermute | solution.py:49
  88.4 0.1 add_select_fusion
  88.5 0.1 reshape.73
  88.6 0.1 concatenate.10.meta
  88.7 1.9 %attention_forward.1 = (f32[3,128,768]{2,1,0:T(8,128)S(1)}, bf16[384,128]{1,0:T(8,128)(2,1)S(1)}) custom-call(s32[13]{0:T(128)S(1)} %concatenate.10.meta, bf16[384,128]{1,0:T(8,128)(2,1)S(1)} %copy-done.14, bf16[2,384,128]{2,1,0:T(8,128)(2,1)S(1)} %pad_maximum_fusion.kv, bf16[2,128,128]{2,1,0:T(8,128)(2,1)S(1)} %collective-permute-done.prev, ...), custom_call_target="tpu_custom_call" | custom-call | tf_op jit(solution)/shard_map/attention_forward/pallas_call | solution.py:199
  90.6 1.0 copy-done.1
  91.7 0.7 copy-done.8
  92.3 1.8 collective-permute-done.10.refs_7_
  94.1 0.7 copy-done.11
  94.8 1.4 copy-done
  96.2 0.9 copy-done.3
  97.1 0.9 copy-done.6
  98.1 0.9 copy-done.9
  99.0 0.9 copy-done.12
  99.9 0.7 copy-done.19
  100.6 4.6 %weight_grad.1 = (f32[24,88,128]{2,1,0:T(8,128)S(1)}, f32[24,88,128]{2,1,0:T(8,128)}) custom-call(s32[13]{0:T(128)S(1)} %copy-done.19, bf16[384,128]{1,0:T(8,128)(2,1)S(1)} %get-tuple-element.38.att, bf16[3072,256]{1,0:T(8,128)(2,1)S(1)} %copy-done, bf16[384,256]{1,0:T(8,128)(2,1)S(1)} %collective-permute-done.2.refs_0_, ...), custom_call_target="tpu_custom_call" | custom-call | tf_op jit(solution)/shard_map/weight_grad/pallas_call | solution.py:212
  105.2 9.6 %collective-permute-start.13 = (f32[24,88,128]{2,1,0:T(8,128)}, f32[24,88,128]{2,1,0:T(8,128)}, u32[]{:S(2)}, u32[]{:S(2)}) collective-permute-start(f32[24,88,128]{2,1,0:T(8,128)} %get-tuple-element.45), channel_id=1, source_target_pairs={{0,16},{16,0},{32,48},{48,32},{64,80},{80,64},{96,112},{112,96},{1... | collective-permute-start | bytes 3244040 | tf_op jit(solution)/shard_map/ppermute | solution.py:40
  114.7 0.0 copy-start.4
  114.8 0.0 copy-start.10
  114.8 0.0 copy-start.15
  114.8 2.1 %collective-permute-start.3 = (bf16[24,88,128]{2,1,0:T(8,128)(2,1)S(1)}, bf16[24,88,128]{2,1,0:T(8,128)(2,1)S(1)}, u32[]{:S(2)}, u32[]{:S(2)}) collective-permute-start(bf16[24,88,128]{2,1,0:T(8,128)(2,1)S(1)} %all-to-all-done.1.own), channel_id=1, source_target_pairs={{0,16},{16,0},{32,48},{48,32},{64,80},{80,64},{96,112},{112,96},{1... | collective-permute-start | bytes 1622024 | tf_op jit(solution)/shard_map/ppermute | solution.py:40
  116.9 1.9 %collective-permute-done.3.other = bf16[24,88,128]{2,1,0:T(8,128)(2,1)S(1)} collective-permute-done((bf16[24,88,128]{2,1,0:T(8,128)(2,1)S(1)}, bf16[24,88,128]{2,1,0:T(8,128)(2,1)S(1)}, u32[]{:S(2)}, u32[]{:S(2)}) %collective-permute-start.3) | collective-permute-done | bytes 540704 | tf_op jit(solution)/shard_map/ppermute | solution.py:40
  118.8 0.7 copy-done.20
  119.4 2.4 %weight_rows.1.w = bf16[16,128,256]{2,1,0:T(8,128)(2,1)S(1)} custom-call(s32[13]{0:T(128)S(1)} %copy-done.20, bf16[24,88,128]{2,1,0:T(8,128)(2,1)S(1)} %all-to-all-done.1.own, bf16[24,88,128]{2,1,0:T(8,128)(2,1)S(1)} %collective-permute-done.3.other), custom_call_target="tpu_custom_call" | custom-call | tf_op jit(solution)/shard_map/weight_rows/pallas_call | solution.py:189
  121.9 5.6 %attention_backward.1 = (f32[384,128]{1,0:T(8,128)}, f32[2,384,128]{2,1,0:T(8,128)S(1)}, bf16[2,128,128]{2,1,0:T(8,128)(2,1)S(1)}, bf16[2,128,128]{2,1,0:T(8,128)(2,1)S(1)}, bf16[4,2,384,128]{3,2,1,0:T(8,128)(2,1)}) custom-call(s32[13]{0:T(128)S(1)} %copy-done.20, bf16[384,128]{1,0:T(8,128)(2,1)S(1)} %copy-done.15, ...), custom_call_target="tpu_custom_call" | custom-call | tf_op jit(solution)/shard_map/attention_backward/pallas_call | solution.py:228
  127.5 3.5 %all-to-all-start.2 = ((bf16[4,2,384,128]{3,2,1,0:T(8,128)(2,1)}), bf16[4,2,384,128]{3,2,1,0:T(8,128)(2,1)S(1)}, u32[]{:S(2)}, u32[]{:S(2)}) async-start(bf16[4,2,384,128]{3,2,1,0:T(8,128)(2,1)} %get-tuple-element.41), calls=%async_computation.2 | async-start | bytes 1572864 | tf_op jit(solution)/shard_map/all_to_all | solution.py:243
  131.0 2.2 %add_convert_fusion = bf16[24,88,128]{2,1,0:T(8,128)(2,1)} fusion(f32[24,88,128]{2,1,0:T(8,128)S(1)} %get-tuple-element.44, f32[24,88,128]{2,1,0:T(8,128)} %collective-permute-done.13), kind=kLoop, calls=%fused_computation.2 | loop fusion | flops 540672 | bytes 2703360 | tf_op jit(solution)/shard_map/convert_element_type | solution.py:221
  133.2 10.1 %all-to-all-done.2 = bf16[4,2,384,128]{3,2,1,0:T(8,128)(2,1)S(1)} async-done(((bf16[4,2,384,128]{3,2,1,0:T(8,128)(2,1)}), bf16[4,2,384,128]{3,2,1,0:T(8,128)(2,1)S(1)}, u32[]{:S(2)}, u32[]{:S(2)}) %all-to-all-start.2) | async-done | bytes 786464 | tf_op jit(solution)/shard_map/all_to_all | solution.py:243
  143.3 6.1 %all-to-all-start.3 = ((bf16[24,88,128]{2,1,0:T(8,128)(2,1)}), bf16[24,88,128]{2,1,0:T(8,128)(2,1)S(1)}, u32[]{:S(2)}, u32[]{:S(2)}) async-start(bf16[24,88,128]{2,1,0:T(8,128)(2,1)} %add_convert_fusion), calls=%async_computation.3 | async-start | bytes 1081344 | tf_op jit(solution)/shard_map/all_to_all | solution.py:222
  149.3 3.7 %collective-permute-start.11 = (bf16[2,128,128]{2,1,0:T(8,128)(2,1)S(1)}, bf16[2,128,128]{2,1,0:T(8,128)(2,1)S(1)}, u32[]{:S(2)}, u32[]{:S(2)}) collective-permute-start(bf16[2,128,128]{2,1,0:T(8,128)(2,1)S(1)} %get-tuple-element.42), channel_id=1, source_target_pairs={{0,752},{16,0},{32,16},{48,32},{64,48},{80,64},{96,80},{112,96},{1... | collective-permute-start | bytes 196616 | tf_op jit(solution)/shard_map/ppermute | solution.py:36
  153.0 3.4 %collective-permute-start.12 = (bf16[2,128,128]{2,1,0:T(8,128)(2,1)S(1)}, bf16[2,128,128]{2,1,0:T(8,128)(2,1)S(1)}, u32[]{:S(2)}, u32[]{:S(2)}) collective-permute-start(bf16[2,128,128]{2,1,0:T(8,128)(2,1)S(1)} %get-tuple-element.43), channel_id=1, source_target_pairs={{0,16},{16,32},{32,48},{48,64},{64,80},{80,96},{96,112},{112,128},... | collective-permute-start | bytes 196616 | tf_op jit(solution)/shard_map/ppermute | solution.py:36
  156.4 0.1 convert_reduce_fusion
  156.6 0.7 collective-permute-done.11
  157.3 5.2 %collective-permute-done.12 = bf16[2,128,128]{2,1,0:T(8,128)(2,1)S(1)} collective-permute-done((bf16[2,128,128]{2,1,0:T(8,128)(2,1)S(1)}, bf16[2,128,128]{2,1,0:T(8,128)(2,1)S(1)}, u32[]{:S(2)}, u32[]{:S(2)}) %collective-permute-start.12) | collective-permute-done | bytes 65568 | tf_op jit(solution)/shard_map/ppermute | solution.py:36
  162.5 0.8 slice_bitcast_fusion
  163.3 6.9 %all-to-all-done.3 = bf16[24,88,128]{2,1,0:T(8,128)(2,1)S(1)} async-done(((bf16[24,88,128]{2,1,0:T(8,128)(2,1)}), bf16[24,88,128]{2,1,0:T(8,128)(2,1)S(1)}, u32[]{:S(2)}, u32[]{:S(2)}) %all-to-all-start.3) | async-done | bytes 540704 | tf_op jit(solution)/shard_map/all_to_all | solution.py:222
  170.2 0.1 convert_reduce_fusion.1
  170.3 0.6 broadcast_in_dim.8
  (48 shorter events, 0.2 us)
Async XLA Ops:
  7.2 87.6 %all-gather.2.cloned.1.call-start = ((), (), s32[]{:S(2)}) async-start(), calls=%async_computation.4 | async-start | bytes 1769472 | tf_op jit(solution)/shard_map/all_gather | solution.py:165
  8.9 5.9 %copy-start.23 = (bf16[384,256]{1,0:T(8,128)(2,1)S(1)}, bf16[384,256]{1,0:T(8,128)(2,1)}, u32[]{:S(2)}) copy-start(bf16[384,256]{1,0:T(8,128)(2,1)} %param.13) | copy-start | bytes 589828
  8.9 26.4 %copy-start.24 = (bf16[1,86,128]{2,1,0:T(8,128)(2,1)S(1)}, bf16[1,86,128]{2,1,0:T(8,128)(2,1)}, u32[]{:S(2)}) copy-start(bf16[1,86,128]{2,1,0:T(8,128)(2,1)} %param.14) | copy-start | bytes 66052
  9.9 25.4 %all-to-all-start = ((bf16[4,2,384,128]{3,2,1,0:T(8,128)(2,1)}), bf16[4,2,384,128]{3,2,1,0:T(8,128)(2,1)S(1)}, u32[]{:S(2)}, u32[]{:S(2)}) async-start(bf16[4,2,384,128]{3,2,1,0:T(8,128)(2,1)} %broadcast_in_dim.6), calls=%async_computation | async-start | bytes 1572864 | tf_op jit(solution)/shard_map/all_to_all | solution.py:170
  14.7 58.9 %copy-start.21 = (bf16[384,128]{1,0:T(8,128)(2,1)S(1)}, bf16[384,128]{1,0:T(8,128)(2,1)}, u32[]{:S(2)}) copy-start(bf16[384,128]{1,0:T(8,128)(2,1)} %param.12) | copy-start | bytes 294916
  14.7 58.9 %copy-start.22 = (bf16[384,128]{1,0:T(8,128)(2,1)S(1)}, bf16[384,128]{1,0:T(8,128)(2,1)}, u32[]{:S(2)}) copy-start(bf16[384,128]{1,0:T(8,128)(2,1)} %param.11) | copy-start | bytes 294916
  14.7 73.7 %copy-start.25 = (s32[3,6]{1,0:T(4,128)S(1)}, s32[3,6]{1,0:T(4,128)}, u32[]{:S(2)}) copy-start(s32[3,6]{1,0:T(4,128)} %param.15) | copy-start | bytes 220
  14.8 73.9 %copy-start.14 = (bf16[384,128]{1,0:T(8,128)(2,1)S(1)}, bf16[384,128]{1,0:T(8,128)(2,1)}, u32[]{:S(2)}) copy-start(bf16[384,128]{1,0:T(8,128)(2,1)} %q.3) | copy-start | bytes 294916
  14.8 20.5 %collective-permute-start.2 = (bf16[384,256]{1,0:T(8,128)(2,1)S(1)}, bf16[384,256]{1,0:T(8,128)(2,1)S(1)}, u32[]{:S(2)}, u32[]{:S(2)}) collective-permute-start(bf16[384,256]{1,0:T(8,128)(2,1)S(1)} %copy-done.23), channel_id=1, source_target_pairs={{0,1},{1,0},{2,3},{3,2},{4,5},{5,4},{6,7},{7,6},{8,9},{9,8},{10,11... | collective-permute-start | bytes 589832 | tf_op jit(solution)/shard_map/ppermute | solution.py:44
  36.2 78.6 %all-to-all-start.1 = ((bf16[24,88,128]{2,1,0:T(8,128)(2,1)}), bf16[24,88,128]{2,1,0:T(8,128)(2,1)S(1)}, u32[]{:S(2)}, u32[]{:S(2)}) async-start(bf16[24,88,128]{2,1,0:T(8,128)(2,1)} %broadcast_in_dim.7), calls=%async_computation.1 | async-start | bytes 1081344 | tf_op jit(solution)/shard_map/all_to_all | solution.py:183
  53.2 10.4 %collective-permute-start.4 = (bf16[384,256]{1,0:T(8,128)(2,1)S(1)}, bf16[384,256]{1,0:T(8,128)(2,1)S(1)}, u32[]{:S(2)}, u32[]{:S(2)}) collective-permute-start(bf16[384,256]{1,0:T(8,128)(2,1)S(1)} %collective-permute-done.2.refs_0_), channel_id=1, source_target_pairs={{0,2},{1,3},{2,4},{3,5},{4,6},{5,7},{6,8},{7,9},{8,10},{9,11},{10,... | collective-permute-start | bytes 589832 | tf_op jit(solution)/shard_map/ppermute | solution.py:49
  56.4 9.2 %collective-permute-start.5 = (bf16[384,256]{1,0:T(8,128)(2,1)S(1)}, bf16[384,256]{1,0:T(8,128)(2,1)S(1)}, u32[]{:S(2)}, u32[]{:S(2)}) collective-permute-start(bf16[384,256]{1,0:T(8,128)(2,1)S(1)} %collective-permute-done.2.refs_0_), channel_id=1, source_target_pairs={{0,14},{1,15},{2,0},{3,1},{4,2},{5,3},{6,4},{7,5},{8,6},{9,7},{10,... | collective-permute-start | bytes 589832 | tf_op jit(solution)/shard_map/ppermute | solution.py:49
  63.6 8.1 %collective-permute-start.6 = (bf16[384,256]{1,0:T(8,128)(2,1)S(1)}, bf16[384,256]{1,0:T(8,128)(2,1)S(1)}, u32[]{:S(2)}, u32[]{:S(2)}) collective-permute-start(bf16[384,256]{1,0:T(8,128)(2,1)S(1)} %collective-permute-done.4.refs_1_), channel_id=1, source_target_pairs={{0,2},{1,3},{2,4},{3,5},{4,6},{5,7},{6,8},{7,9},{8,10},{9,11},{10,... | collective-permute-start | bytes 589832 | tf_op jit(solution)/shard_map/ppermute | solution.py:49
  65.5 16.0 %collective-permute-start.7 = (bf16[384,256]{1,0:T(8,128)(2,1)S(1)}, bf16[384,256]{1,0:T(8,128)(2,1)S(1)}, u32[]{:S(2)}, u32[]{:S(2)}) collective-permute-start(bf16[384,256]{1,0:T(8,128)(2,1)S(1)} %collective-permute-done.5.refs_2_), channel_id=1, source_target_pairs={{0,14},{1,15},{2,0},{3,1},{4,2},{5,3},{6,4},{7,5},{8,6},{9,7},{10,... | collective-permute-start | bytes 589832 | tf_op jit(solution)/shard_map/ppermute | solution.py:49
  71.7 14.7 %collective-permute-start.8 = (bf16[384,256]{1,0:T(8,128)(2,1)S(1)}, bf16[384,256]{1,0:T(8,128)(2,1)S(1)}, u32[]{:S(2)}, u32[]{:S(2)}) collective-permute-start(bf16[384,256]{1,0:T(8,128)(2,1)S(1)} %collective-permute-done.6.refs_3_), channel_id=1, source_target_pairs={{0,2},{1,3},{2,4},{3,5},{4,6},{5,7},{6,8},{7,9},{8,10},{9,11},{10,... | collective-permute-start | bytes 589832 | tf_op jit(solution)/shard_map/ppermute | solution.py:49
  74.3 14.4 %collective-permute-start.1 = (bf16[2,128,128]{2,1,0:T(8,128)(2,1)}, bf16[2,128,128]{2,1,0:T(8,128)(2,1)S(1)}, u32[]{:S(2)}, u32[]{:S(2)}) collective-permute-start(bf16[2,128,128]{2,1,0:T(8,128)(2,1)} %get-tuple-element.48), channel_id=1, source_target_pairs={{0,752},{16,0},{32,16},{48,32},{64,48},{80,64},{96,80},{112,96},{1... | collective-permute-start | bytes 196616 | tf_op jit(solution)/shard_map/ppermute | solution.py:36
  78.5 10.2 %collective-permute-start = (bf16[2,128,128]{2,1,0:T(8,128)(2,1)S(1)}, bf16[2,128,128]{2,1,0:T(8,128)(2,1)S(1)}, u32[]{:S(2)}, u32[]{:S(2)}) collective-permute-start(bf16[2,128,128]{2,1,0:T(8,128)(2,1)S(1)} %get-tuple-element.49), channel_id=1, source_target_pairs={{0,16},{16,32},{32,48},{48,64},{64,80},{80,96},{96,112},{112,128},... | collective-permute-start | bytes 196616 | tf_op jit(solution)/shard_map/ppermute | solution.py:36
  81.6 13.2 %copy-start.2 = (bf16[384,256]{1,0:T(8,128)(2,1)}, bf16[384,256]{1,0:T(8,128)(2,1)S(1)}, u32[]{:S(2)}) copy-start(bf16[384,256]{1,0:T(8,128)(2,1)S(1)} %collective-permute-done.7.refs_4_) | copy-start | bytes 589828
  81.6 10.1 %collective-permute-start.9 = (bf16[384,256]{1,0:T(8,128)(2,1)S(1)}, bf16[384,256]{1,0:T(8,128)(2,1)S(1)}, u32[]{:S(2)}, u32[]{:S(2)}) collective-permute-start(bf16[384,256]{1,0:T(8,128)(2,1)S(1)} %collective-permute-done.7.refs_4_), channel_id=1, source_target_pairs={{0,14},{1,15},{2,0},{3,1},{4,2},{5,3},{6,4},{7,5},{8,6},{9,7},{10,... | collective-permute-start | bytes 589832 | tf_op jit(solution)/shard_map/ppermute | solution.py:49
  86.5 8.3 %copy-start.5 = (bf16[384,256]{1,0:T(8,128)(2,1)}, bf16[384,256]{1,0:T(8,128)(2,1)S(1)}, u32[]{:S(2)}) copy-start(bf16[384,256]{1,0:T(8,128)(2,1)S(1)} %collective-permute-done.8.refs_5_) | copy-start | bytes 589828
  86.5 7.6 %collective-permute-start.10 = (bf16[384,256]{1,0:T(8,128)(2,1)S(1)}, bf16[384,256]{1,0:T(8,128)(2,1)S(1)}, u32[]{:S(2)}, u32[]{:S(2)}) collective-permute-start(bf16[384,256]{1,0:T(8,128)(2,1)S(1)} %collective-permute-done.8.refs_5_), channel_id=1, source_target_pairs={{0,2},{1,3},{2,4},{3,5},{4,6},{5,7},{6,8},{7,9},{8,10},{9,11},{10,... | collective-permute-start | bytes 589832 | tf_op jit(solution)/shard_map/ppermute | solution.py:49
  88.7 6.1 %copy-start.18 = (s32[13]{0:T(128)}, s32[13]{0:T(128)S(1)}, u32[]{:S(2)}) copy-start(s32[13]{0:T(128)S(1)} %concatenate.10.meta) | copy-start | bytes 160
  88.7 6.1 %copy-start.16 = (bf16[2,128,128]{2,1,0:T(8,128)(2,1)}, bf16[2,128,128]{2,1,0:T(8,128)(2,1)S(1)}, u32[]{:S(2)}) copy-start(bf16[2,128,128]{2,1,0:T(8,128)(2,1)S(1)} %collective-permute-done.prev) | copy-start | bytes 196612
  90.6 1.0 copy-start.1
  91.7 0.7 copy-start.8
  94.1 0.7 copy-start.11
  94.8 1.4 copy-start
  96.2 0.9 copy-start.3
  97.1 0.9 copy-start.6
  98.1 0.9 copy-start.9
  99.0 0.9 copy-start.12
  99.9 0.7 copy-start.19
  105.2 25.8 %collective-permute-start.13 = (f32[24,88,128]{2,1,0:T(8,128)}, f32[24,88,128]{2,1,0:T(8,128)}, u32[]{:S(2)}, u32[]{:S(2)}) collective-permute-start(f32[24,88,128]{2,1,0:T(8,128)} %get-tuple-element.45), channel_id=1, source_target_pairs={{0,16},{16,0},{32,48},{48,32},{64,80},{80,64},{96,112},{112,96},{1... | collective-permute-start | bytes 3244040 | tf_op jit(solution)/shard_map/ppermute | solution.py:40
  114.7 7.1 %copy-start.4 = (bf16[384,256]{1,0:T(8,128)(2,1)S(1)}, bf16[384,256]{1,0:T(8,128)(2,1)}, u32[]{:S(2)}) copy-start(bf16[384,256]{1,0:T(8,128)(2,1)} %copy-done.2) | copy-start | bytes 589828
  114.8 7.1 %copy-start.7 = (bf16[384,256]{1,0:T(8,128)(2,1)S(1)}, bf16[384,256]{1,0:T(8,128)(2,1)}, u32[]{:S(2)}) copy-start(bf16[384,256]{1,0:T(8,128)(2,1)} %copy-done.5) | copy-start | bytes 589828
  114.8 7.0 %copy-start.10 = (bf16[384,256]{1,0:T(8,128)(2,1)S(1)}, bf16[384,256]{1,0:T(8,128)(2,1)}, u32[]{:S(2)}) copy-start(bf16[384,256]{1,0:T(8,128)(2,1)} %copy-done.8) | copy-start | bytes 589828
  114.8 7.0 %copy-start.13 = (bf16[384,256]{1,0:T(8,128)(2,1)S(1)}, bf16[384,256]{1,0:T(8,128)(2,1)}, u32[]{:S(2)}) copy-start(bf16[384,256]{1,0:T(8,128)(2,1)} %copy-done.11) | copy-start | bytes 589828
  114.8 7.0 %copy-start.15 = (bf16[384,128]{1,0:T(8,128)(2,1)S(1)}, bf16[384,128]{1,0:T(8,128)(2,1)}, u32[]{:S(2)}) copy-start(bf16[384,128]{1,0:T(8,128)(2,1)} %q.3) | copy-start | bytes 294916
  114.8 7.0 %copy-start.17 = (bf16[2,128,128]{2,1,0:T(8,128)(2,1)S(1)}, bf16[2,128,128]{2,1,0:T(8,128)(2,1)}, u32[]{:S(2)}) copy-start(bf16[2,128,128]{2,1,0:T(8,128)(2,1)} %copy-done.16) | copy-start | bytes 196612
  114.8 4.0 %collective-permute-start.3 = (bf16[24,88,128]{2,1,0:T(8,128)(2,1)S(1)}, bf16[24,88,128]{2,1,0:T(8,128)(2,1)S(1)}, u32[]{:S(2)}, u32[]{:S(2)}) collective-permute-start(bf16[24,88,128]{2,1,0:T(8,128)(2,1)S(1)} %all-to-all-done.1.own), channel_id=1, source_target_pairs={{0,16},{16,0},{32,48},{48,32},{64,80},{80,64},{96,112},{112,96},{1... | collective-permute-start | bytes 1622024 | tf_op jit(solution)/shard_map/ppermute | solution.py:40
  118.8 0.7 copy-start.20
  127.5 15.8 %all-to-all-start.2 = ((bf16[4,2,384,128]{3,2,1,0:T(8,128)(2,1)}), bf16[4,2,384,128]{3,2,1,0:T(8,128)(2,1)S(1)}, u32[]{:S(2)}, u32[]{:S(2)}) async-start(bf16[4,2,384,128]{3,2,1,0:T(8,128)(2,1)} %get-tuple-element.41), calls=%async_computation.2 | async-start | bytes 1572864 | tf_op jit(solution)/shard_map/all_to_all | solution.py:243
  143.3 27.0 %all-to-all-start.3 = ((bf16[24,88,128]{2,1,0:T(8,128)(2,1)}), bf16[24,88,128]{2,1,0:T(8,128)(2,1)S(1)}, u32[]{:S(2)}, u32[]{:S(2)}) async-start(bf16[24,88,128]{2,1,0:T(8,128)(2,1)} %add_convert_fusion), calls=%async_computation.3 | async-start | bytes 1081344 | tf_op jit(solution)/shard_map/all_to_all | solution.py:222
  149.3 8.0 %collective-permute-start.11 = (bf16[2,128,128]{2,1,0:T(8,128)(2,1)S(1)}, bf16[2,128,128]{2,1,0:T(8,128)(2,1)S(1)}, u32[]{:S(2)}, u32[]{:S(2)}) collective-permute-start(bf16[2,128,128]{2,1,0:T(8,128)(2,1)S(1)} %get-tuple-element.42), channel_id=1, source_target_pairs={{0,752},{16,0},{32,16},{48,32},{64,48},{80,64},{96,80},{112,96},{1... | collective-permute-start | bytes 196616 | tf_op jit(solution)/shard_map/ppermute | solution.py:36
  153.0 9.5 %collective-permute-start.12 = (bf16[2,128,128]{2,1,0:T(8,128)(2,1)S(1)}, bf16[2,128,128]{2,1,0:T(8,128)(2,1)S(1)}, u32[]{:S(2)}, u32[]{:S(2)}) collective-permute-start(bf16[2,128,128]{2,1,0:T(8,128)(2,1)S(1)} %get-tuple-element.43), channel_id=1, source_target_pairs={{0,16},{16,32},{32,48},{48,64},{64,80},{80,96},{96,112},{112,128},... | collective-permute-start | bytes 196616 | tf_op jit(solution)/shard_map/ppermute | solution.py:36
Sparse Core Ops, SparseCore 0:
  10.4 48.7 all-gather.1

commit v2 on v1

--- a/solution.py
+++ b/solution.py
@@ -23,7 +23,7 @@
 Y_GROUPS = [[2 * y + z for y in range(NY)] for z in range(2)]
 SMEM = pl.BlockSpec(memory_space=pltpu.SMEM)
 VMEM = pl.BlockSpec(memory_space=pltpu.VMEM)
-PARAMS = pltpu.CompilerParams(vmem_limit_bytes=48 * 1024 * 1024)
+PARAMS = pltpu.CompilerParams(vmem_limit_bytes=12 * 1024 * 1024)
 
 M_X, M_CORE, M_Y, M_Z = 9, 10, 11, 12
 
@@ -32,8 +32,16 @@
     return lax.dot_general(a, b, (((ca,), (cb,)), ((), ())), preferred_element_type=F32)
 
 
-def ctx_shift(value, steps):
-    return lax.ppermute(value, "ctx", [(s, (s + steps) % N_CTX) for s in range(N_CTX)])
+def x_shift(value, steps):
+    pairs = [(s, (s + steps * NZ * 2) % N_CTX) for s in range(N_CTX)]
+    return lax.ppermute(value, "ctx", pairs)
+
+
+def neighbours(first, last, even):
+    inner = core_swap(jnp.where(even, last, first))
+    pairs = [(s, (s - 1 if s % 2 == 0 else s + 1) % N_CTX) for s in range(N_CTX)]
+    outer = lax.ppermute(jnp.where(even, first, last), "ctx", pairs)
+    return jnp.where(even, outer, inner), jnp.where(even, inner, outer)
 
 
 def core_swap(value):
@@ -47,6 +55,10 @@
 def y_shift(value, steps):
     pairs = [(2 * y + z, 2 * ((y + steps) % NY) + z) for y in range(NY) for z in range(2)]
     return lax.ppermute(value, "tp", pairs)
+
+
+def after(value, shards):
+    return jnp.where(shards[0, SHARD, 0] == 0, value, jnp.zeros_like(value))
 
 
 def select(meta, j, which, kv, prev, nxt, far):
@@ -87,23 +99,29 @@
             w_out[t, :, e * 128 : (e + 1) * 128] = rows.astype(BF16)
 
 
-def pieces_of(meta, near, ring):
+RING = (0, -1, 1, -2, 2, -3, 3, -4)
+
+
+def cotangent_kernel(meta, w, att, near_hbm, *refs):
+    ring = refs[:NY]
+    keep, give, grad, near, cols, flat, sem = refs[NY:]
+    copy = pltpu.make_async_copy(near_hbm, near, sem)
+    copy.start()
     y, z = meta[M_Y], meta[M_Z]
+    att_now = att[...]
+    total = jnp.zeros((384, DH), F32)
+    for piece, step in zip(ring, RING):
+        col = 2 * ((y + step + NY) % NY) + 1 - z
+        cot = piece[...]
+        cols[col] = dot(att_now, cot, 0, 0)
+        total = total + dot(cot, w[col], 1, 1)
+    copy.wait()
     for i in range(NY):
-        yield 2 * i + z, lambda i=i: near[i * 384 : (i + 1) * 384]
-    for ref, step in ring:
-        yield 2 * ((y + step + NY) % NY) + 1 - z, lambda ref=ref: ref[...]
-
-
-RING = (0, -1, 1, -2, 2, -3, 3, -4)
-
-
-def weight_grad_kernel(meta, att, near, *refs):
-    ring = list(zip(refs[:NY], RING))
-    keep, give, cols, flat = refs[NY:]
-    att_now = att[...]
-    for col, load in pieces_of(meta, near, ring):
-        cols[col] = dot(att_now, load(), 0, 0)
+        col = 2 * i + z
+        cot = near[i * 384 : (i + 1) * 384]
+        cols[col] = dot(att_now, cot, 0, 0)
+        total = total + dot(cot, w[col], 1, 1)
+    grad[...] = total.astype(BF16)
     for t in range(N_TP):
         for e in range(2):
             flat[pl.ds(2 * t + e, DH, stride=32)] = cols[t, :, e * 128 : (e + 1) * 128]
@@ -116,19 +134,13 @@
         give[i] = jnp.where(first, b, a)
 
 
-def backward_kernel(meta, q, kv, prev, nxt, far, probs, att, w, near, *refs):
-    ring = list(zip(refs[:NY], RING))
-    dq, dkv, dprev, dnext, dfar, acc = refs[NY:]
-    total = jnp.zeros((384, DH), F32)
-    for col, load in pieces_of(meta, near, ring):
-        total = total + dot(load(), w[col], 1, 1)
-    grad_all = total.astype(BF16)
+def backward_kernel(meta, q, kv, prev, nxt, far, probs, att, out_grad, dq, dkv, dprev, dnext, dfar, acc):
     acc[...] = jnp.zeros(acc.shape, F32)
     dkv[...] = jnp.zeros(dkv.shape, F32)
     scale = DH**-0.5
     for j in range(3):
         rows = slice(j * BLK, (j + 1) * BLK)
-        grad = grad_all[rows]
+        grad = out_grad[rows]
         keys = select(meta, j, 0, kv, prev, nxt, far)
         vals = select(meta, j, 1, kv, prev, nxt, far)
         delta = jnp.sum(grad.astype(F32) * att[rows].astype(F32), axis=-1, keepdims=True)
@@ -150,9 +162,26 @@
             for k in range(3):
                 row = pl.multiple_of(meta[3 * j + k] * BLK, BLK)
                 acc[k, which, pl.ds(row, BLK)] += part[(3 + k) * BLK : (4 + k) * BLK]
-    dfar[meta[M_X]] = jnp.zeros(dfar.shape[1:], BF16)
-    for k in range(3):
-        dfar[(meta[M_X] + k + 1) % NX] = acc[k].astype(BF16)
+    dfar[...] = acc[...].astype(BF16)
+
+
+def chunk_sum_kernel(parts, out):
+    total = parts[0].astype(F32)
+    for i in range(1, CHIPS):
+        total = total + parts[i].astype(F32)
+    out[0] = total[:SHARD]
+
+
+def grad_sum_kernel(dkv, prev, nxt, far1, far2, far3, dk, dv):
+    for which, out in ((0, dk), (1, dv)):
+        out[...] = (
+            dkv[which]
+            + far1[which].astype(F32)
+            + far2[which].astype(F32)
+            + far3[which].astype(F32)
+        )
+        out[:BLK] += prev[which].astype(F32)
+        out[2 * BLK :] += nxt[which].astype(F32)
 
 
 def on_device(queries, key_rows, values, cotangent, w_flat, block_keys):
@@ -164,11 +193,16 @@
 
     near = lax.all_gather(cotangent, "tp", axis=0, tiled=True, axis_index_groups=Y_GROUPS)
     twin = twin_swap(cotangent)
+    w_pad = jnp.pad(w_flat[0], ((0, SHARD_PAD - SHARD), (0, 0)))
+    w_own = lax.all_to_all(
+        jnp.broadcast_to(w_pad[None], (CHIPS, SHARD_PAD, 128)),
+        "ctx", 0, 0, tiled=True, axis_index_groups=SAME_CORE,
+    )
     kv = jnp.stack([key_rows, values])
-    prev = ctx_shift(kv[:, 2 * BLK :], 1)
-    nxt = ctx_shift(kv[:, :BLK], -1)
+    even = ctx % 2 == 0
+    prev, nxt = neighbours(kv[:, :BLK], kv[:, 2 * BLK :], even)
     far = lax.all_to_all(
-        jnp.broadcast_to(kv[None], (NX,) + kv.shape),
+        jnp.broadcast_to(after(kv, w_own)[None], (NX,) + kv.shape),
         "ctx", 0, 0, tiled=True, axis_index_groups=X_GROUPS,
     )
     up, down = twin, twin
@@ -179,11 +213,6 @@
         ring += [up, down]
     ring.append(y_shift(up, 1))
 
-    w_pad = jnp.concatenate([w_flat[0], twin[:2, :128]], axis=0)
-    w_own = lax.all_to_all(
-        jnp.broadcast_to(w_pad[None], (CHIPS, SHARD_PAD, 128)),
-        "ctx", 0, 0, tiled=True, axis_index_groups=SAME_CORE,
-    )
     w_other = core_swap(w_own)
     flat_alloc = N_CTX * SHARD + 8
     weight = pl.pallas_call(
@@ -209,20 +238,30 @@
     )(meta, queries, kv, prev, nxt, far)
 
     chunk = jax.ShapeDtypeStruct((CHIPS, SHARD_PAD, 128), F32)
-    keep, give = pl.pallas_call(
-        weight_grad_kernel,
-        out_shape=(chunk, chunk),
-        in_specs=[SMEM] + [VMEM] * (2 + NY),
-        out_specs=(VMEM, VMEM),
-        scratch_shapes=[pltpu.VMEM((N_TP, DH, WCOL), F32), pltpu.VMEM((flat_alloc, 128), F32)],
-        compiler_params=PARAMS,
-        name="weight_grad",
-    )(meta, att, near, *ring)
+    keep, give, out_grad = pl.pallas_call(
+        cotangent_kernel,
+        out_shape=(chunk, chunk, jax.ShapeDtypeStruct((384, DH), BF16)),
+        in_specs=[SMEM, VMEM, VMEM, pl.BlockSpec(memory_space=pltpu.HBM)] + [VMEM] * NY,
+        out_specs=(VMEM, VMEM, VMEM),
+        scratch_shapes=[
+            pltpu.VMEM((NY * 384, WCOL), BF16),
+            pltpu.VMEM((N_TP, DH, WCOL), F32),
+            pltpu.VMEM((flat_alloc, 128), F32),
+            pltpu.SemaphoreType.DMA,
+        ],
+        compiler_params=PARAMS,
+        name="cotangent_products",
+    )(meta, weight, att, near, *ring)
     pair_sum = (keep + core_swap(give)).astype(BF16)
     spread = lax.all_to_all(
         pair_sum, "ctx", 0, 0, tiled=True, axis_index_groups=SAME_CORE
     )
-    weight_grad = jnp.sum(spread.astype(F32), axis=0)[None, :SHARD]
+    weight_grad = pl.pallas_call(
+        chunk_sum_kernel,
+        out_shape=jax.ShapeDtypeStruct((1, SHARD, 128), F32),
+        compiler_params=PARAMS,
+        name="chunk_sum",
+    )(spread)
 
     two = (2, 384, DH)
     dq, dkv, dprev, dnext, dfar = pl.pallas_call(
@@ -232,21 +271,24 @@
             jax.ShapeDtypeStruct(two, F32),
             jax.ShapeDtypeStruct((2, BLK, DH), BF16),
             jax.ShapeDtypeStruct((2, BLK, DH), BF16),
-            jax.ShapeDtypeStruct((NX,) + two, BF16),
+            jax.ShapeDtypeStruct((3,) + two, BF16),
         ),
-        in_specs=[SMEM] + [VMEM] * (9 + NY),
+        in_specs=[SMEM] + [VMEM] * 8,
         out_specs=(VMEM,) * 5,
         scratch_shapes=[pltpu.VMEM((3,) + two, F32)],
         compiler_params=PARAMS,
         name="attention_backward",
-    )(meta, queries, kv, prev, nxt, far, probs, att, weight, near, *ring)
-    from_far = lax.all_to_all(dfar, "ctx", 0, 0, tiled=True, axis_index_groups=X_GROUPS)
-    from_next = ctx_shift(dprev, -1)
-    from_prev = ctx_shift(dnext, 1)
-    total = dkv + jnp.sum(from_far.astype(F32), axis=0)
-    total = total.at[:, 2 * BLK :].add(from_next.astype(F32))
-    total = total.at[:, :BLK].add(from_prev.astype(F32))
-    return dq, total[0], total[1], weight_grad
+    )(meta, queries, kv, prev, nxt, far, probs, att, out_grad)
+    far_back = [x_shift(dfar[k], k + 1) for k in range(3)]
+    from_prev, from_next = neighbours(dprev, dnext, even)
+    grad = jax.ShapeDtypeStruct((384, DH), F32)
+    dk, dv = pl.pallas_call(
+        grad_sum_kernel,
+        out_shape=(grad, grad),
+        compiler_params=PARAMS,
+        name="grad_sum",
+    )(dkv, from_prev, from_next, *far_back)
+    return dq, dk, dv, weight_grad
 
 
 def solution(mesh):

time: 180 us -> 174 us (0.967)
  the two profiles are of different devices: /device:TPU:1 before, /device:TPU:26 now
where the time goes in v2:
time: 174 us; the launch traced here: 173 us
  starting transfers between devices  106 us (61%)
  waiting for transfers between devices  28.8 us (17%)
  between operations  15.2 us (9%)
  Pallas kernels  13 us (7%)
  local copies, waits for them, and re-layouts  8.41 us (5%)
    ppermute x7, starting transfers between devices, y_shift(): return lax.ppermute(value, 'tp', pairs)  26.6 us
    ppermute x1, waiting for transfers between devices, twin_swap(): return lax.ppermute(value, 'tp', [(s, s ^ 1) for s in range(N_TP)])  16.4 us
    ppermute x2, starting transfers between devices, neighbours(): outer = lax.ppermute(jnp.where(even, first, last), 'ctx', pairs)  16.3 us
    all_to_all x1, starting transfers between devices, on_device(): lax.all_to_all(jnp.broadcast_to(w_pad[None], (CHIPS, SHARD_PAD, 128)), 'c...  15.2 us
    all_to_all x1, starting transfers between devices, on_device(): lax.all_to_all(pair_sum, 'ctx', 0, 0, tiled=True, axis_index_groups=SAME_...  14.5 us
    ppermute x3, starting transfers between devices, x_shift(): return lax.ppermute(value, 'ctx', pairs)  10.7 us
    ppermute x1, starting transfers between devices, twin_swap(): return lax.ppermute(value, 'tp', [(s, s ^ 1) for s in range(N_TP)])  10 us
    ppermute x4, starting transfers between devices, core_swap(): return lax.ppermute(value, 'ctx', [(s, s ^ 1) for s in range(N_CTX)])  8.16 us
  transfers between devices with their start and end apart: 21, of which 6 were waited for; matrix products, arithmetic and copies ran while one was open for 2% of the time, Pallas kernels for 4%

profile of v2, /device:TPU:26, one launch (start us, length us, event | category | flops | bytes accessed | tf_op | source)
XLA Modules:
  0.0 173.0 jit_solution(9669768162090207037)
XLA Ops:
  7.2 0.0 all-gather.2.cloned.1.call-start
  7.2 0.7 all-gather.2.cloned.1.call-update
  7.9 0.7 pad.4
  8.7 0.9 broadcast_in_dim.6
  9.6 15.2 %all-to-all-start = ((bf16[24,88,128]{2,1,0:T(8,128)(2,1)}), bf16[24,88,128]{2,1,0:T(8,128)(2,1)S(1)}, u32[]{:S(2)}, u32[]{:S(2)}) async-start(bf16[24,88,128]{2,1,0:T(8,128)(2,1)} %broadcast_in_dim.6), calls=%async_computation | async-start | bytes 1081344 | tf_op jit(solution)/shard_map/all_to_all | solution.py:197
  24.7 10.0 %collective-permute-start.3 = (bf16[384,256]{1,0:T(8,128)(2,1)S(1)}, bf16[384,256]{1,0:T(8,128)(2,1)S(1)}, u32[]{:S(2)}, u32[]{:S(2)}) collective-permute-start(bf16[384,256]{1,0:T(8,128)(2,1)S(1)} %copy-done.12), channel_id=1, source_target_pairs={{0,1},{1,0},{2,3},{3,2},{4,5},{5,4},{6,7},{7,6},{8,9},{9,8},{10,11... | collective-permute-start | bytes 589832 | tf_op jit(solution)/shard_map/ppermute | solution.py:52
  34.8 16.4 %collective-permute-done.3.refs_0_ = bf16[384,256]{1,0:T(8,128)(2,1)S(1)} collective-permute-done((bf16[384,256]{1,0:T(8,128)(2,1)S(1)}, bf16[384,256]{1,0:T(8,128)(2,1)S(1)}, u32[]{:S(2)}, u32[]{:S(2)}) %collective-permute-start.3) | collective-permute-done | bytes 196640 | tf_op jit(solution)/shard_map/ppermute | solution.py:52
  51.2 4.7 %collective-permute-start.4 = (bf16[384,256]{1,0:T(8,128)(2,1)S(1)}, bf16[384,256]{1,0:T(8,128)(2,1)S(1)}, u32[]{:S(2)}, u32[]{:S(2)}) collective-permute-start(bf16[384,256]{1,0:T(8,128)(2,1)S(1)} %collective-permute-done.3.refs_0_), channel_id=1, source_target_pairs={{0,2},{1,3},{2,4},{3,5},{4,6},{5,7},{6,8},{7,9},{8,10},{9,11},{10,... | collective-permute-start | bytes 589832 | tf_op jit(solution)/shard_map/ppermute | solution.py:57
  55.9 1.9 %collective-permute-start.5 = (bf16[384,256]{1,0:T(8,128)(2,1)S(1)}, bf16[384,256]{1,0:T(8,128)(2,1)S(1)}, u32[]{:S(2)}, u32[]{:S(2)}) collective-permute-start(bf16[384,256]{1,0:T(8,128)(2,1)S(1)} %collective-permute-done.3.refs_0_), channel_id=1, source_target_pairs={{0,14},{1,15},{2,0},{3,1},{4,2},{5,3},{6,4},{7,5},{8,6},{9,7},{10,... | collective-permute-start | bytes 589832 | tf_op jit(solution)/shard_map/ppermute | solution.py:57
  57.8 1.8 %collective-permute-done.4.refs_1_ = bf16[384,256]{1,0:T(8,128)(2,1)S(1)} collective-permute-done((bf16[384,256]{1,0:T(8,128)(2,1)S(1)}, bf16[384,256]{1,0:T(8,128)(2,1)S(1)}, u32[]{:S(2)}, u32[]{:S(2)}) %collective-permute-start.4) | collective-permute-done | bytes 196640 | tf_op jit(solution)/shard_map/ppermute | solution.py:57
  59.6 5.6 %collective-permute-start.6 = (bf16[384,256]{1,0:T(8,128)(2,1)S(1)}, bf16[384,256]{1,0:T(8,128)(2,1)S(1)}, u32[]{:S(2)}, u32[]{:S(2)}) collective-permute-start(bf16[384,256]{1,0:T(8,128)(2,1)S(1)} %collective-permute-done.4.refs_1_), channel_id=1, source_target_pairs={{0,2},{1,3},{2,4},{3,5},{4,6},{5,7},{6,8},{7,9},{8,10},{9,11},{10,... | collective-permute-start | bytes 589832 | tf_op jit(solution)/shard_map/ppermute | solution.py:57
  65.2 0.0 all-to-all-done.own
  65.2 0.5 slice.32
  66.4 1.0 broadcast_in_dim.8
  67.4 4.9 %all-to-all-start.1 = ((bf16[4,2,384,128]{3,2,1,0:T(8,128)(2,1)}), bf16[4,2,384,128]{3,2,1,0:T(8,128)(2,1)S(1)}, u32[]{:S(2)}, u32[]{:S(2)}) async-start(bf16[4,2,384,128]{3,2,1,0:T(8,128)(2,1)} %broadcast_in_dim.8), calls=%async_computation.1 | async-start | bytes 1572864 | tf_op jit(solution)/shard_map/all_to_all | solution.py:204
  72.4 1.9 %collective-permute-start.2 = (bf16[24,88,128]{2,1,0:T(8,128)(2,1)S(1)}, bf16[24,88,128]{2,1,0:T(8,128)(2,1)S(1)}, u32[]{:S(2)}, u32[]{:S(2)}) collective-permute-start(bf16[24,88,128]{2,1,0:T(8,128)(2,1)S(1)} %all-to-all-done.own), channel_id=1, source_target_pairs={{0,16},{16,0},{32,48},{48,32},{64,80},{80,64},{96,112},{112,96},{1... | collective-permute-start | bytes 1622024 | tf_op jit(solution)/shard_map/ppermute | solution.py:48
  74.3 2.4 %collective-permute-start.1 = (bf16[2,128,128]{2,1,0:T(8,128)(2,1)S(1)}, bf16[2,128,128]{2,1,0:T(8,128)(2,1)S(1)}, u32[]{:S(2)}, u32[]{:S(2)}) collective-permute-start(bf16[2,128,128]{2,1,0:T(8,128)(2,1)S(1)} %get-tuple-element.37), channel_id=1, source_target_pairs={{0,16},{16,0},{32,48},{48,32},{64,80},{80,64},{96,112},{112,96},{1... | collective-permute-start | bytes 196616 | tf_op jit(solution)/shard_map/ppermute | solution.py:48
  76.7 8.0 %collective-permute-start = (bf16[2,128,128]{2,1,0:T(8,128)(2,1)S(1)}, bf16[2,128,128]{2,1,0:T(8,128)(2,1)S(1)}, u32[]{:S(2)}, u32[]{:S(2)}) collective-permute-start(bf16[2,128,128]{2,1,0:T(8,128)(2,1)S(1)} %get-tuple-element.38), channel_id=1, source_target_pairs={{0,752},{16,32},{32,16},{48,64},{64,48},{80,96},{96,80},{112,128},... | collective-permute-start | bytes 196616 | tf_op jit(solution)/shard_map/ppermute | solution.py:43
  84.7 0.0 collective-permute-done.5.refs_2_
  84.7 0.0 copy-start.6
  84.8 1.9 %collective-permute-start.7 = (bf16[384,256]{1,0:T(8,128)(2,1)S(1)}, bf16[384,256]{1,0:T(8,128)(2,1)}, u32[]{:S(2)}, u32[]{:S(2)}) collective-permute-start(bf16[384,256]{1,0:T(8,128)(2,1)S(1)} %collective-permute-done.5.refs_2_), channel_id=1, source_target_pairs={{0,14},{1,15},{2,0},{3,1},{4,2},{5,3},{6,4},{7,5},{8,6},{9,7},{10,... | collective-permute-start | bytes 589832 | tf_op jit(solution)/shard_map/ppermute | solution.py:57
  86.7 0.0 collective-permute-done.6.refs_3_
  86.7 5.1 %collective-permute-start.8 = (bf16[384,256]{1,0:T(8,128)(2,1)S(1)}, bf16[384,256]{1,0:T(8,128)(2,1)}, u32[]{:S(2)}, u32[]{:S(2)}) collective-permute-start(bf16[384,256]{1,0:T(8,128)(2,1)S(1)} %collective-permute-done.6.refs_3_), channel_id=1, source_target_pairs={{0,2},{1,3},{2,4},{3,5},{4,6},{5,7},{6,8},{7,9},{8,10},{9,11},{10,... | collective-permute-start | bytes 589832 | tf_op jit(solution)/shard_map/ppermute | solution.py:57
  91.8 0.0 copy-start.8
  91.8 0.7 copy-done.8
  92.5 0.1 add_select_fusion
  92.6 0.1 reshape.31
  92.7 0.1 concatenate.7.meta
  92.8 1.9 %collective-permute-done.7.refs_4_ = bf16[384,256]{1,0:T(8,128)(2,1)} collective-permute-done((bf16[384,256]{1,0:T(8,128)(2,1)S(1)}, bf16[384,256]{1,0:T(8,128)(2,1)}, u32[]{:S(2)}, u32[]{:S(2)}) %collective-permute-start.7) | collective-permute-done | bytes 196640 | tf_op jit(solution)/shard_map/ppermute | solution.py:57
  94.6 1.9 %collective-permute-start.9 = (bf16[384,256]{1,0:T(8,128)(2,1)}, bf16[384,256]{1,0:T(8,128)(2,1)}, u32[]{:S(2)}, u32[]{:S(2)}) collective-permute-start(bf16[384,256]{1,0:T(8,128)(2,1)} %collective-permute-done.7.refs_4_), channel_id=1, source_target_pairs={{0,14},{1,15},{2,0},{3,1},{4,2},{5,3},{6,4},{7,5},{8,6},{9,7},{10,... | collective-permute-start | bytes 589832 | tf_op jit(solution)/shard_map/ppermute | solution.py:57
  96.6 0.0 collective-permute-done.8.refs_5_
  96.6 5.5 %collective-permute-start.10 = (bf16[384,256]{1,0:T(8,128)(2,1)}, bf16[384,256]{1,0:T(8,128)(2,1)}, u32[]{:S(2)}, u32[]{:S(2)}) collective-permute-start(bf16[384,256]{1,0:T(8,128)(2,1)} %collective-permute-done.8.refs_5_), channel_id=1, source_target_pairs={{0,2},{1,3},{2,4},{3,5},{4,6},{5,7},{6,8},{7,9},{8,10},{9,11},{10,... | collective-permute-start | bytes 589832 | tf_op jit(solution)/shard_map/ppermute | solution.py:57
  102.0 0.0 collective-permute-done.1
  102.0 0.0 collective-permute-done
  102.1 0.0 copy-start.3
  102.1 0.0 collective-permute-done.2.other
  102.1 2.4 %weight_rows.1.w = bf16[16,128,256]{2,1,0:T(8,128)(2,1)S(1)} custom-call(s32[13]{0:T(128)S(1)} %concatenate.7.meta, bf16[24,88,128]{2,1,0:T(8,128)(2,1)S(1)} %all-to-all-done.own, bf16[24,88,128]{2,1,0:T(8,128)(2,1)S(1)} %collective-permute-done.2.other), custom_call_target="tpu_custom_call" | custom-call | tf_op jit(solution)/shard_map/weight_rows/pallas_call | solution.py:218
  104.5 0.0 copy-start.5
  104.5 0.0 copy-start.7
  104.5 0.0 copy-start.9
  104.5 1.9 %attention_forward.1 = (f32[3,128,768]{2,1,0:T(8,128)S(1)}, bf16[384,128]{1,0:T(8,128)(2,1)S(1)}) custom-call(s32[13]{0:T(128)S(1)} %concatenate.7.meta, bf16[384,128]{1,0:T(8,128)(2,1)S(1)} %copy-done.3, bf16[2,384,128]{2,1,0:T(8,128)(2,1)S(1)} %get-tuple-element.36.kv, bf16[2,128,128]{2,1,0:T(8,128)(2,1)S(1)} %get-tuple-element.44.prev, ...), custom_call_target="tpu_custom_call" | custom-call | tf_op jit(solution)/shard_map/attention_forward/pallas_call | solution.py:228
  106.5 1.0 copy-done.1
  107.5 0.0 collective-permute-done.9.refs_6_
  107.5 0.0 collective-permute-done.10.refs_7_
  107.6 1.4 copy-done
  109.0 5.6 %cotangent_products.1 = (f32[24,88,128]{2,1,0:T(8,128)S(1)}, f32[24,88,128]{2,1,0:T(8,128)S(1)}, bf16[384,128]{1,0:T(8,128)(2,1)S(1)}) custom-call(s32[13]{0:T(128)S(1)} %concatenate.7.meta, bf16[16,128,256]{2,1,0:T(8,128)(2,1)S(1)} %weight_rows.1.w, bf16[384,128]{1,0:T(8,128)(2,1)S(1)} %get-tuple-element.17.att, bf16[3072,256]{1,0:T(8,128)(2,1)S(1)} %copy-done, ...), custom_call_target="tpu_custom_call" | custom-call | tf_op jit(solution)/shard_map/cotangent_products/pallas_call | solution.py:241
  114.5 1.9 %collective-permute-start.16 = (f32[24,88,128]{2,1,0:T(8,128)S(1)}, f32[24,88,128]{2,1,0:T(8,128)S(1)}, u32[]{:S(2)}, u32[]{:S(2)}) collective-permute-start(f32[24,88,128]{2,1,0:T(8,128)S(1)} %get-tuple-element.27), channel_id=1, source_target_pairs={{0,16},{16,0},{32,48},{48,32},{64,80},{80,64},{96,112},{112,96},{1... | collective-permute-start | bytes 3244040 | tf_op jit(solution)/shard_map/ppermute | solution.py:48
  116.5 2.7 %collective-permute-done.16 = f32[24,88,128]{2,1,0:T(8,128)S(1)} collective-permute-done((f32[24,88,128]{2,1,0:T(8,128)S(1)}, f32[24,88,128]{2,1,0:T(8,128)S(1)}, u32[]{:S(2)}, u32[]{:S(2)}) %collective-permute-start.16) | collective-permute-done | bytes 1081376 | tf_op jit(solution)/shard_map/ppermute | solution.py:48
  119.1 1.0 add_convert_fusion
  120.1 14.5 %all-to-all-start.2 = ((bf16[24,88,128]{2,1,0:T(8,128)(2,1)}), bf16[24,88,128]{2,1,0:T(8,128)(2,1)S(1)}, u32[]{:S(2)}, u32[]{:S(2)}) async-start(bf16[24,88,128]{2,1,0:T(8,128)(2,1)} %add_convert_fusion), calls=%async_computation.2 | async-start | bytes 1081344 | tf_op jit(solution)/shard_map/all_to_all | solution.py:256
  134.6 1.3 copy-done.2
  135.9 2.3 %attention_backward.1 = (f32[384,128]{1,0:T(8,128)}, f32[2,384,128]{2,1,0:T(8,128)S(1)}, bf16[2,128,128]{2,1,0:T(8,128)(2,1)S(1)}, bf16[2,128,128]{2,1,0:T(8,128)(2,1)S(1)}, bf16[3,2,384,128]{3,2,1,0:T(8,128)(2,1)S(1)}) custom-call(s32[13]{0:T(128)S(1)} %concatenate.7.meta, bf16[384,128]{1,0:T(8,128)(2,1)S(1)} %copy-done.3, ...), custom_call_target="tpu_custom_call" | custom-call | tf_op jit(solution)/shard_map/attention_backward/pallas_call | solution.py:267
  138.2 1.9 %collective-permute-start.12 = (bf16[2,128,128]{2,1,0:T(8,128)(2,1)S(1)}, bf16[2,128,128]{2,1,0:T(8,128)(2,1)S(1)}, u32[]{:S(2)}, u32[]{:S(2)}) collective-permute-start(bf16[2,128,128]{2,1,0:T(8,128)(2,1)S(1)} %get-tuple-element.41), channel_id=1, source_target_pairs={{0,16},{16,0},{32,48},{48,32},{64,80},{80,64},{96,112},{112,96},{1... | collective-permute-start | bytes 196616 | tf_op jit(solution)/shard_map/ppermute | solution.py:48
  140.1 8.3 %collective-permute-start.11 = (bf16[2,128,128]{2,1,0:T(8,128)(2,1)S(1)}, bf16[2,128,128]{2,1,0:T(8,128)(2,1)S(1)}, u32[]{:S(2)}, u32[]{:S(2)}) collective-permute-start(bf16[2,128,128]{2,1,0:T(8,128)(2,1)S(1)} %get-tuple-element.42), channel_id=1, source_target_pairs={{0,752},{16,32},{32,16},{48,64},{64,48},{80,96},{96,80},{112,128},... | collective-permute-start | bytes 196616 | tf_op jit(solution)/shard_map/ppermute | solution.py:43
  148.4 3.4 %collective-permute-start.13 = (bf16[2,384,128]{2,1,0:T(8,128)(2,1)S(1)}, bf16[2,384,128]{2,1,0:T(8,128)(2,1)S(1)}, u32[]{:S(2)}, u32[]{:S(2)}) collective-permute-start(bf16[2,384,128]{2,1,0:T(8,128)(2,1)S(1)} %get-tuple-element.34), channel_id=1, source_target_pairs={{0,192},{16,208},{32,224},{48,240},{64,256},{80,272},{96,288},{112... | collective-permute-start | bytes 589832 | tf_op jit(solution)/shard_map/ppermute | solution.py:37
  151.8 5.2 %collective-permute-start.14 = (bf16[2,384,128]{2,1,0:T(8,128)(2,1)S(1)}, bf16[2,384,128]{2,1,0:T(8,128)(2,1)S(1)}, u32[]{:S(2)}, u32[]{:S(2)}) collective-permute-start(bf16[2,384,128]{2,1,0:T(8,128)(2,1)S(1)} %get-tuple-element.33), channel_id=1, source_target_pairs={{0,384},{16,400},{32,416},{48,432},{64,448},{80,464},{96,480},{112... | collective-permute-start | bytes 589832 | tf_op jit(solution)/shard_map/ppermute | solution.py:37
  157.1 2.1 %collective-permute-start.15 = (bf16[2,384,128]{2,1,0:T(8,128)(2,1)S(1)}, bf16[2,384,128]{2,1,0:T(8,128)(2,1)S(1)}, u32[]{:S(2)}, u32[]{:S(2)}) collective-permute-start(bf16[2,384,128]{2,1,0:T(8,128)(2,1)S(1)} %get-tuple-element.32), channel_id=1, source_target_pairs={{0,576},{16,592},{32,608},{48,624},{64,640},{80,656},{96,672},{112... | collective-permute-start | bytes 589832 | tf_op jit(solution)/shard_map/ppermute | solution.py:37
  159.2 0.0 collective-permute-done.12
  159.2 0.0 collective-permute-done.13.far1
  159.2 1.7 collective-permute-done.14.far2
  160.9 3.7 %collective-permute-done.15.far3 = bf16[2,384,128]{2,1,0:T(8,128)(2,1)S(1)} collective-permute-done((bf16[2,384,128]{2,1,0:T(8,128)(2,1)S(1)}, bf16[2,384,128]{2,1,0:T(8,128)(2,1)S(1)}, u32[]{:S(2)}, u32[]{:S(2)}) %collective-permute-start.15) | collective-permute-done | bytes 196640 | tf_op jit(solution)/shard_map/ppermute | solution.py:37
  164.6 0.8 grad_sum.1
  165.4 0.1 chunk_sum.1
  165.5 0.7 copy.10
  (28 shorter events, 0.2 us)
Async XLA Ops:
  7.2 17.6 %copy-start.12 = (bf16[384,256]{1,0:T(8,128)(2,1)S(1)}, bf16[384,256]{1,0:T(8,128)(2,1)}, u32[]{:S(2)}) copy-start(bf16[384,256]{1,0:T(8,128)(2,1)} %param.9) | copy-start | bytes 589828
  7.2 59.2 %copy-start.10 = (bf16[384,128]{1,0:T(8,128)(2,1)S(1)}, bf16[384,128]{1,0:T(8,128)(2,1)}, u32[]{:S(2)}) copy-start(bf16[384,128]{1,0:T(8,128)(2,1)} %param.8) | copy-start | bytes 294916
  7.2 59.2 %copy-start.11 = (bf16[384,128]{1,0:T(8,128)(2,1)S(1)}, bf16[384,128]{1,0:T(8,128)(2,1)}, u32[]{:S(2)}) copy-start(bf16[384,128]{1,0:T(8,128)(2,1)} %param.7) | copy-start | bytes 294916
  7.2 100.3 %all-gather.2.cloned.1.call-start = ((), (), s32[]{:S(2)}) async-start(), calls=%async_computation.3 | async-start | bytes 1769472 | tf_op jit(solution)/shard_map/all_gather | solution.py:194
  9.6 55.7 %all-to-all-start = ((bf16[24,88,128]{2,1,0:T(8,128)(2,1)}), bf16[24,88,128]{2,1,0:T(8,128)(2,1)S(1)}, u32[]{:S(2)}, u32[]{:S(2)}) async-start(bf16[24,88,128]{2,1,0:T(8,128)(2,1)} %broadcast_in_dim.6), calls=%async_computation | async-start | bytes 1081344 | tf_op jit(solution)/shard_map/all_to_all | solution.py:197
  24.7 26.5 %collective-permute-start.3 = (bf16[384,256]{1,0:T(8,128)(2,1)S(1)}, bf16[384,256]{1,0:T(8,128)(2,1)S(1)}, u32[]{:S(2)}, u32[]{:S(2)}) collective-permute-start(bf16[384,256]{1,0:T(8,128)(2,1)S(1)} %copy-done.12), channel_id=1, source_target_pairs={{0,1},{1,0},{2,3},{3,2},{4,5},{5,4},{6,7},{7,6},{8,9},{9,8},{10,11... | collective-permute-start | bytes 589832 | tf_op jit(solution)/shard_map/ppermute | solution.py:52
  51.2 8.4 %collective-permute-start.4 = (bf16[384,256]{1,0:T(8,128)(2,1)S(1)}, bf16[384,256]{1,0:T(8,128)(2,1)S(1)}, u32[]{:S(2)}, u32[]{:S(2)}) collective-permute-start(bf16[384,256]{1,0:T(8,128)(2,1)S(1)} %collective-permute-done.3.refs_0_), channel_id=1, source_target_pairs={{0,2},{1,3},{2,4},{3,5},{4,6},{5,7},{6,8},{7,9},{8,10},{9,11},{10,... | collective-permute-start | bytes 589832 | tf_op jit(solution)/shard_map/ppermute | solution.py:57
  55.9 28.8 %collective-permute-start.5 = (bf16[384,256]{1,0:T(8,128)(2,1)S(1)}, bf16[384,256]{1,0:T(8,128)(2,1)S(1)}, u32[]{:S(2)}, u32[]{:S(2)}) collective-permute-start(bf16[384,256]{1,0:T(8,128)(2,1)S(1)} %collective-permute-done.3.refs_0_), channel_id=1, source_target_pairs={{0,14},{1,15},{2,0},{3,1},{4,2},{5,3},{6,4},{7,5},{8,6},{9,7},{10,... | collective-permute-start | bytes 589832 | tf_op jit(solution)/shard_map/ppermute | solution.py:57
  59.6 7.8 %copy-start.4 = (bf16[384,256]{1,0:T(8,128)(2,1)}, bf16[384,256]{1,0:T(8,128)(2,1)S(1)}, u32[]{:S(2)}) copy-start(bf16[384,256]{1,0:T(8,128)(2,1)S(1)} %collective-permute-done.4.refs_1_) | copy-start | bytes 589828
  59.6 27.1 %collective-permute-start.6 = (bf16[384,256]{1,0:T(8,128)(2,1)S(1)}, bf16[384,256]{1,0:T(8,128)(2,1)S(1)}, u32[]{:S(2)}, u32[]{:S(2)}) collective-permute-start(bf16[384,256]{1,0:T(8,128)(2,1)S(1)} %collective-permute-done.4.refs_1_), channel_id=1, source_target_pairs={{0,2},{1,3},{2,4},{3,5},{4,6},{5,7},{6,8},{7,9},{8,10},{9,11},{10,... | collective-permute-start | bytes 589832 | tf_op jit(solution)/shard_map/ppermute | solution.py:57
  67.4 25.1 %copy-start.13 = (s32[3,6]{1,0:T(4,128)S(1)}, s32[3,6]{1,0:T(4,128)}, u32[]{:S(2)}) copy-start(s32[3,6]{1,0:T(4,128)} %param.11) | copy-start | bytes 220
  67.4 37.1 %all-to-all-start.1 = ((bf16[4,2,384,128]{3,2,1,0:T(8,128)(2,1)}), bf16[4,2,384,128]{3,2,1,0:T(8,128)(2,1)S(1)}, u32[]{:S(2)}, u32[]{:S(2)}) async-start(bf16[4,2,384,128]{3,2,1,0:T(8,128)(2,1)} %broadcast_in_dim.8), calls=%async_computation.1 | async-start | bytes 1572864 | tf_op jit(solution)/shard_map/all_to_all | solution.py:204
  72.4 29.7 %collective-permute-start.2 = (bf16[24,88,128]{2,1,0:T(8,128)(2,1)S(1)}, bf16[24,88,128]{2,1,0:T(8,128)(2,1)S(1)}, u32[]{:S(2)}, u32[]{:S(2)}) collective-permute-start(bf16[24,88,128]{2,1,0:T(8,128)(2,1)S(1)} %all-to-all-done.own), channel_id=1, source_target_pairs={{0,16},{16,0},{32,48},{48,32},{64,80},{80,64},{96,112},{112,96},{1... | collective-permute-start | bytes 1622024 | tf_op jit(solution)/shard_map/ppermute | solution.py:48
  74.3 27.7 %collective-permute-start.1 = (bf16[2,128,128]{2,1,0:T(8,128)(2,1)S(1)}, bf16[2,128,128]{2,1,0:T(8,128)(2,1)S(1)}, u32[]{:S(2)}, u32[]{:S(2)}) collective-permute-start(bf16[2,128,128]{2,1,0:T(8,128)(2,1)S(1)} %get-tuple-element.37), channel_id=1, source_target_pairs={{0,16},{16,0},{32,48},{48,32},{64,80},{80,64},{96,112},{112,96},{1... | collective-permute-start | bytes 196616 | tf_op jit(solution)/shard_map/ppermute | solution.py:48
  76.7 25.3 %collective-permute-start = (bf16[2,128,128]{2,1,0:T(8,128)(2,1)S(1)}, bf16[2,128,128]{2,1,0:T(8,128)(2,1)S(1)}, u32[]{:S(2)}, u32[]{:S(2)}) collective-permute-start(bf16[2,128,128]{2,1,0:T(8,128)(2,1)S(1)} %get-tuple-element.38), channel_id=1, source_target_pairs={{0,752},{16,32},{32,16},{48,64},{64,48},{80,96},{96,80},{112,128},... | collective-permute-start | bytes 196616 | tf_op jit(solution)/shard_map/ppermute | solution.py:43
  84.7 17.3 %copy-start.6 = (bf16[384,256]{1,0:T(8,128)(2,1)}, bf16[384,256]{1,0:T(8,128)(2,1)S(1)}, u32[]{:S(2)}) copy-start(bf16[384,256]{1,0:T(8,128)(2,1)S(1)} %collective-permute-done.5.refs_2_) | copy-start | bytes 589828
  84.8 9.9 %collective-permute-start.7 = (bf16[384,256]{1,0:T(8,128)(2,1)S(1)}, bf16[384,256]{1,0:T(8,128)(2,1)}, u32[]{:S(2)}, u32[]{:S(2)}) collective-permute-start(bf16[384,256]{1,0:T(8,128)(2,1)S(1)} %collective-permute-done.5.refs_2_), channel_id=1, source_target_pairs={{0,14},{1,15},{2,0},{3,1},{4,2},{5,3},{6,4},{7,5},{8,6},{9,7},{10,... | collective-permute-start | bytes 589832 | tf_op jit(solution)/shard_map/ppermute | solution.py:57
  86.7 9.9 %collective-permute-start.8 = (bf16[384,256]{1,0:T(8,128)(2,1)S(1)}, bf16[384,256]{1,0:T(8,128)(2,1)}, u32[]{:S(2)}, u32[]{:S(2)}) collective-permute-start(bf16[384,256]{1,0:T(8,128)(2,1)S(1)} %collective-permute-done.6.refs_3_), channel_id=1, source_target_pairs={{0,2},{1,3},{2,4},{3,5},{4,6},{5,7},{6,8},{7,9},{8,10},{9,11},{10,... | collective-permute-start | bytes 589832 | tf_op jit(solution)/shard_map/ppermute | solution.py:57
  91.8 0.7 copy-start.8
  94.6 12.9 %collective-permute-start.9 = (bf16[384,256]{1,0:T(8,128)(2,1)}, bf16[384,256]{1,0:T(8,128)(2,1)}, u32[]{:S(2)}, u32[]{:S(2)}) collective-permute-start(bf16[384,256]{1,0:T(8,128)(2,1)} %collective-permute-done.7.refs_4_), channel_id=1, source_target_pairs={{0,14},{1,15},{2,0},{3,1},{4,2},{5,3},{6,4},{7,5},{8,6},{9,7},{10,... | collective-permute-start | bytes 589832 | tf_op jit(solution)/shard_map/ppermute | solution.py:57
  96.6 10.9 %collective-permute-start.10 = (bf16[384,256]{1,0:T(8,128)(2,1)}, bf16[384,256]{1,0:T(8,128)(2,1)}, u32[]{:S(2)}, u32[]{:S(2)}) collective-permute-start(bf16[384,256]{1,0:T(8,128)(2,1)} %collective-permute-done.8.refs_5_), channel_id=1, source_target_pairs={{0,2},{1,3},{2,4},{3,5},{4,6},{5,7},{6,8},{7,9},{8,10},{9,11},{10,... | collective-permute-start | bytes 589832 | tf_op jit(solution)/shard_map/ppermute | solution.py:57
  102.1 2.4 %copy-start.3 = (bf16[384,128]{1,0:T(8,128)(2,1)S(1)}, bf16[384,128]{1,0:T(8,128)(2,1)}, u32[]{:S(2)}) copy-start(bf16[384,128]{1,0:T(8,128)(2,1)} %q.3) | copy-start | bytes 294916
  104.5 3.1 %copy-start.5 = (bf16[384,256]{1,0:T(8,128)(2,1)S(1)}, bf16[384,256]{1,0:T(8,128)(2,1)}, u32[]{:S(2)}) copy-start(bf16[384,256]{1,0:T(8,128)(2,1)} %copy-done.4) | copy-start | bytes 589828
  104.5 3.0 %copy-start.7 = (bf16[384,256]{1,0:T(8,128)(2,1)S(1)}, bf16[384,256]{1,0:T(8,128)(2,1)}, u32[]{:S(2)}) copy-start(bf16[384,256]{1,0:T(8,128)(2,1)} %copy-done.6) | copy-start | bytes 589828
  104.5 3.0 %copy-start.9 = (bf16[384,256]{1,0:T(8,128)(2,1)S(1)}, bf16[384,256]{1,0:T(8,128)(2,1)}, u32[]{:S(2)}) copy-start(bf16[384,256]{1,0:T(8,128)(2,1)} %copy-done.8) | copy-start | bytes 589828
  106.5 1.0 copy-start.1
  107.5 1.4 copy-start
  114.5 4.6 %collective-permute-start.16 = (f32[24,88,128]{2,1,0:T(8,128)S(1)}, f32[24,88,128]{2,1,0:T(8,128)S(1)}, u32[]{:S(2)}, u32[]{:S(2)}) collective-permute-start(f32[24,88,128]{2,1,0:T(8,128)S(1)} %get-tuple-element.27), channel_id=1, source_target_pairs={{0,16},{16,0},{32,48},{48,32},{64,80},{80,64},{96,112},{112,96},{1... | collective-permute-start | bytes 3244040 | tf_op jit(solution)/shard_map/ppermute | solution.py:48
  120.1 45.3 %all-to-all-start.2 = ((bf16[24,88,128]{2,1,0:T(8,128)(2,1)}), bf16[24,88,128]{2,1,0:T(8,128)(2,1)S(1)}, u32[]{:S(2)}, u32[]{:S(2)}) async-start(bf16[24,88,128]{2,1,0:T(8,128)(2,1)} %add_convert_fusion), calls=%async_computation.2 | async-start | bytes 1081344 | tf_op jit(solution)/shard_map/all_to_all | solution.py:256
  134.6 1.3 copy-start.2
  138.2 21.0 %collective-permute-start.12 = (bf16[2,128,128]{2,1,0:T(8,128)(2,1)S(1)}, bf16[2,128,128]{2,1,0:T(8,128)(2,1)S(1)}, u32[]{:S(2)}, u32[]{:S(2)}) collective-permute-start(bf16[2,128,128]{2,1,0:T(8,128)(2,1)S(1)} %get-tuple-element.41), channel_id=1, source_target_pairs={{0,16},{16,0},{32,48},{48,32},{64,80},{80,64},{96,112},{112,96},{1... | collective-permute-start | bytes 196616 | tf_op jit(solution)/shard_map/ppermute | solution.py:48
  140.1 19.1 %collective-permute-start.11 = (bf16[2,128,128]{2,1,0:T(8,128)(2,1)S(1)}, bf16[2,128,128]{2,1,0:T(8,128)(2,1)S(1)}, u32[]{:S(2)}, u32[]{:S(2)}) collective-permute-start(bf16[2,128,128]{2,1,0:T(8,128)(2,1)S(1)} %get-tuple-element.42), channel_id=1, source_target_pairs={{0,752},{16,32},{32,16},{48,64},{64,48},{80,96},{96,80},{112,128},... | collective-permute-start | bytes 196616 | tf_op jit(solution)/shard_map/ppermute | solution.py:43
  148.4 10.8 %collective-permute-start.13 = (bf16[2,384,128]{2,1,0:T(8,128)(2,1)S(1)}, bf16[2,384,128]{2,1,0:T(8,128)(2,1)S(1)}, u32[]{:S(2)}, u32[]{:S(2)}) collective-permute-start(bf16[2,384,128]{2,1,0:T(8,128)(2,1)S(1)} %get-tuple-element.34), channel_id=1, source_target_pairs={{0,192},{16,208},{32,224},{48,240},{64,256},{80,272},{96,288},{112... | collective-permute-start | bytes 589832 | tf_op jit(solution)/shard_map/ppermute | solution.py:37
  151.8 9.1 %collective-permute-start.14 = (bf16[2,384,128]{2,1,0:T(8,128)(2,1)S(1)}, bf16[2,384,128]{2,1,0:T(8,128)(2,1)S(1)}, u32[]{:S(2)}, u32[]{:S(2)}) collective-permute-start(bf16[2,384,128]{2,1,0:T(8,128)(2,1)S(1)} %get-tuple-element.33), channel_id=1, source_target_pairs={{0,384},{16,400},{32,416},{48,432},{64,448},{80,464},{96,480},{112... | collective-permute-start | bytes 589832 | tf_op jit(solution)/shard_map/ppermute | solution.py:37
  157.1 7.6 %collective-permute-start.15 = (bf16[2,384,128]{2,1,0:T(8,128)(2,1)S(1)}, bf16[2,384,128]{2,1,0:T(8,128)(2,1)S(1)}, u32[]{:S(2)}, u32[]{:S(2)}) collective-permute-start(bf16[2,384,128]{2,1,0:T(8,128)(2,1)S(1)} %get-tuple-element.32), channel_id=1, source_target_pairs={{0,576},{16,592},{32,608},{48,624},{64,640},{80,656},{96,672},{112... | collective-permute-start | bytes 589832 | tf_op jit(solution)/shard_map/ppermute | solution.py:37
Sparse Core Ops, SparseCore 0:
  10.4 51.4 all-gather.1

commit v3 on v2

--- a/solution.py
+++ b/solution.py
@@ -52,13 +52,8 @@
     return lax.ppermute(value, "tp", [(s, s ^ 1) for s in range(N_TP)])
 
 
-def y_shift(value, steps):
-    pairs = [(2 * y + z, 2 * ((y + steps) % NY) + z) for y in range(NY) for z in range(2)]
-    return lax.ppermute(value, "tp", pairs)
-
-
-def after(value, shards):
-    return jnp.where(shards[0, SHARD, 0] == 0, value, jnp.zeros_like(value))
+def after(value, element):
+    return jnp.where(element < jnp.inf, value, jnp.zeros_like(value))
 
 
 def select(meta, j, which, kv, prev, nxt, far):
@@ -99,26 +94,13 @@
             w_out[t, :, e * 128 : (e + 1) * 128] = rows.astype(BF16)
 
 
-RING = (0, -1, 1, -2, 2, -3, 3, -4)
-
-
-def cotangent_kernel(meta, w, att, near_hbm, *refs):
-    ring = refs[:NY]
-    keep, give, grad, near, cols, flat, sem = refs[NY:]
-    copy = pltpu.make_async_copy(near_hbm, near, sem)
-    copy.start()
-    y, z = meta[M_Y], meta[M_Z]
+def cotangent_kernel(meta, w, att, pieces, keep, give, grad, cols, flat):
+    z = meta[M_Z]
     att_now = att[...]
     total = jnp.zeros((384, DH), F32)
-    for piece, step in zip(ring, RING):
-        col = 2 * ((y + step + NY) % NY) + 1 - z
-        cot = piece[...]
-        cols[col] = dot(att_now, cot, 0, 0)
-        total = total + dot(cot, w[col], 1, 1)
-    copy.wait()
-    for i in range(NY):
-        col = 2 * i + z
-        cot = near[i * 384 : (i + 1) * 384]
+    for i in range(N_TP):
+        col = 2 * (i // 2) + (z if i % 2 == 0 else 1 - z)
+        cot = pieces[i * 384 : (i + 1) * 384]
         cols[col] = dot(att_now, cot, 0, 0)
         total = total + dot(cot, w[col], 1, 1)
     grad[...] = total.astype(BF16)
@@ -191,28 +173,23 @@
     place = jnp.stack([ctx // (2 * NZ), ctx % 2, tp // 2, tp % 2]).astype(jnp.int32)
     meta = jnp.concatenate([picked, place])
 
-    near = lax.all_gather(cotangent, "tp", axis=0, tiled=True, axis_index_groups=Y_GROUPS)
     twin = twin_swap(cotangent)
-    w_pad = jnp.pad(w_flat[0], ((0, SHARD_PAD - SHARD), (0, 0)))
+    pieces = lax.all_gather(
+        jnp.concatenate([cotangent, twin], axis=0),
+        "tp", axis=0, tiled=True, axis_index_groups=Y_GROUPS,
+    )
+    w_pad = jnp.concatenate([w_flat[0], twin[: SHARD_PAD - SHARD, :128]], axis=0)
     w_own = lax.all_to_all(
         jnp.broadcast_to(w_pad[None], (CHIPS, SHARD_PAD, 128)),
         "ctx", 0, 0, tiled=True, axis_index_groups=SAME_CORE,
     )
-    kv = jnp.stack([key_rows, values])
+    kv = after(jnp.stack([key_rows, values]), twin[0, 0])
     even = ctx % 2 == 0
     prev, nxt = neighbours(kv[:, :BLK], kv[:, 2 * BLK :], even)
     far = lax.all_to_all(
-        jnp.broadcast_to(after(kv, w_own)[None], (NX,) + kv.shape),
+        jnp.broadcast_to(after(kv, w_own[0, 0, 0])[None], (NX,) + kv.shape),
         "ctx", 0, 0, tiled=True, axis_index_groups=X_GROUPS,
     )
-    up, down = twin, twin
-    ring = [twin]
-    for step in range(1, 4):
-        up = y_shift(up, 1)
-        down = y_shift(down, -1)
-        ring += [up, down]
-    ring.append(y_shift(up, 1))
-
     w_other = core_swap(w_own)
     flat_alloc = N_CTX * SHARD + 8
     weight = pl.pallas_call(
@@ -241,17 +218,15 @@
     keep, give, out_grad = pl.pallas_call(
         cotangent_kernel,
         out_shape=(chunk, chunk, jax.ShapeDtypeStruct((384, DH), BF16)),
-        in_specs=[SMEM, VMEM, VMEM, pl.BlockSpec(memory_space=pltpu.HBM)] + [VMEM] * NY,
+        in_specs=[SMEM, VMEM, VMEM, VMEM],
         out_specs=(VMEM, VMEM, VMEM),
         scratch_shapes=[
-            pltpu.VMEM((NY * 384, WCOL), BF16),
             pltpu.VMEM((N_TP, DH, WCOL), F32),
             pltpu.VMEM((flat_alloc, 128), F32),
-            pltpu.SemaphoreType.DMA,
         ],
         compiler_params=PARAMS,
         name="cotangent_products",
-    )(meta, weight, att, near, *ring)
+    )(meta, weight, att, pieces)
     pair_sum = (keep + core_swap(give)).astype(BF16)
     spread = lax.all_to_all(
         pair_sum, "ctx", 0, 0, tiled=True, axis_index_groups=SAME_CORE

time: 174 us -> 157 us (0.902)
  the two profiles are of different devices: /device:TPU:26 before, /device:TPU:42 now
where the time goes in v3:
time: 157 us; the launch traced here: 156 us
  starting transfers between devices  80.7 us (51%)
  waiting for transfers between devices  38.4 us (24%)
  between operations  15.7 us (10%)
  Pallas kernels  11.8 us (8%)
  local copies, waits for them, and re-layouts  6.3 us (4%)
  other arithmetic  2.83 us (2%)
    all_to_all x1, waiting for transfers between devices, on_device(): lax.all_to_all(jnp.broadcast_to(w_pad[None], (CHIPS, SHARD_PAD, 128)), 'c...  20.1 us
    all_to_all x1, starting transfers between devices, on_device(): lax.all_to_all(jnp.broadcast_to(w_pad[None], (CHIPS, SHARD_PAD, 128)), 'c...  17.6 us
    ppermute x1, starting transfers between devices, twin_swap(): return lax.ppermute(value, 'tp', [(s, s ^ 1) for s in range(N_TP)])  15.1 us
    ppermute x2, starting transfers between devices, neighbours(): outer = lax.ppermute(jnp.where(even, first, last), 'ctx', pairs)  14.4 us
    ppermute x3, starting transfers between devices, x_shift(): return lax.ppermute(value, 'ctx', pairs)  10.7 us
    all_to_all x1, starting transfers between devices, on_device(): lax.all_to_all(pair_sum, 'ctx', 0, 0, tiled=True, axis_index_groups=SAME_...  10.1 us
    ppermute x4, starting transfers between devices, core_swap(): return lax.ppermute(value, 'ctx', [(s, s ^ 1) for s in range(N_CTX)])  8.14 us
    ppermute x3, waiting for transfers between devices, x_shift(): return lax.ppermute(value, 'ctx', pairs)  5.38 us
  transfers between devices with their start and end apart: 14, of which 6 were waited for; matrix products, arithmetic and copies ran while one was open for 2% of the time, Pallas kernels for 5%

profile of v3, /device:TPU:42, one launch (start us, length us, event | category | flops | bytes accessed | tf_op | source)
XLA Modules:
  0.0 155.8 jit_solution(4808865397490275541)
XLA Ops:
  7.2 0.0 copy-start.6
  7.2 0.0 all-gather.2.cloned.1.call-start
  7.2 15.1 %collective-permute-start = (bf16[384,256]{1,0:T(8,128)(2,1)}, bf16[384,256]{1,0:T(8,128)(2,1)S(1)}, u32[]{:S(2)}, u32[]{:S(2)}) collective-permute-start(bf16[384,256]{1,0:T(8,128)(2,1)} %param.9), channel_id=1, source_target_pairs={{0,1},{1,0},{2,3},{3,2},{4,5},{5,4},{6,7},{7,6},{8,9},{9,8},{10,11... | collective-permute-start | bytes 589832 | tf_op jit(solution)/shard_map/ppermute | solution.py:52
  22.4 5.3 %collective-permute-done = bf16[384,256]{1,0:T(8,128)(2,1)S(1)} collective-permute-done((bf16[384,256]{1,0:T(8,128)(2,1)}, bf16[384,256]{1,0:T(8,128)(2,1)S(1)}, u32[]{:S(2)}, u32[]{:S(2)}) %collective-permute-start) | collective-permute-done | bytes 196640 | tf_op jit(solution)/shard_map/ppermute | solution.py:52
  27.7 1.7 %pad_maximum_fusion = bf16[768,256]{1,0:T(8,128)(2,1)} fusion(bf16[384,256]{1,0:T(8,128)(2,1)S(1)} %collective-permute-done, bf16[384,256]{1,0:T(8,128)(2,1)} %param.9), kind=kLoop, calls=%fused_computation.1 | loop fusion | flops 786432 | bytes 786432 | tf_op jit(solution)/shard_map/concatenate | solution.py:178
  29.4 0.0 copy-start.4
  29.4 0.0 copy-start.5
  29.4 0.0 all-gather.2.cloned.1.call-update
  29.4 0.0 copy-done.6
  29.4 0.9 broadcast_in_dim.4
  30.3 17.6 %all-to-all-start = ((bf16[24,88,128]{2,1,0:T(8,128)(2,1)}), bf16[24,88,128]{2,1,0:T(8,128)(2,1)S(1)}, u32[]{:S(2)}, u32[]{:S(2)}) async-start(bf16[24,88,128]{2,1,0:T(8,128)(2,1)} %broadcast_in_dim.4), calls=%async_computation | async-start | bytes 1081344 | tf_op jit(solution)/shard_map/all_to_all | solution.py:182
  47.9 0.5 slice.36
  49.1 20.1 %all-to-all-done.own = bf16[24,88,128]{2,1,0:T(8,128)(2,1)S(1)} async-done(((bf16[24,88,128]{2,1,0:T(8,128)(2,1)}), bf16[24,88,128]{2,1,0:T(8,128)(2,1)S(1)}, u32[]{:S(2)}, u32[]{:S(2)}) %all-to-all-start) | async-done | bytes 540704 | tf_op jit(solution)/shard_map/all_to_all | solution.py:182
  69.2 0.5 slice.40
  70.4 0.0 copy-done.4
  70.4 0.0 copy-done.5
  70.4 1.0 broadcast_in_dim.5
  71.4 0.0 copy-start.7
  71.4 4.7 %all-to-all-start.1 = ((bf16[4,2,384,128]{3,2,1,0:T(8,128)(2,1)}), bf16[4,2,384,128]{3,2,1,0:T(8,128)(2,1)S(1)}, u32[]{:S(2)}, u32[]{:S(2)}) async-start(bf16[4,2,384,128]{3,2,1,0:T(8,128)(2,1)} %broadcast_in_dim.5), calls=%async_computation.1 | async-start | bytes 1572864 | tf_op jit(solution)/shard_map/all_to_all | solution.py:189
  76.1 1.9 %collective-permute-start.3 = (bf16[24,88,128]{2,1,0:T(8,128)(2,1)S(1)}, bf16[24,88,128]{2,1,0:T(8,128)(2,1)S(1)}, u32[]{:S(2)}, u32[]{:S(2)}) collective-permute-start(bf16[24,88,128]{2,1,0:T(8,128)(2,1)S(1)} %all-to-all-done.own), channel_id=1, source_target_pairs={{0,16},{16,0},{32,48},{48,32},{64,80},{80,64},{96,112},{112,96},{1... | collective-permute-start | bytes 1622024 | tf_op jit(solution)/shard_map/ppermute | solution.py:48
  78.0 2.4 %collective-permute-start.2 = (bf16[2,128,128]{2,1,0:T(8,128)(2,1)S(1)}, bf16[2,128,128]{2,1,0:T(8,128)(2,1)S(1)}, u32[]{:S(2)}, u32[]{:S(2)}) collective-permute-start(bf16[2,128,128]{2,1,0:T(8,128)(2,1)S(1)} %get-tuple-element.37), channel_id=1, source_target_pairs={{0,16},{16,0},{32,48},{48,32},{64,80},{80,64},{96,112},{112,96},{1... | collective-permute-start | bytes 196616 | tf_op jit(solution)/shard_map/ppermute | solution.py:48
  80.4 6.1 %collective-permute-start.1 = (bf16[2,128,128]{2,1,0:T(8,128)(2,1)S(1)}, bf16[2,128,128]{2,1,0:T(8,128)(2,1)S(1)}, u32[]{:S(2)}, u32[]{:S(2)}) collective-permute-start(bf16[2,128,128]{2,1,0:T(8,128)(2,1)S(1)} %get-tuple-element.38), channel_id=1, source_target_pairs={{0,752},{16,32},{32,16},{48,64},{64,48},{80,96},{96,80},{112,128},... | collective-permute-start | bytes 196616 | tf_op jit(solution)/shard_map/ppermute | solution.py:43
  86.5 0.0 copy-done.7
  86.5 0.1 add_select_fusion
  86.6 0.1 reshape.34
  86.7 0.1 concatenate.13.meta
  86.8 0.0 collective-permute-done.2
  86.8 4.9 %collective-permute-done.1 = bf16[2,128,128]{2,1,0:T(8,128)(2,1)S(1)} collective-permute-done((bf16[2,128,128]{2,1,0:T(8,128)(2,1)S(1)}, bf16[2,128,128]{2,1,0:T(8,128)(2,1)S(1)}, u32[]{:S(2)}, u32[]{:S(2)}) %collective-permute-start.1) | collective-permute-done | bytes 65568 | tf_op jit(solution)/shard_map/ppermute | solution.py:43
  91.7 0.0 copy-start.1
  91.7 0.0 collective-permute-done.3.other
  91.8 2.4 %weight_rows.1.w = bf16[16,128,256]{2,1,0:T(8,128)(2,1)S(1)} custom-call(s32[13]{0:T(128)S(1)} %concatenate.13.meta, bf16[24,88,128]{2,1,0:T(8,128)(2,1)S(1)} %all-to-all-done.own, bf16[24,88,128]{2,1,0:T(8,128)(2,1)S(1)} %collective-permute-done.3.other), custom_call_target="tpu_custom_call" | custom-call | tf_op jit(solution)/shard_map/weight_rows/pallas_call | solution.py:195
  94.1 0.0 all-to-all-done.1.far
  94.1 0.0 copy-done.1
  94.1 1.9 %attention_forward.1 = (f32[3,128,768]{2,1,0:T(8,128)S(1)}, bf16[384,128]{1,0:T(8,128)(2,1)S(1)}) custom-call(s32[13]{0:T(128)S(1)} %concatenate.13.meta, bf16[384,128]{1,0:T(8,128)(2,1)S(1)} %copy-done.1, bf16[2,384,128]{2,1,0:T(8,128)(2,1)S(1)} %get-tuple-element.33.kv, bf16[2,128,128]{2,1,0:T(8,128)(2,1)S(1)} %get-tuple-element.44.prev, ...), custom_call_target="tpu_custom_call" | custom-call | tf_op jit(solution)/shard_map/attention_forward/pallas_call | solution.py:205
  96.1 0.0 all-gather.2.cloned.1.call-done.pieces
  96.1 0.0 copy-start
  96.1 1.9 %copy-done = bf16[6144,256]{1,0:T(8,128)(2,1)S(1)} copy-done((bf16[6144,256]{1,0:T(8,128)(2,1)S(1)}, bf16[6144,256]{1,0:T(8,128)(2,1)}, u32[]{:S(2)}) %copy-start) | copy-done | bytes 3145752
  98.0 4.4 %cotangent_products.1 = (f32[24,88,128]{2,1,0:T(8,128)S(1)}, f32[24,88,128]{2,1,0:T(8,128)S(1)}, bf16[384,128]{1,0:T(8,128)(2,1)S(1)}) custom-call(s32[13]{0:T(128)S(1)} %concatenate.13.meta, bf16[16,128,256]{2,1,0:T(8,128)(2,1)S(1)} %weight_rows.1.w, bf16[384,128]{1,0:T(8,128)(2,1)S(1)} %get-tuple-element.17.att, bf16[6144,256]{1,0:T(8,128)(2,1)S(1)} %copy-done), custom_call_target="tpu_custom_call" | custom-call | tf_op jit(solution)/shard_map/cotangent_products/pallas_call | solution.py:218
  102.4 0.0 copy-start.2
  102.4 0.6 copy-done.2
  103.0 1.9 %collective-permute-start.9 = (f32[24,88,128]{2,1,0:T(8,128)S(1)}, f32[24,88,128]{2,1,0:T(8,128)S(1)}, u32[]{:S(2)}, u32[]{:S(2)}) collective-permute-start(f32[24,88,128]{2,1,0:T(8,128)S(1)} %get-tuple-element.27), channel_id=1, source_target_pairs={{0,16},{16,0},{32,48},{48,32},{64,80},{80,64},{96,112},{112,96},{1... | collective-permute-start | bytes 3244040 | tf_op jit(solution)/shard_map/ppermute | solution.py:48
  105.0 2.7 %collective-permute-done.9 = f32[24,88,128]{2,1,0:T(8,128)S(1)} collective-permute-done((f32[24,88,128]{2,1,0:T(8,128)S(1)}, f32[24,88,128]{2,1,0:T(8,128)S(1)}, u32[]{:S(2)}, u32[]{:S(2)}) %collective-permute-start.9) | collective-permute-done | bytes 1081376 | tf_op jit(solution)/shard_map/ppermute | solution.py:48
  107.6 0.9 add_convert_fusion
  108.6 0.0 copy-start.3
  108.6 10.1 %all-to-all-start.2 = ((bf16[24,88,128]{2,1,0:T(8,128)(2,1)}), bf16[24,88,128]{2,1,0:T(8,128)(2,1)S(1)}, u32[]{:S(2)}, u32[]{:S(2)}) async-start(bf16[24,88,128]{2,1,0:T(8,128)(2,1)} %add_convert_fusion), calls=%async_computation.2 | async-start | bytes 1081344 | tf_op jit(solution)/shard_map/all_to_all | solution.py:231
  118.7 0.0 copy-done.3
  118.7 2.3 %attention_backward.1 = (f32[384,128]{1,0:T(8,128)}, f32[2,384,128]{2,1,0:T(8,128)S(1)}, bf16[2,128,128]{2,1,0:T(8,128)(2,1)S(1)}, bf16[2,128,128]{2,1,0:T(8,128)(2,1)S(1)}, bf16[3,2,384,128]{3,2,1,0:T(8,128)(2,1)S(1)}) custom-call(s32[13]{0:T(128)S(1)} %concatenate.13.meta, bf16[384,128]{1,0:T(8,128)(2,1)S(1)} %copy-done.1, ...), custom_call_target="tpu_custom_call" | custom-call | tf_op jit(solution)/shard_map/attention_backward/pallas_call | solution.py:242
  121.0 1.9 %collective-permute-start.5 = (bf16[2,128,128]{2,1,0:T(8,128)(2,1)S(1)}, bf16[2,128,128]{2,1,0:T(8,128)(2,1)S(1)}, u32[]{:S(2)}, u32[]{:S(2)}) collective-permute-start(bf16[2,128,128]{2,1,0:T(8,128)(2,1)S(1)} %get-tuple-element.41), channel_id=1, source_target_pairs={{0,16},{16,0},{32,48},{48,32},{64,80},{80,64},{96,112},{112,96},{1... | collective-permute-start | bytes 196616 | tf_op jit(solution)/shard_map/ppermute | solution.py:48
  122.9 8.3 %collective-permute-start.4 = (bf16[2,128,128]{2,1,0:T(8,128)(2,1)S(1)}, bf16[2,128,128]{2,1,0:T(8,128)(2,1)S(1)}, u32[]{:S(2)}, u32[]{:S(2)}) collective-permute-start(bf16[2,128,128]{2,1,0:T(8,128)(2,1)S(1)} %get-tuple-element.42), channel_id=1, source_target_pairs={{0,752},{16,32},{32,16},{48,64},{64,48},{80,96},{96,80},{112,128},... | collective-permute-start | bytes 196616 | tf_op jit(solution)/shard_map/ppermute | solution.py:43
  131.2 3.4 %collective-permute-start.6 = (bf16[2,384,128]{2,1,0:T(8,128)(2,1)S(1)}, bf16[2,384,128]{2,1,0:T(8,128)(2,1)S(1)}, u32[]{:S(2)}, u32[]{:S(2)}) collective-permute-start(bf16[2,384,128]{2,1,0:T(8,128)(2,1)S(1)} %get-tuple-element.36), channel_id=1, source_target_pairs={{0,192},{16,208},{32,224},{48,240},{64,256},{80,272},{96,288},{112... | collective-permute-start | bytes 589832 | tf_op jit(solution)/shard_map/ppermute | solution.py:37
  134.6 5.2 %collective-permute-start.7 = (bf16[2,384,128]{2,1,0:T(8,128)(2,1)S(1)}, bf16[2,384,128]{2,1,0:T(8,128)(2,1)S(1)}, u32[]{:S(2)}, u32[]{:S(2)}) collective-permute-start(bf16[2,384,128]{2,1,0:T(8,128)(2,1)S(1)} %get-tuple-element.35), channel_id=1, source_target_pairs={{0,384},{16,400},{32,416},{48,432},{64,448},{80,464},{96,480},{112... | collective-permute-start | bytes 589832 | tf_op jit(solution)/shard_map/ppermute | solution.py:37
  139.9 2.1 %collective-permute-start.8 = (bf16[2,384,128]{2,1,0:T(8,128)(2,1)S(1)}, bf16[2,384,128]{2,1,0:T(8,128)(2,1)S(1)}, u32[]{:S(2)}, u32[]{:S(2)}) collective-permute-start(bf16[2,384,128]{2,1,0:T(8,128)(2,1)S(1)} %get-tuple-element.34), channel_id=1, source_target_pairs={{0,576},{16,592},{32,608},{48,624},{64,640},{80,656},{96,672},{112... | collective-permute-start | bytes 589832 | tf_op jit(solution)/shard_map/ppermute | solution.py:37
  142.0 0.0 collective-permute-done.5
  142.0 0.0 collective-permute-done.4
  142.0 0.0 collective-permute-done.6.far1
  142.0 1.9 %collective-permute-done.7.far2 = bf16[2,384,128]{2,1,0:T(8,128)(2,1)S(1)} collective-permute-done((bf16[2,384,128]{2,1,0:T(8,128)(2,1)S(1)}, bf16[2,384,128]{2,1,0:T(8,128)(2,1)S(1)}, u32[]{:S(2)}, u32[]{:S(2)}) %collective-permute-start.7) | collective-permute-done | bytes 196640 | tf_op jit(solution)/shard_map/ppermute | solution.py:37
  143.9 3.5 %collective-permute-done.8.far3 = bf16[2,384,128]{2,1,0:T(8,128)(2,1)S(1)} collective-permute-done((bf16[2,384,128]{2,1,0:T(8,128)(2,1)S(1)}, bf16[2,384,128]{2,1,0:T(8,128)(2,1)S(1)}, u32[]{:S(2)}, u32[]{:S(2)}) %collective-permute-start.8) | collective-permute-done | bytes 196640 | tf_op jit(solution)/shard_map/ppermute | solution.py:37
  147.4 0.8 grad_sum.1
  148.2 0.0 all-to-all-done.2.parts
  148.2 0.1 chunk_sum.1
  148.3 0.7 copy.10
  (8 shorter events, 0.2 us)
Async XLA Ops:
  7.2 22.2 %copy-start.6 = (bf16[1,86,128]{2,1,0:T(8,128)(2,1)S(1)}, bf16[1,86,128]{2,1,0:T(8,128)(2,1)}, u32[]{:S(2)}) copy-start(bf16[1,86,128]{2,1,0:T(8,128)(2,1)} %param.10) | copy-start | bytes 66052
  7.2 88.9 %all-gather.2.cloned.1.call-start = ((), (), s32[]{:S(2)}) async-start(), calls=%async_computation.3 | async-start | bytes 3538944 | tf_op jit(solution)/shard_map/all_gather | solution.py:177
  7.2 20.4 %collective-permute-start = (bf16[384,256]{1,0:T(8,128)(2,1)}, bf16[384,256]{1,0:T(8,128)(2,1)S(1)}, u32[]{:S(2)}, u32[]{:S(2)}) collective-permute-start(bf16[384,256]{1,0:T(8,128)(2,1)} %param.9), channel_id=1, source_target_pairs={{0,1},{1,0},{2,3},{3,2},{4,5},{5,4},{6,7},{7,6},{8,9},{9,8},{10,11... | collective-permute-start | bytes 589832 | tf_op jit(solution)/shard_map/ppermute | solution.py:52
  29.4 41.0 %copy-start.4 = (bf16[384,128]{1,0:T(8,128)(2,1)S(1)}, bf16[384,128]{1,0:T(8,128)(2,1)}, u32[]{:S(2)}) copy-start(bf16[384,128]{1,0:T(8,128)(2,1)} %param.8) | copy-start | bytes 294916
  29.4 41.0 %copy-start.5 = (bf16[384,128]{1,0:T(8,128)(2,1)S(1)}, bf16[384,128]{1,0:T(8,128)(2,1)}, u32[]{:S(2)}) copy-start(bf16[384,128]{1,0:T(8,128)(2,1)} %param.7) | copy-start | bytes 294916
  30.3 38.9 %all-to-all-start = ((bf16[24,88,128]{2,1,0:T(8,128)(2,1)}), bf16[24,88,128]{2,1,0:T(8,128)(2,1)S(1)}, u32[]{:S(2)}, u32[]{:S(2)}) async-start(bf16[24,88,128]{2,1,0:T(8,128)(2,1)} %broadcast_in_dim.4), calls=%async_computation | async-start | bytes 1081344 | tf_op jit(solution)/shard_map/all_to_all | solution.py:182
  71.4 15.1 %copy-start.7 = (s32[3,6]{1,0:T(4,128)S(1)}, s32[3,6]{1,0:T(4,128)}, u32[]{:S(2)}) copy-start(s32[3,6]{1,0:T(4,128)} %param.11) | copy-start | bytes 220
  71.4 22.7 %all-to-all-start.1 = ((bf16[4,2,384,128]{3,2,1,0:T(8,128)(2,1)}), bf16[4,2,384,128]{3,2,1,0:T(8,128)(2,1)S(1)}, u32[]{:S(2)}, u32[]{:S(2)}) async-start(bf16[4,2,384,128]{3,2,1,0:T(8,128)(2,1)} %broadcast_in_dim.5), calls=%async_computation.1 | async-start | bytes 1572864 | tf_op jit(solution)/shard_map/all_to_all | solution.py:189
  76.1 15.7 %collective-permute-start.3 = (bf16[24,88,128]{2,1,0:T(8,128)(2,1)S(1)}, bf16[24,88,128]{2,1,0:T(8,128)(2,1)S(1)}, u32[]{:S(2)}, u32[]{:S(2)}) collective-permute-start(bf16[24,88,128]{2,1,0:T(8,128)(2,1)S(1)} %all-to-all-done.own), channel_id=1, source_target_pairs={{0,16},{16,0},{32,48},{48,32},{64,80},{80,64},{96,112},{112,96},{1... | collective-permute-start | bytes 1622024 | tf_op jit(solution)/shard_map/ppermute | solution.py:48
  78.0 8.8 %collective-permute-start.2 = (bf16[2,128,128]{2,1,0:T(8,128)(2,1)S(1)}, bf16[2,128,128]{2,1,0:T(8,128)(2,1)S(1)}, u32[]{:S(2)}, u32[]{:S(2)}) collective-permute-start(bf16[2,128,128]{2,1,0:T(8,128)(2,1)S(1)} %get-tuple-element.37), channel_id=1, source_target_pairs={{0,16},{16,0},{32,48},{48,32},{64,80},{80,64},{96,112},{112,96},{1... | collective-permute-start | bytes 196616 | tf_op jit(solution)/shard_map/ppermute | solution.py:48
  80.4 11.3 %collective-permute-start.1 = (bf16[2,128,128]{2,1,0:T(8,128)(2,1)S(1)}, bf16[2,128,128]{2,1,0:T(8,128)(2,1)S(1)}, u32[]{:S(2)}, u32[]{:S(2)}) collective-permute-start(bf16[2,128,128]{2,1,0:T(8,128)(2,1)S(1)} %get-tuple-element.38), channel_id=1, source_target_pairs={{0,752},{16,32},{32,16},{48,64},{64,48},{80,96},{96,80},{112,128},... | collective-permute-start | bytes 196616 | tf_op jit(solution)/shard_map/ppermute | solution.py:43
  91.7 2.4 %copy-start.1 = (bf16[384,128]{1,0:T(8,128)(2,1)S(1)}, bf16[384,128]{1,0:T(8,128)(2,1)}, u32[]{:S(2)}) copy-start(bf16[384,128]{1,0:T(8,128)(2,1)} %q.3) | copy-start | bytes 294916
  96.1 1.9 %copy-start = (bf16[6144,256]{1,0:T(8,128)(2,1)S(1)}, bf16[6144,256]{1,0:T(8,128)(2,1)}, u32[]{:S(2)}) copy-start(bf16[6144,256]{1,0:T(8,128)(2,1)} %all-gather.2.cloned.1.call-done.pieces) | copy-start | bytes 9437188
  102.4 0.6 copy-start.2
  103.0 4.6 %collective-permute-start.9 = (f32[24,88,128]{2,1,0:T(8,128)S(1)}, f32[24,88,128]{2,1,0:T(8,128)S(1)}, u32[]{:S(2)}, u32[]{:S(2)}) collective-permute-start(f32[24,88,128]{2,1,0:T(8,128)S(1)} %get-tuple-element.27), channel_id=1, source_target_pairs={{0,16},{16,0},{32,48},{48,32},{64,80},{80,64},{96,112},{112,96},{1... | collective-permute-start | bytes 3244040 | tf_op jit(solution)/shard_map/ppermute | solution.py:48
  108.6 10.1 %copy-start.3 = (bf16[384,128]{1,0:T(8,128)(2,1)S(1)}, bf16[384,128]{1,0:T(8,128)(2,1)}, u32[]{:S(2)}) copy-start(bf16[384,128]{1,0:T(8,128)(2,1)} %copy-done.2) | copy-start | bytes 294916
  108.6 39.6 %all-to-all-start.2 = ((bf16[24,88,128]{2,1,0:T(8,128)(2,1)}), bf16[24,88,128]{2,1,0:T(8,128)(2,1)S(1)}, u32[]{:S(2)}, u32[]{:S(2)}) async-start(bf16[24,88,128]{2,1,0:T(8,128)(2,1)} %add_convert_fusion), calls=%async_computation.2 | async-start | bytes 1081344 | tf_op jit(solution)/shard_map/all_to_all | solution.py:231
  121.0 21.0 %collective-permute-start.5 = (bf16[2,128,128]{2,1,0:T(8,128)(2,1)S(1)}, bf16[2,128,128]{2,1,0:T(8,128)(2,1)S(1)}, u32[]{:S(2)}, u32[]{:S(2)}) collective-permute-start(bf16[2,128,128]{2,1,0:T(8,128)(2,1)S(1)} %get-tuple-element.41), channel_id=1, source_target_pairs={{0,16},{16,0},{32,48},{48,32},{64,80},{80,64},{96,112},{112,96},{1... | collective-permute-start | bytes 196616 | tf_op jit(solution)/shard_map/ppermute | solution.py:48
  122.9 19.1 %collective-permute-start.4 = (bf16[2,128,128]{2,1,0:T(8,128)(2,1)S(1)}, bf16[2,128,128]{2,1,0:T(8,128)(2,1)S(1)}, u32[]{:S(2)}, u32[]{:S(2)}) collective-permute-start(bf16[2,128,128]{2,1,0:T(8,128)(2,1)S(1)} %get-tuple-element.42), channel_id=1, source_target_pairs={{0,752},{16,32},{32,16},{48,64},{64,48},{80,96},{96,80},{112,128},... | collective-permute-start | bytes 196616 | tf_op jit(solution)/shard_map/ppermute | solution.py:43
  131.2 10.8 %collective-permute-start.6 = (bf16[2,384,128]{2,1,0:T(8,128)(2,1)S(1)}, bf16[2,384,128]{2,1,0:T(8,128)(2,1)S(1)}, u32[]{:S(2)}, u32[]{:S(2)}) collective-permute-start(bf16[2,384,128]{2,1,0:T(8,128)(2,1)S(1)} %get-tuple-element.36), channel_id=1, source_target_pairs={{0,192},{16,208},{32,224},{48,240},{64,256},{80,272},{96,288},{112... | collective-permute-start | bytes 589832 | tf_op jit(solution)/shard_map/ppermute | solution.py:37
  134.6 9.3 %collective-permute-start.7 = (bf16[2,384,128]{2,1,0:T(8,128)(2,1)S(1)}, bf16[2,384,128]{2,1,0:T(8,128)(2,1)S(1)}, u32[]{:S(2)}, u32[]{:S(2)}) collective-permute-start(bf16[2,384,128]{2,1,0:T(8,128)(2,1)S(1)} %get-tuple-element.35), channel_id=1, source_target_pairs={{0,384},{16,400},{32,416},{48,432},{64,448},{80,464},{96,480},{112... | collective-permute-start | bytes 589832 | tf_op jit(solution)/shard_map/ppermute | solution.py:37
  139.9 7.6 %collective-permute-start.8 = (bf16[2,384,128]{2,1,0:T(8,128)(2,1)S(1)}, bf16[2,384,128]{2,1,0:T(8,128)(2,1)S(1)}, u32[]{:S(2)}, u32[]{:S(2)}) collective-permute-start(bf16[2,384,128]{2,1,0:T(8,128)(2,1)S(1)} %get-tuple-element.34), channel_id=1, source_target_pairs={{0,576},{16,592},{32,608},{48,624},{64,640},{80,656},{96,672},{112... | collective-permute-start | bytes 589832 | tf_op jit(solution)/shard_map/ppermute | solution.py:37
Sparse Core Ops, SparseCore 0:
  29.5 57.9 all-gather.1

commit v4 on v3

--- a/solution.py
+++ b/solution.py
@@ -25,6 +25,10 @@
 VMEM = pl.BlockSpec(memory_space=pltpu.VMEM)
 PARAMS = pltpu.CompilerParams(vmem_limit_bytes=12 * 1024 * 1024)
 
+ROW_LSE, ROW_PICKS, SHARE_ROWS = 384, 387, 392
+
+WIDE = 1024
+
 M_X, M_CORE, M_Y, M_Z = 9, 10, 11, 12
 
 
@@ -61,22 +65,37 @@
     parts.append(prev[which] if j == 0 else kv[which, (j - 1) * BLK : j * BLK])
     parts.append(nxt[which] if j == 2 else kv[which, (j + 1) * BLK : (j + 2) * BLK])
     for k in range(3):
-        source = (meta[M_X] + k + 1) % NX
         row = pl.multiple_of(meta[3 * j + k] * BLK, BLK)
-        parts.append(far[source, which, pl.ds(row, BLK)])
+        parts.append(far[k][which, pl.ds(row, BLK)])
     return jnp.concatenate(parts, axis=0)
 
 
-def forward_kernel(meta, q, kv, prev, nxt, far, probs_out, att_out):
+def as_row(column):
+    return jnp.broadcast_to(column, (BLK, BLK)).T
+
+
+def forward_kernel(meta, q, kv, prev, nxt, far1, far2, far3, probs_out, att_out, share):
+    far = (far1, far2, far3)
     for j in range(3):
         rows = slice(j * BLK, (j + 1) * BLK)
         keys = select(meta, j, 0, kv, prev, nxt, far)
         vals = select(meta, j, 1, kv, prev, nxt, far)
         scores = dot(q[rows], keys, 1, 1) * (DH**-0.5)
-        terms = jnp.exp(scores - jnp.max(scores, axis=-1, keepdims=True))
-        probs = terms / jnp.sum(terms, axis=-1, keepdims=True)
+        top = jnp.max(scores, axis=-1, keepdims=True)
+        terms = jnp.exp(scores - top)
+        total = jnp.sum(terms, axis=-1, keepdims=True)
+        probs = terms / total
         probs_out[j] = probs
-        att_out[rows] = dot(probs.astype(BF16), vals, 1, 0).astype(BF16)
+        att = dot(probs.astype(BF16), vals, 1, 0).astype(BF16)
+        att_out[rows] = att
+        share[rows] = att.astype(F32)
+        share[ROW_LSE + j : ROW_LSE + j + 1] = as_row(top + jnp.log(total))[:1]
+    lane = lax.broadcasted_iota(jnp.int32, (1, BLK), 1)
+    picks = jnp.zeros((1, BLK), F32)
+    for i in range(9):
+        picks = jnp.where(lane == i, meta[i].astype(F32), picks)
+    share[ROW_PICKS : ROW_PICKS + 1] = picks
+    share[ROW_PICKS + 1 :] = jnp.zeros((SHARE_ROWS - ROW_PICKS - 1, BLK), F32)
 
 
 def weight_kernel(meta, own, other, w_out, flat):
@@ -94,7 +113,8 @@
             w_out[t, :, e * 128 : (e + 1) * 128] = rows.astype(BF16)
 
 
-def cotangent_kernel(meta, w, att, pieces, keep, give, grad, cols, flat):
+def cotangent_kernel(meta, far_picks, w, att, pieces, keep, give, grad, wide, cols, flat):
+    del far_picks
     z = meta[M_Z]
     att_now = att[...]
     total = jnp.zeros((384, DH), F32)
@@ -104,6 +124,8 @@
         cols[col] = dot(att_now, cot, 0, 0)
         total = total + dot(cot, w[col], 1, 1)
     grad[...] = total.astype(BF16)
+    wide[:384] = total.astype(BF16)
+    wide[384:] = jnp.zeros((WIDE - 384, DH), BF16)
     for t in range(N_TP):
         for e in range(2):
             flat[pl.ds(2 * t + e, DH, stride=32)] = cols[t, :, e * 128 : (e + 1) * 128]
@@ -116,8 +138,10 @@
         give[i] = jnp.where(first, b, a)
 
 
-def backward_kernel(meta, q, kv, prev, nxt, far, probs, att, out_grad, dq, dkv, dprev, dnext, dfar, acc):
-    acc[...] = jnp.zeros(acc.shape, F32)
+def backward_kernel(
+    meta, q, kv, prev, nxt, far1, far2, far3, probs, att, out_grad, dq, dkv, dprev, dnext
+):
+    far = (far1, far2, far3)
     dkv[...] = jnp.zeros(dkv.shape, F32)
     scale = DH**-0.5
     for j in range(3):
@@ -129,7 +153,11 @@
         p = probs[j]
         ds = (p * (dot(grad, vals, 1, 1) - delta)).astype(BF16)
         dq[rows] = dot(ds, keys, 1, 0) * scale
-        parts = (dot(ds, q[rows], 0, 0) * scale, dot(p.astype(BF16), grad, 0, 0))
+        band = slice(0, 3 * BLK)
+        parts = (
+            dot(ds[:, band], q[rows], 0, 0) * scale,
+            dot(p[:, band].astype(BF16), grad, 0, 0),
+        )
         for which in range(2):
             part = parts[which]
             dkv[which, rows] += part[:BLK]
@@ -138,13 +166,33 @@
             else:
                 dkv[which, (j - 1) * BLK : j * BLK] += part[BLK : 2 * BLK]
             if j == 2:
-                dnext[which] = part[2 * BLK : 3 * BLK].astype(BF16)
+                dnext[which] = part[2 * BLK :].astype(BF16)
             else:
-                dkv[which, (j + 1) * BLK : (j + 2) * BLK] += part[2 * BLK : 3 * BLK]
-            for k in range(3):
-                row = pl.multiple_of(meta[3 * j + k] * BLK, BLK)
-                acc[k, which, pl.ds(row, BLK)] += part[(3 + k) * BLK : (4 + k) * BLK]
-    dfar[...] = acc[...].astype(BF16)
+                dkv[which, (j + 1) * BLK : (j + 2) * BLK] += part[2 * BLK :]
+
+
+def far_kernel(meta, far_picks, kv, far1, far2, far3, share, grads, dkv, prev, nxt, dk, dv):
+    far = (far1, far2, far3)
+    scale = DH**-0.5
+    for which, out in ((0, dk), (1, dv)):
+        out[...] = dkv[which]
+        out[:BLK] += prev[which].astype(F32)
+        out[2 * BLK :] += nxt[which].astype(F32)
+    for k in range(1, 4):
+        source = (meta[M_X] + NX - k) % NX
+        for j in range(3):
+            row = pl.multiple_of(far_picks[source * 9 + 3 * j + k - 1] * BLK, BLK)
+            keys = kv[0, pl.ds(row, BLK)]
+            vals = kv[1, pl.ds(row, BLK)]
+            q = far[3 - k][2, j * BLK : (j + 1) * BLK]
+            grad = grads[pl.ds(pl.multiple_of(source * WIDE + j * BLK, BLK), BLK)]
+            att = share[source, j * BLK : (j + 1) * BLK]
+            lse = share[source, ROW_LSE + j : ROW_LSE + j + 1]
+            probs = jnp.exp(dot(keys, q, 1, 1) * scale - lse)
+            delta = as_row(jnp.sum(grad.astype(F32) * att, axis=-1, keepdims=True))
+            ds = (probs * (dot(vals, grad, 1, 1) - delta)).astype(BF16)
+            dk[pl.ds(row, BLK)] += dot(ds, q, 1, 0) * scale
+            dv[pl.ds(row, BLK)] += dot(probs.astype(BF16), grad, 1, 0)
 
 
 def chunk_sum_kernel(parts, out):
@@ -152,18 +200,6 @@
     for i in range(1, CHIPS):
         total = total + parts[i].astype(F32)
     out[0] = total[:SHARD]
-
-
-def grad_sum_kernel(dkv, prev, nxt, far1, far2, far3, dk, dv):
-    for which, out in ((0, dk), (1, dv)):
-        out[...] = (
-            dkv[which]
-            + far1[which].astype(F32)
-            + far2[which].astype(F32)
-            + far3[which].astype(F32)
-        )
-        out[:BLK] += prev[which].astype(F32)
-        out[2 * BLK :] += nxt[which].astype(F32)
 
 
 def on_device(queries, key_rows, values, cotangent, w_flat, block_keys):
@@ -186,11 +222,9 @@
     kv = after(jnp.stack([key_rows, values]), twin[0, 0])
     even = ctx % 2 == 0
     prev, nxt = neighbours(kv[:, :BLK], kv[:, 2 * BLK :], even)
-    far = lax.all_to_all(
-        jnp.broadcast_to(after(kv, w_own[0, 0, 0])[None], (NX,) + kv.shape),
-        "ctx", 0, 0, tiled=True, axis_index_groups=X_GROUPS,
-    )
-    w_other = core_swap(w_own)
+    kvq = jnp.concatenate([kv, queries[None]], axis=0)
+    far = [x_shift(kvq, -k) for k in (1, 2, 3)]
+    w_other = core_swap(after(w_own, far[2][0, 0, 0] + prev[0, 0, 0]))
     flat_alloc = N_CTX * SHARD + 8
     weight = pl.pallas_call(
         weight_kernel,
@@ -202,31 +236,37 @@
         name="weight_rows",
     )(meta, w_own, w_other)
 
-    probs, att = pl.pallas_call(
+    probs, att, share = pl.pallas_call(
         forward_kernel,
         out_shape=(
             jax.ShapeDtypeStruct((3, BLK, 6 * BLK), F32),
             jax.ShapeDtypeStruct((384, DH), BF16),
+            jax.ShapeDtypeStruct((SHARE_ROWS, DH), F32),
         ),
-        in_specs=[SMEM] + [VMEM] * 5,
-        out_specs=(VMEM, VMEM),
+        in_specs=[SMEM] + [VMEM] * 7,
+        out_specs=(VMEM,) * 3,
         compiler_params=PARAMS,
         name="attention_forward",
-    )(meta, queries, kv, prev, nxt, far)
+    )(meta, queries, kv, prev, nxt, *far)
+    shares = lax.all_to_all(
+        jnp.broadcast_to(share[None], (NX,) + share.shape),
+        "ctx", 0, 0, tiled=True, axis_index_groups=X_GROUPS,
+    )
+    far_picks = shares[:, ROW_PICKS, :9].astype(jnp.int32).reshape(NX * 9)
 
     chunk = jax.ShapeDtypeStruct((CHIPS, SHARD_PAD, 128), F32)
-    keep, give, out_grad = pl.pallas_call(
+    keep, give, out_grad, wide_grad = pl.pallas_call(
         cotangent_kernel,
-        out_shape=(chunk, chunk, jax.ShapeDtypeStruct((384, DH), BF16)),
-        in_specs=[SMEM, VMEM, VMEM, VMEM],
-        out_specs=(VMEM, VMEM, VMEM),
+        out_shape=(chunk, chunk, jax.ShapeDtypeStruct((384, DH), BF16), jax.ShapeDtypeStruct((WIDE, DH), BF16)),
+        in_specs=[SMEM, SMEM, VMEM, VMEM, VMEM],
+        out_specs=(VMEM, VMEM, VMEM, VMEM),
         scratch_shapes=[
             pltpu.VMEM((N_TP, DH, WCOL), F32),
             pltpu.VMEM((flat_alloc, 128), F32),
         ],
         compiler_params=PARAMS,
         name="cotangent_products",
-    )(meta, weight, att, pieces)
+    )(meta, far_picks, weight, att, pieces)
     pair_sum = (keep + core_swap(give)).astype(BF16)
     spread = lax.all_to_all(
         pair_sum, "ctx", 0, 0, tiled=True, axis_index_groups=SAME_CORE
@@ -238,31 +278,30 @@
         name="chunk_sum",
     )(spread)
 
-    two = (2, 384, DH)
-    dq, dkv, dprev, dnext, dfar = pl.pallas_call(
+    grads = lax.all_gather(wide_grad, "ctx", axis=0, tiled=True, axis_index_groups=X_GROUPS)
+    dq, dkv, dprev, dnext = pl.pallas_call(
         backward_kernel,
         out_shape=(
             jax.ShapeDtypeStruct((384, DH), F32),
-            jax.ShapeDtypeStruct(two, F32),
+            jax.ShapeDtypeStruct((2, 384, DH), F32),
             jax.ShapeDtypeStruct((2, BLK, DH), BF16),
             jax.ShapeDtypeStruct((2, BLK, DH), BF16),
-            jax.ShapeDtypeStruct((3,) + two, BF16),
         ),
-        in_specs=[SMEM] + [VMEM] * 8,
-        out_specs=(VMEM,) * 5,
-        scratch_shapes=[pltpu.VMEM((3,) + two, F32)],
+        in_specs=[SMEM] + [VMEM] * 10,
+        out_specs=(VMEM,) * 4,
         compiler_params=PARAMS,
         name="attention_backward",
-    )(meta, queries, kv, prev, nxt, far, probs, att, out_grad)
-    far_back = [x_shift(dfar[k], k + 1) for k in range(3)]
+    )(meta, queries, kv, prev, nxt, *far, probs, att, out_grad)
     from_prev, from_next = neighbours(dprev, dnext, even)
     grad = jax.ShapeDtypeStruct((384, DH), F32)
     dk, dv = pl.pallas_call(
-        grad_sum_kernel,
+        far_kernel,
         out_shape=(grad, grad),
-        compiler_params=PARAMS,
-        name="grad_sum",
-    )(dkv, from_prev, from_next, *far_back)
+        in_specs=[SMEM, SMEM] + [VMEM] * 9,
+        out_specs=(VMEM, VMEM),
+        compiler_params=PARAMS,
+        name="far_gradients",
+    )(meta, far_picks, kv, *far, shares, grads, dkv, from_prev, from_next)
     return dq, dk, dv, weight_grad
 
 

time: 157 us -> 160 us (1.019)
  the two profiles are of different devices: /device:TPU:42 before, /device:TPU:1 now
where the time goes in v4:
time: 160 us; the launch traced here: 159 us
  starting transfers between devices  80.4 us (50%)
  waiting for transfers between devices  24.3 us (15%)
  local copies, waits for them, and re-layouts  17.3 us (11%)
  between operations  16.3 us (10%)
  Pallas kernels  14.9 us (9%)
  other arithmetic  5.55 us (3%)
    ppermute x4, starting transfers between devices, core_swap(): return lax.ppermute(value, 'ctx', [(s, s ^ 1) for s in range(N_CTX)])  20.7 us
    all_to_all x1, starting transfers between devices, on_device(): lax.all_to_all(jnp.broadcast_to(w_pad[None], (CHIPS, SHARD_PAD, 128)), 'c...  15.9 us
    ppermute x1, starting transfers between devices, twin_swap(): return lax.ppermute(value, 'tp', [(s, s ^ 1) for s in range(N_TP)])  15.7 us
    unnamed x47, local copies, waits for them, and re-layouts  13.7 us
    ppermute x3, starting transfers between devices, x_shift(): return lax.ppermute(value, 'ctx', pairs)  10.6 us
    all_gather x1, waiting for transfers between devices, on_device(): lax.all_gather(wide_grad, 'ctx', axis=0, tiled=True, axis_index_groups=X_...  7.64 us
    all_to_all x1, starting transfers between devices, on_device(): lax.all_to_all(pair_sum, 'ctx', 0, 0, tiled=True, axis_index_groups=SAME_...  6.8 us
    ppermute x1, waiting for transfers between devices, twin_swap(): return lax.ppermute(value, 'tp', [(s, s ^ 1) for s in range(N_TP)])  6.75 us
  transfers between devices with their start and end apart: 15, of which 7 were waited for; matrix products, arithmetic and copies ran while one was open for 5% of the time, Pallas kernels for 6%

profile of v4, /device:TPU:1, one launch (start us, length us, event | category | flops | bytes accessed | tf_op | source)
XLA Modules:
  0.0 158.8 jit_solution(14841122950032896418)
XLA Ops:
  7.2 0.0 all-gather.3.cloned.1.call-start
  7.2 15.7 %collective-permute-start = (bf16[384,256]{1,0:T(8,128)(2,1)}, bf16[384,256]{1,0:T(8,128)(2,1)S(1)}, u32[]{:S(2)}, u32[]{:S(2)}) collective-permute-start(bf16[384,256]{1,0:T(8,128)(2,1)} %param.9), channel_id=1, source_target_pairs={{0,1},{1,0},{2,3},{3,2},{4,5},{5,4},{6,7},{7,6},{8,9},{9,8},{10,11... | collective-permute-start | bytes 589832 | tf_op jit(solution)/shard_map/ppermute | solution.py:56
  22.9 6.7 %collective-permute-done = bf16[384,256]{1,0:T(8,128)(2,1)S(1)} collective-permute-done((bf16[384,256]{1,0:T(8,128)(2,1)}, bf16[384,256]{1,0:T(8,128)(2,1)S(1)}, u32[]{:S(2)}, u32[]{:S(2)}) %collective-permute-start) | collective-permute-done | bytes 196640 | tf_op jit(solution)/shard_map/ppermute | solution.py:56
  29.7 1.7 %pad_maximum_fusion = bf16[768,256]{1,0:T(8,128)(2,1)} fusion(bf16[384,256]{1,0:T(8,128)(2,1)S(1)} %collective-permute-done, bf16[384,256]{1,0:T(8,128)(2,1)} %param.9), kind=kLoop, calls=%fused_computation.2 | loop fusion | flops 786432 | bytes 786432 | tf_op jit(solution)/shard_map/concatenate | solution.py:214
  31.4 0.0 all-gather.3.cloned.1.call-update
  31.4 0.0 copy-start.5
  31.5 0.9 broadcast_in_dim.24
  32.3 15.9 %all-to-all-start.1 = ((bf16[24,88,128]{2,1,0:T(8,128)(2,1)}), bf16[24,88,128]{2,1,0:T(8,128)(2,1)S(1)}, u32[]{:S(2)}, u32[]{:S(2)}) async-start(bf16[24,88,128]{2,1,0:T(8,128)(2,1)} %broadcast_in_dim.24), calls=%async_computation.1 | async-start | bytes 1081344 | tf_op jit(solution)/shard_map/all_to_all | solution.py:218
  48.2 0.5 slice.32
  49.5 3.2 %collective-permute-start.5 = (bf16[3,384,128]{2,1,0:T(8,128)(2,1)S(1)}, bf16[3,384,128]{2,1,0:T(8,128)(2,1)S(1)}, u32[]{:S(2)}, u32[]{:S(2)}) collective-permute-start(bf16[3,384,128]{2,1,0:T(8,128)(2,1)S(1)} %pad_maximum_fusion.1), channel_id=1, source_target_pairs={{0,192},{16,208},{32,224},{48,240},{64,256},{80,272},{96,288},{112... | collective-permute-start | bytes 884744 | tf_op jit(solution)/shard_map/ppermute | solution.py:41
  52.7 4.3 %collective-permute-start.4 = (bf16[3,384,128]{2,1,0:T(8,128)(2,1)S(1)}, bf16[3,384,128]{2,1,0:T(8,128)(2,1)S(1)}, u32[]{:S(2)}, u32[]{:S(2)}) collective-permute-start(bf16[3,384,128]{2,1,0:T(8,128)(2,1)S(1)} %pad_maximum_fusion.1), channel_id=1, source_target_pairs={{0,384},{16,400},{32,416},{48,432},{64,448},{80,464},{96,480},{112... | collective-permute-start | bytes 884744 | tf_op jit(solution)/shard_map/ppermute | solution.py:41
  57.0 3.1 %collective-permute-start.3 = (bf16[3,384,128]{2,1,0:T(8,128)(2,1)S(1)}, bf16[3,384,128]{2,1,0:T(8,128)(2,1)S(1)}, u32[]{:S(2)}, u32[]{:S(2)}) collective-permute-start(bf16[3,384,128]{2,1,0:T(8,128)(2,1)S(1)} %pad_maximum_fusion.1), channel_id=1, source_target_pairs={{0,576},{16,592},{32,608},{48,624},{64,640},{80,656},{96,672},{112... | collective-permute-start | bytes 884744 | tf_op jit(solution)/shard_map/ppermute | solution.py:41
  60.1 4.0 %collective-permute-start.2 = (bf16[2,128,128]{2,1,0:T(8,128)(2,1)S(1)}, bf16[2,128,128]{2,1,0:T(8,128)(2,1)S(1)}, u32[]{:S(2)}, u32[]{:S(2)}) collective-permute-start(bf16[2,128,128]{2,1,0:T(8,128)(2,1)S(1)} %get-tuple-element.34), channel_id=1, source_target_pairs={{0,16},{16,0},{32,48},{48,32},{64,80},{80,64},{96,112},{112,96},{1... | collective-permute-start | bytes 196616 | tf_op jit(solution)/shard_map/ppermute | solution.py:52
  64.2 3.0 %collective-permute-start.1 = (bf16[2,128,128]{2,1,0:T(8,128)(2,1)S(1)}, bf16[2,128,128]{2,1,0:T(8,128)(2,1)S(1)}, u32[]{:S(2)}, u32[]{:S(2)}) collective-permute-start(bf16[2,128,128]{2,1,0:T(8,128)(2,1)S(1)} %get-tuple-element.35), channel_id=1, source_target_pairs={{0,752},{16,32},{32,16},{48,64},{64,48},{80,96},{96,80},{112,128},... | collective-permute-start | bytes 196616 | tf_op jit(solution)/shard_map/ppermute | solution.py:47
  67.2 0.1 add_select_fusion
  67.3 0.1 reshape.21
  67.3 0.1 concatenate.12.meta
  67.4 0.0 collective-permute-done.2
  67.4 3.0 %collective-permute-done.1 = bf16[2,128,128]{2,1,0:T(8,128)(2,1)S(1)} collective-permute-done((bf16[2,128,128]{2,1,0:T(8,128)(2,1)S(1)}, bf16[2,128,128]{2,1,0:T(8,128)(2,1)S(1)}, u32[]{:S(2)}, u32[]{:S(2)}) %collective-permute-start.1) | collective-permute-done | bytes 65568 | tf_op jit(solution)/shard_map/ppermute | solution.py:47
  70.4 0.5 slice.38
  70.9 0.0 collective-permute-done.5.far3
  70.9 0.5 slice.37
  72.8 0.0 collective-permute-done.4.far2
  72.8 0.0 collective-permute-done.3.far1
  72.8 1.9 %attention_forward.1 = (f32[3,128,768]{2,1,0:T(8,128)S(1)}, bf16[384,128]{1,0:T(8,128)(2,1)S(1)}, f32[392,128]{1,0:T(8,128)S(1)}) custom-call(s32[13]{0:T(128)S(1)} %concatenate.12.meta, bf16[384,128]{1,0:T(8,128)(2,1)S(1)} %copy-done.5, bf16[2,384,128]{2,1,0:T(8,128)(2,1)S(1)} %maximum_select_fusion.kv, bf16[2,128,128]{2,1,0:T(8,128)(2,1)S(1)} %get-tuple-element.41.prev, ...), custom_call_target="tpu_custom_call" | custom-call | tf_op jit(solution)/shard_map/attention_forward/pallas_call | solution.py:239
  74.7 1.0 copy-done.1
  75.8 0.6 copy-done.7
  76.4 0.0 all-to-all-done.1.own
  76.4 1.0 broadcast_in_dim.23
  77.4 4.4 %all-to-all-start = ((f32[4,392,128]{2,1,0:T(8,128)}), f32[4,392,128]{2,1,0:T(8,128)S(1)}, u32[]{:S(2)}, u32[]{:S(2)}) async-start(f32[4,392,128]{2,1,0:T(8,128)} %broadcast_in_dim.23), calls=%async_computation | async-start | bytes 1605632 | tf_op jit(solution)/shard_map/all_to_all | solution.py:251
  81.8 0.8 broadcast_select_fusion
  82.6 7.4 %collective-permute-start.6 = (bf16[24,88,128]{2,1,0:T(8,128)(2,1)}, bf16[24,88,128]{2,1,0:T(8,128)(2,1)S(1)}, u32[]{:S(2)}, u32[]{:S(2)}) collective-permute-start(bf16[24,88,128]{2,1,0:T(8,128)(2,1)} %broadcast_select_fusion), channel_id=1, source_target_pairs={{0,16},{16,0},{32,48},{48,32},{64,80},{80,64},{96,112},{112,96},{1... | collective-permute-start | bytes 1622024 | tf_op jit(solution)/shard_map/ppermute | solution.py:52
  90.0 0.3 all-to-all-done.share
  90.2 0.1 convert_element_type.11.far_picks
  90.3 1.4 collective-permute-done.6.other
  91.7 0.8 copy-done.9
  92.5 1.0 copy-done.10
  93.6 2.4 %weight_rows.1.w = bf16[16,128,256]{2,1,0:T(8,128)(2,1)S(1)} custom-call(s32[13]{0:T(128)S(1)} %concatenate.12.meta, bf16[24,88,128]{2,1,0:T(8,128)(2,1)S(1)} %all-to-all-done.1.own, bf16[24,88,128]{2,1,0:T(8,128)(2,1)S(1)} %copy-done.10), custom_call_target="tpu_custom_call" | custom-call | tf_op jit(solution)/shard_map/weight_rows/pallas_call | solution.py:229
  95.9 0.0 all-gather.3.cloned.1.call-done.pieces
  96.0 1.9 %copy-done = bf16[6144,256]{1,0:T(8,128)(2,1)S(1)} copy-done((bf16[6144,256]{1,0:T(8,128)(2,1)S(1)}, bf16[6144,256]{1,0:T(8,128)(2,1)}, u32[]{:S(2)}) %copy-start) | copy-done | bytes 3145752
  97.8 0.9 copy-done.14
  98.7 5.4 %cotangent_products.1 = (f32[24,88,128]{2,1,0:T(8,128)S(1)}, f32[24,88,128]{2,1,0:T(8,128)}, bf16[384,128]{1,0:T(8,128)(2,1)S(1)}, bf16[1024,128]{1,0:T(8,128)(2,1)}) custom-call(s32[13]{0:T(128)S(1)} %concatenate.12.meta, s32[36]{0:T(128)S(1)} %convert_element_type.11.far_picks, bf16[16,128,256]{2,1,0:T(8,128)(2,1)S(1)} %weight_rows.1.w, ...), custom_call_target="tpu_custom_call" | custom-call | tf_op jit(solution)/shard_map/cotangent_products/pallas_call | solution.py:258
  104.1 1.0 copy-done.3
  105.1 0.6 copy-done.17
  105.8 7.0 %collective-permute-start.9 = (f32[24,88,128]{2,1,0:T(8,128)}, f32[24,88,128]{2,1,0:T(8,128)S(1)}, u32[]{:S(2)}, u32[]{:S(2)}) collective-permute-start(f32[24,88,128]{2,1,0:T(8,128)} %get-tuple-element.29), channel_id=1, source_target_pairs={{0,16},{16,0},{32,48},{48,32},{64,80},{80,64},{96,112},{112,96},{1... | collective-permute-start | bytes 3244040 | tf_op jit(solution)/shard_map/ppermute | solution.py:52
  112.8 0.0 all-gather.5.cloned.1.call-update
  112.8 2.5 %collective-permute-done.9 = f32[24,88,128]{2,1,0:T(8,128)S(1)} collective-permute-done((f32[24,88,128]{2,1,0:T(8,128)}, f32[24,88,128]{2,1,0:T(8,128)S(1)}, u32[]{:S(2)}, u32[]{:S(2)}) %collective-permute-start.9) | collective-permute-done | bytes 1081376 | tf_op jit(solution)/shard_map/ppermute | solution.py:52
  115.3 2.1 %add_convert_fusion = bf16[24,88,128]{2,1,0:T(8,128)(2,1)} fusion(f32[24,88,128]{2,1,0:T(8,128)} %copy-done.3, f32[24,88,128]{2,1,0:T(8,128)S(1)} %collective-permute-done.9), kind=kLoop, calls=%fused_computation | loop fusion | flops 540672 | bytes 2703360 | tf_op jit(solution)/shard_map/convert_element_type | solution.py:270
  117.5 6.8 %all-to-all-start.2 = ((bf16[24,88,128]{2,1,0:T(8,128)(2,1)}), bf16[24,88,128]{2,1,0:T(8,128)(2,1)S(1)}, u32[]{:S(2)}, u32[]{:S(2)}) async-start(bf16[24,88,128]{2,1,0:T(8,128)(2,1)} %add_convert_fusion), calls=%async_computation.2 | async-start | bytes 1081344 | tf_op jit(solution)/shard_map/all_to_all | solution.py:271
  124.3 1.3 copy-done.2
  125.6 2.1 %attention_backward.1 = (f32[384,128]{1,0:T(8,128)}, f32[2,384,128]{2,1,0:T(8,128)S(1)}, bf16[2,128,128]{2,1,0:T(8,128)(2,1)S(1)}, bf16[2,128,128]{2,1,0:T(8,128)(2,1)S(1)}) custom-call(s32[13]{0:T(128)S(1)} %concatenate.12.meta, bf16[384,128]{1,0:T(8,128)(2,1)S(1)} %copy-done.6, bf16[2,384,128]{2,1,0:T(8,128)(2,1)S(1)} %maximum_select_fusion.kv, ...), custom_call_target="tpu_custom_call" | custom-call | tf_op jit(solution)/shard_map/attention_backward/pallas_call | solution.py:282
  127.7 0.7 copy-done.11
  128.4 2.3 %collective-permute-start.8 = (bf16[2,128,128]{2,1,0:T(8,128)(2,1)S(1)}, bf16[2,128,128]{2,1,0:T(8,128)(2,1)S(1)}, u32[]{:S(2)}, u32[]{:S(2)}) collective-permute-start(bf16[2,128,128]{2,1,0:T(8,128)(2,1)S(1)} %get-tuple-element.38), channel_id=1, source_target_pairs={{0,16},{16,0},{32,48},{48,32},{64,80},{80,64},{96,112},{112,96},{1... | collective-permute-start | bytes 196616 | tf_op jit(solution)/shard_map/ppermute | solution.py:52
  130.8 3.4 %collective-permute-start.7 = (bf16[2,128,128]{2,1,0:T(8,128)(2,1)S(1)}, bf16[2,128,128]{2,1,0:T(8,128)(2,1)S(1)}, u32[]{:S(2)}, u32[]{:S(2)}) collective-permute-start(bf16[2,128,128]{2,1,0:T(8,128)(2,1)S(1)} %get-tuple-element.39), channel_id=1, source_target_pairs={{0,752},{16,32},{32,16},{48,64},{64,48},{80,96},{96,80},{112,128},... | collective-permute-start | bytes 196616 | tf_op jit(solution)/shard_map/ppermute | solution.py:47
  134.2 0.0 collective-permute-done.8
  134.2 2.7 %collective-permute-done.7 = bf16[2,128,128]{2,1,0:T(8,128)(2,1)S(1)} collective-permute-done((bf16[2,128,128]{2,1,0:T(8,128)(2,1)S(1)}, bf16[2,128,128]{2,1,0:T(8,128)(2,1)S(1)}, u32[]{:S(2)}, u32[]{:S(2)}) %collective-permute-start.7) | collective-permute-done | bytes 65568 | tf_op jit(solution)/shard_map/ppermute | solution.py:47
  136.9 0.6 broadcast_select_fusion.1
  137.6 7.6 %all-gather.5.cloned.1.call-done.grads = bf16[4096,128]{1,0:T(8,128)(2,1)} async-done(((bf16[1024,128]{1,0:T(8,128)(2,1)}), bf16[4096,128]{1,0:T(8,128)(2,1)}) %all-gather.5.cloned.1.call-update) | async-done | bytes 1048592 | tf_op jit(solution)/shard_map/all_gather | solution.py:281
  145.2 1.2 copy-done.4
  146.4 1.0 copy-done.12
  147.4 0.8 copy-done.16
  148.3 3.0 %far_gradients.1 = (f32[384,128]{1,0:T(8,128)}, f32[384,128]{1,0:T(8,128)}) custom-call(s32[13]{0:T(128)S(1)} %concatenate.12.meta, s32[36]{0:T(128)S(1)} %convert_element_type.11.far_picks, bf16[2,384,128]{2,1,0:T(8,128)(2,1)S(1)} %maximum_select_fusion.kv, bf16[3,384,128]{2,1,0:T(8,128)(2,1)S(1)} %collective-permute-done.3.far1, ...), custom_call_target="tpu_custom_call" | custom-call | tf_op jit(solution)/shard_map/far_gradients/pallas_call | solution.py:297
  151.2 0.1 chunk_sum.1
  151.3 0.7 copy.10
  (42 shorter events, 0.2 us)
Async XLA Ops:
  7.2 24.3 %copy-start.21 = (bf16[1,86,128]{2,1,0:T(8,128)(2,1)S(1)}, bf16[1,86,128]{2,1,0:T(8,128)(2,1)}, u32[]{:S(2)}) copy-start(bf16[1,86,128]{2,1,0:T(8,128)(2,1)} %param.10) | copy-start | bytes 66052
  7.2 88.8 %all-gather.3.cloned.1.call-start = ((), (), s32[]{:S(2)}) async-start(), calls=%async_computation.3 | async-start | bytes 3538944 | tf_op jit(solution)/shard_map/all_gather | solution.py:213
  7.2 22.4 %collective-permute-start = (bf16[384,256]{1,0:T(8,128)(2,1)}, bf16[384,256]{1,0:T(8,128)(2,1)S(1)}, u32[]{:S(2)}, u32[]{:S(2)}) collective-permute-start(bf16[384,256]{1,0:T(8,128)(2,1)} %param.9), channel_id=1, source_target_pairs={{0,1},{1,0},{2,3},{3,2},{4,5},{5,4},{6,7},{7,6},{8,9},{9,8},{10,11... | collective-permute-start | bytes 589832 | tf_op jit(solution)/shard_map/ppermute | solution.py:56
  31.4 18.0 %copy-start.19 = (bf16[384,128]{1,0:T(8,128)(2,1)S(1)}, bf16[384,128]{1,0:T(8,128)(2,1)}, u32[]{:S(2)}) copy-start(bf16[384,128]{1,0:T(8,128)(2,1)} %param.8) | copy-start | bytes 294916
  31.4 18.0 %copy-start.20 = (bf16[384,128]{1,0:T(8,128)(2,1)S(1)}, bf16[384,128]{1,0:T(8,128)(2,1)}, u32[]{:S(2)}) copy-start(bf16[384,128]{1,0:T(8,128)(2,1)} %param.7) | copy-start | bytes 294916
  31.4 18.1 %copy-start.5 = (bf16[384,128]{1,0:T(8,128)(2,1)S(1)}, bf16[384,128]{1,0:T(8,128)(2,1)}, u32[]{:S(2)}) copy-start(bf16[384,128]{1,0:T(8,128)(2,1)} %q.3) | copy-start | bytes 294916
  32.3 34.8 %copy-start.22 = (s32[3,6]{1,0:T(4,128)S(1)}, s32[3,6]{1,0:T(4,128)}, u32[]{:S(2)}) copy-start(s32[3,6]{1,0:T(4,128)} %param.11) | copy-start | bytes 220
  32.3 44.1 %all-to-all-start.1 = ((bf16[24,88,128]{2,1,0:T(8,128)(2,1)}), bf16[24,88,128]{2,1,0:T(8,128)(2,1)S(1)}, u32[]{:S(2)}, u32[]{:S(2)}) async-start(bf16[24,88,128]{2,1,0:T(8,128)(2,1)} %broadcast_in_dim.24), calls=%async_computation.1 | async-start | bytes 1081344 | tf_op jit(solution)/shard_map/all_to_all | solution.py:218
  49.5 21.4 %collective-permute-start.5 = (bf16[3,384,128]{2,1,0:T(8,128)(2,1)S(1)}, bf16[3,384,128]{2,1,0:T(8,128)(2,1)S(1)}, u32[]{:S(2)}, u32[]{:S(2)}) collective-permute-start(bf16[3,384,128]{2,1,0:T(8,128)(2,1)S(1)} %pad_maximum_fusion.1), channel_id=1, source_target_pairs={{0,192},{16,208},{32,224},{48,240},{64,256},{80,272},{96,288},{112... | collective-permute-start | bytes 884744 | tf_op jit(solution)/shard_map/ppermute | solution.py:41
  52.7 20.1 %collective-permute-start.4 = (bf16[3,384,128]{2,1,0:T(8,128)(2,1)S(1)}, bf16[3,384,128]{2,1,0:T(8,128)(2,1)S(1)}, u32[]{:S(2)}, u32[]{:S(2)}) collective-permute-start(bf16[3,384,128]{2,1,0:T(8,128)(2,1)S(1)} %pad_maximum_fusion.1), channel_id=1, source_target_pairs={{0,384},{16,400},{32,416},{48,432},{64,448},{80,464},{96,480},{112... | collective-permute-start | bytes 884744 | tf_op jit(solution)/shard_map/ppermute | solution.py:41
  57.0 15.8 %collective-permute-start.3 = (bf16[3,384,128]{2,1,0:T(8,128)(2,1)S(1)}, bf16[3,384,128]{2,1,0:T(8,128)(2,1)S(1)}, u32[]{:S(2)}, u32[]{:S(2)}) collective-permute-start(bf16[3,384,128]{2,1,0:T(8,128)(2,1)S(1)} %pad_maximum_fusion.1), channel_id=1, source_target_pairs={{0,576},{16,592},{32,608},{48,624},{64,640},{80,656},{96,672},{112... | collective-permute-start | bytes 884744 | tf_op jit(solution)/shard_map/ppermute | solution.py:41
  60.1 7.3 %collective-permute-start.2 = (bf16[2,128,128]{2,1,0:T(8,128)(2,1)S(1)}, bf16[2,128,128]{2,1,0:T(8,128)(2,1)S(1)}, u32[]{:S(2)}, u32[]{:S(2)}) collective-permute-start(bf16[2,128,128]{2,1,0:T(8,128)(2,1)S(1)} %get-tuple-element.34), channel_id=1, source_target_pairs={{0,16},{16,0},{32,48},{48,32},{64,80},{80,64},{96,112},{112,96},{1... | collective-permute-start | bytes 196616 | tf_op jit(solution)/shard_map/ppermute | solution.py:52
  64.2 6.2 %collective-permute-start.1 = (bf16[2,128,128]{2,1,0:T(8,128)(2,1)S(1)}, bf16[2,128,128]{2,1,0:T(8,128)(2,1)S(1)}, u32[]{:S(2)}, u32[]{:S(2)}) collective-permute-start(bf16[2,128,128]{2,1,0:T(8,128)(2,1)S(1)} %get-tuple-element.35), channel_id=1, source_target_pairs={{0,752},{16,32},{32,16},{48,64},{64,48},{80,96},{96,80},{112,128},... | collective-permute-start | bytes 196616 | tf_op jit(solution)/shard_map/ppermute | solution.py:47
  74.7 1.0 copy-start.1
  75.8 0.6 copy-start.7
  76.4 1.0 copy-start.13
  77.4 12.8 %all-to-all-start = ((f32[4,392,128]{2,1,0:T(8,128)}), f32[4,392,128]{2,1,0:T(8,128)S(1)}, u32[]{:S(2)}, u32[]{:S(2)}) async-start(f32[4,392,128]{2,1,0:T(8,128)} %broadcast_in_dim.23), calls=%async_computation | async-start | bytes 1605632 | tf_op jit(solution)/shard_map/all_to_all | solution.py:251
  81.7 63.5 %all-gather.5.cloned.1.call-start = ((), (), s32[]{:S(2)}) async-start(), calls=%async_computation.4 | async-start | bytes 1310720 | tf_op jit(solution)/shard_map/all_gather | solution.py:281
  82.6 9.1 %collective-permute-start.6 = (bf16[24,88,128]{2,1,0:T(8,128)(2,1)}, bf16[24,88,128]{2,1,0:T(8,128)(2,1)S(1)}, u32[]{:S(2)}, u32[]{:S(2)}) collective-permute-start(bf16[24,88,128]{2,1,0:T(8,128)(2,1)} %broadcast_select_fusion), channel_id=1, source_target_pairs={{0,16},{16,0},{32,48},{48,32},{64,80},{80,64},{96,112},{112,96},{1... | collective-permute-start | bytes 1622024 | tf_op jit(solution)/shard_map/ppermute | solution.py:52
  91.7 0.8 copy-start.9
  92.5 1.0 copy-start.10
  96.0 1.9 %copy-start = (bf16[6144,256]{1,0:T(8,128)(2,1)S(1)}, bf16[6144,256]{1,0:T(8,128)(2,1)}, u32[]{:S(2)}) copy-start(bf16[6144,256]{1,0:T(8,128)(2,1)} %all-gather.3.cloned.1.call-done.pieces) | copy-start | bytes 9437188
  97.8 0.9 copy-start.14
  104.1 1.0 copy-start.3
  105.1 0.6 copy-start.17
  105.8 9.5 %collective-permute-start.9 = (f32[24,88,128]{2,1,0:T(8,128)}, f32[24,88,128]{2,1,0:T(8,128)S(1)}, u32[]{:S(2)}, u32[]{:S(2)}) collective-permute-start(f32[24,88,128]{2,1,0:T(8,128)} %get-tuple-element.29), channel_id=1, source_target_pairs={{0,16},{16,0},{32,48},{48,32},{64,80},{80,64},{96,112},{112,96},{1... | collective-permute-start | bytes 3244040 | tf_op jit(solution)/shard_map/ppermute | solution.py:52
  117.4 6.8 %copy-start.6 = (bf16[384,128]{1,0:T(8,128)(2,1)S(1)}, bf16[384,128]{1,0:T(8,128)(2,1)}, u32[]{:S(2)}) copy-start(bf16[384,128]{1,0:T(8,128)(2,1)} %q.3) | copy-start | bytes 294916
  117.4 6.8 %copy-start.8 = (bf16[2,128,128]{2,1,0:T(8,128)(2,1)S(1)}, bf16[2,128,128]{2,1,0:T(8,128)(2,1)}, u32[]{:S(2)}) copy-start(bf16[2,128,128]{2,1,0:T(8,128)(2,1)} %copy-done.7) | copy-start | bytes 196612
  117.4 6.8 %copy-start.15 = (bf16[384,128]{1,0:T(8,128)(2,1)S(1)}, bf16[384,128]{1,0:T(8,128)(2,1)}, u32[]{:S(2)}) copy-start(bf16[384,128]{1,0:T(8,128)(2,1)} %copy-done.13) | copy-start | bytes 294916
  117.5 6.8 %copy-start.18 = (bf16[384,128]{1,0:T(8,128)(2,1)S(1)}, bf16[384,128]{1,0:T(8,128)(2,1)}, u32[]{:S(2)}) copy-start(bf16[384,128]{1,0:T(8,128)(2,1)} %copy-done.17) | copy-start | bytes 294916
  117.5 33.8 %all-to-all-start.2 = ((bf16[24,88,128]{2,1,0:T(8,128)(2,1)}), bf16[24,88,128]{2,1,0:T(8,128)(2,1)S(1)}, u32[]{:S(2)}, u32[]{:S(2)}) async-start(bf16[24,88,128]{2,1,0:T(8,128)(2,1)} %add_convert_fusion), calls=%async_computation.2 | async-start | bytes 1081344 | tf_op jit(solution)/shard_map/all_to_all | solution.py:271
  124.3 1.3 copy-start.2
  127.7 0.7 copy-start.11
  128.4 5.7 %collective-permute-start.8 = (bf16[2,128,128]{2,1,0:T(8,128)(2,1)S(1)}, bf16[2,128,128]{2,1,0:T(8,128)(2,1)S(1)}, u32[]{:S(2)}, u32[]{:S(2)}) collective-permute-start(bf16[2,128,128]{2,1,0:T(8,128)(2,1)S(1)} %get-tuple-element.38), channel_id=1, source_target_pairs={{0,16},{16,0},{32,48},{48,32},{64,80},{80,64},{96,112},{112,96},{1... | collective-permute-start | bytes 196616 | tf_op jit(solution)/shard_map/ppermute | solution.py:52
  130.8 6.1 %collective-permute-start.7 = (bf16[2,128,128]{2,1,0:T(8,128)(2,1)S(1)}, bf16[2,128,128]{2,1,0:T(8,128)(2,1)S(1)}, u32[]{:S(2)}, u32[]{:S(2)}) collective-permute-start(bf16[2,128,128]{2,1,0:T(8,128)(2,1)S(1)} %get-tuple-element.39), channel_id=1, source_target_pairs={{0,752},{16,32},{32,16},{48,64},{64,48},{80,96},{96,80},{112,128},... | collective-permute-start | bytes 196616 | tf_op jit(solution)/shard_map/ppermute | solution.py:47
  145.2 1.2 copy-start.4
  146.4 1.0 copy-start.12
  147.4 0.8 copy-start.16
Sparse Core Ops, SparseCore 0:
  31.5 58.1 all-gather.2
  112.9 32.2 all-gather.4

commit v5 on v3

--- a/solution.py
+++ b/solution.py
@@ -61,13 +61,13 @@
     parts.append(prev[which] if j == 0 else kv[which, (j - 1) * BLK : j * BLK])
     parts.append(nxt[which] if j == 2 else kv[which, (j + 1) * BLK : (j + 2) * BLK])
     for k in range(3):
-        source = (meta[M_X] + k + 1) % NX
         row = pl.multiple_of(meta[3 * j + k] * BLK, BLK)
-        parts.append(far[source, which, pl.ds(row, BLK)])
+        parts.append(far[k][which, pl.ds(row, BLK)])
     return jnp.concatenate(parts, axis=0)
 
 
-def forward_kernel(meta, q, kv, prev, nxt, far, probs_out, att_out):
+def forward_kernel(meta, q, kv, prev, nxt, far1, far2, far3, probs_out, att_out):
+    far = (far1, far2, far3)
     for j in range(3):
         rows = slice(j * BLK, (j + 1) * BLK)
         keys = select(meta, j, 0, kv, prev, nxt, far)
@@ -116,7 +116,11 @@
         give[i] = jnp.where(first, b, a)
 
 
-def backward_kernel(meta, q, kv, prev, nxt, far, probs, att, out_grad, dq, dkv, dprev, dnext, dfar, acc):
+def backward_kernel(
+    meta, q, kv, prev, nxt, far1, far2, far3, probs, att, out_grad,
+    dq, dkv, dprev, dnext, dfar, acc,
+):
+    far = (far1, far2, far3)
     acc[...] = jnp.zeros(acc.shape, F32)
     dkv[...] = jnp.zeros(dkv.shape, F32)
     scale = DH**-0.5
@@ -147,6 +151,11 @@
     dfar[...] = acc[...].astype(BF16)
 
 
+def pair_sum_kernel(keep, other, dkv, out):
+    del dkv
+    out[...] = (keep[...] + other[...]).astype(BF16)
+
+
 def chunk_sum_kernel(parts, out):
     total = parts[0].astype(F32)
     for i in range(1, CHIPS):
@@ -186,11 +195,9 @@
     kv = after(jnp.stack([key_rows, values]), twin[0, 0])
     even = ctx % 2 == 0
     prev, nxt = neighbours(kv[:, :BLK], kv[:, 2 * BLK :], even)
-    far = lax.all_to_all(
-        jnp.broadcast_to(after(kv, w_own[0, 0, 0])[None], (NX,) + kv.shape),
-        "ctx", 0, 0, tiled=True, axis_index_groups=X_GROUPS,
-    )
-    w_other = core_swap(w_own)
+    far = [x_shift(kv, -k) for k in (1, 2, 3)]
+    arrived = [piece[0, 0, 0] for piece in (prev, nxt, *far)]
+    w_other = core_swap(after(w_own, sum(arrived)))
     flat_alloc = N_CTX * SHARD + 8
     weight = pl.pallas_call(
         weight_kernel,
@@ -208,11 +215,11 @@
             jax.ShapeDtypeStruct((3, BLK, 6 * BLK), F32),
             jax.ShapeDtypeStruct((384, DH), BF16),
         ),
-        in_specs=[SMEM] + [VMEM] * 5,
+        in_specs=[SMEM] + [VMEM] * 7,
         out_specs=(VMEM, VMEM),
         compiler_params=PARAMS,
         name="attention_forward",
-    )(meta, queries, kv, prev, nxt, far)
+    )(meta, queries, kv, prev, nxt, *far)
 
     chunk = jax.ShapeDtypeStruct((CHIPS, SHARD_PAD, 128), F32)
     keep, give, out_grad = pl.pallas_call(
@@ -227,17 +234,6 @@
         compiler_params=PARAMS,
         name="cotangent_products",
     )(meta, weight, att, pieces)
-    pair_sum = (keep + core_swap(give)).astype(BF16)
-    spread = lax.all_to_all(
-        pair_sum, "ctx", 0, 0, tiled=True, axis_index_groups=SAME_CORE
-    )
-    weight_grad = pl.pallas_call(
-        chunk_sum_kernel,
-        out_shape=jax.ShapeDtypeStruct((1, SHARD, 128), F32),
-        compiler_params=PARAMS,
-        name="chunk_sum",
-    )(spread)
-
     two = (2, 384, DH)
     dq, dkv, dprev, dnext, dfar = pl.pallas_call(
         backward_kernel,
@@ -248,12 +244,30 @@
             jax.ShapeDtypeStruct((2, BLK, DH), BF16),
             jax.ShapeDtypeStruct((3,) + two, BF16),
         ),
-        in_specs=[SMEM] + [VMEM] * 8,
+        in_specs=[SMEM] + [VMEM] * 10,
         out_specs=(VMEM,) * 5,
         scratch_shapes=[pltpu.VMEM((3,) + two, F32)],
         compiler_params=PARAMS,
         name="attention_backward",
-    )(meta, queries, kv, prev, nxt, far, probs, att, out_grad)
+    )(meta, queries, kv, prev, nxt, *far, probs, att, out_grad)
+    pair_sum = pl.pallas_call(
+        pair_sum_kernel,
+        out_shape=jax.ShapeDtypeStruct((CHIPS, SHARD_PAD, 128), BF16),
+        in_specs=[VMEM, VMEM, pl.BlockSpec(memory_space=pl.ANY)],
+        out_specs=VMEM,
+        compiler_params=PARAMS,
+        name="pair_sum",
+    )(keep, core_swap(give), dkv)
+    spread = lax.all_to_all(
+        pair_sum, "ctx", 0, 0, tiled=True, axis_index_groups=SAME_CORE
+    )
+    weight_grad = pl.pallas_call(
+        chunk_sum_kernel,
+        out_shape=jax.ShapeDtypeStruct((1, SHARD, 128), F32),
+        compiler_params=PARAMS,
+        name="chunk_sum",
+    )(spread)
+
     far_back = [x_shift(dfar[k], k + 1) for k in range(3)]
     from_prev, from_next = neighbours(dprev, dnext, even)
     grad = jax.ShapeDtypeStruct((384, DH), F32)

time: 157 us -> 151 us (0.962)
  the two profiles are of different devices: /device:TPU:42 before, /device:TPU:6 now
where the time goes in v5:
time: 151 us; the launch traced here: 150 us
  starting transfers between devices  87.7 us (58%)
  between operations  18.3 us (12%)
  waiting for transfers between devices  16 us (11%)
  Pallas kernels  12.7 us (8%)
  local copies, waits for them, and re-layouts  12.1 us (8%)
  other arithmetic  2.75 us (2%)
    ppermute x6, starting transfers between devices, x_shift(): return lax.ppermute(value, 'ctx', pairs)  18.6 us
    all_to_all x1, starting transfers between devices, on_device(): lax.all_to_all(jnp.broadcast_to(w_pad[None], (CHIPS, SHARD_PAD, 128)), 'c...  17.5 us
    ppermute x2, starting transfers between devices, neighbours(): outer = lax.ppermute(jnp.where(even, first, last), 'ctx', pairs)  17.1 us
    ppermute x1, starting transfers between devices, twin_swap(): return lax.ppermute(value, 'tp', [(s, s ^ 1) for s in range(N_TP)])  15.1 us
    all_to_all x1, starting transfers between devices, on_device(): lax.all_to_all(pair_sum, 'ctx', 0, 0, tiled=True, axis_index_groups=SAME_...  11.6 us
    unnamed x41, local copies, waits for them, and re-layouts  7.94 us
    ppermute x6, waiting for transfers between devices, x_shift(): return lax.ppermute(value, 'ctx', pairs)  7.84 us
    ppermute x4, starting transfers between devices, core_swap(): return lax.ppermute(value, 'ctx', [(s, s ^ 1) for s in range(N_CTX)])  7.67 us
  transfers between devices with their start and end apart: 16, of which 6 were waited for; matrix products, arithmetic and copies ran while one was open for 3% of the time, Pallas kernels for 5%

profile of v5, /device:TPU:6, one launch (start us, length us, event | category | flops | bytes accessed | tf_op | source)
XLA Modules:
  0.0 149.6 jit_solution(10440740362800473860)
XLA Ops:
  7.2 0.0 all-gather.2.cloned.1.call-start
  7.2 15.1 %collective-permute-start = (bf16[384,256]{1,0:T(8,128)(2,1)}, bf16[384,256]{1,0:T(8,128)(2,1)S(1)}, u32[]{:S(2)}, u32[]{:S(2)}) collective-permute-start(bf16[384,256]{1,0:T(8,128)(2,1)} %param.9), channel_id=1, source_target_pairs={{0,1},{1,0},{2,3},{3,2},{4,5},{5,4},{6,7},{7,6},{8,9},{9,8},{10,11... | collective-permute-start | bytes 589832 | tf_op jit(solution)/shard_map/ppermute | solution.py:52
  22.4 5.3 %collective-permute-done = bf16[384,256]{1,0:T(8,128)(2,1)S(1)} collective-permute-done((bf16[384,256]{1,0:T(8,128)(2,1)}, bf16[384,256]{1,0:T(8,128)(2,1)S(1)}, u32[]{:S(2)}, u32[]{:S(2)}) %collective-permute-start) | collective-permute-done | bytes 196640 | tf_op jit(solution)/shard_map/ppermute | solution.py:52
  27.7 1.7 %pad_maximum_fusion = bf16[768,256]{1,0:T(8,128)(2,1)} fusion(bf16[384,256]{1,0:T(8,128)(2,1)S(1)} %collective-permute-done, bf16[384,256]{1,0:T(8,128)(2,1)} %param.9), kind=kLoop, calls=%fused_computation.1 | loop fusion | flops 786432 | bytes 786432 | tf_op jit(solution)/shard_map/concatenate | solution.py:187
  29.4 0.0 all-gather.2.cloned.1.call-update
  29.4 0.9 broadcast_in_dim.13
  30.3 17.5 %all-to-all-start = ((bf16[24,88,128]{2,1,0:T(8,128)(2,1)}), bf16[24,88,128]{2,1,0:T(8,128)(2,1)S(1)}, u32[]{:S(2)}, u32[]{:S(2)}) async-start(bf16[24,88,128]{2,1,0:T(8,128)(2,1)} %broadcast_in_dim.13), calls=%async_computation | async-start | bytes 1081344 | tf_op jit(solution)/shard_map/all_to_all | solution.py:191
  47.9 0.0 copy-start.19
  47.9 0.0 copy-start.7
  47.9 0.5 slice.52
  49.2 1.9 %collective-permute-start.2 = (bf16[2,128,128]{2,1,0:T(8,128)(2,1)S(1)}, bf16[2,128,128]{2,1,0:T(8,128)(2,1)S(1)}, u32[]{:S(2)}, u32[]{:S(2)}) collective-permute-start(bf16[2,128,128]{2,1,0:T(8,128)(2,1)S(1)} %get-tuple-element.35), channel_id=1, source_target_pairs={{0,16},{16,0},{32,48},{48,32},{64,80},{80,64},{96,112},{112,96},{1... | collective-permute-start | bytes 196616 | tf_op jit(solution)/shard_map/ppermute | solution.py:48
  51.1 8.6 %collective-permute-start.1 = (bf16[2,128,128]{2,1,0:T(8,128)(2,1)S(1)}, bf16[2,128,128]{2,1,0:T(8,128)(2,1)S(1)}, u32[]{:S(2)}, u32[]{:S(2)}) collective-permute-start(bf16[2,128,128]{2,1,0:T(8,128)(2,1)S(1)} %get-tuple-element.36), channel_id=1, source_target_pairs={{0,752},{16,32},{32,16},{48,64},{64,48},{80,96},{96,80},{112,128},... | collective-permute-start | bytes 196616 | tf_op jit(solution)/shard_map/ppermute | solution.py:43
  59.7 2.5 %collective-permute-start.3 = (bf16[2,384,128]{2,1,0:T(8,128)(2,1)S(1)}, bf16[2,384,128]{2,1,0:T(8,128)(2,1)S(1)}, u32[]{:S(2)}, u32[]{:S(2)}) collective-permute-start(bf16[2,384,128]{2,1,0:T(8,128)(2,1)S(1)} %maximum_select_fusion.kv), channel_id=1, source_target_pairs={{0,576},{16,592},{32,608},{48,624},{64,640},{80,656},{96,672},{112... | collective-permute-start | bytes 589832 | tf_op jit(solution)/shard_map/ppermute | solution.py:37
  62.1 5.2 %collective-permute-start.4 = (bf16[2,384,128]{2,1,0:T(8,128)(2,1)S(1)}, bf16[2,384,128]{2,1,0:T(8,128)(2,1)S(1)}, u32[]{:S(2)}, u32[]{:S(2)}) collective-permute-start(bf16[2,384,128]{2,1,0:T(8,128)(2,1)S(1)} %maximum_select_fusion.kv), channel_id=1, source_target_pairs={{0,384},{16,400},{32,416},{48,432},{64,448},{80,464},{96,480},{112... | collective-permute-start | bytes 589832 | tf_op jit(solution)/shard_map/ppermute | solution.py:37
  67.4 1.9 %collective-permute-start.5 = (bf16[2,384,128]{2,1,0:T(8,128)(2,1)S(1)}, bf16[2,384,128]{2,1,0:T(8,128)(2,1)S(1)}, u32[]{:S(2)}, u32[]{:S(2)}) collective-permute-start(bf16[2,384,128]{2,1,0:T(8,128)(2,1)S(1)} %maximum_select_fusion.kv), channel_id=1, source_target_pairs={{0,192},{16,208},{32,224},{48,240},{64,256},{80,272},{96,288},{112... | collective-permute-start | bytes 589832 | tf_op jit(solution)/shard_map/ppermute | solution.py:37
  69.3 0.0 collective-permute-done.2
  69.3 0.0 collective-permute-done.1
  69.3 0.0 copy-start.1
  69.4 0.0 copy-start.3
  69.4 0.5 slice.56
  69.9 0.5 slice.57
  71.6 0.0 collective-permute-done.3.far1
  71.6 0.5 slice.58
  72.8 0.0 collective-permute-done.4.far2
  72.8 0.5 slice.59
  74.0 1.0 collective-permute-done.5.far3
  74.9 0.5 slice.60
  76.1 0.0 all-to-all-done.own
  76.1 0.9 broadcast_select_fusion
  77.0 1.9 %collective-permute-start.6 = (bf16[24,88,128]{2,1,0:T(8,128)(2,1)}, bf16[24,88,128]{2,1,0:T(8,128)(2,1)S(1)}, u32[]{:S(2)}, u32[]{:S(2)}) collective-permute-start(bf16[24,88,128]{2,1,0:T(8,128)(2,1)} %broadcast_select_fusion), channel_id=1, source_target_pairs={{0,16},{16,0},{32,48},{48,32},{64,80},{80,64},{96,112},{112,96},{1... | collective-permute-start | bytes 1622024 | tf_op jit(solution)/shard_map/ppermute | solution.py:48
  78.9 0.1 add_select_fusion
  79.0 0.1 reshape.18
  79.1 0.1 concatenate.9.meta
  79.2 1.9 %attention_forward.1 = (f32[3,128,768]{2,1,0:T(8,128)S(1)}, bf16[384,128]{1,0:T(8,128)(2,1)S(1)}) custom-call(s32[13]{0:T(128)S(1)} %concatenate.9.meta, bf16[384,128]{1,0:T(8,128)(2,1)S(1)} %copy-done.7, bf16[2,384,128]{2,1,0:T(8,128)(2,1)S(1)} %maximum_select_fusion.kv, bf16[2,128,128]{2,1,0:T(8,128)(2,1)S(1)} %get-tuple-element.42.prev, ...), custom_call_target="tpu_custom_call" | custom-call | tf_op jit(solution)/shard_map/attention_forward/pallas_call | solution.py:212
  81.2 0.0 copy-start.9
  81.2 0.6 copy-done.9
  81.8 0.0 collective-permute-done.6.other
  81.8 0.8 copy-done.5
  82.6 1.1 copy-done.6
  83.7 0.7 copy-done.14
  84.3 2.4 %weight_rows.1.w = bf16[16,128,256]{2,1,0:T(8,128)(2,1)S(1)} custom-call(s32[13]{0:T(128)S(1)} %copy-done.14, bf16[24,88,128]{2,1,0:T(8,128)(2,1)S(1)} %all-to-all-done.own, bf16[24,88,128]{2,1,0:T(8,128)(2,1)S(1)} %copy-done.6), custom_call_target="tpu_custom_call" | custom-call | tf_op jit(solution)/shard_map/weight_rows/pallas_call | solution.py:202
  86.7 2.8 %all-gather.2.cloned.1.call-done.pieces = bf16[6144,256]{1,0:T(8,128)(2,1)} async-done(((bf16[768,256]{1,0:T(8,128)(2,1)}), bf16[6144,256]{1,0:T(8,128)(2,1)}) %all-gather.2.cloned.1.call-update) | async-done | bytes 3145744 | tf_op jit(solution)/shard_map/all_gather | solution.py:186
  89.5 1.9 %copy-done = bf16[6144,256]{1,0:T(8,128)(2,1)S(1)} copy-done((bf16[6144,256]{1,0:T(8,128)(2,1)S(1)}, bf16[6144,256]{1,0:T(8,128)(2,1)}, u32[]{:S(2)}) %copy-start) | copy-done | bytes 3145752
  91.4 0.9 copy-done.10
  92.3 0.7 copy-done.15
  93.0 4.4 %cotangent_products.1 = (f32[24,88,128]{2,1,0:T(8,128)S(1)}, f32[24,88,128]{2,1,0:T(8,128)S(1)}, bf16[384,128]{1,0:T(8,128)(2,1)S(1)}) custom-call(s32[13]{0:T(128)S(1)} %copy-done.15, bf16[16,128,256]{2,1,0:T(8,128)(2,1)S(1)} %weight_rows.1.w, bf16[384,128]{1,0:T(8,128)(2,1)S(1)} %copy-done.10, bf16[6144,256]{1,0:T(8,128)(2,1)S(1)} %copy-done), custom_call_target="tpu_custom_call" | custom-call | tf_op jit(solution)/shard_map/cotangent_products/pallas_call | solution.py:225
  97.4 1.9 %collective-permute-start.12 = (f32[24,88,128]{2,1,0:T(8,128)S(1)}, f32[24,88,128]{2,1,0:T(8,128)S(1)}, u32[]{:S(2)}, u32[]{:S(2)}) collective-permute-start(f32[24,88,128]{2,1,0:T(8,128)S(1)} %get-tuple-element.27), channel_id=1, source_target_pairs={{0,16},{16,0},{32,48},{48,32},{64,80},{80,64},{96,112},{112,96},{1... | collective-permute-start | bytes 3244040 | tf_op jit(solution)/shard_map/ppermute | solution.py:48
  99.3 2.2 %attention_backward.1 = (f32[384,128]{1,0:T(8,128)}, f32[2,384,128]{2,1,0:T(8,128)S(1)}, bf16[2,128,128]{2,1,0:T(8,128)(2,1)S(1)}, bf16[2,128,128]{2,1,0:T(8,128)(2,1)S(1)}, bf16[3,2,384,128]{3,2,1,0:T(8,128)(2,1)S(1)}) custom-call(s32[13]{0:T(128)S(1)} %copy-done.15, bf16[384,128]{1,0:T(8,128)(2,1)S(1)} %copy-done.8, ...), custom_call_target="tpu_custom_call" | custom-call | tf_op jit(solution)/shard_map/attention_backward/pallas_call | solution.py:238
  101.6 0.6 copy-done.11
  102.2 0.9 pair_sum.1
  103.1 11.6 %all-to-all-start.1 = ((bf16[24,88,128]{2,1,0:T(8,128)(2,1)}), bf16[24,88,128]{2,1,0:T(8,128)(2,1)S(1)}, u32[]{:S(2)}, u32[]{:S(2)}) async-start(bf16[24,88,128]{2,1,0:T(8,128)(2,1)} %pair_sum.1), calls=%async_computation.1 | async-start | bytes 1081344 | tf_op jit(solution)/shard_map/all_to_all | solution.py:261
  114.7 1.9 %collective-permute-start.8 = (bf16[2,128,128]{2,1,0:T(8,128)(2,1)S(1)}, bf16[2,128,128]{2,1,0:T(8,128)(2,1)S(1)}, u32[]{:S(2)}, u32[]{:S(2)}) collective-permute-start(bf16[2,128,128]{2,1,0:T(8,128)(2,1)S(1)} %get-tuple-element.39), channel_id=1, source_target_pairs={{0,16},{16,0},{32,48},{48,32},{64,80},{80,64},{96,112},{112,96},{1... | collective-permute-start | bytes 196616 | tf_op jit(solution)/shard_map/ppermute | solution.py:48
  116.7 8.6 %collective-permute-start.7 = (bf16[2,128,128]{2,1,0:T(8,128)(2,1)S(1)}, bf16[2,128,128]{2,1,0:T(8,128)(2,1)S(1)}, u32[]{:S(2)}, u32[]{:S(2)}) collective-permute-start(bf16[2,128,128]{2,1,0:T(8,128)(2,1)S(1)} %get-tuple-element.40), channel_id=1, source_target_pairs={{0,752},{16,32},{32,16},{48,64},{64,48},{80,96},{96,80},{112,128},... | collective-permute-start | bytes 196616 | tf_op jit(solution)/shard_map/ppermute | solution.py:43
  125.3 4.3 %collective-permute-start.9 = (bf16[2,384,128]{2,1,0:T(8,128)(2,1)S(1)}, bf16[2,384,128]{2,1,0:T(8,128)(2,1)S(1)}, u32[]{:S(2)}, u32[]{:S(2)}) collective-permute-start(bf16[2,384,128]{2,1,0:T(8,128)(2,1)S(1)} %get-tuple-element.34), channel_id=1, source_target_pairs={{0,192},{16,208},{32,224},{48,240},{64,256},{80,272},{96,288},{112... | collective-permute-start | bytes 589832 | tf_op jit(solution)/shard_map/ppermute | solution.py:37
  129.6 2.1 %collective-permute-start.10 = (bf16[2,384,128]{2,1,0:T(8,128)(2,1)S(1)}, bf16[2,384,128]{2,1,0:T(8,128)(2,1)S(1)}, u32[]{:S(2)}, u32[]{:S(2)}) collective-permute-start(bf16[2,384,128]{2,1,0:T(8,128)(2,1)S(1)} %get-tuple-element.33), channel_id=1, source_target_pairs={{0,384},{16,400},{32,416},{48,432},{64,448},{80,464},{96,480},{112... | collective-permute-start | bytes 589832 | tf_op jit(solution)/shard_map/ppermute | solution.py:37
  131.8 2.6 %collective-permute-start.11 = (bf16[2,384,128]{2,1,0:T(8,128)(2,1)S(1)}, bf16[2,384,128]{2,1,0:T(8,128)(2,1)S(1)}, u32[]{:S(2)}, u32[]{:S(2)}) collective-permute-start(bf16[2,384,128]{2,1,0:T(8,128)(2,1)S(1)} %get-tuple-element.32), channel_id=1, source_target_pairs={{0,576},{16,592},{32,608},{48,624},{64,640},{80,656},{96,672},{112... | collective-permute-start | bytes 589832 | tf_op jit(solution)/shard_map/ppermute | solution.py:37
  134.3 0.0 collective-permute-done.7
  134.4 1.3 collective-permute-done.9.far1
  135.7 3.5 %collective-permute-done.10.far2 = bf16[2,384,128]{2,1,0:T(8,128)(2,1)S(1)} collective-permute-done((bf16[2,384,128]{2,1,0:T(8,128)(2,1)S(1)}, bf16[2,384,128]{2,1,0:T(8,128)(2,1)S(1)}, u32[]{:S(2)}, u32[]{:S(2)}) %collective-permute-start.10) | collective-permute-done | bytes 196640 | tf_op jit(solution)/shard_map/ppermute | solution.py:37
  139.2 2.0 %collective-permute-done.11.far3 = bf16[2,384,128]{2,1,0:T(8,128)(2,1)S(1)} collective-permute-done((bf16[2,384,128]{2,1,0:T(8,128)(2,1)S(1)}, bf16[2,384,128]{2,1,0:T(8,128)(2,1)S(1)}, u32[]{:S(2)}, u32[]{:S(2)}) %collective-permute-start.11) | collective-permute-done | bytes 196640 | tf_op jit(solution)/shard_map/ppermute | solution.py:37
  141.2 0.8 grad_sum.1
  142.0 0.0 all-to-all-done.1.parts
  142.0 0.1 chunk_sum.1
  142.1 0.7 copy.10
  (37 shorter events, 0.2 us)
Async XLA Ops:
  7.2 22.3 %copy-start.18 = (bf16[1,86,128]{2,1,0:T(8,128)(2,1)S(1)}, bf16[1,86,128]{2,1,0:T(8,128)(2,1)}, u32[]{:S(2)}) copy-start(bf16[1,86,128]{2,1,0:T(8,128)(2,1)} %param.10) | copy-start | bytes 66052
  7.2 82.3 %all-gather.2.cloned.1.call-start = ((), (), s32[]{:S(2)}) async-start(), calls=%async_computation.2 | async-start | bytes 3538944 | tf_op jit(solution)/shard_map/all_gather | solution.py:186
  7.2 20.4 %collective-permute-start = (bf16[384,256]{1,0:T(8,128)(2,1)}, bf16[384,256]{1,0:T(8,128)(2,1)S(1)}, u32[]{:S(2)}, u32[]{:S(2)}) collective-permute-start(bf16[384,256]{1,0:T(8,128)(2,1)} %param.9), channel_id=1, source_target_pairs={{0,1},{1,0},{2,3},{3,2},{4,5},{5,4},{6,7},{7,6},{8,9},{9,8},{10,11... | collective-permute-start | bytes 589832 | tf_op jit(solution)/shard_map/ppermute | solution.py:52
  29.4 19.7 %copy-start.16 = (bf16[384,128]{1,0:T(8,128)(2,1)S(1)}, bf16[384,128]{1,0:T(8,128)(2,1)}, u32[]{:S(2)}) copy-start(bf16[384,128]{1,0:T(8,128)(2,1)} %param.8) | copy-start | bytes 294916
  29.4 19.7 %copy-start.17 = (bf16[384,128]{1,0:T(8,128)(2,1)S(1)}, bf16[384,128]{1,0:T(8,128)(2,1)}, u32[]{:S(2)}) copy-start(bf16[384,128]{1,0:T(8,128)(2,1)} %param.7) | copy-start | bytes 294916
  30.3 45.8 %all-to-all-start = ((bf16[24,88,128]{2,1,0:T(8,128)(2,1)}), bf16[24,88,128]{2,1,0:T(8,128)(2,1)S(1)}, u32[]{:S(2)}, u32[]{:S(2)}) async-start(bf16[24,88,128]{2,1,0:T(8,128)(2,1)} %broadcast_in_dim.13), calls=%async_computation | async-start | bytes 1081344 | tf_op jit(solution)/shard_map/all_to_all | solution.py:191
  47.9 31.1 %copy-start.19 = (s32[3,6]{1,0:T(4,128)S(1)}, s32[3,6]{1,0:T(4,128)}, u32[]{:S(2)}) copy-start(s32[3,6]{1,0:T(4,128)} %param.11) | copy-start | bytes 220
  47.9 31.3 %copy-start.7 = (bf16[384,128]{1,0:T(8,128)(2,1)S(1)}, bf16[384,128]{1,0:T(8,128)(2,1)}, u32[]{:S(2)}) copy-start(bf16[384,128]{1,0:T(8,128)(2,1)} %q.3) | copy-start | bytes 294916
  49.2 20.1 %collective-permute-start.2 = (bf16[2,128,128]{2,1,0:T(8,128)(2,1)S(1)}, bf16[2,128,128]{2,1,0:T(8,128)(2,1)S(1)}, u32[]{:S(2)}, u32[]{:S(2)}) collective-permute-start(bf16[2,128,128]{2,1,0:T(8,128)(2,1)S(1)} %get-tuple-element.35), channel_id=1, source_target_pairs={{0,16},{16,0},{32,48},{48,32},{64,80},{80,64},{96,112},{112,96},{1... | collective-permute-start | bytes 196616 | tf_op jit(solution)/shard_map/ppermute | solution.py:48
  51.1 18.2 %collective-permute-start.1 = (bf16[2,128,128]{2,1,0:T(8,128)(2,1)S(1)}, bf16[2,128,128]{2,1,0:T(8,128)(2,1)S(1)}, u32[]{:S(2)}, u32[]{:S(2)}) collective-permute-start(bf16[2,128,128]{2,1,0:T(8,128)(2,1)S(1)} %get-tuple-element.36), channel_id=1, source_target_pairs={{0,752},{16,32},{32,16},{48,64},{64,48},{80,96},{96,80},{112,128},... | collective-permute-start | bytes 196616 | tf_op jit(solution)/shard_map/ppermute | solution.py:43
  59.7 11.9 %collective-permute-start.3 = (bf16[2,384,128]{2,1,0:T(8,128)(2,1)S(1)}, bf16[2,384,128]{2,1,0:T(8,128)(2,1)S(1)}, u32[]{:S(2)}, u32[]{:S(2)}) collective-permute-start(bf16[2,384,128]{2,1,0:T(8,128)(2,1)S(1)} %maximum_select_fusion.kv), channel_id=1, source_target_pairs={{0,576},{16,592},{32,608},{48,624},{64,640},{80,656},{96,672},{112... | collective-permute-start | bytes 589832 | tf_op jit(solution)/shard_map/ppermute | solution.py:37
  62.1 10.6 %collective-permute-start.4 = (bf16[2,384,128]{2,1,0:T(8,128)(2,1)S(1)}, bf16[2,384,128]{2,1,0:T(8,128)(2,1)S(1)}, u32[]{:S(2)}, u32[]{:S(2)}) collective-permute-start(bf16[2,384,128]{2,1,0:T(8,128)(2,1)S(1)} %maximum_select_fusion.kv), channel_id=1, source_target_pairs={{0,384},{16,400},{32,416},{48,432},{64,448},{80,464},{96,480},{112... | collective-permute-start | bytes 589832 | tf_op jit(solution)/shard_map/ppermute | solution.py:37
  67.4 7.6 %collective-permute-start.5 = (bf16[2,384,128]{2,1,0:T(8,128)(2,1)S(1)}, bf16[2,384,128]{2,1,0:T(8,128)(2,1)S(1)}, u32[]{:S(2)}, u32[]{:S(2)}) collective-permute-start(bf16[2,384,128]{2,1,0:T(8,128)(2,1)S(1)} %maximum_select_fusion.kv), channel_id=1, source_target_pairs={{0,192},{16,208},{32,224},{48,240},{64,256},{80,272},{96,288},{112... | collective-permute-start | bytes 589832 | tf_op jit(solution)/shard_map/ppermute | solution.py:37
  69.3 11.8 %copy-start.1 = (bf16[2,128,128]{2,1,0:T(8,128)(2,1)}, bf16[2,128,128]{2,1,0:T(8,128)(2,1)S(1)}, u32[]{:S(2)}) copy-start(bf16[2,128,128]{2,1,0:T(8,128)(2,1)S(1)} %get-tuple-element.41.nxt) | copy-start | bytes 196612
  69.4 11.8 %copy-start.3 = (bf16[2,128,128]{2,1,0:T(8,128)(2,1)}, bf16[2,128,128]{2,1,0:T(8,128)(2,1)S(1)}, u32[]{:S(2)}) copy-start(bf16[2,128,128]{2,1,0:T(8,128)(2,1)S(1)} %get-tuple-element.42.prev) | copy-start | bytes 196612
  77.0 4.8 %collective-permute-start.6 = (bf16[24,88,128]{2,1,0:T(8,128)(2,1)}, bf16[24,88,128]{2,1,0:T(8,128)(2,1)S(1)}, u32[]{:S(2)}, u32[]{:S(2)}) collective-permute-start(bf16[24,88,128]{2,1,0:T(8,128)(2,1)} %broadcast_select_fusion), channel_id=1, source_target_pairs={{0,16},{16,0},{32,48},{48,32},{64,80},{80,64},{96,112},{112,96},{1... | collective-permute-start | bytes 1622024 | tf_op jit(solution)/shard_map/ppermute | solution.py:48
  79.2 2.0 %copy-start.13 = (s32[13]{0:T(128)}, s32[13]{0:T(128)S(1)}, u32[]{:S(2)}) copy-start(s32[13]{0:T(128)S(1)} %concatenate.9.meta) | copy-start | bytes 160
  81.2 0.6 copy-start.9
  81.8 0.8 copy-start.5
  82.6 1.1 copy-start.6
  83.7 0.7 copy-start.14
  89.5 1.9 %copy-start = (bf16[6144,256]{1,0:T(8,128)(2,1)S(1)}, bf16[6144,256]{1,0:T(8,128)(2,1)}, u32[]{:S(2)}) copy-start(bf16[6144,256]{1,0:T(8,128)(2,1)} %all-gather.2.cloned.1.call-done.pieces) | copy-start | bytes 9437188
  91.4 0.9 copy-start.10
  92.3 0.7 copy-start.15
  93.0 6.3 %copy-start.2 = (bf16[2,128,128]{2,1,0:T(8,128)(2,1)S(1)}, bf16[2,128,128]{2,1,0:T(8,128)(2,1)}, u32[]{:S(2)}) copy-start(bf16[2,128,128]{2,1,0:T(8,128)(2,1)} %copy-done.1) | copy-start | bytes 196612
  93.0 6.3 %copy-start.4 = (bf16[2,128,128]{2,1,0:T(8,128)(2,1)S(1)}, bf16[2,128,128]{2,1,0:T(8,128)(2,1)}, u32[]{:S(2)}) copy-start(bf16[2,128,128]{2,1,0:T(8,128)(2,1)} %copy-done.3) | copy-start | bytes 196612
  93.0 6.4 %copy-start.8 = (bf16[384,128]{1,0:T(8,128)(2,1)S(1)}, bf16[384,128]{1,0:T(8,128)(2,1)}, u32[]{:S(2)}) copy-start(bf16[384,128]{1,0:T(8,128)(2,1)} %q.3) | copy-start | bytes 294916
  97.4 4.8 %collective-permute-start.12 = (f32[24,88,128]{2,1,0:T(8,128)S(1)}, f32[24,88,128]{2,1,0:T(8,128)S(1)}, u32[]{:S(2)}, u32[]{:S(2)}) collective-permute-start(f32[24,88,128]{2,1,0:T(8,128)S(1)} %get-tuple-element.27), channel_id=1, source_target_pairs={{0,16},{16,0},{32,48},{48,32},{64,80},{80,64},{96,112},{112,96},{1... | collective-permute-start | bytes 3244040 | tf_op jit(solution)/shard_map/ppermute | solution.py:48
  101.5 0.6 copy-start.11
  103.1 11.6 %copy-start.12 = (bf16[2,128,128]{2,1,0:T(8,128)(2,1)S(1)}, bf16[2,128,128]{2,1,0:T(8,128)(2,1)}, u32[]{:S(2)}) copy-start(bf16[2,128,128]{2,1,0:T(8,128)(2,1)} %copy-done.11) | copy-start | bytes 196612
  103.1 38.9 %all-to-all-start.1 = ((bf16[24,88,128]{2,1,0:T(8,128)(2,1)}), bf16[24,88,128]{2,1,0:T(8,128)(2,1)S(1)}, u32[]{:S(2)}, u32[]{:S(2)}) async-start(bf16[24,88,128]{2,1,0:T(8,128)(2,1)} %pair_sum.1), calls=%async_computation.1 | async-start | bytes 1081344 | tf_op jit(solution)/shard_map/all_to_all | solution.py:261
  114.7 19.6 %collective-permute-start.8 = (bf16[2,128,128]{2,1,0:T(8,128)(2,1)S(1)}, bf16[2,128,128]{2,1,0:T(8,128)(2,1)S(1)}, u32[]{:S(2)}, u32[]{:S(2)}) collective-permute-start(bf16[2,128,128]{2,1,0:T(8,128)(2,1)S(1)} %get-tuple-element.39), channel_id=1, source_target_pairs={{0,16},{16,0},{32,48},{48,32},{64,80},{80,64},{96,112},{112,96},{1... | collective-permute-start | bytes 196616 | tf_op jit(solution)/shard_map/ppermute | solution.py:48
  116.7 17.7 %collective-permute-start.7 = (bf16[2,128,128]{2,1,0:T(8,128)(2,1)S(1)}, bf16[2,128,128]{2,1,0:T(8,128)(2,1)S(1)}, u32[]{:S(2)}, u32[]{:S(2)}) collective-permute-start(bf16[2,128,128]{2,1,0:T(8,128)(2,1)S(1)} %get-tuple-element.40), channel_id=1, source_target_pairs={{0,752},{16,32},{32,16},{48,64},{64,48},{80,96},{96,80},{112,128},... | collective-permute-start | bytes 196616 | tf_op jit(solution)/shard_map/ppermute | solution.py:43
  125.3 10.4 %collective-permute-start.9 = (bf16[2,384,128]{2,1,0:T(8,128)(2,1)S(1)}, bf16[2,384,128]{2,1,0:T(8,128)(2,1)S(1)}, u32[]{:S(2)}, u32[]{:S(2)}) collective-permute-start(bf16[2,384,128]{2,1,0:T(8,128)(2,1)S(1)} %get-tuple-element.34), channel_id=1, source_target_pairs={{0,192},{16,208},{32,224},{48,240},{64,256},{80,272},{96,288},{112... | collective-permute-start | bytes 589832 | tf_op jit(solution)/shard_map/ppermute | solution.py:37
  129.6 9.6 %collective-permute-start.10 = (bf16[2,384,128]{2,1,0:T(8,128)(2,1)S(1)}, bf16[2,384,128]{2,1,0:T(8,128)(2,1)S(1)}, u32[]{:S(2)}, u32[]{:S(2)}) collective-permute-start(bf16[2,384,128]{2,1,0:T(8,128)(2,1)S(1)} %get-tuple-element.33), channel_id=1, source_target_pairs={{0,384},{16,400},{32,416},{48,432},{64,448},{80,464},{96,480},{112... | collective-permute-start | bytes 589832 | tf_op jit(solution)/shard_map/ppermute | solution.py:37
  131.8 9.5 %collective-permute-start.11 = (bf16[2,384,128]{2,1,0:T(8,128)(2,1)S(1)}, bf16[2,384,128]{2,1,0:T(8,128)(2,1)S(1)}, u32[]{:S(2)}, u32[]{:S(2)}) collective-permute-start(bf16[2,384,128]{2,1,0:T(8,128)(2,1)S(1)} %get-tuple-element.32), channel_id=1, source_target_pairs={{0,576},{16,592},{32,608},{48,624},{64,640},{80,656},{96,672},{112... | collective-permute-start | bytes 589832 | tf_op jit(solution)/shard_map/ppermute | solution.py:37
Sparse Core Ops, SparseCore 0:
  29.5 59.9 all-gather.1

commit v6 on v5

--- a/solution.py
+++ b/solution.py
@@ -23,6 +23,7 @@
 Y_GROUPS = [[2 * y + z for y in range(NY)] for z in range(2)]
 SMEM = pl.BlockSpec(memory_space=pltpu.SMEM)
 VMEM = pl.BlockSpec(memory_space=pltpu.VMEM)
+ANY = pl.BlockSpec(memory_space=pl.ANY)
 PARAMS = pltpu.CompilerParams(vmem_limit_bytes=12 * 1024 * 1024)
 
 M_X, M_CORE, M_Y, M_Z = 9, 10, 11, 12
@@ -37,10 +38,14 @@
     return lax.ppermute(value, "ctx", pairs)
 
 
+def outer_swap(value):
+    pairs = [(s, (s - 1 if s % 2 == 0 else s + 1) % N_CTX) for s in range(N_CTX)]
+    return lax.ppermute(value, "ctx", pairs)
+
+
 def neighbours(first, last, even):
     inner = core_swap(jnp.where(even, last, first))
-    pairs = [(s, (s - 1 if s % 2 == 0 else s + 1) % N_CTX) for s in range(N_CTX)]
-    outer = lax.ppermute(jnp.where(even, first, last), "ctx", pairs)
+    outer = outer_swap(jnp.where(even, first, last))
     return jnp.where(even, outer, inner), jnp.where(even, inner, outer)
 
 
@@ -77,6 +82,17 @@
         probs = terms / jnp.sum(terms, axis=-1, keepdims=True)
         probs_out[j] = probs
         att_out[rows] = dot(probs.astype(BF16), vals, 1, 0).astype(BF16)
+
+
+def join_kernel(own, twin, out, sems):
+    copies = [
+        pltpu.make_async_copy(own, out.at[:384], sems.at[0]),
+        pltpu.make_async_copy(twin, out.at[384:], sems.at[1]),
+    ]
+    for copy in copies:
+        copy.start()
+    for copy in copies:
+        copy.wait()
 
 
 def weight_kernel(meta, own, other, w_out, flat):
@@ -94,12 +110,20 @@
             w_out[t, :, e * 128 : (e + 1) * 128] = rows.astype(BF16)
 
 
-def cotangent_kernel(meta, w, att, pieces, keep, give, grad, cols, flat):
-    z = meta[M_Z]
+def cotangent_kernel(w, att_any, pieces_any, keep, give, grad, att, pieces, cols, flat, sems):
+    copies = [pltpu.make_async_copy(att_any, att, sems.at[N_TP])]
+    for i in range(N_TP):
+        rows = slice(i * 384, (i + 1) * 384)
+        copies.append(pltpu.make_async_copy(pieces_any.at[rows], pieces.at[rows], sems.at[i]))
+    for copy in copies:
+        copy.start()
+    z = lax.axis_index("tp") % 2
+    copies[0].wait()
     att_now = att[...]
     total = jnp.zeros((384, DH), F32)
     for i in range(N_TP):
         col = 2 * (i // 2) + (z if i % 2 == 0 else 1 - z)
+        copies[i + 1].wait()
         cot = pieces[i * 384 : (i + 1) * 384]
         cols[col] = dot(att_now, cot, 0, 0)
         total = total + dot(cot, w[col], 1, 1)
@@ -108,7 +132,7 @@
         for e in range(2):
             flat[pl.ds(2 * t + e, DH, stride=32)] = cols[t, :, e * 128 : (e + 1) * 128]
     flat[FLAT_ROWS:] = jnp.zeros((flat.shape[0] - FLAT_ROWS, 128), F32)
-    first = meta[M_CORE] == 0
+    first = lax.axis_index("ctx") % 2 == 0
     for i in range(CHIPS):
         a = flat[2 * i * SHARD : 2 * i * SHARD + SHARD_PAD]
         b = flat[(2 * i + 1) * SHARD : (2 * i + 1) * SHARD + SHARD_PAD]
@@ -118,12 +142,14 @@
 
 def backward_kernel(
     meta, q, kv, prev, nxt, far1, far2, far3, probs, att, out_grad,
-    dq, dkv, dprev, dnext, dfar, acc,
+    dq, dkv, inner, outer, dfar1, dfar2, dfar3, acc,
 ):
     far = (far1, far2, far3)
+    even = lax.axis_index("ctx") % 2 == 0
     acc[...] = jnp.zeros(acc.shape, F32)
     dkv[...] = jnp.zeros(dkv.shape, F32)
     scale = DH**-0.5
+    to_prev = []
     for j in range(3):
         rows = slice(j * BLK, (j + 1) * BLK)
         grad = out_grad[rows]
@@ -138,17 +164,20 @@
             part = parts[which]
             dkv[which, rows] += part[:BLK]
             if j == 0:
-                dprev[which] = part[BLK : 2 * BLK].astype(BF16)
+                to_prev.append(part[BLK : 2 * BLK])
             else:
                 dkv[which, (j - 1) * BLK : j * BLK] += part[BLK : 2 * BLK]
             if j == 2:
-                dnext[which] = part[2 * BLK : 3 * BLK].astype(BF16)
+                to_next = part[2 * BLK : 3 * BLK]
+                inner[which] = jnp.where(even, to_next, to_prev[which]).astype(BF16)
+                outer[which] = jnp.where(even, to_prev[which], to_next).astype(BF16)
             else:
                 dkv[which, (j + 1) * BLK : (j + 2) * BLK] += part[2 * BLK : 3 * BLK]
             for k in range(3):
                 row = pl.multiple_of(meta[3 * j + k] * BLK, BLK)
                 acc[k, which, pl.ds(row, BLK)] += part[(3 + k) * BLK : (4 + k) * BLK]
-    dfar[...] = acc[...].astype(BF16)
+    for k, out in enumerate((dfar1, dfar2, dfar3)):
+        out[...] = acc[k].astype(BF16)
 
 
 def pair_sum_kernel(keep, other, dkv, out):
@@ -163,16 +192,18 @@
     out[0] = total[:SHARD]
 
 
-def grad_sum_kernel(dkv, prev, nxt, far1, far2, far3, dk, dv):
+def far_sum_kernel(dkv, far1, far2, far3, out):
+    parts = [far[...].astype(F32) for far in (far1, far2, far3)]
+    out[...] = dkv[...] + parts[0] + parts[1] + parts[2]
+
+
+def band_sum_kernel(total, inner, outer, dk, dv):
+    even = lax.axis_index("ctx") % 2 == 0
     for which, out in ((0, dk), (1, dv)):
-        out[...] = (
-            dkv[which]
-            + far1[which].astype(F32)
-            + far2[which].astype(F32)
-            + far3[which].astype(F32)
-        )
-        out[:BLK] += prev[which].astype(F32)
-        out[2 * BLK :] += nxt[which].astype(F32)
+        near, away = inner[which].astype(F32), outer[which].astype(F32)
+        out[...] = total[which]
+        out[:BLK] += jnp.where(even, away, near)
+        out[2 * BLK :] += jnp.where(even, near, away)
 
 
 def on_device(queries, key_rows, values, cotangent, w_flat, block_keys):
@@ -183,8 +214,16 @@
     meta = jnp.concatenate([picked, place])
 
     twin = twin_swap(cotangent)
+    joined = pl.pallas_call(
+        join_kernel,
+        out_shape=jax.ShapeDtypeStruct((2 * 384, WCOL), BF16),
+        in_specs=[ANY, ANY],
+        out_specs=ANY,
+        scratch_shapes=[pltpu.SemaphoreType.DMA((2,))],
+        name="join_pieces",
+    )(cotangent, twin)
     pieces = lax.all_gather(
-        jnp.concatenate([cotangent, twin], axis=0),
+        joined,
         "tp", axis=0, tiled=True, axis_index_groups=Y_GROUPS,
     )
     w_pad = jnp.concatenate([w_flat[0], twin[: SHARD_PAD - SHARD, :128]], axis=0)
@@ -225,27 +264,30 @@
     keep, give, out_grad = pl.pallas_call(
         cotangent_kernel,
         out_shape=(chunk, chunk, jax.ShapeDtypeStruct((384, DH), BF16)),
-        in_specs=[SMEM, VMEM, VMEM, VMEM],
+        in_specs=[VMEM, ANY, ANY],
         out_specs=(VMEM, VMEM, VMEM),
         scratch_shapes=[
+            pltpu.VMEM((384, DH), BF16),
+            pltpu.VMEM((N_TP * 384, WCOL), BF16),
             pltpu.VMEM((N_TP, DH, WCOL), F32),
             pltpu.VMEM((flat_alloc, 128), F32),
+            pltpu.SemaphoreType.DMA((N_TP + 1,)),
         ],
-        compiler_params=PARAMS,
+        compiler_params=pltpu.CompilerParams(vmem_limit_bytes=52 * 1024 * 1024),
         name="cotangent_products",
-    )(meta, weight, att, pieces)
+    )(weight, att, pieces)
     two = (2, 384, DH)
-    dq, dkv, dprev, dnext, dfar = pl.pallas_call(
+    dq, dkv, inner, outer, *dfar = pl.pallas_call(
         backward_kernel,
         out_shape=(
             jax.ShapeDtypeStruct((384, DH), F32),
             jax.ShapeDtypeStruct(two, F32),
             jax.ShapeDtypeStruct((2, BLK, DH), BF16),
             jax.ShapeDtypeStruct((2, BLK, DH), BF16),
-            jax.ShapeDtypeStruct((3,) + two, BF16),
-        ),
+        )
+        + (jax.ShapeDtypeStruct(two, BF16),) * 3,
         in_specs=[SMEM] + [VMEM] * 10,
-        out_specs=(VMEM,) * 5,
+        out_specs=(VMEM,) * 7,
         scratch_shapes=[pltpu.VMEM((3,) + two, F32)],
         compiler_params=PARAMS,
         name="attention_backward",
@@ -253,7 +295,7 @@
     pair_sum = pl.pallas_call(
         pair_sum_kernel,
         out_shape=jax.ShapeDtypeStruct((CHIPS, SHARD_PAD, 128), BF16),
-        in_specs=[VMEM, VMEM, pl.BlockSpec(memory_space=pl.ANY)],
+        in_specs=[VMEM, VMEM, ANY],
         out_specs=VMEM,
         compiler_params=PARAMS,
         name="pair_sum",
@@ -269,14 +311,19 @@
     )(spread)
 
     far_back = [x_shift(dfar[k], k + 1) for k in range(3)]
-    from_prev, from_next = neighbours(dprev, dnext, even)
+    total = pl.pallas_call(
+        far_sum_kernel,
+        out_shape=jax.ShapeDtypeStruct(two, F32),
+        compiler_params=PARAMS,
+        name="far_sum",
+    )(dkv, *far_back)
     grad = jax.ShapeDtypeStruct((384, DH), F32)
     dk, dv = pl.pallas_call(
-        grad_sum_kernel,
+        band_sum_kernel,
         out_shape=(grad, grad),
         compiler_params=PARAMS,
-        name="grad_sum",
-    )(dkv, from_prev, from_next, *far_back)
+        name="band_sum",
+    )(total, core_swap(inner), outer_swap(outer))
     return dq, dk, dv, weight_grad
 
 

time: 151 us -> 162 us (1.073)
  the two profiles are of different devices: /device:TPU:6 before, /device:TPU:8 now
where the time goes in v6:
time: 162 us
  starting transfers between devices  89.6 us (55%)
  Pallas kernels  29.2 us (18%)
  between operations  18.5 us (11%)
  waiting for transfers between devices  11.7 us (7%)
  local copies, waits for them, and re-layouts  11.6 us (7%)
    ppermute x6, starting transfers between devices, x_shift(): return lax.ppermute(value, 'ctx', pairs)  19.7 us
    ppermute x2, starting transfers between devices, outer_swap(): return lax.ppermute(value, 'ctx', pairs)  18.5 us
    all_to_all x1, starting transfers between devices, on_device(): lax.all_to_all(jnp.broadcast_to(w_pad[None], (CHIPS, SHARD_PAD, 128)), 'c...  17.2 us
    ppermute x1, starting transfers between devices, twin_swap(): return lax.ppermute(value, 'tp', [(s, s ^ 1) for s in range(N_TP)])  15.1 us
    pallas_call x1, Pallas kernels, on_device(): pl.pallas_call(join_kernel, out_shape=jax.ShapeDtypeStruct((2 * 384, WCOL...  13 us
    all_to_all x1, starting transfers between devices, on_device(): lax.all_to_all(pair_sum, 'ctx', 0, 0, tiled=True, axis_index_groups=SAME_...  11.2 us
    ppermute x4, starting transfers between devices, core_swap(): return lax.ppermute(value, 'ctx', [(s, s ^ 1) for s in range(N_CTX)])  7.76 us
    pallas_call x1, Pallas kernels, on_device(): pl.pallas_call(cotangent_kernel, out_shape=(chunk, chunk, jax.ShapeDtypeS...  7.72 us
  transfers between devices with their start and end apart: 16, of which 5 were waited for; matrix products, arithmetic and copies ran while one was open for 4% of the time, Pallas kernels for 5%

profile of v6, /device:TPU:8, one launch (start us, length us, event | category | flops | bytes accessed | tf_op | source)
XLA Modules:
  0.0 161.6 jit_solution(11191170256525852076)
XLA Ops:
  7.2 0.0 all-gather.2.cloned.1.call-start
  7.2 15.1 %collective-permute-start = (bf16[384,256]{1,0:T(8,128)(2,1)}, bf16[384,256]{1,0:T(8,128)(2,1)S(1)}, u32[]{:S(2)}, u32[]{:S(2)}) collective-permute-start(bf16[384,256]{1,0:T(8,128)(2,1)} %own.1), channel_id=1, source_target_pairs={{0,1},{1,0},{2,3},{3,2},{4,5},{5,4},{6,7},{7,6},{8,9},{9,8},{10,11... | collective-permute-start | bytes 589832 | tf_op jit(solution)/shard_map/ppermute | solution.py:57
  22.4 5.3 %collective-permute-done.twin = bf16[384,256]{1,0:T(8,128)(2,1)S(1)} collective-permute-done((bf16[384,256]{1,0:T(8,128)(2,1)}, bf16[384,256]{1,0:T(8,128)(2,1)S(1)}, u32[]{:S(2)}, u32[]{:S(2)}) %collective-permute-start) | collective-permute-done | bytes 196640 | tf_op jit(solution)/shard_map/ppermute | solution.py:57
  27.7 0.7 copy-done.16
  28.3 13.0 %join_pieces.1 = bf16[768,256]{1,0:T(8,128)(2,1)} custom-call(bf16[384,256]{1,0:T(8,128)(2,1)} %own.1, bf16[384,256]{1,0:T(8,128)(2,1)} %copy-done.16), custom_call_target="tpu_custom_call" | custom-call | tf_op jit(solution)/shard_map/join_pieces/pallas_call | solution.py:217
  41.4 0.0 copy-start.17
  41.4 0.0 copy-start.18
  41.4 0.0 all-gather.2.cloned.1.call-update
  41.4 0.7 slice.43
  42.2 0.9 broadcast_in_dim.13
  43.0 17.2 %all-to-all-start = ((bf16[24,88,128]{2,1,0:T(8,128)(2,1)}), bf16[24,88,128]{2,1,0:T(8,128)(2,1)S(1)}, u32[]{:S(2)}, u32[]{:S(2)}) async-start(bf16[24,88,128]{2,1,0:T(8,128)(2,1)} %broadcast_in_dim.13), calls=%async_computation | async-start | bytes 1081344 | tf_op jit(solution)/shard_map/all_to_all | solution.py:230
  60.3 0.0 copy-start.20
  60.3 0.0 copy-start.7
  60.3 1.2 slice.40
  62.3 1.9 %collective-permute-start.2 = (bf16[2,128,128]{2,1,0:T(8,128)(2,1)S(1)}, bf16[2,128,128]{2,1,0:T(8,128)(2,1)S(1)}, u32[]{:S(2)}, u32[]{:S(2)}) collective-permute-start(bf16[2,128,128]{2,1,0:T(8,128)(2,1)S(1)} %get-tuple-element.36), channel_id=1, source_target_pairs={{0,16},{16,0},{32,48},{48,32},{64,80},{80,64},{96,112},{112,96},{1... | collective-permute-start | bytes 196616 | tf_op jit(solution)/shard_map/ppermute | solution.py:53
  64.2 10.8 %collective-permute-start.1 = (bf16[2,128,128]{2,1,0:T(8,128)(2,1)S(1)}, bf16[2,128,128]{2,1,0:T(8,128)(2,1)S(1)}, u32[]{:S(2)}, u32[]{:S(2)}) collective-permute-start(bf16[2,128,128]{2,1,0:T(8,128)(2,1)S(1)} %get-tuple-element.37), channel_id=1, source_target_pairs={{0,752},{16,32},{32,16},{48,64},{64,48},{80,96},{96,80},{112,128},... | collective-permute-start | bytes 196616 | tf_op jit(solution)/shard_map/ppermute | solution.py:43
  75.0 2.7 %collective-permute-start.3 = (bf16[2,384,128]{2,1,0:T(8,128)(2,1)S(1)}, bf16[2,384,128]{2,1,0:T(8,128)(2,1)S(1)}, u32[]{:S(2)}, u32[]{:S(2)}) collective-permute-start(bf16[2,384,128]{2,1,0:T(8,128)(2,1)S(1)} %maximum_select_fusion.kv), channel_id=1, source_target_pairs={{0,576},{16,592},{32,608},{48,624},{64,640},{80,656},{96,672},{112... | collective-permute-start | bytes 589832 | tf_op jit(solution)/shard_map/ppermute | solution.py:38
  77.8 2.5 %collective-permute-start.4 = (bf16[2,384,128]{2,1,0:T(8,128)(2,1)S(1)}, bf16[2,384,128]{2,1,0:T(8,128)(2,1)S(1)}, u32[]{:S(2)}, u32[]{:S(2)}) collective-permute-start(bf16[2,384,128]{2,1,0:T(8,128)(2,1)S(1)} %maximum_select_fusion.kv), channel_id=1, source_target_pairs={{0,384},{16,400},{32,416},{48,432},{64,448},{80,464},{96,480},{112... | collective-permute-start | bytes 589832 | tf_op jit(solution)/shard_map/ppermute | solution.py:38
  80.2 2.8 %collective-permute-start.5 = (bf16[2,384,128]{2,1,0:T(8,128)(2,1)S(1)}, bf16[2,384,128]{2,1,0:T(8,128)(2,1)S(1)}, u32[]{:S(2)}, u32[]{:S(2)}) collective-permute-start(bf16[2,384,128]{2,1,0:T(8,128)(2,1)S(1)} %maximum_select_fusion.kv), channel_id=1, source_target_pairs={{0,192},{16,208},{32,224},{48,240},{64,256},{80,272},{96,288},{112... | collective-permute-start | bytes 589832 | tf_op jit(solution)/shard_map/ppermute | solution.py:38
  83.0 0.0 collective-permute-done.2
  83.0 0.0 collective-permute-done.1
  83.1 0.0 copy-start.1
  83.1 0.0 copy-start.3
  83.1 0.5 slice.44
  83.6 0.5 slice.45
  85.4 0.0 collective-permute-done.3.far1
  85.5 0.5 slice.46
  86.6 0.2 collective-permute-done.4.far2
  86.8 0.5 slice.47
  88.0 1.1 collective-permute-done.5.far3
  89.1 0.5 slice.48
  90.3 0.0 all-to-all-done.own
  90.3 0.8 broadcast_select_fusion
  91.1 1.9 %collective-permute-start.6 = (bf16[24,88,128]{2,1,0:T(8,128)(2,1)}, bf16[24,88,128]{2,1,0:T(8,128)(2,1)S(1)}, u32[]{:S(2)}, u32[]{:S(2)}) collective-permute-start(bf16[24,88,128]{2,1,0:T(8,128)(2,1)} %broadcast_select_fusion), channel_id=1, source_target_pairs={{0,16},{16,0},{32,48},{48,32},{64,80},{80,64},{96,112},{112,96},{1... | collective-permute-start | bytes 1622024 | tf_op jit(solution)/shard_map/ppermute | solution.py:53
  93.1 0.1 add_select_fusion
  93.2 0.1 reshape.18
  93.3 0.1 concatenate.6.meta
  93.3 1.9 %attention_forward.1 = (f32[3,128,768]{2,1,0:T(8,128)S(1)}, bf16[384,128]{1,0:T(8,128)(2,1)S(1)}) custom-call(s32[13]{0:T(128)S(1)} %concatenate.6.meta, bf16[384,128]{1,0:T(8,128)(2,1)S(1)} %copy-done.7, bf16[2,384,128]{2,1,0:T(8,128)(2,1)S(1)} %maximum_select_fusion.kv, bf16[2,128,128]{2,1,0:T(8,128)(2,1)S(1)} %get-tuple-element.39.prev, ...), custom_call_target="tpu_custom_call" | custom-call | tf_op jit(solution)/shard_map/attention_forward/pallas_call | solution.py:251
  95.3 0.0 copy-start.9
  95.3 0.6 copy-done.9
  96.0 0.8 copy-done.5
  96.8 1.0 copy-done.6
  97.8 0.7 copy-done.12
  98.5 2.4 %weight_rows.1.w = bf16[16,128,256]{2,1,0:T(8,128)(2,1)S(1)} custom-call(s32[13]{0:T(128)S(1)} %copy-done.12, bf16[24,88,128]{2,1,0:T(8,128)(2,1)S(1)} %all-to-all-done.own, bf16[24,88,128]{2,1,0:T(8,128)(2,1)S(1)} %copy-done.6), custom_call_target="tpu_custom_call" | custom-call | tf_op jit(solution)/shard_map/weight_rows/pallas_call | solution.py:241
  100.8 0.4 all-gather.2.cloned.1.call-done.pieces_any
  101.3 0.9 copy-done.10
  102.2 7.7 %cotangent_products.1 = (f32[24,88,128]{2,1,0:T(8,128)}, f32[24,88,128]{2,1,0:T(8,128)}, bf16[384,128]{1,0:T(8,128)(2,1)S(1)}) custom-call(bf16[16,128,256]{2,1,0:T(8,128)(2,1)S(1)} %weight_rows.1.w, bf16[384,128]{1,0:T(8,128)(2,1)S(1)} %copy-done.10, bf16[6144,256]{1,0:T(8,128)(2,1)} %all-gather.2.cloned.1.call-done.pieces_any), custom_call_target="tpu_custom_call" | custom-call | tf_op jit(solution)/shard_map/cotangent_products/pallas_call | solution.py:264
  109.9 2.0 %collective-permute-start.12 = (f32[24,88,128]{2,1,0:T(8,128)}, f32[24,88,128]{2,1,0:T(8,128)S(1)}, u32[]{:S(2)}, u32[]{:S(2)}) collective-permute-start(f32[24,88,128]{2,1,0:T(8,128)} %get-tuple-element.31), channel_id=1, source_target_pairs={{0,16},{16,0},{32,48},{48,32},{64,80},{80,64},{96,112},{112,96},{1... | collective-permute-start | bytes 3244040 | tf_op jit(solution)/shard_map/ppermute | solution.py:53
  112.0 2.3 %attention_backward.1 = (f32[384,128]{1,0:T(8,128)}, f32[2,384,128]{2,1,0:T(8,128)S(1)}, bf16[2,128,128]{2,1,0:T(8,128)(2,1)S(1)}, bf16[2,128,128]{2,1,0:T(8,128...) custom-call(s32[13]{0:T(128)S(1)} %copy-done.13, ...), custom_call_target="tpu_custom_call" | custom-call | tf_op jit(solution)/shard_map/attention_backward/pallas_call | solution.py:280
  114.3 0.6 copy-done.14
  114.9 0.9 pair_sum.1
  115.8 11.2 %all-to-all-start.1 = ((bf16[24,88,128]{2,1,0:T(8,128)(2,1)}), bf16[24,88,128]{2,1,0:T(8,128)(2,1)S(1)}, u32[]{:S(2)}, u32[]{:S(2)}) async-start(bf16[24,88,128]{2,1,0:T(8,128)(2,1)} %pair_sum.1), calls=%async_computation.1 | async-start | bytes 1081344 | tf_op jit(solution)/shard_map/all_to_all | solution.py:303
  127.0 3.8 %collective-permute-start.7 = (bf16[2,384,128]{2,1,0:T(8,128)(2,1)S(1)}, bf16[2,384,128]{2,1,0:T(8,128)(2,1)S(1)}, u32[]{:S(2)}, u32[]{:S(2)}) collective-permute-start(bf16[2,384,128]{2,1,0:T(8,128)(2,1)S(1)} %get-tuple-element.23), channel_id=1, source_target_pairs={{0,192},{16,208},{32,224},{48,240},{64,256},{80,272},{96,288},{112... | collective-permute-start | bytes 589832 | tf_op jit(solution)/shard_map/ppermute | solution.py:38
  130.8 4.6 %collective-permute-start.8 = (bf16[2,384,128]{2,1,0:T(8,128)(2,1)S(1)}, bf16[2,384,128]{2,1,0:T(8,128)(2,1)S(1)}, u32[]{:S(2)}, u32[]{:S(2)}) collective-permute-start(bf16[2,384,128]{2,1,0:T(8,128)(2,1)S(1)} %get-tuple-element.24), channel_id=1, source_target_pairs={{0,384},{16,400},{32,416},{48,432},{64,448},{80,464},{96,480},{112... | collective-permute-start | bytes 589832 | tf_op jit(solution)/shard_map/ppermute | solution.py:38
  135.4 3.4 %collective-permute-start.9 = (bf16[2,384,128]{2,1,0:T(8,128)(2,1)S(1)}, bf16[2,384,128]{2,1,0:T(8,128)(2,1)S(1)}, u32[]{:S(2)}, u32[]{:S(2)}) collective-permute-start(bf16[2,384,128]{2,1,0:T(8,128)(2,1)S(1)} %get-tuple-element.25), channel_id=1, source_target_pairs={{0,576},{16,592},{32,608},{48,624},{64,640},{80,656},{96,672},{112... | collective-permute-start | bytes 589832 | tf_op jit(solution)/shard_map/ppermute | solution.py:38
  138.8 1.9 %collective-permute-start.10 = (bf16[2,128,128]{2,1,0:T(8,128)(2,1)S(1)}, bf16[2,128,128]{2,1,0:T(8,128)(2,1)S(1)}, u32[]{:S(2)}, u32[]{:S(2)}) collective-permute-start(bf16[2,128,128]{2,1,0:T(8,128)(2,1)S(1)} %copy-done.15), channel_id=1, source_target_pairs={{0,16},{16,0},{32,48},{48,32},{64,80},{80,64},{96,112},{112,96},{1... | collective-permute-start | bytes 196616 | tf_op jit(solution)/shard_map/ppermute | solution.py:53
  140.7 7.7 %collective-permute-start.11 = (bf16[2,128,128]{2,1,0:T(8,128)(2,1)S(1)}, bf16[2,128,128]{2,1,0:T(8,128)(2,1)S(1)}, u32[]{:S(2)}, u32[]{:S(2)}) collective-permute-start(bf16[2,128,128]{2,1,0:T(8,128)(2,1)S(1)} %get-tuple-element.27), channel_id=1, source_target_pairs={{0,752},{16,32},{32,16},{48,64},{64,48},{80,96},{96,80},{112,128},... | collective-permute-start | bytes 196616 | tf_op jit(solution)/shard_map/ppermute | solution.py:43
  148.4 0.0 collective-permute-done.7.far1
  148.4 0.0 collective-permute-done.8.far2
  148.5 0.1 far_sum.1.total
  148.6 4.6 %collective-permute-done.11.outer = bf16[2,128,128]{2,1,0:T(8,128)(2,1)S(1)} collective-permute-done((bf16[2,128,128]{2,1,0:T(8,128)(2,1)S(1)}, bf16[2,128,128]{2,1,0:T(8,128)(2,1)S(1)}, u32[]{:S(2)}, u32[]{:S(2)}) %collective-permute-start.11) | collective-permute-done | bytes 65568 | tf_op jit(solution)/shard_map/ppermute | solution.py:43
  153.2 0.8 band_sum.1
  154.0 0.1 chunk_sum.1
  154.0 0.7 copy.10
  (37 shorter events, 0.1 us)
Async XLA Ops:
  7.2 35.0 %copy-start.19 = (bf16[1,86,128]{2,1,0:T(8,128)(2,1)S(1)}, bf16[1,86,128]{2,1,0:T(8,128)(2,1)}, u32[]{:S(2)}) copy-start(bf16[1,86,128]{2,1,0:T(8,128)(2,1)} %param.10) | copy-start | bytes 66052
  7.2 94.1 %all-gather.2.cloned.1.call-start = ((), (), s32[]{:S(2)}) async-start(), calls=%async_computation.2 | async-start | bytes 3538944 | tf_op jit(solution)/shard_map/all_gather | solution.py:225
  7.2 20.4 %collective-permute-start = (bf16[384,256]{1,0:T(8,128)(2,1)}, bf16[384,256]{1,0:T(8,128)(2,1)S(1)}, u32[]{:S(2)}, u32[]{:S(2)}) collective-permute-start(bf16[384,256]{1,0:T(8,128)(2,1)} %own.1), channel_id=1, source_target_pairs={{0,1},{1,0},{2,3},{3,2},{4,5},{5,4},{6,7},{7,6},{8,9},{9,8},{10,11... | collective-permute-start | bytes 589832 | tf_op jit(solution)/shard_map/ppermute | solution.py:57
  27.7 0.7 copy-start.16
  41.4 20.8 %copy-start.17 = (bf16[384,128]{1,0:T(8,128)(2,1)S(1)}, bf16[384,128]{1,0:T(8,128)(2,1)}, u32[]{:S(2)}) copy-start(bf16[384,128]{1,0:T(8,128)(2,1)} %param.8) | copy-start | bytes 294916
  41.4 20.8 %copy-start.18 = (bf16[384,128]{1,0:T(8,128)(2,1)S(1)}, bf16[384,128]{1,0:T(8,128)(2,1)}, u32[]{:S(2)}) copy-start(bf16[384,128]{1,0:T(8,128)(2,1)} %param.7) | copy-start | bytes 294916
  43.0 47.2 %all-to-all-start = ((bf16[24,88,128]{2,1,0:T(8,128)(2,1)}), bf16[24,88,128]{2,1,0:T(8,128)(2,1)S(1)}, u32[]{:S(2)}, u32[]{:S(2)}) async-start(bf16[24,88,128]{2,1,0:T(8,128)(2,1)} %broadcast_in_dim.13), calls=%async_computation | async-start | bytes 1081344 | tf_op jit(solution)/shard_map/all_to_all | solution.py:230
  60.3 32.8 %copy-start.20 = (s32[3,6]{1,0:T(4,128)S(1)}, s32[3,6]{1,0:T(4,128)}, u32[]{:S(2)}) copy-start(s32[3,6]{1,0:T(4,128)} %param.11) | copy-start | bytes 220
  60.3 33.1 %copy-start.7 = (bf16[384,128]{1,0:T(8,128)(2,1)S(1)}, bf16[384,128]{1,0:T(8,128)(2,1)}, u32[]{:S(2)}) copy-start(bf16[384,128]{1,0:T(8,128)(2,1)} %q.3) | copy-start | bytes 294916
  62.3 20.7 %collective-permute-start.2 = (bf16[2,128,128]{2,1,0:T(8,128)(2,1)S(1)}, bf16[2,128,128]{2,1,0:T(8,128)(2,1)S(1)}, u32[]{:S(2)}, u32[]{:S(2)}) collective-permute-start(bf16[2,128,128]{2,1,0:T(8,128)(2,1)S(1)} %get-tuple-element.36), channel_id=1, source_target_pairs={{0,16},{16,0},{32,48},{48,32},{64,80},{80,64},{96,112},{112,96},{1... | collective-permute-start | bytes 196616 | tf_op jit(solution)/shard_map/ppermute | solution.py:53
  64.2 18.8 %collective-permute-start.1 = (bf16[2,128,128]{2,1,0:T(8,128)(2,1)S(1)}, bf16[2,128,128]{2,1,0:T(8,128)(2,1)S(1)}, u32[]{:S(2)}, u32[]{:S(2)}) collective-permute-start(bf16[2,128,128]{2,1,0:T(8,128)(2,1)S(1)} %get-tuple-element.37), channel_id=1, source_target_pairs={{0,752},{16,32},{32,16},{48,64},{64,48},{80,96},{96,80},{112,128},... | collective-permute-start | bytes 196616 | tf_op jit(solution)/shard_map/ppermute | solution.py:43
  75.0 10.4 %collective-permute-start.3 = (bf16[2,384,128]{2,1,0:T(8,128)(2,1)S(1)}, bf16[2,384,128]{2,1,0:T(8,128)(2,1)S(1)}, u32[]{:S(2)}, u32[]{:S(2)}) collective-permute-start(bf16[2,384,128]{2,1,0:T(8,128)(2,1)S(1)} %maximum_select_fusion.kv), channel_id=1, source_target_pairs={{0,576},{16,592},{32,608},{48,624},{64,640},{80,656},{96,672},{112... | collective-permute-start | bytes 589832 | tf_op jit(solution)/shard_map/ppermute | solution.py:38
  77.8 9.1 %collective-permute-start.4 = (bf16[2,384,128]{2,1,0:T(8,128)(2,1)S(1)}, bf16[2,384,128]{2,1,0:T(8,128)(2,1)S(1)}, u32[]{:S(2)}, u32[]{:S(2)}) collective-permute-start(bf16[2,384,128]{2,1,0:T(8,128)(2,1)S(1)} %maximum_select_fusion.kv), channel_id=1, source_target_pairs={{0,384},{16,400},{32,416},{48,432},{64,448},{80,464},{96,480},{112... | collective-permute-start | bytes 589832 | tf_op jit(solution)/shard_map/ppermute | solution.py:38
  80.2 8.9 %collective-permute-start.5 = (bf16[2,384,128]{2,1,0:T(8,128)(2,1)S(1)}, bf16[2,384,128]{2,1,0:T(8,128)(2,1)S(1)}, u32[]{:S(2)}, u32[]{:S(2)}) collective-permute-start(bf16[2,384,128]{2,1,0:T(8,128)(2,1)S(1)} %maximum_select_fusion.kv), channel_id=1, source_target_pairs={{0,192},{16,208},{32,224},{48,240},{64,256},{80,272},{96,288},{112... | collective-permute-start | bytes 589832 | tf_op jit(solution)/shard_map/ppermute | solution.py:38
  83.1 12.2 %copy-start.1 = (bf16[2,128,128]{2,1,0:T(8,128)(2,1)}, bf16[2,128,128]{2,1,0:T(8,128)(2,1)S(1)}, u32[]{:S(2)}) copy-start(bf16[2,128,128]{2,1,0:T(8,128)(2,1)S(1)} %get-tuple-element.38.nxt) | copy-start | bytes 196612
  83.1 12.2 %copy-start.3 = (bf16[2,128,128]{2,1,0:T(8,128)(2,1)}, bf16[2,128,128]{2,1,0:T(8,128)(2,1)S(1)}, u32[]{:S(2)}) copy-start(bf16[2,128,128]{2,1,0:T(8,128)(2,1)S(1)} %get-tuple-element.39.prev) | copy-start | bytes 196612
  91.1 4.8 %collective-permute-start.6 = (bf16[24,88,128]{2,1,0:T(8,128)(2,1)}, bf16[24,88,128]{2,1,0:T(8,128)(2,1)S(1)}, u32[]{:S(2)}, u32[]{:S(2)}) collective-permute-start(bf16[24,88,128]{2,1,0:T(8,128)(2,1)} %broadcast_select_fusion), channel_id=1, source_target_pairs={{0,16},{16,0},{32,48},{48,32},{64,80},{80,64},{96,112},{112,96},{1... | collective-permute-start | bytes 1622024 | tf_op jit(solution)/shard_map/ppermute | solution.py:53
  93.3 2.0 %copy-start.11 = (s32[13]{0:T(128)}, s32[13]{0:T(128)S(1)}, u32[]{:S(2)}) copy-start(s32[13]{0:T(128)S(1)} %concatenate.6.meta) | copy-start | bytes 160
  95.3 0.6 copy-start.9
  96.0 0.8 copy-start.5
  96.8 1.0 copy-start.6
  97.8 0.7 copy-start.12
  101.3 0.9 copy-start.10
  102.2 9.8 %copy-start.2 = (bf16[2,128,128]{2,1,0:T(8,128)(2,1)S(1)}, bf16[2,128,128]{2,1,0:T(8,128)(2,1)}, u32[]{:S(2)}) copy-start(bf16[2,128,128]{2,1,0:T(8,128)(2,1)} %copy-done.1) | copy-start | bytes 196612
  102.2 9.8 %copy-start.4 = (bf16[2,128,128]{2,1,0:T(8,128)(2,1)S(1)}, bf16[2,128,128]{2,1,0:T(8,128)(2,1)}, u32[]{:S(2)}) copy-start(bf16[2,128,128]{2,1,0:T(8,128)(2,1)} %copy-done.3) | copy-start | bytes 196612
  102.2 9.8 %copy-start.8 = (bf16[384,128]{1,0:T(8,128)(2,1)S(1)}, bf16[384,128]{1,0:T(8,128)(2,1)}, u32[]{:S(2)}) copy-start(bf16[384,128]{1,0:T(8,128)(2,1)} %q.3) | copy-start | bytes 294916
  102.2 9.8 %copy-start.13 = (s32[13]{0:T(128)S(1)}, s32[13]{0:T(128)}, u32[]{:S(2)}) copy-start(s32[13]{0:T(128)} %copy-done.11) | copy-start | bytes 160
  109.9 5.0 %collective-permute-start.12 = (f32[24,88,128]{2,1,0:T(8,128)}, f32[24,88,128]{2,1,0:T(8,128)S(1)}, u32[]{:S(2)}, u32[]{:S(2)}) collective-permute-start(f32[24,88,128]{2,1,0:T(8,128)} %get-tuple-element.31), channel_id=1, source_target_pairs={{0,16},{16,0},{32,48},{48,32},{64,80},{80,64},{96,112},{112,96},{1... | collective-permute-start | bytes 3244040 | tf_op jit(solution)/shard_map/ppermute | solution.py:53
  112.0 3.0 %copy-start = (f32[24,88,128]{2,1,0:T(8,128)S(1)}, f32[24,88,128]{2,1,0:T(8,128)}, u32[]{:S(2)}) copy-start(f32[24,88,128]{2,1,0:T(8,128)} %get-tuple-element.30.keep) | copy-start | bytes 3244036
  114.3 0.6 copy-start.14
  115.8 22.9 %copy-start.15 = (bf16[2,128,128]{2,1,0:T(8,128)(2,1)S(1)}, bf16[2,128,128]{2,1,0:T(8,128)(2,1)}, u32[]{:S(2)}) copy-start(bf16[2,128,128]{2,1,0:T(8,128)(2,1)} %copy-done.14) | copy-start | bytes 196612
  115.8 38.1 %all-to-all-start.1 = ((bf16[24,88,128]{2,1,0:T(8,128)(2,1)}), bf16[24,88,128]{2,1,0:T(8,128)(2,1)S(1)}, u32[]{:S(2)}, u32[]{:S(2)}) async-start(bf16[24,88,128]{2,1,0:T(8,128)(2,1)} %pair_sum.1), calls=%async_computation.1 | async-start | bytes 1081344 | tf_op jit(solution)/shard_map/all_to_all | solution.py:303
  127.0 21.4 %collective-permute-start.7 = (bf16[2,384,128]{2,1,0:T(8,128)(2,1)S(1)}, bf16[2,384,128]{2,1,0:T(8,128)(2,1)S(1)}, u32[]{:S(2)}, u32[]{:S(2)}) collective-permute-start(bf16[2,384,128]{2,1,0:T(8,128)(2,1)S(1)} %get-tuple-element.23), channel_id=1, source_target_pairs={{0,192},{16,208},{32,224},{48,240},{64,256},{80,272},{96,288},{112... | collective-permute-start | bytes 589832 | tf_op jit(solution)/shard_map/ppermute | solution.py:38
  130.8 17.7 %collective-permute-start.8 = (bf16[2,384,128]{2,1,0:T(8,128)(2,1)S(1)}, bf16[2,384,128]{2,1,0:T(8,128)(2,1)S(1)}, u32[]{:S(2)}, u32[]{:S(2)}) collective-permute-start(bf16[2,384,128]{2,1,0:T(8,128)(2,1)S(1)} %get-tuple-element.24), channel_id=1, source_target_pairs={{0,384},{16,400},{32,416},{48,432},{64,448},{80,464},{96,480},{112... | collective-permute-start | bytes 589832 | tf_op jit(solution)/shard_map/ppermute | solution.py:38
  135.4 13.1 %collective-permute-start.9 = (bf16[2,384,128]{2,1,0:T(8,128)(2,1)S(1)}, bf16[2,384,128]{2,1,0:T(8,128)(2,1)S(1)}, u32[]{:S(2)}, u32[]{:S(2)}) collective-permute-start(bf16[2,384,128]{2,1,0:T(8,128)(2,1)S(1)} %get-tuple-element.25), channel_id=1, source_target_pairs={{0,576},{16,592},{32,608},{48,624},{64,640},{80,656},{96,672},{112... | collective-permute-start | bytes 589832 | tf_op jit(solution)/shard_map/ppermute | solution.py:38
  138.8 9.8 %collective-permute-start.10 = (bf16[2,128,128]{2,1,0:T(8,128)(2,1)S(1)}, bf16[2,128,128]{2,1,0:T(8,128)(2,1)S(1)}, u32[]{:S(2)}, u32[]{:S(2)}) collective-permute-start(bf16[2,128,128]{2,1,0:T(8,128)(2,1)S(1)} %copy-done.15), channel_id=1, source_target_pairs={{0,16},{16,0},{32,48},{48,32},{64,80},{80,64},{96,112},{112,96},{1... | collective-permute-start | bytes 196616 | tf_op jit(solution)/shard_map/ppermute | solution.py:53
  140.7 12.5 %collective-permute-start.11 = (bf16[2,128,128]{2,1,0:T(8,128)(2,1)S(1)}, bf16[2,128,128]{2,1,0:T(8,128)(2,1)S(1)}, u32[]{:S(2)}, u32[]{:S(2)}) collective-permute-start(bf16[2,128,128]{2,1,0:T(8,128)(2,1)S(1)} %get-tuple-element.27), channel_id=1, source_target_pairs={{0,752},{16,32},{32,16},{48,64},{64,48},{80,96},{96,80},{112,128},... | collective-permute-start | bytes 196616 | tf_op jit(solution)/shard_map/ppermute | solution.py:43
Sparse Core Ops, SparseCore 0:
  41.5 59.6 all-gather.1

commit v7 on v5

--- a/solution.py
+++ b/solution.py
@@ -20,9 +20,15 @@
 WCOL = 256
 SAME_CORE = [[2 * i + core for i in range(CHIPS)] for core in range(2)]
 X_GROUPS = [[x * NZ * 2 + rest for x in range(NX)] for rest in range(NZ * 2)]
+Z_GROUPS = [
+    [(x * NZ + z) * 2 + core for z in range(NZ)] for x in range(NX) for core in range(2)
+]
+X_FAR = NZ * SHARD_PAD
+X_ROWS = X_FAR + 2 * 384
 Y_GROUPS = [[2 * y + z for y in range(NY)] for z in range(2)]
 SMEM = pl.BlockSpec(memory_space=pltpu.SMEM)
 VMEM = pl.BlockSpec(memory_space=pltpu.VMEM)
+ANY = pl.BlockSpec(memory_space=pl.ANY)
 PARAMS = pltpu.CompilerParams(vmem_limit_bytes=12 * 1024 * 1024)
 
 M_X, M_CORE, M_Y, M_Z = 9, 10, 11, 12
@@ -37,10 +43,14 @@
     return lax.ppermute(value, "ctx", pairs)
 
 
+def outer_swap(value):
+    pairs = [(s, (s - 1 if s % 2 == 0 else s + 1) % N_CTX) for s in range(N_CTX)]
+    return lax.ppermute(value, "ctx", pairs)
+
+
 def neighbours(first, last, even):
     inner = core_swap(jnp.where(even, last, first))
-    pairs = [(s, (s - 1 if s % 2 == 0 else s + 1) % N_CTX) for s in range(N_CTX)]
-    outer = lax.ppermute(jnp.where(even, first, last), "ctx", pairs)
+    outer = outer_swap(jnp.where(even, first, last))
     return jnp.where(even, outer, inner), jnp.where(even, inner, outer)
 
 
@@ -66,7 +76,8 @@
     return jnp.concatenate(parts, axis=0)
 
 
-def forward_kernel(meta, q, kv, prev, nxt, far1, far2, far3, probs_out, att_out):
+def forward_kernel(meta, w, q, kv, prev, nxt, far1, far2, far3, probs_out, att_out):
+    del w
     far = (far1, far2, far3)
     for j in range(3):
         rows = slice(j * BLK, (j + 1) * BLK)
@@ -94,8 +105,8 @@
             w_out[t, :, e * 128 : (e + 1) * 128] = rows.astype(BF16)
 
 
-def cotangent_kernel(meta, w, att, pieces, keep, give, grad, cols, flat):
-    z = meta[M_Z]
+def cotangent_kernel(w, att, pieces, keep, give, grad, cols, flat):
+    z = lax.axis_index("tp") % 2
     att_now = att[...]
     total = jnp.zeros((384, DH), F32)
     for i in range(N_TP):
@@ -108,7 +119,7 @@
         for e in range(2):
             flat[pl.ds(2 * t + e, DH, stride=32)] = cols[t, :, e * 128 : (e + 1) * 128]
     flat[FLAT_ROWS:] = jnp.zeros((flat.shape[0] - FLAT_ROWS, 128), F32)
-    first = meta[M_CORE] == 0
+    first = lax.axis_index("ctx") % 2 == 0
     for i in range(CHIPS):
         a = flat[2 * i * SHARD : 2 * i * SHARD + SHARD_PAD]
         b = flat[(2 * i + 1) * SHARD : (2 * i + 1) * SHARD + SHARD_PAD]
@@ -118,12 +129,14 @@
 
 def backward_kernel(
     meta, q, kv, prev, nxt, far1, far2, far3, probs, att, out_grad,
-    dq, dkv, dprev, dnext, dfar, acc,
+    dq, dkv, inner, outer, dfar1, dfar2, dfar3, acc,
 ):
     far = (far1, far2, far3)
+    even = lax.axis_index("ctx") % 2 == 0
     acc[...] = jnp.zeros(acc.shape, F32)
     dkv[...] = jnp.zeros(dkv.shape, F32)
     scale = DH**-0.5
+    to_prev = []
     for j in range(3):
         rows = slice(j * BLK, (j + 1) * BLK)
         grad = out_grad[rows]
@@ -138,41 +151,58 @@
             part = parts[which]
             dkv[which, rows] += part[:BLK]
             if j == 0:
-                dprev[which] = part[BLK : 2 * BLK].astype(BF16)
+                to_prev.append(part[BLK : 2 * BLK])
             else:
                 dkv[which, (j - 1) * BLK : j * BLK] += part[BLK : 2 * BLK]
             if j == 2:
-                dnext[which] = part[2 * BLK : 3 * BLK].astype(BF16)
+                to_next = part[2 * BLK : 3 * BLK]
+                inner[which] = jnp.where(even, to_next, to_prev[which]).astype(BF16)
+                outer[which] = jnp.where(even, to_prev[which], to_next).astype(BF16)
             else:
                 dkv[which, (j + 1) * BLK : (j + 2) * BLK] += part[2 * BLK : 3 * BLK]
             for k in range(3):
                 row = pl.multiple_of(meta[3 * j + k] * BLK, BLK)
                 acc[k, which, pl.ds(row, BLK)] += part[(3 + k) * BLK : (4 + k) * BLK]
-    dfar[...] = acc[...].astype(BF16)
-
-
-def pair_sum_kernel(keep, other, dkv, out):
-    del dkv
-    out[...] = (keep[...] + other[...]).astype(BF16)
-
-
-def chunk_sum_kernel(parts, out):
+    for k, out in enumerate((dfar1, dfar2, dfar3)):
+        out[...] = acc[k].astype(BF16)
+
+
+def x_parts_kernel(keep, other, far1, far2, far3, out):
+    x = lax.axis_index("ctx") // (2 * NZ)
+    for i in range(CHIPS):
+        row = (i % NZ) * SHARD_PAD
+        out[i // NZ, row : row + SHARD_PAD] = (keep[i] + other[i]).astype(BF16)
+    out[x, X_FAR:] = jnp.zeros((X_ROWS - X_FAR, DH), BF16)
+    for k, far in enumerate((far1, far2, far3)):
+        for which in range(2):
+            row = X_FAR + which * 384
+            out[(x + k + 1) % NX, row : row + 384] = far[which]
+
+
+def x_sum_kernel(parts, dkv, inner, outer, z_parts, dk, dv):
+    even = lax.axis_index("ctx") % 2 == 0
+    for i in range(NZ):
+        rows = slice(i * SHARD_PAD, (i + 1) * SHARD_PAD)
+        chunk = parts[0, rows].astype(F32)
+        for x in range(1, NX):
+            chunk = chunk + parts[x, rows].astype(F32)
+        z_parts[i] = chunk.astype(BF16)
+    for which, out in ((0, dk), (1, dv)):
+        rows = slice(X_FAR + which * 384, X_FAR + (which + 1) * 384)
+        own = dkv[which]
+        for x in range(NX):
+            own = own + parts[x, rows].astype(F32)
+        out[...] = own
+        near, away = inner[which].astype(F32), outer[which].astype(F32)
+        out[:BLK] += jnp.where(even, away, near)
+        out[2 * BLK :] += jnp.where(even, near, away)
+
+
+def z_sum_kernel(parts, out):
     total = parts[0].astype(F32)
-    for i in range(1, CHIPS):
+    for i in range(1, NZ):
         total = total + parts[i].astype(F32)
     out[0] = total[:SHARD]
-
-
-def grad_sum_kernel(dkv, prev, nxt, far1, far2, far3, dk, dv):
-    for which, out in ((0, dk), (1, dv)):
-        out[...] = (
-            dkv[which]
-            + far1[which].astype(F32)
-            + far2[which].astype(F32)
-            + far3[which].astype(F32)
-        )
-        out[:BLK] += prev[which].astype(F32)
-        out[2 * BLK :] += nxt[which].astype(F32)
 
 
 def on_device(queries, key_rows, values, cotangent, w_flat, block_keys):
@@ -215,17 +245,17 @@
             jax.ShapeDtypeStruct((3, BLK, 6 * BLK), F32),
             jax.ShapeDtypeStruct((384, DH), BF16),
         ),
-        in_specs=[SMEM] + [VMEM] * 7,
+        in_specs=[SMEM, ANY] + [VMEM] * 7,
         out_specs=(VMEM, VMEM),
         compiler_params=PARAMS,
         name="attention_forward",
-    )(meta, queries, kv, prev, nxt, *far)
+    )(meta, weight, queries, kv, prev, nxt, *far)
 
     chunk = jax.ShapeDtypeStruct((CHIPS, SHARD_PAD, 128), F32)
     keep, give, out_grad = pl.pallas_call(
         cotangent_kernel,
         out_shape=(chunk, chunk, jax.ShapeDtypeStruct((384, DH), BF16)),
-        in_specs=[SMEM, VMEM, VMEM, VMEM],
+        in_specs=[VMEM, VMEM, VMEM],
         out_specs=(VMEM, VMEM, VMEM),
         scratch_shapes=[
             pltpu.VMEM((N_TP, DH, WCOL), F32),
@@ -233,50 +263,48 @@
         ],
         compiler_params=PARAMS,
         name="cotangent_products",
-    )(meta, weight, att, pieces)
+    )(weight, att, pieces)
     two = (2, 384, DH)
-    dq, dkv, dprev, dnext, dfar = pl.pallas_call(
+    dq, dkv, inner, outer, *dfar = pl.pallas_call(
         backward_kernel,
         out_shape=(
             jax.ShapeDtypeStruct((384, DH), F32),
             jax.ShapeDtypeStruct(two, F32),
             jax.ShapeDtypeStruct((2, BLK, DH), BF16),
             jax.ShapeDtypeStruct((2, BLK, DH), BF16),
-            jax.ShapeDtypeStruct((3,) + two, BF16),
-        ),
+        )
+        + (jax.ShapeDtypeStruct(two, BF16),) * 3,
         in_specs=[SMEM] + [VMEM] * 10,
-        out_specs=(VMEM,) * 5,
+        out_specs=(VMEM,) * 7,
         scratch_shapes=[pltpu.VMEM((3,) + two, F32)],
         compiler_params=PARAMS,
         name="attention_backward",
     )(meta, queries, kv, prev, nxt, *far, probs, att, out_grad)
-    pair_sum = pl.pallas_call(
-        pair_sum_kernel,
-        out_shape=jax.ShapeDtypeStruct((CHIPS, SHARD_PAD, 128), BF16),
-        in_specs=[VMEM, VMEM, pl.BlockSpec(memory_space=pl.ANY)],
-        out_specs=VMEM,
-        compiler_params=PARAMS,
-        name="pair_sum",
-    )(keep, core_swap(give), dkv)
-    spread = lax.all_to_all(
-        pair_sum, "ctx", 0, 0, tiled=True, axis_index_groups=SAME_CORE
-    )
+    x_parts = pl.pallas_call(
+        x_parts_kernel,
+        out_shape=jax.ShapeDtypeStruct((NX, X_ROWS, DH), BF16),
+        compiler_params=PARAMS,
+        name="x_parts",
+    )(keep, core_swap(give), *dfar)
+    from_x = lax.all_to_all(x_parts, "ctx", 0, 0, tiled=True, axis_index_groups=X_GROUPS)
+    grad = jax.ShapeDtypeStruct((384, DH), F32)
+    z_parts, dk, dv = pl.pallas_call(
+        x_sum_kernel,
+        out_shape=(
+            jax.ShapeDtypeStruct((NZ, SHARD_PAD, 128), BF16),
+            grad,
+            grad,
+        ),
+        compiler_params=PARAMS,
+        name="x_sum",
+    )(from_x, dkv, core_swap(inner), outer_swap(outer))
+    from_z = lax.all_to_all(z_parts, "ctx", 0, 0, tiled=True, axis_index_groups=Z_GROUPS)
     weight_grad = pl.pallas_call(
-        chunk_sum_kernel,
+        z_sum_kernel,
         out_shape=jax.ShapeDtypeStruct((1, SHARD, 128), F32),
         compiler_params=PARAMS,
-        name="chunk_sum",
-    )(spread)
-
-    far_back = [x_shift(dfar[k], k + 1) for k in range(3)]
-    from_prev, from_next = neighbours(dprev, dnext, even)
-    grad = jax.ShapeDtypeStruct((384, DH), F32)
-    dk, dv = pl.pallas_call(
-        grad_sum_kernel,
-        out_shape=(grad, grad),
-        compiler_params=PARAMS,
-        name="grad_sum",
-    )(dkv, from_prev, from_next, *far_back)
+        name="z_sum",
+    )(from_z)
     return dq, dk, dv, weight_grad
 
 

time: 151 us -> 152 us (level)
  the two profiles are of different devices: /device:TPU:6 before, /device:TPU:1 now
where the time goes in v7:
time: 152 us; the launch traced here: 150 us
  starting transfers between devices  66.8 us (44%)
  waiting for transfers between devices  23.3 us (15%)
  between operations  18.3 us (12%)
  blocking collectives  15.2 us (10%)
  local copies, waits for them, and re-layouts  12.6 us (8%)
  Pallas kernels  11.7 us (8%)
  other arithmetic  1.9 us (1%)
    all_to_all x1, starting transfers between devices, on_device(): lax.all_to_all(jnp.broadcast_to(w_pad[None], (CHIPS, SHARD_PAD, 128)), 'c...  15.7 us
    ppermute x1, starting transfers between devices, twin_swap(): return lax.ppermute(value, 'tp', [(s, s ^ 1) for s in range(N_TP)])  15.7 us
    ppermute x4, starting transfers between devices, core_swap(): return lax.ppermute(value, 'ctx', [(s, s ^ 1) for s in range(N_CTX)])  15.2 us
    all_to_all x1, blocking collectives, on_device(): lax.all_to_all(z_parts, 'ctx', 0, 0, tiled=True, axis_index_groups=Z_GROUPS)  15.2 us
    all_to_all x1, waiting for transfers between devices, on_device(): lax.all_to_all(x_parts, 'ctx', 0, 0, tiled=True, axis_index_groups=X_GROUPS)  10.5 us
    ppermute x3, starting transfers between devices, x_shift(): return lax.ppermute(value, 'ctx', pairs)  9.28 us
    unnamed x41, local copies, waits for them, and re-layouts  8.38 us
    ppermute x2, starting transfers between devices, outer_swap(): return lax.ppermute(value, 'ctx', pairs)  6.78 us
  transfers between devices with their start and end apart: 13, of which 6 were waited for; matrix products, arithmetic and copies ran while one was open for 3% of the time, Pallas kernels for 4%

profile of v7, /device:TPU:1, one launch (start us, length us, event | category | flops | bytes accessed | tf_op | source)
XLA Modules:
  0.0 149.9 jit_solution(8111305668684046929)
XLA Ops:
  7.2 0.0 all-gather.2.cloned.1.call-start
  7.2 15.7 %collective-permute-start = (bf16[384,256]{1,0:T(8,128)(2,1)}, bf16[384,256]{1,0:T(8,128)(2,1)S(1)}, u32[]{:S(2)}, u32[]{:S(2)}) collective-permute-start(bf16[384,256]{1,0:T(8,128)(2,1)} %param.9), channel_id=1, source_target_pairs={{0,1},{1,0},{2,3},{3,2},{4,5},{5,4},{6,7},{7,6},{8,9},{9,8},{10,11... | collective-permute-start | bytes 589832 | tf_op jit(solution)/shard_map/ppermute | solution.py:62
  22.9 6.7 %collective-permute-done = bf16[384,256]{1,0:T(8,128)(2,1)S(1)} collective-permute-done((bf16[384,256]{1,0:T(8,128)(2,1)}, bf16[384,256]{1,0:T(8,128)(2,1)S(1)}, u32[]{:S(2)}, u32[]{:S(2)}) %collective-permute-start) | collective-permute-done | bytes 196640 | tf_op jit(solution)/shard_map/ppermute | solution.py:62
  29.7 1.7 %pad_maximum_fusion = bf16[768,256]{1,0:T(8,128)(2,1)} fusion(bf16[384,256]{1,0:T(8,128)(2,1)S(1)} %collective-permute-done, bf16[384,256]{1,0:T(8,128)(2,1)} %param.9), kind=kLoop, calls=%fused_computation.1 | loop fusion | flops 786432 | bytes 786432 | tf_op jit(solution)/shard_map/concatenate | solution.py:217
  31.4 0.0 all-gather.2.cloned.1.call-update
  31.4 0.9 broadcast_in_dim.13
  32.3 15.7 %all-to-all-start = ((bf16[24,88,128]{2,1,0:T(8,128)(2,1)}), bf16[24,88,128]{2,1,0:T(8,128)(2,1)S(1)}, u32[]{:S(2)}, u32[]{:S(2)}) async-start(bf16[24,88,128]{2,1,0:T(8,128)(2,1)} %broadcast_in_dim.13), calls=%async_computation | async-start | bytes 1081344 | tf_op jit(solution)/shard_map/all_to_all | solution.py:221
  48.1 0.0 copy-start.19
  48.1 0.5 slice.40
  49.3 2.9 %collective-permute-start.2 = (bf16[2,128,128]{2,1,0:T(8,128)(2,1)S(1)}, bf16[2,128,128]{2,1,0:T(8,128)(2,1)S(1)}, u32[]{:S(2)}, u32[]{:S(2)}) collective-permute-start(bf16[2,128,128]{2,1,0:T(8,128)(2,1)S(1)} %get-tuple-element.38), channel_id=1, source_target_pairs={{0,16},{16,0},{32,48},{48,32},{64,80},{80,64},{96,112},{112,96},{1... | collective-permute-start | bytes 196616 | tf_op jit(solution)/shard_map/ppermute | solution.py:58
  52.2 3.4 %collective-permute-start.1 = (bf16[2,128,128]{2,1,0:T(8,128)(2,1)S(1)}, bf16[2,128,128]{2,1,0:T(8,128)(2,1)S(1)}, u32[]{:S(2)}, u32[]{:S(2)}) collective-permute-start(bf16[2,128,128]{2,1,0:T(8,128)(2,1)S(1)} %get-tuple-element.39), channel_id=1, source_target_pairs={{0,752},{16,32},{32,16},{48,64},{64,48},{80,96},{96,80},{112,128},... | collective-permute-start | bytes 196616 | tf_op jit(solution)/shard_map/ppermute | solution.py:48
  55.6 4.3 %collective-permute-start.3 = (bf16[2,384,128]{2,1,0:T(8,128)(2,1)S(1)}, bf16[2,384,128]{2,1,0:T(8,128)(2,1)S(1)}, u32[]{:S(2)}, u32[]{:S(2)}) collective-permute-start(bf16[2,384,128]{2,1,0:T(8,128)(2,1)S(1)} %maximum_select_fusion.kv), channel_id=1, source_target_pairs={{0,576},{16,592},{32,608},{48,624},{64,640},{80,656},{96,672},{112... | collective-permute-start | bytes 589832 | tf_op jit(solution)/shard_map/ppermute | solution.py:43
  59.9 2.5 %collective-permute-start.4 = (bf16[2,384,128]{2,1,0:T(8,128)(2,1)S(1)}, bf16[2,384,128]{2,1,0:T(8,128)(2,1)S(1)}, u32[]{:S(2)}, u32[]{:S(2)}) collective-permute-start(bf16[2,384,128]{2,1,0:T(8,128)(2,1)S(1)} %maximum_select_fusion.kv), channel_id=1, source_target_pairs={{0,384},{16,400},{32,416},{48,432},{64,448},{80,464},{96,480},{112... | collective-permute-start | bytes 589832 | tf_op jit(solution)/shard_map/ppermute | solution.py:43
  62.4 2.5 %collective-permute-start.5 = (bf16[2,384,128]{2,1,0:T(8,128)(2,1)S(1)}, bf16[2,384,128]{2,1,0:T(8,128)(2,1)S(1)}, u32[]{:S(2)}, u32[]{:S(2)}) collective-permute-start(bf16[2,384,128]{2,1,0:T(8,128)(2,1)S(1)} %maximum_select_fusion.kv), channel_id=1, source_target_pairs={{0,192},{16,208},{32,224},{48,240},{64,256},{80,272},{96,288},{112... | collective-permute-start | bytes 589832 | tf_op jit(solution)/shard_map/ppermute | solution.py:43
  64.9 0.0 collective-permute-done.2
  64.9 0.0 collective-permute-done.1
  65.0 0.0 copy-start.1
  65.0 0.0 copy-start.4
  65.0 0.5 slice.44
  65.5 0.6 slice.45
  67.4 0.0 collective-permute-done.3.far1
  67.4 0.5 slice.46
  68.6 0.9 collective-permute-done.4.far2
  69.4 0.5 slice.47
  70.6 1.3 collective-permute-done.5.far3
  72.0 0.5 slice.48
  73.1 0.0 all-to-all-done.own
  73.2 7.1 %collective-permute-start.6 = (bf16[24,88,128]{2,1,0:T(8,128)(2,1)S(1)}, bf16[24,88,128]{2,1,0:T(8,128)(2,1)S(1)}, u32[]{:S(2)}, u32[]{:S(2)}) collective-permute-start(bf16[24,88,128]{2,1,0:T(8,128)(2,1)S(1)} %broadcast_select_fusion), channel_id=1, source_target_pairs={{0,16},{16,0},{32,48},{48,32},{64,80},{80,64},{96,112},{112,96},{1... | collective-permute-start | bytes 1622024 | tf_op jit(solution)/shard_map/ppermute | solution.py:58
  80.3 0.0 copy-done.19
  80.4 0.1 add_select_fusion
  80.4 0.1 reshape.18
  80.5 0.1 concatenate.9.meta
  80.6 1.2 collective-permute-done.6.other
  81.9 0.0 copy-done.1
  81.9 2.3 %weight_rows.1.w = bf16[16,128,256]{2,1,0:T(8,128)(2,1)S(1)} custom-call(s32[13]{0:T(128)S(1)} %concatenate.9.meta, bf16[24,88,128]{2,1,0:T(8,128)(2,1)S(1)} %all-to-all-done.own, bf16[24,88,128]{2,1,0:T(8,128)(2,1)S(1)} %collective-permute-done.6.other), custom_call_target="tpu_custom_call" | custom-call | tf_op jit(solution)/shard_map/weight_rows/pallas_call | solution.py:232
  84.2 0.0 copy-start.9
  84.2 0.5 copy-done.9
  84.7 0.8 copy-done.2
  85.6 0.8 copy-done.5
  86.4 0.9 copy-done.8
  87.3 0.7 copy-done.10
  88.0 1.9 %attention_forward.1 = (f32[3,128,768]{2,1,0:T(8,128)S(1)}, bf16[384,128]{1,0:T(8,128)(2,1)S(1)}) custom-call(s32[13]{0:T(128)S(1)} %copy-done.10, bf16[16,128,256]{2,1,0:T(8,128)(2,1)S(1)} %weight_rows.1.w, bf16[384,128]{1,0:T(8,128)(2,1)S(1)} %copy-done.8, bf16[2,384,128]{2,1,0:T(8,128)(2,1)S(1)} %maximum_select_fusion.kv, ...), custom_call_target="tpu_custom_call" | custom-call | tf_op jit(solution)/shard_map/attention_forward/pallas_call | solution.py:242
  89.9 0.0 all-gather.2.cloned.1.call-done.pieces
  90.0 1.9 %copy-done = bf16[6144,256]{1,0:T(8,128)(2,1)S(1)} copy-done((bf16[6144,256]{1,0:T(8,128)(2,1)S(1)}, bf16[6144,256]{1,0:T(8,128)(2,1)}, u32[]{:S(2)}) %copy-start) | copy-done | bytes 3145752
  91.8 2.9 %cotangent_products.1 = (f32[24,88,128]{2,1,0:T(8,128)S(1)}, f32[24,88,128]{2,1,0:T(8,128)S(1)}, bf16[384,128]{1,0:T(8,128)(2,1)S(1)}) custom-call(bf16[16,128,256]{2,1,0:T(8,128)(2,1)S(1)} %weight_rows.1.w, bf16[384,128]{1,0:T(8,128)(2,1)S(1)} %get-tuple-element.20.att, bf16[6144,256]{1,0:T(8,128)(2,1)S(1)} %copy-done), custom_call_target="tpu_custom_call" | custom-call | tf_op jit(solution)/shard_map/cotangent_products/pallas_call | solution.py:255
  94.7 3.0 %collective-permute-start.7 = (f32[24,88,128]{2,1,0:T(8,128)S(1)}, f32[24,88,128]{2,1,0:T(8,128)S(1)}, u32[]{:S(2)}, u32[]{:S(2)}) collective-permute-start(f32[24,88,128]{2,1,0:T(8,128)S(1)} %get-tuple-element.24), channel_id=1, source_target_pairs={{0,16},{16,0},{32,48},{48,32},{64,80},{80,64},{96,112},{112,96},{1... | collective-permute-start | bytes 3244040 | tf_op jit(solution)/shard_map/ppermute | solution.py:58
  97.8 0.0 copy-done.3
  97.8 0.0 copy-done.11
  97.8 2.3 %attention_backward.1 = (f32[384,128]{1,0:T(8,128)}, f32[2,384,128]{2,1,0:T(8,128)S(1)}, bf16[2,128,128]{2,1,0:T(8,128)(2,1)S(1)}, bf16[2,128,128]{2,1,0:T(8,128...) custom-call(s32[13]{0:T(128)S(1)} %copy-done.11, ...), custom_call_target="tpu_custom_call" | custom-call | tf_op jit(solution)/shard_map/attention_backward/pallas_call | solution.py:268
  100.2 0.8 copy-done.6
  100.9 0.6 copy-done.12
  101.6 0.6 copy-done.14
  102.2 0.0 collective-permute-done.7.other
  102.2 1.3 x_parts.1
  103.5 4.1 %all-to-all-start.1 = ((bf16[4,1296,128]{2,1,0:T(8,128)(2,1)}), bf16[4,1296,128]{2,1,0:T(8,128)(2,1)S(1)}, u32[]{:S(2)}, u32[]{:S(2)}) async-start(bf16[4,1296,128]{2,1,0:T(8,128)(2,1)} %x_parts.1), calls=%async_computation.1 | async-start | bytes 2654208 | tf_op jit(solution)/shard_map/all_to_all | solution.py:289
  107.6 2.2 %collective-permute-start.8 = (bf16[2,128,128]{2,1,0:T(8,128)(2,1)S(1)}, bf16[2,128,128]{2,1,0:T(8,128)(2,1)S(1)}, u32[]{:S(2)}, u32[]{:S(2)}) collective-permute-start(bf16[2,128,128]{2,1,0:T(8,128)(2,1)S(1)} %copy-done.15), channel_id=1, source_target_pairs={{0,16},{16,0},{32,48},{48,32},{64,80},{80,64},{96,112},{112,96},{1... | collective-permute-start | bytes 196616 | tf_op jit(solution)/shard_map/ppermute | solution.py:58
  109.8 0.0 copy-done.13
  109.8 3.4 %collective-permute-start.9 = (bf16[2,128,128]{2,1,0:T(8,128)(2,1)S(1)}, bf16[2,128,128]{2,1,0:T(8,128)(2,1)S(1)}, u32[]{:S(2)}, u32[]{:S(2)}) collective-permute-start(bf16[2,128,128]{2,1,0:T(8,128)(2,1)S(1)} %copy-done.13), channel_id=1, source_target_pairs={{0,752},{16,32},{32,16},{48,64},{64,48},{80,96},{96,80},{112,128},... | collective-permute-start | bytes 196616 | tf_op jit(solution)/shard_map/ppermute | solution.py:48
  113.2 0.0 collective-permute-done.8.inner
  113.2 2.5 %collective-permute-done.9.outer = bf16[2,128,128]{2,1,0:T(8,128)(2,1)S(1)} collective-permute-done((bf16[2,128,128]{2,1,0:T(8,128)(2,1)S(1)}, bf16[2,128,128]{2,1,0:T(8,128)(2,1)S(1)}, u32[]{:S(2)}, u32[]{:S(2)}) %collective-permute-start.9) | collective-permute-done | bytes 65568 | tf_op jit(solution)/shard_map/ppermute | solution.py:48
  115.7 10.5 %all-to-all-done.1.parts = bf16[4,1296,128]{2,1,0:T(8,128)(2,1)S(1)} async-done(((bf16[4,1296,128]{2,1,0:T(8,128)(2,1)}), bf16[4,1296,128]{2,1,0:T(8,128)(2,1)S(1)}, u32[]{:S(2)}, u32[]{:S(2)}) %all-to-all-start.1) | async-done | bytes 1327136 | tf_op jit(solution)/shard_map/all_to_all | solution.py:289
  126.2 0.9 x_sum.1
  127.1 15.2 %all_to_all.15.parts = bf16[6,88,128]{2,1,0:T(8,128)(2,1)S(1)} all-to-all(bf16[6,88,128]{2,1,0:T(8,128)(2,1)S(1)} %get-tuple-element.33), channel_id=1, replica_groups={{0,32,64,96,128,160},{16,48,80,112,144,176},{192,224,256,288,320,352},{..., dimensions={0} | all-to-all | bytes 270336 | tf_op jit(solution)/shard_map/all_to_all | solution.py:301
  142.4 0.7 copy.10
  (29 shorter events, 0.2 us)
Async XLA Ops:
  7.2 24.3 %copy-start.18 = (bf16[1,86,128]{2,1,0:T(8,128)(2,1)S(1)}, bf16[1,86,128]{2,1,0:T(8,128)(2,1)}, u32[]{:S(2)}) copy-start(bf16[1,86,128]{2,1,0:T(8,128)(2,1)} %param.10) | copy-start | bytes 66052
  7.2 82.8 %all-gather.2.cloned.1.call-start = ((), (), s32[]{:S(2)}) async-start(), calls=%async_computation.3 | async-start | bytes 3538944 | tf_op jit(solution)/shard_map/all_gather | solution.py:216
  7.2 22.4 %collective-permute-start = (bf16[384,256]{1,0:T(8,128)(2,1)}, bf16[384,256]{1,0:T(8,128)(2,1)S(1)}, u32[]{:S(2)}, u32[]{:S(2)}) collective-permute-start(bf16[384,256]{1,0:T(8,128)(2,1)} %param.9), channel_id=1, source_target_pairs={{0,1},{1,0},{2,3},{3,2},{4,5},{5,4},{6,7},{7,6},{8,9},{9,8},{10,11... | collective-permute-start | bytes 589832 | tf_op jit(solution)/shard_map/ppermute | solution.py:62
  31.4 17.9 %copy-start.16 = (bf16[384,128]{1,0:T(8,128)(2,1)S(1)}, bf16[384,128]{1,0:T(8,128)(2,1)}, u32[]{:S(2)}) copy-start(bf16[384,128]{1,0:T(8,128)(2,1)} %param.8) | copy-start | bytes 294916
  31.4 17.9 %copy-start.17 = (bf16[384,128]{1,0:T(8,128)(2,1)S(1)}, bf16[384,128]{1,0:T(8,128)(2,1)}, u32[]{:S(2)}) copy-start(bf16[384,128]{1,0:T(8,128)(2,1)} %param.7) | copy-start | bytes 294916
  32.3 40.8 %all-to-all-start = ((bf16[24,88,128]{2,1,0:T(8,128)(2,1)}), bf16[24,88,128]{2,1,0:T(8,128)(2,1)S(1)}, u32[]{:S(2)}, u32[]{:S(2)}) async-start(bf16[24,88,128]{2,1,0:T(8,128)(2,1)} %broadcast_in_dim.13), calls=%async_computation | async-start | bytes 1081344 | tf_op jit(solution)/shard_map/all_to_all | solution.py:221
  48.1 32.3 %copy-start.19 = (s32[3,6]{1,0:T(4,128)S(1)}, s32[3,6]{1,0:T(4,128)}, u32[]{:S(2)}) copy-start(s32[3,6]{1,0:T(4,128)} %param.11) | copy-start | bytes 220
  49.3 15.6 %collective-permute-start.2 = (bf16[2,128,128]{2,1,0:T(8,128)(2,1)S(1)}, bf16[2,128,128]{2,1,0:T(8,128)(2,1)S(1)}, u32[]{:S(2)}, u32[]{:S(2)}) collective-permute-start(bf16[2,128,128]{2,1,0:T(8,128)(2,1)S(1)} %get-tuple-element.38), channel_id=1, source_target_pairs={{0,16},{16,0},{32,48},{48,32},{64,80},{80,64},{96,112},{112,96},{1... | collective-permute-start | bytes 196616 | tf_op jit(solution)/shard_map/ppermute | solution.py:58
  52.2 12.7 %collective-permute-start.1 = (bf16[2,128,128]{2,1,0:T(8,128)(2,1)S(1)}, bf16[2,128,128]{2,1,0:T(8,128)(2,1)S(1)}, u32[]{:S(2)}, u32[]{:S(2)}) collective-permute-start(bf16[2,128,128]{2,1,0:T(8,128)(2,1)S(1)} %get-tuple-element.39), channel_id=1, source_target_pairs={{0,752},{16,32},{32,16},{48,64},{64,48},{80,96},{96,80},{112,128},... | collective-permute-start | bytes 196616 | tf_op jit(solution)/shard_map/ppermute | solution.py:48
  55.6 11.8 %collective-permute-start.3 = (bf16[2,384,128]{2,1,0:T(8,128)(2,1)S(1)}, bf16[2,384,128]{2,1,0:T(8,128)(2,1)S(1)}, u32[]{:S(2)}, u32[]{:S(2)}) collective-permute-start(bf16[2,384,128]{2,1,0:T(8,128)(2,1)S(1)} %maximum_select_fusion.kv), channel_id=1, source_target_pairs={{0,576},{16,592},{32,608},{48,624},{64,640},{80,656},{96,672},{112... | collective-permute-start | bytes 589832 | tf_op jit(solution)/shard_map/ppermute | solution.py:43
  59.9 9.5 %collective-permute-start.4 = (bf16[2,384,128]{2,1,0:T(8,128)(2,1)S(1)}, bf16[2,384,128]{2,1,0:T(8,128)(2,1)S(1)}, u32[]{:S(2)}, u32[]{:S(2)}) collective-permute-start(bf16[2,384,128]{2,1,0:T(8,128)(2,1)S(1)} %maximum_select_fusion.kv), channel_id=1, source_target_pairs={{0,384},{16,400},{32,416},{48,432},{64,448},{80,464},{96,480},{112... | collective-permute-start | bytes 589832 | tf_op jit(solution)/shard_map/ppermute | solution.py:43
  62.4 9.5 %collective-permute-start.5 = (bf16[2,384,128]{2,1,0:T(8,128)(2,1)S(1)}, bf16[2,384,128]{2,1,0:T(8,128)(2,1)S(1)}, u32[]{:S(2)}, u32[]{:S(2)}) collective-permute-start(bf16[2,384,128]{2,1,0:T(8,128)(2,1)S(1)} %maximum_select_fusion.kv), channel_id=1, source_target_pairs={{0,192},{16,208},{32,224},{48,240},{64,256},{80,272},{96,288},{112... | collective-permute-start | bytes 589832 | tf_op jit(solution)/shard_map/ppermute | solution.py:43
  65.0 16.9 %copy-start.1 = (bf16[2,128,128]{2,1,0:T(8,128)(2,1)}, bf16[2,128,128]{2,1,0:T(8,128)(2,1)S(1)}, u32[]{:S(2)}) copy-start(bf16[2,128,128]{2,1,0:T(8,128)(2,1)S(1)} %get-tuple-element.40.nxt) | copy-start | bytes 196612
  65.0 16.9 %copy-start.4 = (bf16[2,128,128]{2,1,0:T(8,128)(2,1)}, bf16[2,128,128]{2,1,0:T(8,128)(2,1)S(1)}, u32[]{:S(2)}) copy-start(bf16[2,128,128]{2,1,0:T(8,128)(2,1)S(1)} %get-tuple-element.41.prev) | copy-start | bytes 196612
  73.2 8.7 %collective-permute-start.6 = (bf16[24,88,128]{2,1,0:T(8,128)(2,1)S(1)}, bf16[24,88,128]{2,1,0:T(8,128)(2,1)S(1)}, u32[]{:S(2)}, u32[]{:S(2)}) collective-permute-start(bf16[24,88,128]{2,1,0:T(8,128)(2,1)S(1)} %broadcast_select_fusion), channel_id=1, source_target_pairs={{0,16},{16,0},{32,48},{48,32},{64,80},{80,64},{96,112},{112,96},{1... | collective-permute-start | bytes 1622024 | tf_op jit(solution)/shard_map/ppermute | solution.py:58
  84.2 0.5 copy-start.9
  84.7 0.8 copy-start.2
  85.6 0.8 copy-start.5
  86.4 0.9 copy-start.8
  87.3 0.7 copy-start.10
  89.9 1.9 %copy-start = (bf16[6144,256]{1,0:T(8,128)(2,1)S(1)}, bf16[6144,256]{1,0:T(8,128)(2,1)}, u32[]{:S(2)}) copy-start(bf16[6144,256]{1,0:T(8,128)(2,1)} %all-gather.2.cloned.1.call-done.pieces) | copy-start | bytes 9437188
  91.8 6.0 %copy-start.3 = (bf16[2,128,128]{2,1,0:T(8,128)(2,1)S(1)}, bf16[2,128,128]{2,1,0:T(8,128)(2,1)}, u32[]{:S(2)}) copy-start(bf16[2,128,128]{2,1,0:T(8,128)(2,1)} %copy-done.1) | copy-start | bytes 196612
  91.8 6.0 %copy-start.11 = (s32[13]{0:T(128)S(1)}, s32[13]{0:T(128)}, u32[]{:S(2)}) copy-start(s32[13]{0:T(128)} %copy-done.9) | copy-start | bytes 160
  94.7 7.5 %collective-permute-start.7 = (f32[24,88,128]{2,1,0:T(8,128)S(1)}, f32[24,88,128]{2,1,0:T(8,128)S(1)}, u32[]{:S(2)}, u32[]{:S(2)}) collective-permute-start(f32[24,88,128]{2,1,0:T(8,128)S(1)} %get-tuple-element.24), channel_id=1, source_target_pairs={{0,16},{16,0},{32,48},{48,32},{64,80},{80,64},{96,112},{112,96},{1... | collective-permute-start | bytes 3244040 | tf_op jit(solution)/shard_map/ppermute | solution.py:58
  100.2 0.8 copy-start.6
  100.9 0.6 copy-start.12
  101.6 0.6 copy-start.14
  103.5 4.1 %copy-start.15 = (bf16[2,128,128]{2,1,0:T(8,128)(2,1)S(1)}, bf16[2,128,128]{2,1,0:T(8,128)(2,1)}, u32[]{:S(2)}) copy-start(bf16[2,128,128]{2,1,0:T(8,128)(2,1)} %copy-done.14) | copy-start | bytes 196612
  103.5 6.3 %copy-start.13 = (bf16[2,128,128]{2,1,0:T(8,128)(2,1)S(1)}, bf16[2,128,128]{2,1,0:T(8,128)(2,1)}, u32[]{:S(2)}) copy-start(bf16[2,128,128]{2,1,0:T(8,128)(2,1)} %copy-done.12) | copy-start | bytes 196612
  103.5 22.7 %copy-start.7 = (f32[2,384,128]{2,1,0:T(8,128)S(1)}, f32[2,384,128]{2,1,0:T(8,128)}, u32[]{:S(2)}) copy-start(f32[2,384,128]{2,1,0:T(8,128)} %copy-done.6) | copy-start | bytes 1179652
  103.5 22.7 %all-to-all-start.1 = ((bf16[4,1296,128]{2,1,0:T(8,128)(2,1)}), bf16[4,1296,128]{2,1,0:T(8,128)(2,1)S(1)}, u32[]{:S(2)}, u32[]{:S(2)}) async-start(bf16[4,1296,128]{2,1,0:T(8,128)(2,1)} %x_parts.1), calls=%async_computation.1 | async-start | bytes 2654208 | tf_op jit(solution)/shard_map/all_to_all | solution.py:289
  107.6 5.6 %collective-permute-start.8 = (bf16[2,128,128]{2,1,0:T(8,128)(2,1)S(1)}, bf16[2,128,128]{2,1,0:T(8,128)(2,1)S(1)}, u32[]{:S(2)}, u32[]{:S(2)}) collective-permute-start(bf16[2,128,128]{2,1,0:T(8,128)(2,1)S(1)} %copy-done.15), channel_id=1, source_target_pairs={{0,16},{16,0},{32,48},{48,32},{64,80},{80,64},{96,112},{112,96},{1... | collective-permute-start | bytes 196616 | tf_op jit(solution)/shard_map/ppermute | solution.py:58
  109.8 5.9 %collective-permute-start.9 = (bf16[2,128,128]{2,1,0:T(8,128)(2,1)S(1)}, bf16[2,128,128]{2,1,0:T(8,128)(2,1)S(1)}, u32[]{:S(2)}, u32[]{:S(2)}) collective-permute-start(bf16[2,128,128]{2,1,0:T(8,128)(2,1)S(1)} %copy-done.13), channel_id=1, source_target_pairs={{0,752},{16,32},{32,16},{48,64},{64,48},{80,96},{96,80},{112,128},... | collective-permute-start | bytes 196616 | tf_op jit(solution)/shard_map/ppermute | solution.py:48
Sparse Core Ops, SparseCore 0:
  31.5 58.2 all-gather.1

commit v8 on v5

--- a/solution.py
+++ b/solution.py
@@ -23,6 +23,7 @@
 Y_GROUPS = [[2 * y + z for y in range(NY)] for z in range(2)]
 SMEM = pl.BlockSpec(memory_space=pltpu.SMEM)
 VMEM = pl.BlockSpec(memory_space=pltpu.VMEM)
+ANY = pl.BlockSpec(memory_space=pl.ANY)
 PARAMS = pltpu.CompilerParams(vmem_limit_bytes=12 * 1024 * 1024)
 
 M_X, M_CORE, M_Y, M_Z = 9, 10, 11, 12
@@ -37,10 +38,14 @@
     return lax.ppermute(value, "ctx", pairs)
 
 
+def outer_swap(value):
+    pairs = [(s, (s - 1 if s % 2 == 0 else s + 1) % N_CTX) for s in range(N_CTX)]
+    return lax.ppermute(value, "ctx", pairs)
+
+
 def neighbours(first, last, even):
     inner = core_swap(jnp.where(even, last, first))
-    pairs = [(s, (s - 1 if s % 2 == 0 else s + 1) % N_CTX) for s in range(N_CTX)]
-    outer = lax.ppermute(jnp.where(even, first, last), "ctx", pairs)
+    outer = outer_swap(jnp.where(even, first, last))
     return jnp.where(even, outer, inner), jnp.where(even, inner, outer)
 
 
@@ -66,7 +71,8 @@
     return jnp.concatenate(parts, axis=0)
 
 
-def forward_kernel(meta, q, kv, prev, nxt, far1, far2, far3, probs_out, att_out):
+def forward_kernel(meta, w, q, kv, prev, nxt, far1, far2, far3, probs_out, att_out):
+    del w
     far = (far1, far2, far3)
     for j in range(3):
         rows = slice(j * BLK, (j + 1) * BLK)
@@ -94,8 +100,8 @@
             w_out[t, :, e * 128 : (e + 1) * 128] = rows.astype(BF16)
 
 
-def cotangent_kernel(meta, w, att, pieces, keep, give, grad, cols, flat):
-    z = meta[M_Z]
+def cotangent_kernel(w, att, pieces, keep, give, grad, cols, flat):
+    z = lax.axis_index("tp") % 2
     att_now = att[...]
     total = jnp.zeros((384, DH), F32)
     for i in range(N_TP):
@@ -108,7 +114,7 @@
         for e in range(2):
             flat[pl.ds(2 * t + e, DH, stride=32)] = cols[t, :, e * 128 : (e + 1) * 128]
     flat[FLAT_ROWS:] = jnp.zeros((flat.shape[0] - FLAT_ROWS, 128), F32)
-    first = meta[M_CORE] == 0
+    first = lax.axis_index("ctx") % 2 == 0
     for i in range(CHIPS):
         a = flat[2 * i * SHARD : 2 * i * SHARD + SHARD_PAD]
         b = flat[(2 * i + 1) * SHARD : (2 * i + 1) * SHARD + SHARD_PAD]
@@ -118,12 +124,14 @@
 
 def backward_kernel(
     meta, q, kv, prev, nxt, far1, far2, far3, probs, att, out_grad,
-    dq, dkv, dprev, dnext, dfar, acc,
+    dq, dkv, inner, outer, dfar, acc,
 ):
     far = (far1, far2, far3)
+    even = lax.axis_index("ctx") % 2 == 0
     acc[...] = jnp.zeros(acc.shape, F32)
     dkv[...] = jnp.zeros(dkv.shape, F32)
     scale = DH**-0.5
+    to_prev = []
     for j in range(3):
         rows = slice(j * BLK, (j + 1) * BLK)
         grad = out_grad[rows]
@@ -138,11 +146,13 @@
             part = parts[which]
             dkv[which, rows] += part[:BLK]
             if j == 0:
-                dprev[which] = part[BLK : 2 * BLK].astype(BF16)
+                to_prev.append(part[BLK : 2 * BLK])
             else:
                 dkv[which, (j - 1) * BLK : j * BLK] += part[BLK : 2 * BLK]
             if j == 2:
-                dnext[which] = part[2 * BLK : 3 * BLK].astype(BF16)
+                to_next = part[2 * BLK : 3 * BLK]
+                inner[which] = jnp.where(even, to_next, to_prev[which]).astype(BF16)
+                outer[which] = jnp.where(even, to_prev[which], to_next).astype(BF16)
             else:
                 dkv[which, (j + 1) * BLK : (j + 2) * BLK] += part[2 * BLK : 3 * BLK]
             for k in range(3):
@@ -163,16 +173,22 @@
     out[0] = total[:SHARD]
 
 
-def grad_sum_kernel(dkv, prev, nxt, far1, far2, far3, dk, dv):
+def outer_sum_kernel(dkv, outer, out):
+    even = lax.axis_index("ctx") % 2 == 0
+    away = outer[...].astype(F32)
+    out[...] = dkv[...]
+    out[:, :BLK] += jnp.where(even, away, 0.0)
+    out[:, 2 * BLK :] += jnp.where(even, 0.0, away)
+
+
+def last_sum_kernel(total, far1, far2, far3, inner, dk, dv):
+    even = lax.axis_index("ctx") % 2 == 0
     for which, out in ((0, dk), (1, dv)):
-        out[...] = (
-            dkv[which]
-            + far1[which].astype(F32)
-            + far2[which].astype(F32)
-            + far3[which].astype(F32)
-        )
-        out[:BLK] += prev[which].astype(F32)
-        out[2 * BLK :] += nxt[which].astype(F32)
+        parts = [far[which].astype(F32) for far in (far1, far2, far3)]
+        out[...] = total[which] + parts[0] + parts[1] + parts[2]
+        near = inner[which].astype(F32)
+        out[:BLK] += jnp.where(even, 0.0, near)
+        out[2 * BLK :] += jnp.where(even, near, 0.0)
 
 
 def on_device(queries, key_rows, values, cotangent, w_flat, block_keys):
@@ -215,17 +231,17 @@
             jax.ShapeDtypeStruct((3, BLK, 6 * BLK), F32),
             jax.ShapeDtypeStruct((384, DH), BF16),
         ),
-        in_specs=[SMEM] + [VMEM] * 7,
+        in_specs=[SMEM, ANY] + [VMEM] * 7,
         out_specs=(VMEM, VMEM),
         compiler_params=PARAMS,
         name="attention_forward",
-    )(meta, queries, kv, prev, nxt, *far)
+    )(meta, weight, queries, kv, prev, nxt, *far)
 
     chunk = jax.ShapeDtypeStruct((CHIPS, SHARD_PAD, 128), F32)
     keep, give, out_grad = pl.pallas_call(
         cotangent_kernel,
         out_shape=(chunk, chunk, jax.ShapeDtypeStruct((384, DH), BF16)),
-        in_specs=[SMEM, VMEM, VMEM, VMEM],
+        in_specs=[VMEM, VMEM, VMEM],
         out_specs=(VMEM, VMEM, VMEM),
         scratch_shapes=[
             pltpu.VMEM((N_TP, DH, WCOL), F32),
@@ -233,9 +249,9 @@
         ],
         compiler_params=PARAMS,
         name="cotangent_products",
-    )(meta, weight, att, pieces)
+    )(weight, att, pieces)
     two = (2, 384, DH)
-    dq, dkv, dprev, dnext, dfar = pl.pallas_call(
+    dq, dkv, inner, outer, dfar = pl.pallas_call(
         backward_kernel,
         out_shape=(
             jax.ShapeDtypeStruct((384, DH), F32),
@@ -253,7 +269,7 @@
     pair_sum = pl.pallas_call(
         pair_sum_kernel,
         out_shape=jax.ShapeDtypeStruct((CHIPS, SHARD_PAD, 128), BF16),
-        in_specs=[VMEM, VMEM, pl.BlockSpec(memory_space=pl.ANY)],
+        in_specs=[VMEM, VMEM, ANY],
         out_specs=VMEM,
         compiler_params=PARAMS,
         name="pair_sum",
@@ -267,16 +283,19 @@
         compiler_params=PARAMS,
         name="chunk_sum",
     )(spread)
-
-    far_back = [x_shift(dfar[k], k + 1) for k in range(3)]
-    from_prev, from_next = neighbours(dprev, dnext, even)
+    total = pl.pallas_call(
+        outer_sum_kernel,
+        out_shape=jax.ShapeDtypeStruct(two, F32),
+        compiler_params=PARAMS,
+        name="outer_sum",
+    )(dkv, outer_swap(outer))
     grad = jax.ShapeDtypeStruct((384, DH), F32)
     dk, dv = pl.pallas_call(
-        grad_sum_kernel,
+        last_sum_kernel,
         out_shape=(grad, grad),
         compiler_params=PARAMS,
-        name="grad_sum",
-    )(dkv, from_prev, from_next, *far_back)
+        name="last_sum",
+    )(total, *[x_shift(dfar[k], k + 1) for k in range(3)], core_swap(inner))
     return dq, dk, dv, weight_grad
 
 

time: 151 us -> 147 us (0.974)
  the two profiles are of different devices: /device:TPU:6 before, /device:TPU:1 now
where the time goes in v8:
time: 147 us; the launch traced here: 144 us
  starting transfers between devices  88.6 us (60%)
  between operations  18.4 us (13%)
  local copies, waits for them, and re-layouts  12.7 us (9%)
  Pallas kernels  11.4 us (8%)
  waiting for transfers between devices  11.2 us (8%)
  other arithmetic  1.9 us (1%)
    ppermute x6, starting transfers between devices, x_shift(): return lax.ppermute(value, 'ctx', pairs)  19.9 us
    ppermute x4, starting transfers between devices, core_swap(): return lax.ppermute(value, 'ctx', [(s, s ^ 1) for s in range(N_CTX)])  18.6 us
    all_to_all x1, starting transfers between devices, on_device(): lax.all_to_all(jnp.broadcast_to(w_pad[None], (CHIPS, SHARD_PAD, 128)), 'c...  15.7 us
    ppermute x1, starting transfers between devices, twin_swap(): return lax.ppermute(value, 'tp', [(s, s ^ 1) for s in range(N_TP)])  15.7 us
    all_to_all x1, starting transfers between devices, on_device(): lax.all_to_all(pair_sum, 'ctx', 0, 0, tiled=True, axis_index_groups=SAME_...  11 us
    unnamed x45, local copies, waits for them, and re-layouts  8.5 us
    ppermute x2, starting transfers between devices, outer_swap(): return lax.ppermute(value, 'ctx', pairs)  7.76 us
    ppermute x1, waiting for transfers between devices, twin_swap(): return lax.ppermute(value, 'tp', [(s, s ^ 1) for s in range(N_TP)])  6.75 us
  transfers between devices with their start and end apart: 16, of which 5 were waited for; matrix products, arithmetic and copies ran while one was open for 3% of the time, Pallas kernels for 5%

profile of v8, /device:TPU:1, one launch (start us, length us, event | category | flops | bytes accessed | tf_op | source)
XLA Modules:
  0.0 144.2 jit_solution(14394871508167326564)
XLA Ops:
  7.2 0.0 all-gather.2.cloned.1.call-start
  7.2 15.7 %collective-permute-start = (bf16[384,256]{1,0:T(8,128)(2,1)}, bf16[384,256]{1,0:T(8,128)(2,1)S(1)}, u32[]{:S(2)}, u32[]{:S(2)}) collective-permute-start(bf16[384,256]{1,0:T(8,128)(2,1)} %param.9), channel_id=1, source_target_pairs={{0,1},{1,0},{2,3},{3,2},{4,5},{5,4},{6,7},{7,6},{8,9},{9,8},{10,11... | collective-permute-start | bytes 589832 | tf_op jit(solution)/shard_map/ppermute | solution.py:57
  22.9 6.7 %collective-permute-done = bf16[384,256]{1,0:T(8,128)(2,1)S(1)} collective-permute-done((bf16[384,256]{1,0:T(8,128)(2,1)}, bf16[384,256]{1,0:T(8,128)(2,1)S(1)}, u32[]{:S(2)}, u32[]{:S(2)}) %collective-permute-start) | collective-permute-done | bytes 196640 | tf_op jit(solution)/shard_map/ppermute | solution.py:57
  29.7 1.7 %pad_maximum_fusion = bf16[768,256]{1,0:T(8,128)(2,1)} fusion(bf16[384,256]{1,0:T(8,128)(2,1)S(1)} %collective-permute-done, bf16[384,256]{1,0:T(8,128)(2,1)} %param.9), kind=kLoop, calls=%fused_computation.1 | loop fusion | flops 786432 | bytes 786432 | tf_op jit(solution)/shard_map/concatenate | solution.py:203
  31.4 0.0 all-gather.2.cloned.1.call-update
  31.4 0.9 broadcast_in_dim.13
  32.3 15.7 %all-to-all-start = ((bf16[24,88,128]{2,1,0:T(8,128)(2,1)}), bf16[24,88,128]{2,1,0:T(8,128)(2,1)S(1)}, u32[]{:S(2)}, u32[]{:S(2)}) async-start(bf16[24,88,128]{2,1,0:T(8,128)(2,1)} %broadcast_in_dim.13), calls=%async_computation | async-start | bytes 1081344 | tf_op jit(solution)/shard_map/all_to_all | solution.py:207
  48.1 0.0 copy-start.21
  48.1 0.5 slice.52
  49.4 2.9 %collective-permute-start.2 = (bf16[2,128,128]{2,1,0:T(8,128)(2,1)S(1)}, bf16[2,128,128]{2,1,0:T(8,128)(2,1)S(1)}, u32[]{:S(2)}, u32[]{:S(2)}) collective-permute-start(bf16[2,128,128]{2,1,0:T(8,128)(2,1)S(1)} %get-tuple-element.35), channel_id=1, source_target_pairs={{0,16},{16,0},{32,48},{48,32},{64,80},{80,64},{96,112},{112,96},{1... | collective-permute-start | bytes 196616 | tf_op jit(solution)/shard_map/ppermute | solution.py:53
  52.3 3.4 %collective-permute-start.1 = (bf16[2,128,128]{2,1,0:T(8,128)(2,1)S(1)}, bf16[2,128,128]{2,1,0:T(8,128)(2,1)S(1)}, u32[]{:S(2)}, u32[]{:S(2)}) collective-permute-start(bf16[2,128,128]{2,1,0:T(8,128)(2,1)S(1)} %get-tuple-element.36), channel_id=1, source_target_pairs={{0,752},{16,32},{32,16},{48,64},{64,48},{80,96},{96,80},{112,128},... | collective-permute-start | bytes 196616 | tf_op jit(solution)/shard_map/ppermute | solution.py:43
  55.6 4.3 %collective-permute-start.3 = (bf16[2,384,128]{2,1,0:T(8,128)(2,1)S(1)}, bf16[2,384,128]{2,1,0:T(8,128)(2,1)S(1)}, u32[]{:S(2)}, u32[]{:S(2)}) collective-permute-start(bf16[2,384,128]{2,1,0:T(8,128)(2,1)S(1)} %maximum_select_fusion.kv), channel_id=1, source_target_pairs={{0,576},{16,592},{32,608},{48,624},{64,640},{80,656},{96,672},{112... | collective-permute-start | bytes 589832 | tf_op jit(solution)/shard_map/ppermute | solution.py:38
  60.0 2.5 %collective-permute-start.4 = (bf16[2,384,128]{2,1,0:T(8,128)(2,1)S(1)}, bf16[2,384,128]{2,1,0:T(8,128)(2,1)S(1)}, u32[]{:S(2)}, u32[]{:S(2)}) collective-permute-start(bf16[2,384,128]{2,1,0:T(8,128)(2,1)S(1)} %maximum_select_fusion.kv), channel_id=1, source_target_pairs={{0,384},{16,400},{32,416},{48,432},{64,448},{80,464},{96,480},{112... | collective-permute-start | bytes 589832 | tf_op jit(solution)/shard_map/ppermute | solution.py:38
  62.4 2.5 %collective-permute-start.5 = (bf16[2,384,128]{2,1,0:T(8,128)(2,1)S(1)}, bf16[2,384,128]{2,1,0:T(8,128)(2,1)S(1)}, u32[]{:S(2)}, u32[]{:S(2)}) collective-permute-start(bf16[2,384,128]{2,1,0:T(8,128)(2,1)S(1)} %maximum_select_fusion.kv), channel_id=1, source_target_pairs={{0,192},{16,208},{32,224},{48,240},{64,256},{80,272},{96,288},{112... | collective-permute-start | bytes 589832 | tf_op jit(solution)/shard_map/ppermute | solution.py:38
  64.9 0.0 collective-permute-done.2
  65.0 0.0 copy-start.1
  65.0 0.0 copy-start.4
  65.0 0.5 slice.56
  65.5 0.5 slice.57
  67.2 0.5 slice.58
  68.4 1.0 collective-permute-done.4.far2
  69.5 0.5 slice.59
  70.6 1.3 collective-permute-done.5.far3
  72.0 0.5 slice.60
  73.2 0.0 all-to-all-done.own
  73.2 7.1 %collective-permute-start.6 = (bf16[24,88,128]{2,1,0:T(8,128)(2,1)S(1)}, bf16[24,88,128]{2,1,0:T(8,128)(2,1)S(1)}, u32[]{:S(2)}, u32[]{:S(2)}) collective-permute-start(bf16[24,88,128]{2,1,0:T(8,128)(2,1)S(1)} %broadcast_select_fusion), channel_id=1, source_target_pairs={{0,16},{16,0},{32,48},{48,32},{64,80},{80,64},{96,112},{112,96},{1... | collective-permute-start | bytes 1622024 | tf_op jit(solution)/shard_map/ppermute | solution.py:53
  80.4 0.1 add_select_fusion
  80.4 0.1 reshape.18
  80.5 0.1 concatenate.9.meta
  80.6 1.2 collective-permute-done.6.other
  81.9 2.3 %weight_rows.1.w = bf16[16,128,256]{2,1,0:T(8,128)(2,1)S(1)} custom-call(s32[13]{0:T(128)S(1)} %concatenate.9.meta, bf16[24,88,128]{2,1,0:T(8,128)(2,1)S(1)} %all-to-all-done.own, bf16[24,88,128]{2,1,0:T(8,128)(2,1)S(1)} %collective-permute-done.6.other), custom_call_target="tpu_custom_call" | custom-call | tf_op jit(solution)/shard_map/weight_rows/pallas_call | solution.py:218
  84.2 0.0 copy-start.11
  84.2 0.5 copy-done.11
  84.7 0.8 copy-done.2
  85.6 0.8 copy-done.5
  86.4 0.9 copy-done.7
  87.3 0.7 copy-done.12
  88.0 1.9 %attention_forward.1 = (f32[3,128,768]{2,1,0:T(8,128)S(1)}, bf16[384,128]{1,0:T(8,128)(2,1)S(1)}) custom-call(s32[13]{0:T(128)S(1)} %copy-done.12, bf16[16,128,256]{2,1,0:T(8,128)(2,1)S(1)} %weight_rows.1.w, bf16[384,128]{1,0:T(8,128)(2,1)S(1)} %copy-done.7, bf16[2,384,128]{2,1,0:T(8,128)(2,1)S(1)} %maximum_select_fusion.kv, ...), custom_call_target="tpu_custom_call" | custom-call | tf_op jit(solution)/shard_map/attention_forward/pallas_call | solution.py:228
  89.9 0.0 copy-start.9
  89.9 0.0 all-gather.2.cloned.1.call-done.pieces
  90.0 1.9 %copy-done = bf16[6144,256]{1,0:T(8,128)(2,1)S(1)} copy-done((bf16[6144,256]{1,0:T(8,128)(2,1)S(1)}, bf16[6144,256]{1,0:T(8,128)(2,1)}, u32[]{:S(2)}) %copy-start) | copy-done | bytes 3145752
  91.9 2.9 %cotangent_products.1 = (f32[24,88,128]{2,1,0:T(8,128)S(1)}, f32[24,88,128]{2,1,0:T(8,128)S(1)}, bf16[384,128]{1,0:T(8,128)(2,1)S(1)}) custom-call(bf16[16,128,256]{2,1,0:T(8,128)(2,1)S(1)} %weight_rows.1.w, bf16[384,128]{1,0:T(8,128)(2,1)S(1)} %get-tuple-element.17.att, bf16[6144,256]{1,0:T(8,128)(2,1)S(1)} %copy-done), custom_call_target="tpu_custom_call" | custom-call | tf_op jit(solution)/shard_map/cotangent_products/pallas_call | solution.py:241
  94.8 3.0 %collective-permute-start.12 = (f32[24,88,128]{2,1,0:T(8,128)S(1)}, f32[24,88,128]{2,1,0:T(8,128)S(1)}, u32[]{:S(2)}, u32[]{:S(2)}) collective-permute-start(f32[24,88,128]{2,1,0:T(8,128)S(1)} %get-tuple-element.27), channel_id=1, source_target_pairs={{0,16},{16,0},{32,48},{48,32},{64,80},{80,64},{96,112},{112,96},{1... | collective-permute-start | bytes 3244040 | tf_op jit(solution)/shard_map/ppermute | solution.py:53
  97.9 0.0 copy-start.10
  97.9 0.9 copy-done.10
  98.8 2.3 %attention_backward.1 = (f32[384,128]{1,0:T(8,128)}, f32[2,384,128]{2,1,0:T(8,128)S(1)}, bf16[2,128,128]{2,1,0:T(8,128)(2,1)S(1)}, bf16[2,128,128]{2,1,0:T(8,128)(2,1)S(1)}, bf16[3,2,384,128]{3,2,1,0:T(8,128)(2,1)S(1)}) custom-call(s32[13]{0:T(128)S(1)} %copy-done.13, bf16[384,128]{1,0:T(8,128)(2,1)S(1)} %copy-done.8, ...), custom_call_target="tpu_custom_call" | custom-call | tf_op jit(solution)/shard_map/attention_backward/pallas_call | solution.py:254
  101.1 0.6 copy-done.14
  101.7 0.6 copy-done.16
  102.3 0.9 pair_sum.1
  103.3 11.0 %all-to-all-start.1 = ((bf16[24,88,128]{2,1,0:T(8,128)(2,1)}), bf16[24,88,128]{2,1,0:T(8,128)(2,1)S(1)}, u32[]{:S(2)}, u32[]{:S(2)}) async-start(bf16[24,88,128]{2,1,0:T(8,128)(2,1)} %pair_sum.1), calls=%async_computation.1 | async-start | bytes 1081344 | tf_op jit(solution)/shard_map/all_to_all | solution.py:277
  114.3 3.2 %collective-permute-start.8 = (bf16[2,384,128]{2,1,0:T(8,128)(2,1)S(1)}, bf16[2,384,128]{2,1,0:T(8,128)(2,1)S(1)}, u32[]{:S(2)}, u32[]{:S(2)}) collective-permute-start(bf16[2,384,128]{2,1,0:T(8,128)(2,1)S(1)} %get-tuple-element.34), channel_id=1, source_target_pairs={{0,192},{16,208},{32,224},{48,240},{64,256},{80,272},{96,288},{112... | collective-permute-start | bytes 589832 | tf_op jit(solution)/shard_map/ppermute | solution.py:38
  117.5 4.3 %collective-permute-start.9 = (bf16[2,384,128]{2,1,0:T(8,128)(2,1)S(1)}, bf16[2,384,128]{2,1,0:T(8,128)(2,1)S(1)}, u32[]{:S(2)}, u32[]{:S(2)}) collective-permute-start(bf16[2,384,128]{2,1,0:T(8,128)(2,1)S(1)} %get-tuple-element.33), channel_id=1, source_target_pairs={{0,384},{16,400},{32,416},{48,432},{64,448},{80,464},{96,480},{112... | collective-permute-start | bytes 589832 | tf_op jit(solution)/shard_map/ppermute | solution.py:38
  121.8 3.1 %collective-permute-start.10 = (bf16[2,384,128]{2,1,0:T(8,128)(2,1)S(1)}, bf16[2,384,128]{2,1,0:T(8,128)(2,1)S(1)}, u32[]{:S(2)}, u32[]{:S(2)}) collective-permute-start(bf16[2,384,128]{2,1,0:T(8,128)(2,1)S(1)} %get-tuple-element.32), channel_id=1, source_target_pairs={{0,576},{16,592},{32,608},{48,624},{64,640},{80,656},{96,672},{112... | collective-permute-start | bytes 589832 | tf_op jit(solution)/shard_map/ppermute | solution.py:38
  124.9 4.4 %collective-permute-start.7 = (bf16[2,128,128]{2,1,0:T(8,128)(2,1)S(1)}, bf16[2,128,128]{2,1,0:T(8,128)(2,1)S(1)}, u32[]{:S(2)}, u32[]{:S(2)}) collective-permute-start(bf16[2,128,128]{2,1,0:T(8,128)(2,1)S(1)} %copy-done.17), channel_id=1, source_target_pairs={{0,752},{16,32},{32,16},{48,64},{64,48},{80,96},{96,80},{112,128},... | collective-permute-start | bytes 196616 | tf_op jit(solution)/shard_map/ppermute | solution.py:43
  129.3 5.5 %collective-permute-start.11 = (bf16[2,128,128]{2,1,0:T(8,128)(2,1)S(1)}, bf16[2,128,128]{2,1,0:T(8,128)(2,1)S(1)}, u32[]{:S(2)}, u32[]{:S(2)}) collective-permute-start(bf16[2,128,128]{2,1,0:T(8,128)(2,1)S(1)} %copy-done.15), channel_id=1, source_target_pairs={{0,16},{16,0},{32,48},{48,32},{64,80},{80,64},{96,112},{112,96},{1... | collective-permute-start | bytes 196616 | tf_op jit(solution)/shard_map/ppermute | solution.py:53
  134.9 0.0 collective-permute-done.7.outer
  134.9 0.1 outer_sum.1.total
  134.9 0.8 collective-permute-done.11.inner
  135.7 0.0 collective-permute-done.8.far1
  135.7 0.0 collective-permute-done.9.far2
  135.7 0.0 collective-permute-done.10.far3
  135.7 0.8 last_sum.1
  136.6 0.1 chunk_sum.1
  136.7 0.7 copy.10
  (40 shorter events, 0.2 us)
Async XLA Ops:
  7.2 24.3 %copy-start.20 = (bf16[1,86,128]{2,1,0:T(8,128)(2,1)S(1)}, bf16[1,86,128]{2,1,0:T(8,128)(2,1)}, u32[]{:S(2)}) copy-start(bf16[1,86,128]{2,1,0:T(8,128)(2,1)} %param.10) | copy-start | bytes 66052
  7.2 82.8 %all-gather.2.cloned.1.call-start = ((), (), s32[]{:S(2)}) async-start(), calls=%async_computation.2 | async-start | bytes 3538944 | tf_op jit(solution)/shard_map/all_gather | solution.py:202
  7.2 22.4 %collective-permute-start = (bf16[384,256]{1,0:T(8,128)(2,1)}, bf16[384,256]{1,0:T(8,128)(2,1)S(1)}, u32[]{:S(2)}, u32[]{:S(2)}) collective-permute-start(bf16[384,256]{1,0:T(8,128)(2,1)} %param.9), channel_id=1, source_target_pairs={{0,1},{1,0},{2,3},{3,2},{4,5},{5,4},{6,7},{7,6},{8,9},{9,8},{10,11... | collective-permute-start | bytes 589832 | tf_op jit(solution)/shard_map/ppermute | solution.py:57
  31.4 17.9 %copy-start.18 = (bf16[384,128]{1,0:T(8,128)(2,1)S(1)}, bf16[384,128]{1,0:T(8,128)(2,1)}, u32[]{:S(2)}) copy-start(bf16[384,128]{1,0:T(8,128)(2,1)} %param.8) | copy-start | bytes 294916
  31.4 17.9 %copy-start.19 = (bf16[384,128]{1,0:T(8,128)(2,1)S(1)}, bf16[384,128]{1,0:T(8,128)(2,1)}, u32[]{:S(2)}) copy-start(bf16[384,128]{1,0:T(8,128)(2,1)} %param.7) | copy-start | bytes 294916
  32.3 40.8 %all-to-all-start = ((bf16[24,88,128]{2,1,0:T(8,128)(2,1)}), bf16[24,88,128]{2,1,0:T(8,128)(2,1)S(1)}, u32[]{:S(2)}, u32[]{:S(2)}) async-start(bf16[24,88,128]{2,1,0:T(8,128)(2,1)} %broadcast_in_dim.13), calls=%async_computation | async-start | bytes 1081344 | tf_op jit(solution)/shard_map/all_to_all | solution.py:207
  48.1 32.3 %copy-start.21 = (s32[3,6]{1,0:T(4,128)S(1)}, s32[3,6]{1,0:T(4,128)}, u32[]{:S(2)}) copy-start(s32[3,6]{1,0:T(4,128)} %param.11) | copy-start | bytes 220
  49.4 15.6 %collective-permute-start.2 = (bf16[2,128,128]{2,1,0:T(8,128)(2,1)S(1)}, bf16[2,128,128]{2,1,0:T(8,128)(2,1)S(1)}, u32[]{:S(2)}, u32[]{:S(2)}) collective-permute-start(bf16[2,128,128]{2,1,0:T(8,128)(2,1)S(1)} %get-tuple-element.35), channel_id=1, source_target_pairs={{0,16},{16,0},{32,48},{48,32},{64,80},{80,64},{96,112},{112,96},{1... | collective-permute-start | bytes 196616 | tf_op jit(solution)/shard_map/ppermute | solution.py:53
  52.3 12.7 %collective-permute-start.1 = (bf16[2,128,128]{2,1,0:T(8,128)(2,1)S(1)}, bf16[2,128,128]{2,1,0:T(8,128)(2,1)S(1)}, u32[]{:S(2)}, u32[]{:S(2)}) collective-permute-start(bf16[2,128,128]{2,1,0:T(8,128)(2,1)S(1)} %get-tuple-element.36), channel_id=1, source_target_pairs={{0,752},{16,32},{32,16},{48,64},{64,48},{80,96},{96,80},{112,128},... | collective-permute-start | bytes 196616 | tf_op jit(solution)/shard_map/ppermute | solution.py:43
  55.6 11.6 %collective-permute-start.3 = (bf16[2,384,128]{2,1,0:T(8,128)(2,1)S(1)}, bf16[2,384,128]{2,1,0:T(8,128)(2,1)S(1)}, u32[]{:S(2)}, u32[]{:S(2)}) collective-permute-start(bf16[2,384,128]{2,1,0:T(8,128)(2,1)S(1)} %maximum_select_fusion.kv), channel_id=1, source_target_pairs={{0,576},{16,592},{32,608},{48,624},{64,640},{80,656},{96,672},{112... | collective-permute-start | bytes 589832 | tf_op jit(solution)/shard_map/ppermute | solution.py:38
  60.0 9.5 %collective-permute-start.4 = (bf16[2,384,128]{2,1,0:T(8,128)(2,1)S(1)}, bf16[2,384,128]{2,1,0:T(8,128)(2,1)S(1)}, u32[]{:S(2)}, u32[]{:S(2)}) collective-permute-start(bf16[2,384,128]{2,1,0:T(8,128)(2,1)S(1)} %maximum_select_fusion.kv), channel_id=1, source_target_pairs={{0,384},{16,400},{32,416},{48,432},{64,448},{80,464},{96,480},{112... | collective-permute-start | bytes 589832 | tf_op jit(solution)/shard_map/ppermute | solution.py:38
  62.4 9.5 %collective-permute-start.5 = (bf16[2,384,128]{2,1,0:T(8,128)(2,1)S(1)}, bf16[2,384,128]{2,1,0:T(8,128)(2,1)S(1)}, u32[]{:S(2)}, u32[]{:S(2)}) collective-permute-start(bf16[2,384,128]{2,1,0:T(8,128)(2,1)S(1)} %maximum_select_fusion.kv), channel_id=1, source_target_pairs={{0,192},{16,208},{32,224},{48,240},{64,256},{80,272},{96,288},{112... | collective-permute-start | bytes 589832 | tf_op jit(solution)/shard_map/ppermute | solution.py:38
  65.0 16.9 %copy-start.1 = (bf16[2,128,128]{2,1,0:T(8,128)(2,1)}, bf16[2,128,128]{2,1,0:T(8,128)(2,1)S(1)}, u32[]{:S(2)}) copy-start(bf16[2,128,128]{2,1,0:T(8,128)(2,1)S(1)} %get-tuple-element.37.nxt) | copy-start | bytes 196612
  65.0 16.9 %copy-start.4 = (bf16[2,128,128]{2,1,0:T(8,128)(2,1)}, bf16[2,128,128]{2,1,0:T(8,128)(2,1)S(1)}, u32[]{:S(2)}) copy-start(bf16[2,128,128]{2,1,0:T(8,128)(2,1)S(1)} %get-tuple-element.38.prev) | copy-start | bytes 196612
  73.2 8.7 %collective-permute-start.6 = (bf16[24,88,128]{2,1,0:T(8,128)(2,1)S(1)}, bf16[24,88,128]{2,1,0:T(8,128)(2,1)S(1)}, u32[]{:S(2)}, u32[]{:S(2)}) collective-permute-start(bf16[24,88,128]{2,1,0:T(8,128)(2,1)S(1)} %broadcast_select_fusion), channel_id=1, source_target_pairs={{0,16},{16,0},{32,48},{48,32},{64,80},{80,64},{96,112},{112,96},{1... | collective-permute-start | bytes 1622024 | tf_op jit(solution)/shard_map/ppermute | solution.py:53
  84.2 0.5 copy-start.11
  84.7 0.8 copy-start.2
  85.6 0.8 copy-start.5
  86.4 0.9 copy-start.7
  87.3 0.7 copy-start.12
  89.9 4.9 %copy-start.9 = (bf16[384,128]{1,0:T(8,128)(2,1)}, bf16[384,128]{1,0:T(8,128)(2,1)S(1)}, u32[]{:S(2)}) copy-start(bf16[384,128]{1,0:T(8,128)(2,1)S(1)} %get-tuple-element.17.att) | copy-start | bytes 294916
  90.0 1.9 %copy-start = (bf16[6144,256]{1,0:T(8,128)(2,1)S(1)}, bf16[6144,256]{1,0:T(8,128)(2,1)}, u32[]{:S(2)}) copy-start(bf16[6144,256]{1,0:T(8,128)(2,1)} %all-gather.2.cloned.1.call-done.pieces) | copy-start | bytes 9437188
  91.9 6.0 %copy-start.3 = (bf16[2,128,128]{2,1,0:T(8,128)(2,1)S(1)}, bf16[2,128,128]{2,1,0:T(8,128)(2,1)}, u32[]{:S(2)}) copy-start(bf16[2,128,128]{2,1,0:T(8,128)(2,1)} %copy-done.1) | copy-start | bytes 196612
  91.9 6.0 %copy-start.6 = (bf16[2,128,128]{2,1,0:T(8,128)(2,1)S(1)}, bf16[2,128,128]{2,1,0:T(8,128)(2,1)}, u32[]{:S(2)}) copy-start(bf16[2,128,128]{2,1,0:T(8,128)(2,1)} %copy-done.4) | copy-start | bytes 196612
  91.9 6.0 %copy-start.8 = (bf16[384,128]{1,0:T(8,128)(2,1)S(1)}, bf16[384,128]{1,0:T(8,128)(2,1)}, u32[]{:S(2)}) copy-start(bf16[384,128]{1,0:T(8,128)(2,1)} %q.3) | copy-start | bytes 294916
  91.9 6.0 %copy-start.13 = (s32[13]{0:T(128)S(1)}, s32[13]{0:T(128)}, u32[]{:S(2)}) copy-start(s32[13]{0:T(128)} %copy-done.11) | copy-start | bytes 160
  94.8 7.5 %collective-permute-start.12 = (f32[24,88,128]{2,1,0:T(8,128)S(1)}, f32[24,88,128]{2,1,0:T(8,128)S(1)}, u32[]{:S(2)}, u32[]{:S(2)}) collective-permute-start(f32[24,88,128]{2,1,0:T(8,128)S(1)} %get-tuple-element.27), channel_id=1, source_target_pairs={{0,16},{16,0},{32,48},{48,32},{64,80},{80,64},{96,112},{112,96},{1... | collective-permute-start | bytes 3244040 | tf_op jit(solution)/shard_map/ppermute | solution.py:53
  97.9 0.9 copy-start.10
  101.1 0.6 copy-start.14
  101.7 0.6 copy-start.16
  103.3 21.6 %copy-start.17 = (bf16[2,128,128]{2,1,0:T(8,128)(2,1)S(1)}, bf16[2,128,128]{2,1,0:T(8,128)(2,1)}, u32[]{:S(2)}) copy-start(bf16[2,128,128]{2,1,0:T(8,128)(2,1)} %copy-done.16) | copy-start | bytes 196612
  103.3 26.0 %copy-start.15 = (bf16[2,128,128]{2,1,0:T(8,128)(2,1)S(1)}, bf16[2,128,128]{2,1,0:T(8,128)(2,1)}, u32[]{:S(2)}) copy-start(bf16[2,128,128]{2,1,0:T(8,128)(2,1)} %copy-done.14) | copy-start | bytes 196612
  103.3 33.3 %all-to-all-start.1 = ((bf16[24,88,128]{2,1,0:T(8,128)(2,1)}), bf16[24,88,128]{2,1,0:T(8,128)(2,1)S(1)}, u32[]{:S(2)}, u32[]{:S(2)}) async-start(bf16[24,88,128]{2,1,0:T(8,128)(2,1)} %pair_sum.1), calls=%async_computation.1 | async-start | bytes 1081344 | tf_op jit(solution)/shard_map/all_to_all | solution.py:277
  114.3 21.5 %collective-permute-start.8 = (bf16[2,384,128]{2,1,0:T(8,128)(2,1)S(1)}, bf16[2,384,128]{2,1,0:T(8,128)(2,1)S(1)}, u32[]{:S(2)}, u32[]{:S(2)}) collective-permute-start(bf16[2,384,128]{2,1,0:T(8,128)(2,1)S(1)} %get-tuple-element.34), channel_id=1, source_target_pairs={{0,192},{16,208},{32,224},{48,240},{64,256},{80,272},{96,288},{112... | collective-permute-start | bytes 589832 | tf_op jit(solution)/shard_map/ppermute | solution.py:38
  117.5 18.3 %collective-permute-start.9 = (bf16[2,384,128]{2,1,0:T(8,128)(2,1)S(1)}, bf16[2,384,128]{2,1,0:T(8,128)(2,1)S(1)}, u32[]{:S(2)}, u32[]{:S(2)}) collective-permute-start(bf16[2,384,128]{2,1,0:T(8,128)(2,1)S(1)} %get-tuple-element.33), channel_id=1, source_target_pairs={{0,384},{16,400},{32,416},{48,432},{64,448},{80,464},{96,480},{112... | collective-permute-start | bytes 589832 | tf_op jit(solution)/shard_map/ppermute | solution.py:38
  121.8 14.0 %collective-permute-start.10 = (bf16[2,384,128]{2,1,0:T(8,128)(2,1)S(1)}, bf16[2,384,128]{2,1,0:T(8,128)(2,1)S(1)}, u32[]{:S(2)}, u32[]{:S(2)}) collective-permute-start(bf16[2,384,128]{2,1,0:T(8,128)(2,1)S(1)} %get-tuple-element.32), channel_id=1, source_target_pairs={{0,576},{16,592},{32,608},{48,624},{64,640},{80,656},{96,672},{112... | collective-permute-start | bytes 589832 | tf_op jit(solution)/shard_map/ppermute | solution.py:38
  124.9 10.0 %collective-permute-start.7 = (bf16[2,128,128]{2,1,0:T(8,128)(2,1)S(1)}, bf16[2,128,128]{2,1,0:T(8,128)(2,1)S(1)}, u32[]{:S(2)}, u32[]{:S(2)}) collective-permute-start(bf16[2,128,128]{2,1,0:T(8,128)(2,1)S(1)} %copy-done.17), channel_id=1, source_target_pairs={{0,752},{16,32},{32,16},{48,64},{64,48},{80,96},{96,80},{112,128},... | collective-permute-start | bytes 196616 | tf_op jit(solution)/shard_map/ppermute | solution.py:43
  129.3 6.4 %collective-permute-start.11 = (bf16[2,128,128]{2,1,0:T(8,128)(2,1)S(1)}, bf16[2,128,128]{2,1,0:T(8,128)(2,1)S(1)}, u32[]{:S(2)}, u32[]{:S(2)}) collective-permute-start(bf16[2,128,128]{2,1,0:T(8,128)(2,1)S(1)} %copy-done.15), channel_id=1, source_target_pairs={{0,16},{16,0},{32,48},{48,32},{64,80},{80,64},{96,112},{112,96},{1... | collective-permute-start | bytes 196616 | tf_op jit(solution)/shard_map/ppermute | solution.py:53
Sparse Core Ops, SparseCore 0:
  31.5 58.1 all-gather.1

commit v9 on v8

--- a/solution.py
+++ b/solution.py
@@ -100,9 +100,10 @@
             w_out[t, :, e * 128 : (e + 1) * 128] = rows.astype(BF16)
 
 
-def cotangent_kernel(w, att, pieces, keep, give, grad, cols, flat):
+def cotangent_kernel(w, att, pieces, keep, give, grad, att_out, cols, flat):
     z = lax.axis_index("tp") % 2
     att_now = att[...]
+    att_out[...] = att_now
     total = jnp.zeros((384, DH), F32)
     for i in range(N_TP):
         col = 2 * (i // 2) + (z if i % 2 == 0 else 1 - z)
@@ -124,7 +125,7 @@
 
 def backward_kernel(
     meta, q, kv, prev, nxt, far1, far2, far3, probs, att, out_grad,
-    dq, dkv, inner, outer, dfar, acc,
+    dq, dkv, band, dfar, acc,
 ):
     far = (far1, far2, far3)
     even = lax.axis_index("ctx") % 2 == 0
@@ -151,8 +152,10 @@
                 dkv[which, (j - 1) * BLK : j * BLK] += part[BLK : 2 * BLK]
             if j == 2:
                 to_next = part[2 * BLK : 3 * BLK]
-                inner[which] = jnp.where(even, to_next, to_prev[which]).astype(BF16)
-                outer[which] = jnp.where(even, to_prev[which], to_next).astype(BF16)
+                inner = jnp.where(even, to_next, to_prev[which])
+                outer = jnp.where(even, to_prev[which], to_next)
+                band[which, :BLK] = outer.astype(BF16)
+                band[which, BLK:] = inner.astype(BF16)
             else:
                 dkv[which, (j + 1) * BLK : (j + 2) * BLK] += part[2 * BLK : 3 * BLK]
             for k in range(3):
@@ -173,22 +176,14 @@
     out[0] = total[:SHARD]
 
 
-def outer_sum_kernel(dkv, outer, out):
-    even = lax.axis_index("ctx") % 2 == 0
-    away = outer[...].astype(F32)
-    out[...] = dkv[...]
-    out[:, :BLK] += jnp.where(even, away, 0.0)
-    out[:, 2 * BLK :] += jnp.where(even, 0.0, away)
-
-
-def last_sum_kernel(total, far1, far2, far3, inner, dk, dv):
+def grad_sum_kernel(dkv, prev, nxt, far1, far2, far3, inner, dk, dv):
     even = lax.axis_index("ctx") % 2 == 0
     for which, out in ((0, dk), (1, dv)):
         parts = [far[which].astype(F32) for far in (far1, far2, far3)]
-        out[...] = total[which] + parts[0] + parts[1] + parts[2]
+        out[...] = dkv[which] + parts[0] + parts[1] + parts[2]
         near = inner[which].astype(F32)
-        out[:BLK] += jnp.where(even, 0.0, near)
-        out[2 * BLK :] += jnp.where(even, near, 0.0)
+        out[:BLK] += prev[which].astype(F32) + jnp.where(even, 0.0, near)
+        out[2 * BLK :] += nxt[which].astype(F32) + jnp.where(even, near, 0.0)
 
 
 def on_device(queries, key_rows, values, cotangent, w_flat, block_keys):
@@ -238,11 +233,11 @@
     )(meta, weight, queries, kv, prev, nxt, *far)
 
     chunk = jax.ShapeDtypeStruct((CHIPS, SHARD_PAD, 128), F32)
-    keep, give, out_grad = pl.pallas_call(
+    keep, give, out_grad, att_here = pl.pallas_call(
         cotangent_kernel,
-        out_shape=(chunk, chunk, jax.ShapeDtypeStruct((384, DH), BF16)),
+        out_shape=(chunk, chunk) + (jax.ShapeDtypeStruct((384, DH), BF16),) * 2,
         in_specs=[VMEM, VMEM, VMEM],
-        out_specs=(VMEM, VMEM, VMEM),
+        out_specs=(VMEM,) * 4,
         scratch_shapes=[
             pltpu.VMEM((N_TP, DH, WCOL), F32),
             pltpu.VMEM((flat_alloc, 128), F32),
@@ -251,21 +246,20 @@
         name="cotangent_products",
     )(weight, att, pieces)
     two = (2, 384, DH)
-    dq, dkv, inner, outer, dfar = pl.pallas_call(
+    dq, dkv, band, dfar = pl.pallas_call(
         backward_kernel,
         out_shape=(
             jax.ShapeDtypeStruct((384, DH), F32),
             jax.ShapeDtypeStruct(two, F32),
-            jax.ShapeDtypeStruct((2, BLK, DH), BF16),
-            jax.ShapeDtypeStruct((2, BLK, DH), BF16),
+            jax.ShapeDtypeStruct((2, 2 * BLK, DH), BF16),
             jax.ShapeDtypeStruct((3,) + two, BF16),
         ),
         in_specs=[SMEM] + [VMEM] * 10,
-        out_specs=(VMEM,) * 5,
+        out_specs=(VMEM,) * 4,
         scratch_shapes=[pltpu.VMEM((3,) + two, F32)],
         compiler_params=PARAMS,
         name="attention_backward",
-    )(meta, queries, kv, prev, nxt, *far, probs, att, out_grad)
+    )(meta, queries, kv, prev, nxt, *far, probs, att_here, out_grad)
     pair_sum = pl.pallas_call(
         pair_sum_kernel,
         out_shape=jax.ShapeDtypeStruct((CHIPS, SHARD_PAD, 128), BF16),
@@ -283,19 +277,19 @@
         compiler_params=PARAMS,
         name="chunk_sum",
     )(spread)
-    total = pl.pallas_call(
-        outer_sum_kernel,
-        out_shape=jax.ShapeDtypeStruct(two, F32),
-        compiler_params=PARAMS,
-        name="outer_sum",
-    )(dkv, outer_swap(outer))
+    far_back = [x_shift(dfar[k], k + 1) for k in range(3)]
+    from_inner = core_swap(band[:, BLK:])
+    from_outer = outer_swap(band[:, :BLK])
+    zeros = jnp.zeros_like(from_outer)
+    from_prev = jnp.where(even, from_outer, zeros)
+    from_next = jnp.where(even, zeros, from_outer)
     grad = jax.ShapeDtypeStruct((384, DH), F32)
     dk, dv = pl.pallas_call(
-        last_sum_kernel,
+        grad_sum_kernel,
         out_shape=(grad, grad),
         compiler_params=PARAMS,
-        name="last_sum",
-    )(total, *[x_shift(dfar[k], k + 1) for k in range(3)], core_swap(inner))
+        name="grad_sum",
+    )(dkv, from_prev, from_next, far_back[1], far_back[0], far_back[2], from_inner)
     return dq, dk, dv, weight_grad
 
 

time: 147 us -> 145 us (0.986); the launches traced: 144 us -> 144 us
  starting transfers between devices: 88.6 us -> 90.4 us
  local copies, waits for them, and re-layouts: 12.7 us -> 11.2 us
    ppermute x4, starting transfers between devices: 18.6 us -> 20.5 us  [core_swap(): return lax.ppermute(value, 'ctx', [(s, s ^ 1) for s in range(N_CTX)])]
    unnamed x45 -> x37, local copies, waits for them, and re-layouts: 8.5 us -> 6.98 us
    pallas_call x3 -> x2, Pallas kernels: 3.78 us -> 3.74 us  [the longest x1 2.91 us: on_device(): pl.pallas_call(cotangent_kernel, out_shape=(chunk, chunk) + (jax.ShapeDty...]
where the time goes in v9:
time: 145 us; the launch traced here: 144 us
  starting transfers between devices  90.4 us (62%)
  between operations  18.5 us (13%)
  Pallas kernels  11.3 us (8%)
  local copies, waits for them, and re-layouts  11.2 us (8%)
  waiting for transfers between devices  11.1 us (8%)
  other arithmetic  1.91 us (1%)
    ppermute x4, starting transfers between devices, core_swap(): return lax.ppermute(value, 'ctx', [(s, s ^ 1) for s in range(N_CTX)])  20.5 us
    ppermute x6, starting transfers between devices, x_shift(): return lax.ppermute(value, 'ctx', pairs)  20.4 us
    all_to_all x1, starting transfers between devices, on_device(): lax.all_to_all(jnp.broadcast_to(w_pad[None], (CHIPS, SHARD_PAD, 128)), 'c...  15.7 us
    ppermute x1, starting transfers between devices, twin_swap(): return lax.ppermute(value, 'tp', [(s, s ^ 1) for s in range(N_TP)])  15.7 us
    all_to_all x1, starting transfers between devices, on_device(): lax.all_to_all(pair_sum, 'ctx', 0, 0, tiled=True, axis_index_groups=SAME_...  11 us
    ppermute x2, starting transfers between devices, outer_swap(): return lax.ppermute(value, 'ctx', pairs)  7.03 us
    unnamed x37, local copies, waits for them, and re-layouts  6.98 us
    ppermute x1, waiting for transfers between devices, twin_swap(): return lax.ppermute(value, 'tp', [(s, s ^ 1) for s in range(N_TP)])  6.75 us
  transfers between devices with their start and end apart: 16, of which 5 were waited for; matrix products, arithmetic and copies ran while one was open for 3% of the time, Pallas kernels for 5%

profile of v9, /device:TPU:1, one launch (start us, length us, event | category | flops | bytes accessed | tf_op | source)
XLA Modules:
  0.0 144.4 jit_solution(15217492796311274548)
XLA Ops:
  7.2 0.0 all-gather.2.cloned.1.call-start
  7.2 15.7 %collective-permute-start = (bf16[384,256]{1,0:T(8,128)(2,1)}, bf16[384,256]{1,0:T(8,128)(2,1)S(1)}, u32[]{:S(2)}, u32[]{:S(2)}) collective-permute-start(bf16[384,256]{1,0:T(8,128)(2,1)} %param.9), channel_id=1, source_target_pairs={{0,1},{1,0},{2,3},{3,2},{4,5},{5,4},{6,7},{7,6},{8,9},{9,8},{10,11... | collective-permute-start | bytes 589832 | tf_op jit(solution)/shard_map/ppermute | solution.py:57
  22.9 6.7 %collective-permute-done = bf16[384,256]{1,0:T(8,128)(2,1)S(1)} collective-permute-done((bf16[384,256]{1,0:T(8,128)(2,1)}, bf16[384,256]{1,0:T(8,128)(2,1)S(1)}, u32[]{:S(2)}, u32[]{:S(2)}) %collective-permute-start) | collective-permute-done | bytes 196640 | tf_op jit(solution)/shard_map/ppermute | solution.py:57
  29.7 1.7 %pad_maximum_fusion = bf16[768,256]{1,0:T(8,128)(2,1)} fusion(bf16[384,256]{1,0:T(8,128)(2,1)S(1)} %collective-permute-done, bf16[384,256]{1,0:T(8,128)(2,1)} %param.9), kind=kLoop, calls=%fused_computation.1 | loop fusion | flops 786432 | bytes 786432 | tf_op jit(solution)/shard_map/concatenate | solution.py:198
  31.4 0.0 all-gather.2.cloned.1.call-update
  31.4 0.9 broadcast_in_dim.16
  32.3 15.7 %all-to-all-start = ((bf16[24,88,128]{2,1,0:T(8,128)(2,1)}), bf16[24,88,128]{2,1,0:T(8,128)(2,1)S(1)}, u32[]{:S(2)}, u32[]{:S(2)}) async-start(bf16[24,88,128]{2,1,0:T(8,128)(2,1)} %broadcast_in_dim.16), calls=%async_computation | async-start | bytes 1081344 | tf_op jit(solution)/shard_map/all_to_all | solution.py:202
  48.1 0.0 copy-start.17
  48.1 0.5 slice.60
  49.3 0.0 copy-done.14
  49.3 2.9 %collective-permute-start.2 = (bf16[2,128,128]{2,1,0:T(8,128)(2,1)S(1)}, bf16[2,128,128]{2,1,0:T(8,128)(2,1)S(1)}, u32[]{:S(2)}, u32[]{:S(2)}) collective-permute-start(bf16[2,128,128]{2,1,0:T(8,128)(2,1)S(1)} %get-tuple-element.35), channel_id=1, source_target_pairs={{0,16},{16,0},{32,48},{48,32},{64,80},{80,64},{96,112},{112,96},{1... | collective-permute-start | bytes 196616 | tf_op jit(solution)/shard_map/ppermute | solution.py:53
  52.2 3.4 %collective-permute-start.1 = (bf16[2,128,128]{2,1,0:T(8,128)(2,1)S(1)}, bf16[2,128,128]{2,1,0:T(8,128)(2,1)S(1)}, u32[]{:S(2)}, u32[]{:S(2)}) collective-permute-start(bf16[2,128,128]{2,1,0:T(8,128)(2,1)S(1)} %get-tuple-element.36), channel_id=1, source_target_pairs={{0,752},{16,32},{32,16},{48,64},{64,48},{80,96},{96,80},{112,128},... | collective-permute-start | bytes 196616 | tf_op jit(solution)/shard_map/ppermute | solution.py:43
  55.6 4.3 %collective-permute-start.3 = (bf16[2,384,128]{2,1,0:T(8,128)(2,1)S(1)}, bf16[2,384,128]{2,1,0:T(8,128)(2,1)S(1)}, u32[]{:S(2)}, u32[]{:S(2)}) collective-permute-start(bf16[2,384,128]{2,1,0:T(8,128)(2,1)S(1)} %maximum_select_fusion.kv), channel_id=1, source_target_pairs={{0,576},{16,592},{32,608},{48,624},{64,640},{80,656},{96,672},{112... | collective-permute-start | bytes 589832 | tf_op jit(solution)/shard_map/ppermute | solution.py:38
  59.9 2.5 %collective-permute-start.4 = (bf16[2,384,128]{2,1,0:T(8,128)(2,1)S(1)}, bf16[2,384,128]{2,1,0:T(8,128)(2,1)S(1)}, u32[]{:S(2)}, u32[]{:S(2)}) collective-permute-start(bf16[2,384,128]{2,1,0:T(8,128)(2,1)S(1)} %maximum_select_fusion.kv), channel_id=1, source_target_pairs={{0,384},{16,400},{32,416},{48,432},{64,448},{80,464},{96,480},{112... | collective-permute-start | bytes 589832 | tf_op jit(solution)/shard_map/ppermute | solution.py:38
  62.4 2.5 %collective-permute-start.5 = (bf16[2,384,128]{2,1,0:T(8,128)(2,1)S(1)}, bf16[2,384,128]{2,1,0:T(8,128)(2,1)S(1)}, u32[]{:S(2)}, u32[]{:S(2)}) collective-permute-start(bf16[2,384,128]{2,1,0:T(8,128)(2,1)S(1)} %maximum_select_fusion.kv), channel_id=1, source_target_pairs={{0,192},{16,208},{32,224},{48,240},{64,256},{80,272},{96,288},{112... | collective-permute-start | bytes 589832 | tf_op jit(solution)/shard_map/ppermute | solution.py:38
  64.9 0.0 collective-permute-done.2
  64.9 0.0 collective-permute-done.1
  65.0 0.0 copy-start.1
  65.0 0.0 copy-start.4
  65.0 0.5 slice.64
  65.5 0.6 slice.65
  67.4 0.0 collective-permute-done.3.far1
  67.5 0.5 slice.66
  68.6 0.8 collective-permute-done.4.far2
  69.4 0.5 slice.67
  70.6 1.3 collective-permute-done.5.far3
  72.0 0.5 slice.68
  73.1 0.0 all-to-all-done.own
  73.2 7.1 %collective-permute-start.6 = (bf16[24,88,128]{2,1,0:T(8,128)(2,1)S(1)}, bf16[24,88,128]{2,1,0:T(8,128)(2,1)S(1)}, u32[]{:S(2)}, u32[]{:S(2)}) collective-permute-start(bf16[24,88,128]{2,1,0:T(8,128)(2,1)S(1)} %broadcast_select_fusion), channel_id=1, source_target_pairs={{0,16},{16,0},{32,48},{48,32},{64,80},{80,64},{96,112},{112,96},{1... | collective-permute-start | bytes 1622024 | tf_op jit(solution)/shard_map/ppermute | solution.py:53
  80.3 0.1 add_select_fusion
  80.4 0.1 reshape.18
  80.5 0.1 concatenate.9.meta
  80.6 1.2 collective-permute-done.6.other
  81.9 2.3 %weight_rows.1.w = bf16[16,128,256]{2,1,0:T(8,128)(2,1)S(1)} custom-call(s32[13]{0:T(128)S(1)} %concatenate.9.meta, bf16[24,88,128]{2,1,0:T(8,128)(2,1)S(1)} %all-to-all-done.own, bf16[24,88,128]{2,1,0:T(8,128)(2,1)S(1)} %collective-permute-done.6.other), custom_call_target="tpu_custom_call" | custom-call | tf_op jit(solution)/shard_map/weight_rows/pallas_call | solution.py:213
  84.2 0.0 copy-start.11
  84.2 0.5 copy-done.11
  84.7 0.8 copy-done.2
  85.6 0.8 copy-done.5
  86.4 0.9 copy-done.7
  87.3 0.7 copy-done.12
  88.0 1.9 %attention_forward.1 = (f32[3,128,768]{2,1,0:T(8,128)S(1)}, bf16[384,128]{1,0:T(8,128)(2,1)S(1)}) custom-call(s32[13]{0:T(128)S(1)} %copy-done.12, bf16[16,128,256]{2,1,0:T(8,128)(2,1)S(1)} %weight_rows.1.w, bf16[384,128]{1,0:T(8,128)(2,1)S(1)} %copy-done.7, bf16[2,384,128]{2,1,0:T(8,128)(2,1)S(1)} %maximum_select_fusion.kv, ...), custom_call_target="tpu_custom_call" | custom-call | tf_op jit(solution)/shard_map/attention_forward/pallas_call | solution.py:223
  89.9 0.0 all-gather.2.cloned.1.call-done.pieces
  89.9 1.9 %copy-done = bf16[6144,256]{1,0:T(8,128)(2,1)S(1)} copy-done((bf16[6144,256]{1,0:T(8,128)(2,1)S(1)}, bf16[6144,256]{1,0:T(8,128)(2,1)}, u32[]{:S(2)}) %copy-start) | copy-done | bytes 3145752
  91.8 2.9 %cotangent_products.1 = (f32[24,88,128]{2,1,0:T(8,128)S(1)}, f32[24,88,128]{2,1,0:T(8,128)S(1)}, bf16[384,128]{1,0:T(8,128)(2,1)S(1)}, bf16[384,128]{1,0:T(8,128)(2,1)S(1)}) custom-call(bf16[16,128,256]{2,1,0:T(8,128)(2,1)S(1)} %weight_rows.1.w, bf16[384,128]{1,0:T(8,128)(2,1)S(1)} %get-tuple-element.17.att, bf16[6144,256]{1,0:T(8,128)(2,1)S(1)} %copy-done), custom_call_target="tpu_custom_call" | custom-call | tf_op jit(solution)/shard_map/cotangent_products/pallas_call | solution.py:236
  94.8 3.0 %collective-permute-start.12 = (f32[24,88,128]{2,1,0:T(8,128)S(1)}, f32[24,88,128]{2,1,0:T(8,128)S(1)}, u32[]{:S(2)}, u32[]{:S(2)}) collective-permute-start(f32[24,88,128]{2,1,0:T(8,128)S(1)} %get-tuple-element.27), channel_id=1, source_target_pairs={{0,16},{16,0},{32,48},{48,32},{64,80},{80,64},{96,112},{112,96},{1... | collective-permute-start | bytes 3244040 | tf_op jit(solution)/shard_map/ppermute | solution.py:53
  97.8 2.3 %attention_backward.1 = (f32[384,128]{1,0:T(8,128)}, f32[2,384,128]{2,1,0:T(8,128)S(1)}, bf16[2,256,128]{2,1,0:T(8,128)(2,1)S(1)}, bf16[3,2,384,128]{3,2,1,0:T(8,128)(2,1)S(1)}) custom-call(s32[13]{0:T(128)S(1)} %copy-done.13, bf16[384,128]{1,0:T(8,128)(2,1)S(1)} %copy-done.8, bf16[2,384,128]{2,1,0:T(8,128)(2,1)S(1)} %maximum_select_fusion.kv, ...), custom_call_target="tpu_custom_call" | custom-call | tf_op jit(solution)/shard_map/attention_backward/pallas_call | solution.py:249
  100.2 0.7 copy-done.9
  100.8 0.0 collective-permute-done.12.other
  100.8 0.9 pair_sum.1
  101.7 11.0 %all-to-all-start.1 = ((bf16[24,88,128]{2,1,0:T(8,128)(2,1)}), bf16[24,88,128]{2,1,0:T(8,128)(2,1)S(1)}, u32[]{:S(2)}, u32[]{:S(2)}) async-start(bf16[24,88,128]{2,1,0:T(8,128)(2,1)} %pair_sum.1), calls=%async_computation.1 | async-start | bytes 1081344 | tf_op jit(solution)/shard_map/all_to_all | solution.py:271
  112.7 3.7 %collective-permute-start.7 = (bf16[2,128,128]{2,1,0:T(8,128)(2,1)S(1)}, bf16[2,128,128]{2,1,0:T(8,128)(2,1)S(1)}, u32[]{:S(2)}, u32[]{:S(2)}) collective-permute-start(bf16[2,128,128]{2,1,0:T(8,128)(2,1)S(1)} %get-tuple-element.38), channel_id=1, source_target_pairs={{0,752},{16,32},{32,16},{48,64},{64,48},{80,96},{96,80},{112,128},... | collective-permute-start | bytes 196616 | tf_op jit(solution)/shard_map/ppermute | solution.py:43
  116.4 4.6 %collective-permute-start.8 = (bf16[2,384,128]{2,1,0:T(8,128)(2,1)S(1)}, bf16[2,384,128]{2,1,0:T(8,128)(2,1)S(1)}, u32[]{:S(2)}, u32[]{:S(2)}) collective-permute-start(bf16[2,384,128]{2,1,0:T(8,128)(2,1)S(1)} %get-tuple-element.34), channel_id=1, source_target_pairs={{0,384},{16,400},{32,416},{48,432},{64,448},{80,464},{96,480},{112... | collective-permute-start | bytes 589832 | tf_op jit(solution)/shard_map/ppermute | solution.py:38
  121.0 2.2 %collective-permute-start.9 = (bf16[2,384,128]{2,1,0:T(8,128)(2,1)S(1)}, bf16[2,384,128]{2,1,0:T(8,128)(2,1)S(1)}, u32[]{:S(2)}, u32[]{:S(2)}) collective-permute-start(bf16[2,384,128]{2,1,0:T(8,128)(2,1)S(1)} %get-tuple-element.33), channel_id=1, source_target_pairs={{0,192},{16,208},{32,224},{48,240},{64,256},{80,272},{96,288},{112... | collective-permute-start | bytes 589832 | tf_op jit(solution)/shard_map/ppermute | solution.py:38
  123.3 4.3 %collective-permute-start.10 = (bf16[2,384,128]{2,1,0:T(8,128)(2,1)S(1)}, bf16[2,384,128]{2,1,0:T(8,128)(2,1)S(1)}, u32[]{:S(2)}, u32[]{:S(2)}) collective-permute-start(bf16[2,384,128]{2,1,0:T(8,128)(2,1)S(1)} %get-tuple-element.32), channel_id=1, source_target_pairs={{0,576},{16,592},{32,608},{48,624},{64,640},{80,656},{96,672},{112... | collective-permute-start | bytes 589832 | tf_op jit(solution)/shard_map/ppermute | solution.py:38
  127.6 7.5 %collective-permute-start.11 = (bf16[2,128,128]{2,1,0:T(8,128)(2,1)S(1)}, bf16[2,128,128]{2,1,0:T(8,128)(2,1)S(1)}, u32[]{:S(2)}, u32[]{:S(2)}) collective-permute-start(bf16[2,128,128]{2,1,0:T(8,128)(2,1)S(1)} %get-tuple-element.37), channel_id=1, source_target_pairs={{0,16},{16,0},{32,48},{48,32},{64,80},{80,64},{96,112},{112,96},{1... | collective-permute-start | bytes 196616 | tf_op jit(solution)/shard_map/ppermute | solution.py:53
  135.1 0.0 collective-permute-done.7
  135.1 0.8 collective-permute-done.11.inner
  135.9 0.0 collective-permute-done.8.far1
  135.9 0.0 collective-permute-done.9.far2
  135.9 0.0 collective-permute-done.10.far3
  135.9 0.8 grad_sum.1
  136.8 0.0 all-to-all-done.1.parts
  136.8 0.1 chunk_sum.1
  136.9 0.7 copy.10
  (33 shorter events, 0.2 us)
Async XLA Ops:
  7.2 24.2 %copy-start.16 = (bf16[1,86,128]{2,1,0:T(8,128)(2,1)S(1)}, bf16[1,86,128]{2,1,0:T(8,128)(2,1)}, u32[]{:S(2)}) copy-start(bf16[1,86,128]{2,1,0:T(8,128)(2,1)} %param.10) | copy-start | bytes 66052
  7.2 82.7 %all-gather.2.cloned.1.call-start = ((), (), s32[]{:S(2)}) async-start(), calls=%async_computation.2 | async-start | bytes 3538944 | tf_op jit(solution)/shard_map/all_gather | solution.py:197
  7.2 22.4 %collective-permute-start = (bf16[384,256]{1,0:T(8,128)(2,1)}, bf16[384,256]{1,0:T(8,128)(2,1)S(1)}, u32[]{:S(2)}, u32[]{:S(2)}) collective-permute-start(bf16[384,256]{1,0:T(8,128)(2,1)} %param.9), channel_id=1, source_target_pairs={{0,1},{1,0},{2,3},{3,2},{4,5},{5,4},{6,7},{7,6},{8,9},{9,8},{10,11... | collective-permute-start | bytes 589832 | tf_op jit(solution)/shard_map/ppermute | solution.py:57
  31.4 17.9 %copy-start.14 = (bf16[384,128]{1,0:T(8,128)(2,1)S(1)}, bf16[384,128]{1,0:T(8,128)(2,1)}, u32[]{:S(2)}) copy-start(bf16[384,128]{1,0:T(8,128)(2,1)} %param.8) | copy-start | bytes 294916
  31.4 17.9 %copy-start.15 = (bf16[384,128]{1,0:T(8,128)(2,1)S(1)}, bf16[384,128]{1,0:T(8,128)(2,1)}, u32[]{:S(2)}) copy-start(bf16[384,128]{1,0:T(8,128)(2,1)} %param.7) | copy-start | bytes 294916
  32.3 40.8 %all-to-all-start = ((bf16[24,88,128]{2,1,0:T(8,128)(2,1)}), bf16[24,88,128]{2,1,0:T(8,128)(2,1)S(1)}, u32[]{:S(2)}, u32[]{:S(2)}) async-start(bf16[24,88,128]{2,1,0:T(8,128)(2,1)} %broadcast_in_dim.16), calls=%async_computation | async-start | bytes 1081344 | tf_op jit(solution)/shard_map/all_to_all | solution.py:202
  48.1 32.3 %copy-start.17 = (s32[3,6]{1,0:T(4,128)S(1)}, s32[3,6]{1,0:T(4,128)}, u32[]{:S(2)}) copy-start(s32[3,6]{1,0:T(4,128)} %param.11) | copy-start | bytes 220
  49.3 15.6 %collective-permute-start.2 = (bf16[2,128,128]{2,1,0:T(8,128)(2,1)S(1)}, bf16[2,128,128]{2,1,0:T(8,128)(2,1)S(1)}, u32[]{:S(2)}, u32[]{:S(2)}) collective-permute-start(bf16[2,128,128]{2,1,0:T(8,128)(2,1)S(1)} %get-tuple-element.35), channel_id=1, source_target_pairs={{0,16},{16,0},{32,48},{48,32},{64,80},{80,64},{96,112},{112,96},{1... | collective-permute-start | bytes 196616 | tf_op jit(solution)/shard_map/ppermute | solution.py:53
  52.2 12.7 %collective-permute-start.1 = (bf16[2,128,128]{2,1,0:T(8,128)(2,1)S(1)}, bf16[2,128,128]{2,1,0:T(8,128)(2,1)S(1)}, u32[]{:S(2)}, u32[]{:S(2)}) collective-permute-start(bf16[2,128,128]{2,1,0:T(8,128)(2,1)S(1)} %get-tuple-element.36), channel_id=1, source_target_pairs={{0,752},{16,32},{32,16},{48,64},{64,48},{80,96},{96,80},{112,128},... | collective-permute-start | bytes 196616 | tf_op jit(solution)/shard_map/ppermute | solution.py:43
  55.6 11.8 %collective-permute-start.3 = (bf16[2,384,128]{2,1,0:T(8,128)(2,1)S(1)}, bf16[2,384,128]{2,1,0:T(8,128)(2,1)S(1)}, u32[]{:S(2)}, u32[]{:S(2)}) collective-permute-start(bf16[2,384,128]{2,1,0:T(8,128)(2,1)S(1)} %maximum_select_fusion.kv), channel_id=1, source_target_pairs={{0,576},{16,592},{32,608},{48,624},{64,640},{80,656},{96,672},{112... | collective-permute-start | bytes 589832 | tf_op jit(solution)/shard_map/ppermute | solution.py:38
  59.9 9.5 %collective-permute-start.4 = (bf16[2,384,128]{2,1,0:T(8,128)(2,1)S(1)}, bf16[2,384,128]{2,1,0:T(8,128)(2,1)S(1)}, u32[]{:S(2)}, u32[]{:S(2)}) collective-permute-start(bf16[2,384,128]{2,1,0:T(8,128)(2,1)S(1)} %maximum_select_fusion.kv), channel_id=1, source_target_pairs={{0,384},{16,400},{32,416},{48,432},{64,448},{80,464},{96,480},{112... | collective-permute-start | bytes 589832 | tf_op jit(solution)/shard_map/ppermute | solution.py:38
  62.4 9.5 %collective-permute-start.5 = (bf16[2,384,128]{2,1,0:T(8,128)(2,1)S(1)}, bf16[2,384,128]{2,1,0:T(8,128)(2,1)S(1)}, u32[]{:S(2)}, u32[]{:S(2)}) collective-permute-start(bf16[2,384,128]{2,1,0:T(8,128)(2,1)S(1)} %maximum_select_fusion.kv), channel_id=1, source_target_pairs={{0,192},{16,208},{32,224},{48,240},{64,256},{80,272},{96,288},{112... | collective-permute-start | bytes 589832 | tf_op jit(solution)/shard_map/ppermute | solution.py:38
  65.0 16.9 %copy-start.1 = (bf16[2,128,128]{2,1,0:T(8,128)(2,1)}, bf16[2,128,128]{2,1,0:T(8,128)(2,1)S(1)}, u32[]{:S(2)}) copy-start(bf16[2,128,128]{2,1,0:T(8,128)(2,1)S(1)} %get-tuple-element.39.nxt) | copy-start | bytes 196612
  65.0 16.9 %copy-start.4 = (bf16[2,128,128]{2,1,0:T(8,128)(2,1)}, bf16[2,128,128]{2,1,0:T(8,128)(2,1)S(1)}, u32[]{:S(2)}) copy-start(bf16[2,128,128]{2,1,0:T(8,128)(2,1)S(1)} %get-tuple-element.40.prev) | copy-start | bytes 196612
  73.2 8.7 %collective-permute-start.6 = (bf16[24,88,128]{2,1,0:T(8,128)(2,1)S(1)}, bf16[24,88,128]{2,1,0:T(8,128)(2,1)S(1)}, u32[]{:S(2)}, u32[]{:S(2)}) collective-permute-start(bf16[24,88,128]{2,1,0:T(8,128)(2,1)S(1)} %broadcast_select_fusion), channel_id=1, source_target_pairs={{0,16},{16,0},{32,48},{48,32},{64,80},{80,64},{96,112},{112,96},{1... | collective-permute-start | bytes 1622024 | tf_op jit(solution)/shard_map/ppermute | solution.py:53
  84.2 0.5 copy-start.11
  84.7 0.8 copy-start.2
  85.6 0.8 copy-start.5
  86.4 0.9 copy-start.7
  87.3 0.7 copy-start.12
  89.9 1.9 %copy-start = (bf16[6144,256]{1,0:T(8,128)(2,1)S(1)}, bf16[6144,256]{1,0:T(8,128)(2,1)}, u32[]{:S(2)}) copy-start(bf16[6144,256]{1,0:T(8,128)(2,1)} %all-gather.2.cloned.1.call-done.pieces) | copy-start | bytes 9437188
  91.8 6.0 %copy-start.3 = (bf16[2,128,128]{2,1,0:T(8,128)(2,1)S(1)}, bf16[2,128,128]{2,1,0:T(8,128)(2,1)}, u32[]{:S(2)}) copy-start(bf16[2,128,128]{2,1,0:T(8,128)(2,1)} %copy-done.1) | copy-start | bytes 196612
  91.8 6.0 %copy-start.6 = (bf16[2,128,128]{2,1,0:T(8,128)(2,1)S(1)}, bf16[2,128,128]{2,1,0:T(8,128)(2,1)}, u32[]{:S(2)}) copy-start(bf16[2,128,128]{2,1,0:T(8,128)(2,1)} %copy-done.4) | copy-start | bytes 196612
  91.8 6.0 %copy-start.8 = (bf16[384,128]{1,0:T(8,128)(2,1)S(1)}, bf16[384,128]{1,0:T(8,128)(2,1)}, u32[]{:S(2)}) copy-start(bf16[384,128]{1,0:T(8,128)(2,1)} %q.3) | copy-start | bytes 294916
  91.8 6.0 %copy-start.13 = (s32[13]{0:T(128)S(1)}, s32[13]{0:T(128)}, u32[]{:S(2)}) copy-start(s32[13]{0:T(128)} %copy-done.11) | copy-start | bytes 160
  94.8 6.1 %collective-permute-start.12 = (f32[24,88,128]{2,1,0:T(8,128)S(1)}, f32[24,88,128]{2,1,0:T(8,128)S(1)}, u32[]{:S(2)}, u32[]{:S(2)}) collective-permute-start(f32[24,88,128]{2,1,0:T(8,128)S(1)} %get-tuple-element.27), channel_id=1, source_target_pairs={{0,16},{16,0},{32,48},{48,32},{64,80},{80,64},{96,112},{112,96},{1... | collective-permute-start | bytes 3244040 | tf_op jit(solution)/shard_map/ppermute | solution.py:53
  100.2 0.7 copy-start.9
  101.7 11.0 %copy-start.10 = (bf16[2,256,128]{2,1,0:T(8,128)(2,1)S(1)}, bf16[2,256,128]{2,1,0:T(8,128)(2,1)}, u32[]{:S(2)}) copy-start(bf16[2,256,128]{2,1,0:T(8,128)(2,1)} %copy-done.9) | copy-start | bytes 393220
  101.7 35.1 %all-to-all-start.1 = ((bf16[24,88,128]{2,1,0:T(8,128)(2,1)}), bf16[24,88,128]{2,1,0:T(8,128)(2,1)S(1)}, u32[]{:S(2)}, u32[]{:S(2)}) async-start(bf16[24,88,128]{2,1,0:T(8,128)(2,1)} %pair_sum.1), calls=%async_computation.1 | async-start | bytes 1081344 | tf_op jit(solution)/shard_map/all_to_all | solution.py:271
  112.7 22.3 %collective-permute-start.7 = (bf16[2,128,128]{2,1,0:T(8,128)(2,1)S(1)}, bf16[2,128,128]{2,1,0:T(8,128)(2,1)S(1)}, u32[]{:S(2)}, u32[]{:S(2)}) collective-permute-start(bf16[2,128,128]{2,1,0:T(8,128)(2,1)S(1)} %get-tuple-element.38), channel_id=1, source_target_pairs={{0,752},{16,32},{32,16},{48,64},{64,48},{80,96},{96,80},{112,128},... | collective-permute-start | bytes 196616 | tf_op jit(solution)/shard_map/ppermute | solution.py:43
  116.4 19.5 %collective-permute-start.8 = (bf16[2,384,128]{2,1,0:T(8,128)(2,1)S(1)}, bf16[2,384,128]{2,1,0:T(8,128)(2,1)S(1)}, u32[]{:S(2)}, u32[]{:S(2)}) collective-permute-start(bf16[2,384,128]{2,1,0:T(8,128)(2,1)S(1)} %get-tuple-element.34), channel_id=1, source_target_pairs={{0,384},{16,400},{32,416},{48,432},{64,448},{80,464},{96,480},{112... | collective-permute-start | bytes 589832 | tf_op jit(solution)/shard_map/ppermute | solution.py:38
  121.0 14.9 %collective-permute-start.9 = (bf16[2,384,128]{2,1,0:T(8,128)(2,1)S(1)}, bf16[2,384,128]{2,1,0:T(8,128)(2,1)S(1)}, u32[]{:S(2)}, u32[]{:S(2)}) collective-permute-start(bf16[2,384,128]{2,1,0:T(8,128)(2,1)S(1)} %get-tuple-element.33), channel_id=1, source_target_pairs={{0,192},{16,208},{32,224},{48,240},{64,256},{80,272},{96,288},{112... | collective-permute-start | bytes 589832 | tf_op jit(solution)/shard_map/ppermute | solution.py:38
  123.3 12.7 %collective-permute-start.10 = (bf16[2,384,128]{2,1,0:T(8,128)(2,1)S(1)}, bf16[2,384,128]{2,1,0:T(8,128)(2,1)S(1)}, u32[]{:S(2)}, u32[]{:S(2)}) collective-permute-start(bf16[2,384,128]{2,1,0:T(8,128)(2,1)S(1)} %get-tuple-element.32), channel_id=1, source_target_pairs={{0,576},{16,592},{32,608},{48,624},{64,640},{80,656},{96,672},{112... | collective-permute-start | bytes 589832 | tf_op jit(solution)/shard_map/ppermute | solution.py:38
  127.6 8.4 %collective-permute-start.11 = (bf16[2,128,128]{2,1,0:T(8,128)(2,1)S(1)}, bf16[2,128,128]{2,1,0:T(8,128)(2,1)S(1)}, u32[]{:S(2)}, u32[]{:S(2)}) collective-permute-start(bf16[2,128,128]{2,1,0:T(8,128)(2,1)S(1)} %get-tuple-element.37), channel_id=1, source_target_pairs={{0,16},{16,0},{32,48},{48,32},{64,80},{80,64},{96,112},{112,96},{1... | collective-permute-start | bytes 196616 | tf_op jit(solution)/shard_map/ppermute | solution.py:53
Sparse Core Ops, SparseCore 0:
  31.5 58.1 all-gather.1

commit v10 on v9

--- a/solution.py
+++ b/solution.py
@@ -125,11 +125,11 @@
 
 def backward_kernel(
     meta, q, kv, prev, nxt, far1, far2, far3, probs, att, out_grad,
-    dq, dkv, band, dfar, acc,
+    dq, band, dkv,
 ):
     far = (far1, far2, far3)
     even = lax.axis_index("ctx") % 2 == 0
-    acc[...] = jnp.zeros(acc.shape, F32)
+    x = lax.axis_index("ctx") // (2 * NZ)
     dkv[...] = jnp.zeros(dkv.shape, F32)
     scale = DH**-0.5
     to_prev = []
@@ -145,11 +145,11 @@
         parts = (dot(ds, q[rows], 0, 0) * scale, dot(p.astype(BF16), grad, 0, 0))
         for which in range(2):
             part = parts[which]
-            dkv[which, rows] += part[:BLK]
+            dkv[x, which, rows] += part[:BLK]
             if j == 0:
                 to_prev.append(part[BLK : 2 * BLK])
             else:
-                dkv[which, (j - 1) * BLK : j * BLK] += part[BLK : 2 * BLK]
+                dkv[x, which, (j - 1) * BLK : j * BLK] += part[BLK : 2 * BLK]
             if j == 2:
                 to_next = part[2 * BLK : 3 * BLK]
                 inner = jnp.where(even, to_next, to_prev[which])
@@ -157,11 +157,10 @@
                 band[which, :BLK] = outer.astype(BF16)
                 band[which, BLK:] = inner.astype(BF16)
             else:
-                dkv[which, (j + 1) * BLK : (j + 2) * BLK] += part[2 * BLK : 3 * BLK]
+                dkv[x, which, (j + 1) * BLK : (j + 2) * BLK] += part[2 * BLK : 3 * BLK]
             for k in range(3):
                 row = pl.multiple_of(meta[3 * j + k] * BLK, BLK)
-                acc[k, which, pl.ds(row, BLK)] += part[(3 + k) * BLK : (4 + k) * BLK]
-    dfar[...] = acc[...].astype(BF16)
+                dkv[(x + k + 1) % NX, which, pl.ds(row, BLK)] += part[(3 + k) * BLK : (4 + k) * BLK]
 
 
 def pair_sum_kernel(keep, other, dkv, out):
@@ -169,18 +168,18 @@
     out[...] = (keep[...] + other[...]).astype(BF16)
 
 
-def chunk_sum_kernel(parts, out):
+def chunk_sum_kernel(parts, dk, out):
+    del dk
     total = parts[0].astype(F32)
     for i in range(1, CHIPS):
         total = total + parts[i].astype(F32)
     out[0] = total[:SHARD]
 
 
-def grad_sum_kernel(dkv, prev, nxt, far1, far2, far3, inner, dk, dv):
+def grad_sum_kernel(total, prev, nxt, inner, dk, dv):
     even = lax.axis_index("ctx") % 2 == 0
     for which, out in ((0, dk), (1, dv)):
-        parts = [far[which].astype(F32) for far in (far1, far2, far3)]
-        out[...] = dkv[which] + parts[0] + parts[1] + parts[2]
+        out[...] = total[which]
         near = inner[which].astype(F32)
         out[:BLK] += prev[which].astype(F32) + jnp.where(even, 0.0, near)
         out[2 * BLK :] += nxt[which].astype(F32) + jnp.where(even, near, 0.0)
@@ -246,17 +245,15 @@
         name="cotangent_products",
     )(weight, att, pieces)
     two = (2, 384, DH)
-    dq, dkv, band, dfar = pl.pallas_call(
+    dq, band, dkv = pl.pallas_call(
         backward_kernel,
         out_shape=(
             jax.ShapeDtypeStruct((384, DH), F32),
-            jax.ShapeDtypeStruct(two, F32),
             jax.ShapeDtypeStruct((2, 2 * BLK, DH), BF16),
-            jax.ShapeDtypeStruct((3,) + two, BF16),
+            jax.ShapeDtypeStruct((NX,) + two, F32),
         ),
         in_specs=[SMEM] + [VMEM] * 10,
-        out_specs=(VMEM,) * 4,
-        scratch_shapes=[pltpu.VMEM((3,) + two, F32)],
+        out_specs=(VMEM,) * 3,
         compiler_params=PARAMS,
         name="attention_backward",
     )(meta, queries, kv, prev, nxt, *far, probs, att_here, out_grad)
@@ -271,13 +268,10 @@
     spread = lax.all_to_all(
         pair_sum, "ctx", 0, 0, tiled=True, axis_index_groups=SAME_CORE
     )
-    weight_grad = pl.pallas_call(
-        chunk_sum_kernel,
-        out_shape=jax.ShapeDtypeStruct((1, SHARD, 128), F32),
-        compiler_params=PARAMS,
-        name="chunk_sum",
-    )(spread)
-    far_back = [x_shift(dfar[k], k + 1) for k in range(3)]
+    total = lax.psum_scatter(
+        dkv.reshape(NX * 768, DH), "ctx", scatter_dimension=0, tiled=True,
+        axis_index_groups=X_GROUPS,
+    ).reshape(two)
     from_inner = core_swap(band[:, BLK:])
     from_outer = outer_swap(band[:, :BLK])
     zeros = jnp.zeros_like(from_outer)
@@ -289,7 +283,15 @@
         out_shape=(grad, grad),
         compiler_params=PARAMS,
         name="grad_sum",
-    )(dkv, from_prev, from_next, far_back[1], far_back[0], far_back[2], from_inner)
+    )(total, from_prev, from_next, from_inner)
+    weight_grad = pl.pallas_call(
+        chunk_sum_kernel,
+        out_shape=jax.ShapeDtypeStruct((1, SHARD, 128), F32),
+        in_specs=[VMEM, ANY],
+        out_specs=VMEM,
+        compiler_params=PARAMS,
+        name="chunk_sum",
+    )(spread, dk)
     return dq, dk, dv, weight_grad
 
 

time: 145 us -> 149 us (1.028)
  waiting for transfers between devices: 11.1 us -> 22.8 us
  starting transfers between devices: 90.4 us -> 80.6 us
    ppermute x6 -> x3, starting transfers between devices: 20.4 us -> 9.28 us  [x_shift(): return lax.ppermute(value, 'ctx', pairs)]
    reduce_scatter x0 -> x1, waiting for transfers between devices: none -> 9.15 us  [on_device(): lax.psum_scatter(dkv.reshape(NX * 768, DH), 'ctx', scatter_dimension=0, t...]
    ppermute x4, waiting for transfers between devices: 2.1 us -> 4.62 us  [core_swap(): return lax.ppermute(value, 'ctx', [(s, s ^ 1) for s in range(N_CTX)])]
    unnamed x37 -> x39, local copies, waits for them, and re-layouts: 6.98 us -> 8.25 us
  transfers between devices with their start and end apart: 16 -> 14, of which waited for: 5 -> 7; matrix products, arithmetic and copies ran while one was open for 3% -> 3% of each run, Pallas kernels for 5% -> 4%
where the time goes in v10:
time: 149 us; the launch traced here: 148 us
  starting transfers between devices  80.6 us (54%)
  waiting for transfers between devices  22.8 us (15%)
  between operations  18.4 us (12%)
  local copies, waits for them, and re-layouts  12.4 us (8%)
  Pallas kernels  11.8 us (8%)
  other arithmetic  1.92 us (1%)
    ppermute x4, starting transfers between devices, core_swap(): return lax.ppermute(value, 'ctx', [(s, s ^ 1) for s in range(N_CTX)])  21.6 us
    all_to_all x1, starting transfers between devices, on_device(): lax.all_to_all(jnp.broadcast_to(w_pad[None], (CHIPS, SHARD_PAD, 128)), 'c...  15.7 us
    ppermute x1, starting transfers between devices, twin_swap(): return lax.ppermute(value, 'tp', [(s, s ^ 1) for s in range(N_TP)])  15.7 us
    all_to_all x1, starting transfers between devices, on_device(): lax.all_to_all(pair_sum, 'ctx', 0, 0, tiled=True, axis_index_groups=SAME_...  10.8 us
    ppermute x3, starting transfers between devices, x_shift(): return lax.ppermute(value, 'ctx', pairs)  9.28 us
    reduce_scatter x1, waiting for transfers between devices, on_device(): lax.psum_scatter(dkv.reshape(NX * 768, DH), 'ctx', scatter_dimension=0, t...  9.15 us
    unnamed x39, local copies, waits for them, and re-layouts  8.25 us
    ppermute x2, starting transfers between devices, outer_swap(): return lax.ppermute(value, 'ctx', pairs)  7.38 us
  transfers between devices with their start and end apart: 14, of which 7 were waited for; matrix products, arithmetic and copies ran while one was open for 3% of the time, Pallas kernels for 4%

profile of v10, /device:TPU:1, one launch (start us, length us, event | category | flops | bytes accessed | tf_op | source)
XLA Modules:
  0.0 148.0 jit_solution(11154178030844302397)
XLA Ops:
  7.2 0.0 all-gather.2.cloned.1.call-start
  7.2 15.7 %collective-permute-start = (bf16[384,256]{1,0:T(8,128)(2,1)}, bf16[384,256]{1,0:T(8,128)(2,1)S(1)}, u32[]{:S(2)}, u32[]{:S(2)}) collective-permute-start(bf16[384,256]{1,0:T(8,128)(2,1)} %param.9), channel_id=1, source_target_pairs={{0,1},{1,0},{2,3},{3,2},{4,5},{5,4},{6,7},{7,6},{8,9},{9,8},{10,11... | collective-permute-start | bytes 589832 | tf_op jit(solution)/shard_map/ppermute | solution.py:57
  22.9 6.7 %collective-permute-done = bf16[384,256]{1,0:T(8,128)(2,1)S(1)} collective-permute-done((bf16[384,256]{1,0:T(8,128)(2,1)}, bf16[384,256]{1,0:T(8,128)(2,1)S(1)}, u32[]{:S(2)}, u32[]{:S(2)}) %collective-permute-start) | collective-permute-done | bytes 196640 | tf_op jit(solution)/shard_map/ppermute | solution.py:57
  29.7 1.7 %pad_maximum_fusion = bf16[768,256]{1,0:T(8,128)(2,1)} fusion(bf16[384,256]{1,0:T(8,128)(2,1)S(1)} %collective-permute-done, bf16[384,256]{1,0:T(8,128)(2,1)} %param.9), kind=kLoop, calls=%fused_computation.1 | loop fusion | flops 786432 | bytes 786432 | tf_op jit(solution)/shard_map/concatenate | solution.py:197
  31.4 0.0 all-gather.2.cloned.1.call-update
  31.4 0.9 broadcast_in_dim.16
  32.3 15.7 %all-to-all-start = ((bf16[24,88,128]{2,1,0:T(8,128)(2,1)}), bf16[24,88,128]{2,1,0:T(8,128)(2,1)S(1)}, u32[]{:S(2)}, u32[]{:S(2)}) async-start(bf16[24,88,128]{2,1,0:T(8,128)(2,1)} %broadcast_in_dim.16), calls=%async_computation | async-start | bytes 1081344 | tf_op jit(solution)/shard_map/all_to_all | solution.py:201
  48.1 0.0 copy-start.18
  48.1 0.0 reduce-scatter.2.cloned.1.call-start
  48.1 0.5 slice.48
  49.4 2.9 %collective-permute-start.2 = (bf16[2,128,128]{2,1,0:T(8,128)(2,1)S(1)}, bf16[2,128,128]{2,1,0:T(8,128)(2,1)S(1)}, u32[]{:S(2)}, u32[]{:S(2)}) collective-permute-start(bf16[2,128,128]{2,1,0:T(8,128)(2,1)S(1)} %get-tuple-element.30), channel_id=1, source_target_pairs={{0,16},{16,0},{32,48},{48,32},{64,80},{80,64},{96,112},{112,96},{1... | collective-permute-start | bytes 196616 | tf_op jit(solution)/shard_map/ppermute | solution.py:53
  52.3 3.4 %collective-permute-start.1 = (bf16[2,128,128]{2,1,0:T(8,128)(2,1)S(1)}, bf16[2,128,128]{2,1,0:T(8,128)(2,1)S(1)}, u32[]{:S(2)}, u32[]{:S(2)}) collective-permute-start(bf16[2,128,128]{2,1,0:T(8,128)(2,1)S(1)} %get-tuple-element.31), channel_id=1, source_target_pairs={{0,752},{16,32},{32,16},{48,64},{64,48},{80,96},{96,80},{112,128},... | collective-permute-start | bytes 196616 | tf_op jit(solution)/shard_map/ppermute | solution.py:43
  55.7 4.3 %collective-permute-start.3 = (bf16[2,384,128]{2,1,0:T(8,128)(2,1)S(1)}, bf16[2,384,128]{2,1,0:T(8,128)(2,1)S(1)}, u32[]{:S(2)}, u32[]{:S(2)}) collective-permute-start(bf16[2,384,128]{2,1,0:T(8,128)(2,1)S(1)} %maximum_select_fusion.kv), channel_id=1, source_target_pairs={{0,576},{16,592},{32,608},{48,624},{64,640},{80,656},{96,672},{112... | collective-permute-start | bytes 589832 | tf_op jit(solution)/shard_map/ppermute | solution.py:38
  60.0 2.5 %collective-permute-start.4 = (bf16[2,384,128]{2,1,0:T(8,128)(2,1)S(1)}, bf16[2,384,128]{2,1,0:T(8,128)(2,1)S(1)}, u32[]{:S(2)}, u32[]{:S(2)}) collective-permute-start(bf16[2,384,128]{2,1,0:T(8,128)(2,1)S(1)} %maximum_select_fusion.kv), channel_id=1, source_target_pairs={{0,384},{16,400},{32,416},{48,432},{64,448},{80,464},{96,480},{112... | collective-permute-start | bytes 589832 | tf_op jit(solution)/shard_map/ppermute | solution.py:38
  62.5 2.5 %collective-permute-start.5 = (bf16[2,384,128]{2,1,0:T(8,128)(2,1)S(1)}, bf16[2,384,128]{2,1,0:T(8,128)(2,1)S(1)}, u32[]{:S(2)}, u32[]{:S(2)}) collective-permute-start(bf16[2,384,128]{2,1,0:T(8,128)(2,1)S(1)} %maximum_select_fusion.kv), channel_id=1, source_target_pairs={{0,192},{16,208},{32,224},{48,240},{64,256},{80,272},{96,288},{112... | collective-permute-start | bytes 589832 | tf_op jit(solution)/shard_map/ppermute | solution.py:38
  65.0 0.0 collective-permute-done.2
  65.0 0.0 collective-permute-done.1
  65.0 0.0 copy-start.3
  65.0 0.0 copy-start.6
  65.0 0.5 slice.52
  65.6 0.5 slice.53
  67.4 0.0 collective-permute-done.3.far1
  67.4 0.5 slice.54
  68.6 0.9 collective-permute-done.4.far2
  69.5 0.5 slice.55
  70.6 1.3 collective-permute-done.5.far3
  72.0 0.5 slice.56
  73.2 0.0 all-to-all-done.own
  73.2 7.1 %collective-permute-start.6 = (bf16[24,88,128]{2,1,0:T(8,128)(2,1)S(1)}, bf16[24,88,128]{2,1,0:T(8,128)(2,1)S(1)}, u32[]{:S(2)}, u32[]{:S(2)}) collective-permute-start(bf16[24,88,128]{2,1,0:T(8,128)(2,1)S(1)} %broadcast_select_fusion), channel_id=1, source_target_pairs={{0,16},{16,0},{32,48},{48,32},{64,80},{80,64},{96,112},{112,96},{1... | collective-permute-start | bytes 1622024 | tf_op jit(solution)/shard_map/ppermute | solution.py:53
  80.4 0.0 copy-done.18
  80.4 0.1 add_select_fusion
  80.5 0.1 reshape.24
  80.6 0.1 concatenate.9.meta
  80.7 1.2 collective-permute-done.6.other
  81.9 0.0 copy-done.3
  81.9 2.3 %weight_rows.1.w = bf16[16,128,256]{2,1,0:T(8,128)(2,1)S(1)} custom-call(s32[13]{0:T(128)S(1)} %concatenate.9.meta, bf16[24,88,128]{2,1,0:T(8,128)(2,1)S(1)} %all-to-all-done.own, bf16[24,88,128]{2,1,0:T(8,128)(2,1)S(1)} %collective-permute-done.6.other), custom_call_target="tpu_custom_call" | custom-call | tf_op jit(solution)/shard_map/weight_rows/pallas_call | solution.py:212
  84.3 0.0 copy-start.11
  84.3 0.5 copy-done.11
  84.8 0.8 copy-done.4
  85.6 0.8 copy-done.7
  86.5 0.9 copy-done.8
  87.4 0.7 copy-done.12
  88.0 1.9 %attention_forward.1 = (f32[3,128,768]{2,1,0:T(8,128)S(1)}, bf16[384,128]{1,0:T(8,128)(2,1)S(1)}) custom-call(s32[13]{0:T(128)S(1)} %copy-done.12, bf16[16,128,256]{2,1,0:T(8,128)(2,1)S(1)} %weight_rows.1.w, bf16[384,128]{1,0:T(8,128)(2,1)S(1)} %copy-done.8, bf16[2,384,128]{2,1,0:T(8,128)(2,1)S(1)} %maximum_select_fusion.kv, ...), custom_call_target="tpu_custom_call" | custom-call | tf_op jit(solution)/shard_map/attention_forward/pallas_call | solution.py:222
  90.0 0.0 all-gather.2.cloned.1.call-done.pieces
  90.0 1.9 %copy-done = bf16[6144,256]{1,0:T(8,128)(2,1)S(1)} copy-done((bf16[6144,256]{1,0:T(8,128)(2,1)S(1)}, bf16[6144,256]{1,0:T(8,128)(2,1)}, u32[]{:S(2)}) %copy-start) | copy-done | bytes 3145752
  91.9 2.9 %cotangent_products.1 = (f32[24,88,128]{2,1,0:T(8,128)S(1)}, f32[24,88,128]{2,1,0:T(8,128)S(1)}, bf16[384,128]{1,0:T(8,128)(2,1)S(1)}, bf16[384,128]{1,0:T(8,128)(2,1)S(1)}) custom-call(bf16[16,128,256]{2,1,0:T(8,128)(2,1)S(1)} %weight_rows.1.w, bf16[384,128]{1,0:T(8,128)(2,1)S(1)} %get-tuple-element.16.att, bf16[6144,256]{1,0:T(8,128)(2,1)S(1)} %copy-done), custom_call_target="tpu_custom_call" | custom-call | tf_op jit(solution)/shard_map/cotangent_products/pallas_call | solution.py:235
  94.8 2.9 %attention_backward.1 = (f32[384,128]{1,0:T(8,128)}, bf16[2,256,128]{2,1,0:T(8,128)(2,1)S(1)}, f32[4,2,384,128]{3,2,1,0:T(8,128)}) custom-call(s32[13]{0:T(128)S(1)} %copy-done.13, bf16[384,128]{1,0:T(8,128)(2,1)S(1)} %copy-done.8, bf16[2,384,128]{2,1,0:T(8,128)(2,1)S(1)} %maximum_select_fusion.kv, bf16[2,128,128]{2,1,0:T(8,128)(2,1)S(1)} %copy-done.7, ...), custom_call_target="tpu_custom_call" | custom-call | tf_op jit(solution)/shard_map/attention_backward/pallas_call | solution.py:248
  97.7 0.0 copy-done.14
  97.7 0.0 reduce-scatter.2.cloned.1.call-update
  97.8 3.2 %collective-permute-start.9 = (f32[24,88,128]{2,1,0:T(8,128)}, f32[24,88,128]{2,1,0:T(8,128)S(1)}, u32[]{:S(2)}, u32[]{:S(2)}) collective-permute-start(f32[24,88,128]{2,1,0:T(8,128)} %copy-done.14), channel_id=1, source_target_pairs={{0,16},{16,0},{32,48},{48,32},{64,80},{80,64},{96,112},{112,96},{1... | collective-permute-start | bytes 3244040 | tf_op jit(solution)/shard_map/ppermute | solution.py:53
  100.9 2.5 %collective-permute-done.9.other = f32[24,88,128]{2,1,0:T(8,128)S(1)} collective-permute-done((f32[24,88,128]{2,1,0:T(8,128)}, f32[24,88,128]{2,1,0:T(8,128)S(1)}, u32[]{:S(2)}, u32[]{:S(2)}) %collective-permute-start.9) | collective-permute-done | bytes 1081376 | tf_op jit(solution)/shard_map/ppermute | solution.py:53
  103.5 0.9 pair_sum.1
  104.4 10.8 %all-to-all-start.1 = ((bf16[24,88,128]{2,1,0:T(8,128)(2,1)}), bf16[24,88,128]{2,1,0:T(8,128)(2,1)S(1)}, u32[]{:S(2)}, u32[]{:S(2)}) async-start(bf16[24,88,128]{2,1,0:T(8,128)(2,1)} %pair_sum.1), calls=%async_computation.2 | async-start | bytes 1081344 | tf_op jit(solution)/shard_map/all_to_all | solution.py:268
  115.2 4.0 %collective-permute-start.7 = (bf16[2,128,128]{2,1,0:T(8,128)(2,1)S(1)}, bf16[2,128,128]{2,1,0:T(8,128)(2,1)S(1)}, u32[]{:S(2)}, u32[]{:S(2)}) collective-permute-start(bf16[2,128,128]{2,1,0:T(8,128)(2,1)S(1)} %get-tuple-element.33), channel_id=1, source_target_pairs={{0,752},{16,32},{32,16},{48,64},{64,48},{80,96},{96,80},{112,128},... | collective-permute-start | bytes 196616 | tf_op jit(solution)/shard_map/ppermute | solution.py:43
  119.2 8.4 %collective-permute-start.8 = (bf16[2,128,128]{2,1,0:T(8,128)(2,1)S(1)}, bf16[2,128,128]{2,1,0:T(8,128)(2,1)S(1)}, u32[]{:S(2)}, u32[]{:S(2)}) collective-permute-start(bf16[2,128,128]{2,1,0:T(8,128)(2,1)S(1)} %get-tuple-element.32), channel_id=1, source_target_pairs={{0,16},{16,0},{32,48},{48,32},{64,80},{80,64},{96,112},{112,96},{1... | collective-permute-start | bytes 196616 | tf_op jit(solution)/shard_map/ppermute | solution.py:53
  127.6 0.0 collective-permute-done.7
  127.7 0.8 collective-permute-done.8.inner
  128.5 9.2 %reduce-scatter.2.cloned.1.call-done = f32[768,128]{1,0:T(8,128)} async-done(((f32[3072,128]{1,0:T(8,128)}), f32[768,128]{1,0:T(8,128)}) %reduce-scatter.2.cloned.1.call-update) | async-done | bytes 393232 | tf_op jit(solution)/shard_map/reduce_scatter | solution.py:271
  137.7 1.0 copy-done.9
  138.7 0.8 grad_sum.1
  139.5 0.0 all-to-all-done.1.parts
  139.5 0.9 copy-done.10
  140.4 0.1 chunk_sum.1
  140.5 0.7 copy.10
  (31 shorter events, 0.2 us)
Async XLA Ops:
  7.2 24.3 %copy-start.17 = (bf16[1,86,128]{2,1,0:T(8,128)(2,1)S(1)}, bf16[1,86,128]{2,1,0:T(8,128)(2,1)}, u32[]{:S(2)}) copy-start(bf16[1,86,128]{2,1,0:T(8,128)(2,1)} %param.10) | copy-start | bytes 66052
  7.2 82.8 %all-gather.2.cloned.1.call-start = ((), (), s32[]{:S(2)}) async-start(), calls=%async_computation.3 | async-start | bytes 3538944 | tf_op jit(solution)/shard_map/all_gather | solution.py:196
  7.2 22.4 %collective-permute-start = (bf16[384,256]{1,0:T(8,128)(2,1)}, bf16[384,256]{1,0:T(8,128)(2,1)S(1)}, u32[]{:S(2)}, u32[]{:S(2)}) collective-permute-start(bf16[384,256]{1,0:T(8,128)(2,1)} %param.9), channel_id=1, source_target_pairs={{0,1},{1,0},{2,3},{3,2},{4,5},{5,4},{6,7},{7,6},{8,9},{9,8},{10,11... | collective-permute-start | bytes 589832 | tf_op jit(solution)/shard_map/ppermute | solution.py:57
  31.4 17.9 %copy-start.15 = (bf16[384,128]{1,0:T(8,128)(2,1)S(1)}, bf16[384,128]{1,0:T(8,128)(2,1)}, u32[]{:S(2)}) copy-start(bf16[384,128]{1,0:T(8,128)(2,1)} %param.8) | copy-start | bytes 294916
  31.4 17.9 %copy-start.16 = (bf16[384,128]{1,0:T(8,128)(2,1)S(1)}, bf16[384,128]{1,0:T(8,128)(2,1)}, u32[]{:S(2)}) copy-start(bf16[384,128]{1,0:T(8,128)(2,1)} %param.7) | copy-start | bytes 294916
  32.3 40.9 %all-to-all-start = ((bf16[24,88,128]{2,1,0:T(8,128)(2,1)}), bf16[24,88,128]{2,1,0:T(8,128)(2,1)S(1)}, u32[]{:S(2)}, u32[]{:S(2)}) async-start(bf16[24,88,128]{2,1,0:T(8,128)(2,1)} %broadcast_in_dim.16), calls=%async_computation | async-start | bytes 1081344 | tf_op jit(solution)/shard_map/all_to_all | solution.py:201
  48.1 32.3 %copy-start.18 = (s32[3,6]{1,0:T(4,128)S(1)}, s32[3,6]{1,0:T(4,128)}, u32[]{:S(2)}) copy-start(s32[3,6]{1,0:T(4,128)} %param.11) | copy-start | bytes 220
  48.1 89.6 %reduce-scatter.2.cloned.1.call-start = ((), (), s32[]{:S(2)}) async-start(), calls=%async_computation.4 | async-start | bytes 1966080 | tf_op jit(solution)/shard_map/reduce_scatter | solution.py:271
  49.4 15.6 %collective-permute-start.2 = (bf16[2,128,128]{2,1,0:T(8,128)(2,1)S(1)}, bf16[2,128,128]{2,1,0:T(8,128)(2,1)S(1)}, u32[]{:S(2)}, u32[]{:S(2)}) collective-permute-start(bf16[2,128,128]{2,1,0:T(8,128)(2,1)S(1)} %get-tuple-element.30), channel_id=1, source_target_pairs={{0,16},{16,0},{32,48},{48,32},{64,80},{80,64},{96,112},{112,96},{1... | collective-permute-start | bytes 196616 | tf_op jit(solution)/shard_map/ppermute | solution.py:53
  52.3 12.7 %collective-permute-start.1 = (bf16[2,128,128]{2,1,0:T(8,128)(2,1)S(1)}, bf16[2,128,128]{2,1,0:T(8,128)(2,1)S(1)}, u32[]{:S(2)}, u32[]{:S(2)}) collective-permute-start(bf16[2,128,128]{2,1,0:T(8,128)(2,1)S(1)} %get-tuple-element.31), channel_id=1, source_target_pairs={{0,752},{16,32},{32,16},{48,64},{64,48},{80,96},{96,80},{112,128},... | collective-permute-start | bytes 196616 | tf_op jit(solution)/shard_map/ppermute | solution.py:43
  55.7 11.7 %collective-permute-start.3 = (bf16[2,384,128]{2,1,0:T(8,128)(2,1)S(1)}, bf16[2,384,128]{2,1,0:T(8,128)(2,1)S(1)}, u32[]{:S(2)}, u32[]{:S(2)}) collective-permute-start(bf16[2,384,128]{2,1,0:T(8,128)(2,1)S(1)} %maximum_select_fusion.kv), channel_id=1, source_target_pairs={{0,576},{16,592},{32,608},{48,624},{64,640},{80,656},{96,672},{112... | collective-permute-start | bytes 589832 | tf_op jit(solution)/shard_map/ppermute | solution.py:38
  60.0 9.5 %collective-permute-start.4 = (bf16[2,384,128]{2,1,0:T(8,128)(2,1)S(1)}, bf16[2,384,128]{2,1,0:T(8,128)(2,1)S(1)}, u32[]{:S(2)}, u32[]{:S(2)}) collective-permute-start(bf16[2,384,128]{2,1,0:T(8,128)(2,1)S(1)} %maximum_select_fusion.kv), channel_id=1, source_target_pairs={{0,384},{16,400},{32,416},{48,432},{64,448},{80,464},{96,480},{112... | collective-permute-start | bytes 589832 | tf_op jit(solution)/shard_map/ppermute | solution.py:38
  62.5 9.5 %collective-permute-start.5 = (bf16[2,384,128]{2,1,0:T(8,128)(2,1)S(1)}, bf16[2,384,128]{2,1,0:T(8,128)(2,1)S(1)}, u32[]{:S(2)}, u32[]{:S(2)}) collective-permute-start(bf16[2,384,128]{2,1,0:T(8,128)(2,1)S(1)} %maximum_select_fusion.kv), channel_id=1, source_target_pairs={{0,192},{16,208},{32,224},{48,240},{64,256},{80,272},{96,288},{112... | collective-permute-start | bytes 589832 | tf_op jit(solution)/shard_map/ppermute | solution.py:38
  65.0 16.9 %copy-start.3 = (bf16[2,128,128]{2,1,0:T(8,128)(2,1)}, bf16[2,128,128]{2,1,0:T(8,128)(2,1)S(1)}, u32[]{:S(2)}) copy-start(bf16[2,128,128]{2,1,0:T(8,128)(2,1)S(1)} %get-tuple-element.34.nxt) | copy-start | bytes 196612
  65.0 16.9 %copy-start.6 = (bf16[2,128,128]{2,1,0:T(8,128)(2,1)}, bf16[2,128,128]{2,1,0:T(8,128)(2,1)S(1)}, u32[]{:S(2)}) copy-start(bf16[2,128,128]{2,1,0:T(8,128)(2,1)S(1)} %get-tuple-element.35.prev) | copy-start | bytes 196612
  73.2 8.7 %collective-permute-start.6 = (bf16[24,88,128]{2,1,0:T(8,128)(2,1)S(1)}, bf16[24,88,128]{2,1,0:T(8,128)(2,1)S(1)}, u32[]{:S(2)}, u32[]{:S(2)}) collective-permute-start(bf16[24,88,128]{2,1,0:T(8,128)(2,1)S(1)} %broadcast_select_fusion), channel_id=1, source_target_pairs={{0,16},{16,0},{32,48},{48,32},{64,80},{80,64},{96,112},{112,96},{1... | collective-permute-start | bytes 1622024 | tf_op jit(solution)/shard_map/ppermute | solution.py:53
  84.3 0.5 copy-start.11
  84.8 0.8 copy-start.4
  85.6 0.8 copy-start.7
  86.5 0.9 copy-start.8
  87.4 0.7 copy-start.12
  90.0 1.9 %copy-start = (bf16[6144,256]{1,0:T(8,128)(2,1)S(1)}, bf16[6144,256]{1,0:T(8,128)(2,1)}, u32[]{:S(2)}) copy-start(bf16[6144,256]{1,0:T(8,128)(2,1)} %all-gather.2.cloned.1.call-done.pieces) | copy-start | bytes 9437188
  91.9 2.9 %copy-start.5 = (bf16[2,128,128]{2,1,0:T(8,128)(2,1)S(1)}, bf16[2,128,128]{2,1,0:T(8,128)(2,1)}, u32[]{:S(2)}) copy-start(bf16[2,128,128]{2,1,0:T(8,128)(2,1)} %copy-done.3) | copy-start | bytes 196612
  91.9 2.9 %copy-start.13 = (s32[13]{0:T(128)S(1)}, s32[13]{0:T(128)}, u32[]{:S(2)}) copy-start(s32[13]{0:T(128)} %copy-done.11) | copy-start | bytes 160
  94.8 2.9 %copy-start.1 = (f32[24,88,128]{2,1,0:T(8,128)}, f32[24,88,128]{2,1,0:T(8,128)S(1)}, u32[]{:S(2)}) copy-start(f32[24,88,128]{2,1,0:T(8,128)S(1)} %get-tuple-element.24.keep) | copy-start | bytes 3244036
  94.8 2.9 %copy-start.14 = (f32[24,88,128]{2,1,0:T(8,128)}, f32[24,88,128]{2,1,0:T(8,128)S(1)}, u32[]{:S(2)}) copy-start(f32[24,88,128]{2,1,0:T(8,128)S(1)} %get-tuple-element.25) | copy-start | bytes 3244036
  97.7 5.7 %copy-start.2 = (f32[24,88,128]{2,1,0:T(8,128)S(1)}, f32[24,88,128]{2,1,0:T(8,128)}, u32[]{:S(2)}) copy-start(f32[24,88,128]{2,1,0:T(8,128)} %copy-done.1) | copy-start | bytes 3244036
  97.8 5.7 %collective-permute-start.9 = (f32[24,88,128]{2,1,0:T(8,128)}, f32[24,88,128]{2,1,0:T(8,128)S(1)}, u32[]{:S(2)}, u32[]{:S(2)}) collective-permute-start(f32[24,88,128]{2,1,0:T(8,128)} %copy-done.14), channel_id=1, source_target_pairs={{0,16},{16,0},{32,48},{48,32},{64,80},{80,64},{96,112},{112,96},{1... | collective-permute-start | bytes 3244040 | tf_op jit(solution)/shard_map/ppermute | solution.py:53
  104.4 35.1 %all-to-all-start.1 = ((bf16[24,88,128]{2,1,0:T(8,128)(2,1)}), bf16[24,88,128]{2,1,0:T(8,128)(2,1)S(1)}, u32[]{:S(2)}, u32[]{:S(2)}) async-start(bf16[24,88,128]{2,1,0:T(8,128)(2,1)} %pair_sum.1), calls=%async_computation.2 | async-start | bytes 1081344 | tf_op jit(solution)/shard_map/all_to_all | solution.py:268
  115.2 12.5 %collective-permute-start.7 = (bf16[2,128,128]{2,1,0:T(8,128)(2,1)S(1)}, bf16[2,128,128]{2,1,0:T(8,128)(2,1)S(1)}, u32[]{:S(2)}, u32[]{:S(2)}) collective-permute-start(bf16[2,128,128]{2,1,0:T(8,128)(2,1)S(1)} %get-tuple-element.33), channel_id=1, source_target_pairs={{0,752},{16,32},{32,16},{48,64},{64,48},{80,96},{96,80},{112,128},... | collective-permute-start | bytes 196616 | tf_op jit(solution)/shard_map/ppermute | solution.py:43
  119.2 9.3 %collective-permute-start.8 = (bf16[2,128,128]{2,1,0:T(8,128)(2,1)S(1)}, bf16[2,128,128]{2,1,0:T(8,128)(2,1)S(1)}, u32[]{:S(2)}, u32[]{:S(2)}) collective-permute-start(bf16[2,128,128]{2,1,0:T(8,128)(2,1)S(1)} %get-tuple-element.32), channel_id=1, source_target_pairs={{0,16},{16,0},{32,48},{48,32},{64,80},{80,64},{96,112},{112,96},{1... | collective-permute-start | bytes 196616 | tf_op jit(solution)/shard_map/ppermute | solution.py:53
  137.7 1.0 copy-start.9
  139.5 0.9 copy-start.10
Sparse Core Ops, SparseCore 0:
  31.5 58.2 all-gather.1
  97.9 39.7 reduce-scatter.1

commit v11 on v9

--- a/solution.py
+++ b/solution.py
@@ -26,7 +26,13 @@
 ANY = pl.BlockSpec(memory_space=pl.ANY)
 PARAMS = pltpu.CompilerParams(vmem_limit_bytes=12 * 1024 * 1024)
 
+STEPS = 4
+
 M_X, M_CORE, M_Y, M_Z = 9, 10, 11, 12
+
+
+def whole(*shape):
+    return pl.BlockSpec(shape, lambda step: (0,) * len(shape), pipeline_mode=pl.Buffered(1))
 
 
 def dot(a, b, ca, cb):
@@ -100,27 +106,37 @@
             w_out[t, :, e * 128 : (e + 1) * 128] = rows.astype(BF16)
 
 
-def cotangent_kernel(w, att, pieces, keep, give, grad, att_out, cols, flat):
+def cotangent_kernel(w, att, pieces, keep, give, grad, att_out, cols, flat, total):
+    step = pl.program_id(0)
     z = lax.axis_index("tp") % 2
     att_now = att[...]
-    att_out[...] = att_now
-    total = jnp.zeros((384, DH), F32)
-    for i in range(N_TP):
-        col = 2 * (i // 2) + (z if i % 2 == 0 else 1 - z)
+
+    @pl.when(step == 0)
+    def _():
+        att_out[...] = att_now
+        total[...] = jnp.zeros(total.shape, F32)
+
+    here = jnp.zeros((384, DH), F32)
+    for i in range(N_TP // STEPS):
+        col = 2 * (step * (NY // STEPS) + i // 2) + (z if i % 2 == 0 else 1 - z)
         cot = pieces[i * 384 : (i + 1) * 384]
         cols[col] = dot(att_now, cot, 0, 0)
-        total = total + dot(cot, w[col], 1, 1)
-    grad[...] = total.astype(BF16)
-    for t in range(N_TP):
-        for e in range(2):
-            flat[pl.ds(2 * t + e, DH, stride=32)] = cols[t, :, e * 128 : (e + 1) * 128]
-    flat[FLAT_ROWS:] = jnp.zeros((flat.shape[0] - FLAT_ROWS, 128), F32)
-    first = lax.axis_index("ctx") % 2 == 0
-    for i in range(CHIPS):
-        a = flat[2 * i * SHARD : 2 * i * SHARD + SHARD_PAD]
-        b = flat[(2 * i + 1) * SHARD : (2 * i + 1) * SHARD + SHARD_PAD]
-        keep[i] = jnp.where(first, a, b)
-        give[i] = jnp.where(first, b, a)
+        here = here + dot(cot, w[col], 1, 1)
+    total[...] += here
+
+    @pl.when(step == STEPS - 1)
+    def _():
+        grad[...] = total[...].astype(BF16)
+        for t in range(N_TP):
+            for e in range(2):
+                flat[pl.ds(2 * t + e, DH, stride=32)] = cols[t, :, e * 128 : (e + 1) * 128]
+        flat[FLAT_ROWS:] = jnp.zeros((flat.shape[0] - FLAT_ROWS, 128), F32)
+        first = lax.axis_index("ctx") % 2 == 0
+        for i in range(CHIPS):
+            a = flat[2 * i * SHARD : 2 * i * SHARD + SHARD_PAD]
+            b = flat[(2 * i + 1) * SHARD : (2 * i + 1) * SHARD + SHARD_PAD]
+            keep[i] = jnp.where(first, a, b)
+            give[i] = jnp.where(first, b, a)
 
 
 def backward_kernel(
@@ -173,7 +189,7 @@
     total = parts[0].astype(F32)
     for i in range(1, CHIPS):
         total = total + parts[i].astype(F32)
-    out[0] = total[:SHARD]
+    out[...] = total[:SHARD].reshape(SHARD, 1, 128)
 
 
 def grad_sum_kernel(dkv, prev, nxt, far1, far2, far3, inner, dk, dv):
@@ -236,13 +252,24 @@
     keep, give, out_grad, att_here = pl.pallas_call(
         cotangent_kernel,
         out_shape=(chunk, chunk) + (jax.ShapeDtypeStruct((384, DH), BF16),) * 2,
-        in_specs=[VMEM, VMEM, VMEM],
-        out_specs=(VMEM,) * 4,
+        grid=(STEPS,),
+        in_specs=[
+            whole(N_TP, DH, WCOL),
+            whole(384, DH),
+            pl.BlockSpec((N_TP * 384 // STEPS, WCOL), lambda step: (step, 0)),
+        ],
+        out_specs=(
+            whole(*chunk.shape),
+            whole(*chunk.shape),
+            whole(384, DH),
+            whole(384, DH),
+        ),
         scratch_shapes=[
             pltpu.VMEM((N_TP, DH, WCOL), F32),
             pltpu.VMEM((flat_alloc, 128), F32),
+            pltpu.VMEM((384, DH), F32),
         ],
-        compiler_params=PARAMS,
+        compiler_params=pltpu.CompilerParams(vmem_limit_bytes=50 * 1024 * 1024),
         name="cotangent_products",
     )(weight, att, pieces)
     two = (2, 384, DH)
@@ -273,10 +300,10 @@
     )
     weight_grad = pl.pallas_call(
         chunk_sum_kernel,
-        out_shape=jax.ShapeDtypeStruct((1, SHARD, 128), F32),
+        out_shape=jax.ShapeDtypeStruct((SHARD, 1, 128), F32),
         compiler_params=PARAMS,
         name="chunk_sum",
-    )(spread)
+    )(spread).transpose(1, 0, 2)
     far_back = [x_shift(dfar[k], k + 1) for k in range(3)]
     from_inner = core_swap(band[:, BLK:])
     from_outer = outer_swap(band[:, :BLK])

time: 145 us -> 147 us (1.014)
  Pallas kernels: 11.3 us -> 15.5 us
  local copies, waits for them, and re-layouts: 11.2 us -> 8.69 us
    pallas_call x1, Pallas kernels: 2.91 us -> 6.42 us  [on_device(): pl.pallas_call(cotangent_kernel, out_shape=(chunk, chunk) + (jax.ShapeDty...]
    unnamed x37 -> x34, local copies, waits for them, and re-layouts: 6.98 us -> 4.45 us
where the time goes in v11:
time: 147 us; the launch traced here: 146 us
  starting transfers between devices  90.3 us (61%)
  between operations  18.4 us (13%)
  Pallas kernels  15.5 us (11%)
  waiting for transfers between devices  11.1 us (8%)
  local copies, waits for them, and re-layouts  8.69 us (6%)
  other arithmetic  1.92 us (1%)
    ppermute x4, starting transfers between devices, core_swap(): return lax.ppermute(value, 'ctx', [(s, s ^ 1) for s in range(N_CTX)])  20.5 us
    ppermute x6, starting transfers between devices, x_shift(): return lax.ppermute(value, 'ctx', pairs)  20.4 us
    all_to_all x1, starting transfers between devices, on_device(): lax.all_to_all(jnp.broadcast_to(w_pad[None], (CHIPS, SHARD_PAD, 128)), 'c...  15.7 us
    ppermute x1, starting transfers between devices, twin_swap(): return lax.ppermute(value, 'tp', [(s, s ^ 1) for s in range(N_TP)])  15.7 us
    all_to_all x1, starting transfers between devices, on_device(): lax.all_to_all(pair_sum, 'ctx', 0, 0, tiled=True, axis_index_groups=SAME_...  11 us
    ppermute x2, starting transfers between devices, outer_swap(): return lax.ppermute(value, 'ctx', pairs)  7.01 us
    ppermute x1, waiting for transfers between devices, twin_swap(): return lax.ppermute(value, 'tp', [(s, s ^ 1) for s in range(N_TP)])  6.75 us
    pallas_call x1, Pallas kernels, on_device(): pl.pallas_call(cotangent_kernel, out_shape=(chunk, chunk) + (jax.ShapeDty...  6.42 us
  transfers between devices with their start and end apart: 16, of which 5 were waited for; matrix products, arithmetic and copies ran while one was open for 3% of the time, Pallas kernels for 5%

profile of v11, /device:TPU:1, one launch (start us, length us, event | category | flops | bytes accessed | tf_op | source)
XLA Modules:
  0.0 145.9 jit_solution(12943025596759718149)
XLA Ops:
  7.2 0.0 all-gather.2.cloned.1.call-start
  7.2 15.7 %collective-permute-start = (bf16[384,256]{1,0:T(8,128)(2,1)}, bf16[384,256]{1,0:T(8,128)(2,1)S(1)}, u32[]{:S(2)}, u32[]{:S(2)}) collective-permute-start(bf16[384,256]{1,0:T(8,128)(2,1)} %param.9), channel_id=1, source_target_pairs={{0,1},{1,0},{2,3},{3,2},{4,5},{5,4},{6,7},{7,6},{8,9},{9,8},{10,11... | collective-permute-start | bytes 589832 | tf_op jit(solution)/shard_map/ppermute | solution.py:63
  22.9 6.7 %collective-permute-done = bf16[384,256]{1,0:T(8,128)(2,1)S(1)} collective-permute-done((bf16[384,256]{1,0:T(8,128)(2,1)}, bf16[384,256]{1,0:T(8,128)(2,1)S(1)}, u32[]{:S(2)}, u32[]{:S(2)}) %collective-permute-start) | collective-permute-done | bytes 196640 | tf_op jit(solution)/shard_map/ppermute | solution.py:63
  29.7 1.7 %pad_maximum_fusion = bf16[768,256]{1,0:T(8,128)(2,1)} fusion(bf16[384,256]{1,0:T(8,128)(2,1)S(1)} %collective-permute-done, bf16[384,256]{1,0:T(8,128)(2,1)} %param.9), kind=kLoop, calls=%fused_computation.1 | loop fusion | flops 786432 | bytes 786432 | tf_op jit(solution)/shard_map/concatenate | solution.py:214
  31.4 0.0 all-gather.2.cloned.1.call-update
  31.4 0.9 broadcast_in_dim.16
  32.3 15.7 %all-to-all-start = ((bf16[24,88,128]{2,1,0:T(8,128)(2,1)}), bf16[24,88,128]{2,1,0:T(8,128)(2,1)S(1)}, u32[]{:S(2)}, u32[]{:S(2)}) async-start(bf16[24,88,128]{2,1,0:T(8,128)(2,1)} %broadcast_in_dim.16), calls=%async_computation | async-start | bytes 1081344 | tf_op jit(solution)/shard_map/all_to_all | solution.py:218
  48.1 0.0 copy-start.16
  48.1 0.5 slice.60
  49.3 2.9 %collective-permute-start.2 = (bf16[2,128,128]{2,1,0:T(8,128)(2,1)S(1)}, bf16[2,128,128]{2,1,0:T(8,128)(2,1)S(1)}, u32[]{:S(2)}, u32[]{:S(2)}) collective-permute-start(bf16[2,128,128]{2,1,0:T(8,128)(2,1)S(1)} %get-tuple-element.31), channel_id=1, source_target_pairs={{0,16},{16,0},{32,48},{48,32},{64,80},{80,64},{96,112},{112,96},{1... | collective-permute-start | bytes 196616 | tf_op jit(solution)/shard_map/ppermute | solution.py:59
  52.2 3.4 %collective-permute-start.1 = (bf16[2,128,128]{2,1,0:T(8,128)(2,1)S(1)}, bf16[2,128,128]{2,1,0:T(8,128)(2,1)S(1)}, u32[]{:S(2)}, u32[]{:S(2)}) collective-permute-start(bf16[2,128,128]{2,1,0:T(8,128)(2,1)S(1)} %get-tuple-element.32), channel_id=1, source_target_pairs={{0,752},{16,32},{32,16},{48,64},{64,48},{80,96},{96,80},{112,128},... | collective-permute-start | bytes 196616 | tf_op jit(solution)/shard_map/ppermute | solution.py:49
  55.6 4.3 %collective-permute-start.3 = (bf16[2,384,128]{2,1,0:T(8,128)(2,1)S(1)}, bf16[2,384,128]{2,1,0:T(8,128)(2,1)S(1)}, u32[]{:S(2)}, u32[]{:S(2)}) collective-permute-start(bf16[2,384,128]{2,1,0:T(8,128)(2,1)S(1)} %maximum_select_fusion.kv), channel_id=1, source_target_pairs={{0,576},{16,592},{32,608},{48,624},{64,640},{80,656},{96,672},{112... | collective-permute-start | bytes 589832 | tf_op jit(solution)/shard_map/ppermute | solution.py:44
  59.9 2.5 %collective-permute-start.4 = (bf16[2,384,128]{2,1,0:T(8,128)(2,1)S(1)}, bf16[2,384,128]{2,1,0:T(8,128)(2,1)S(1)}, u32[]{:S(2)}, u32[]{:S(2)}) collective-permute-start(bf16[2,384,128]{2,1,0:T(8,128)(2,1)S(1)} %maximum_select_fusion.kv), channel_id=1, source_target_pairs={{0,384},{16,400},{32,416},{48,432},{64,448},{80,464},{96,480},{112... | collective-permute-start | bytes 589832 | tf_op jit(solution)/shard_map/ppermute | solution.py:44
  62.4 2.5 %collective-permute-start.5 = (bf16[2,384,128]{2,1,0:T(8,128)(2,1)S(1)}, bf16[2,384,128]{2,1,0:T(8,128)(2,1)S(1)}, u32[]{:S(2)}, u32[]{:S(2)}) collective-permute-start(bf16[2,384,128]{2,1,0:T(8,128)(2,1)S(1)} %maximum_select_fusion.kv), channel_id=1, source_target_pairs={{0,192},{16,208},{32,224},{48,240},{64,256},{80,272},{96,288},{112... | collective-permute-start | bytes 589832 | tf_op jit(solution)/shard_map/ppermute | solution.py:44
  64.9 0.0 collective-permute-done.2
  64.9 0.0 collective-permute-done.1
  65.0 0.0 copy-start
  65.0 0.0 copy-start.3
  65.0 0.5 slice.64
  65.5 0.6 slice.65
  67.4 0.0 collective-permute-done.3.far1
  67.4 0.5 slice.66
  68.6 0.9 collective-permute-done.4.far2
  69.4 0.5 slice.67
  70.6 1.3 collective-permute-done.5.far3
  72.0 0.5 slice.68
  73.1 0.0 all-to-all-done.own
  73.2 7.1 %collective-permute-start.6 = (bf16[24,88,128]{2,1,0:T(8,128)(2,1)S(1)}, bf16[24,88,128]{2,1,0:T(8,128)(2,1)S(1)}, u32[]{:S(2)}, u32[]{:S(2)}) collective-permute-start(bf16[24,88,128]{2,1,0:T(8,128)(2,1)S(1)} %broadcast_select_fusion), channel_id=1, source_target_pairs={{0,16},{16,0},{32,48},{48,32},{64,80},{80,64},{96,112},{112,96},{1... | collective-permute-start | bytes 1622024 | tf_op jit(solution)/shard_map/ppermute | solution.py:59
  80.3 0.1 add_select_fusion
  80.4 0.1 reshape.18
  80.5 0.1 concatenate.9.meta
  80.6 1.2 collective-permute-done.6.other
  81.9 2.3 %weight_rows.1.w = bf16[16,128,256]{2,1,0:T(8,128)(2,1)S(1)} custom-call(s32[13]{0:T(128)S(1)} %concatenate.9.meta, bf16[24,88,128]{2,1,0:T(8,128)(2,1)S(1)} %all-to-all-done.own, bf16[24,88,128]{2,1,0:T(8,128)(2,1)S(1)} %collective-permute-done.6.other), custom_call_target="tpu_custom_call" | custom-call | tf_op jit(solution)/shard_map/weight_rows/pallas_call | solution.py:229
  84.2 0.0 copy-start.10
  84.2 0.5 copy-done.10
  84.7 0.8 copy-done.1
  85.6 0.8 copy-done.4
  86.4 0.9 copy-done.6
  87.3 0.7 copy-done.11
  88.0 1.9 %attention_forward.1 = (f32[3,128,768]{2,1,0:T(8,128)S(1)}, bf16[384,128]{1,0:T(8,128)(2,1)S(1)}) custom-call(s32[13]{0:T(128)S(1)} %copy-done.11, bf16[16,128,256]{2,1,0:T(8,128)(2,1)S(1)} %weight_rows.1.w, bf16[384,128]{1,0:T(8,128)(2,1)S(1)} %copy-done.6, bf16[2,384,128]{2,1,0:T(8,128)(2,1)S(1)} %maximum_select_fusion.kv, ...), custom_call_target="tpu_custom_call" | custom-call | tf_op jit(solution)/shard_map/attention_forward/pallas_call | solution.py:239
  89.9 0.0 all-gather.2.cloned.1.call-done.pieces
  89.9 0.0 copy-start.2
  89.9 0.0 copy-start.5
  90.0 0.0 copy-start.7
  90.0 0.0 copy-start.12
  90.0 6.4 %cotangent_products.1 = (f32[24,88,128]{2,1,0:T(8,128)S(1)}, f32[24,88,128]{2,1,0:T(8,128)S(1)}, bf16[384,128]{1,0:T(8,128)(2,1)S(1)}, bf16[384,128]{1,0:T(8,128)(2,1)S(1)}) custom-call(bf16[16,128,256]{2,1,0:T(8,128)(2,1)S(1)} %weight_rows.1.w, bf16[384,128]{1,0:T(8,128)(2,1)S(1)} %get-tuple-element.17.att, ...), custom_call_target="tpu_custom_call" | custom-call | tf_op jit(solution)/shard_map/cotangent_products/pallas_call | solution.py:252
  96.4 3.0 %collective-permute-start.12 = (f32[24,88,128]{2,1,0:T(8,128)S(1)}, f32[24,88,128]{2,1,0:T(8,128)S(1)}, u32[]{:S(2)}, u32[]{:S(2)}) collective-permute-start(f32[24,88,128]{2,1,0:T(8,128)S(1)} %get-tuple-element.27), channel_id=1, source_target_pairs={{0,16},{16,0},{32,48},{48,32},{64,80},{80,64},{96,112},{112,96},{1... | collective-permute-start | bytes 3244040 | tf_op jit(solution)/shard_map/ppermute | solution.py:59
  99.4 2.3 %attention_backward.1 = (f32[384,128]{1,0:T(8,128)}, f32[2,384,128]{2,1,0:T(8,128)S(1)}, bf16[2,256,128]{2,1,0:T(8,128)(2,1)S(1)}, bf16[3,2,384,128]{3,2,1,0:T(8,128)(2,1)S(1)}) custom-call(s32[13]{0:T(128)S(1)} %copy-done.12, bf16[384,128]{1,0:T(8,128)(2,1)S(1)} %copy-done.7, bf16[2,384,128]{2,1,0:T(8,128)(2,1)S(1)} %maximum_select_fusion.kv, ...), custom_call_target="tpu_custom_call" | custom-call | tf_op jit(solution)/shard_map/attention_backward/pallas_call | solution.py:276
  101.8 0.7 copy-done.8
  102.4 0.0 collective-permute-done.12.other
  102.4 0.9 pair_sum.1
  103.3 11.0 %all-to-all-start.1 = ((bf16[24,88,128]{2,1,0:T(8,128)(2,1)}), bf16[24,88,128]{2,1,0:T(8,128)(2,1)S(1)}, u32[]{:S(2)}, u32[]{:S(2)}) async-start(bf16[24,88,128]{2,1,0:T(8,128)(2,1)} %pair_sum.1), calls=%async_computation.1 | async-start | bytes 1081344 | tf_op jit(solution)/shard_map/all_to_all | solution.py:298
  114.3 3.6 %collective-permute-start.7 = (bf16[2,128,128]{2,1,0:T(8,128)(2,1)S(1)}, bf16[2,128,128]{2,1,0:T(8,128)(2,1)S(1)}, u32[]{:S(2)}, u32[]{:S(2)}) collective-permute-start(bf16[2,128,128]{2,1,0:T(8,128)(2,1)S(1)} %get-tuple-element.34), channel_id=1, source_target_pairs={{0,752},{16,32},{32,16},{48,64},{64,48},{80,96},{96,80},{112,128},... | collective-permute-start | bytes 196616 | tf_op jit(solution)/shard_map/ppermute | solution.py:49
  118.0 4.6 %collective-permute-start.8 = (bf16[2,384,128]{2,1,0:T(8,128)(2,1)S(1)}, bf16[2,384,128]{2,1,0:T(8,128)(2,1)S(1)}, u32[]{:S(2)}, u32[]{:S(2)}) collective-permute-start(bf16[2,384,128]{2,1,0:T(8,128)(2,1)S(1)} %get-tuple-element.30), channel_id=1, source_target_pairs={{0,384},{16,400},{32,416},{48,432},{64,448},{80,464},{96,480},{112... | collective-permute-start | bytes 589832 | tf_op jit(solution)/shard_map/ppermute | solution.py:44
  122.6 2.2 %collective-permute-start.9 = (bf16[2,384,128]{2,1,0:T(8,128)(2,1)S(1)}, bf16[2,384,128]{2,1,0:T(8,128)(2,1)S(1)}, u32[]{:S(2)}, u32[]{:S(2)}) collective-permute-start(bf16[2,384,128]{2,1,0:T(8,128)(2,1)S(1)} %get-tuple-element.29), channel_id=1, source_target_pairs={{0,192},{16,208},{32,224},{48,240},{64,256},{80,272},{96,288},{112... | collective-permute-start | bytes 589832 | tf_op jit(solution)/shard_map/ppermute | solution.py:44
  124.8 4.3 %collective-permute-start.10 = (bf16[2,384,128]{2,1,0:T(8,128)(2,1)S(1)}, bf16[2,384,128]{2,1,0:T(8,128)(2,1)S(1)}, u32[]{:S(2)}, u32[]{:S(2)}) collective-permute-start(bf16[2,384,128]{2,1,0:T(8,128)(2,1)S(1)} %get-tuple-element.28), channel_id=1, source_target_pairs={{0,576},{16,592},{32,608},{48,624},{64,640},{80,656},{96,672},{112... | collective-permute-start | bytes 589832 | tf_op jit(solution)/shard_map/ppermute | solution.py:44
  129.1 7.5 %collective-permute-start.11 = (bf16[2,128,128]{2,1,0:T(8,128)(2,1)S(1)}, bf16[2,128,128]{2,1,0:T(8,128)(2,1)S(1)}, u32[]{:S(2)}, u32[]{:S(2)}) collective-permute-start(bf16[2,128,128]{2,1,0:T(8,128)(2,1)S(1)} %get-tuple-element.33), channel_id=1, source_target_pairs={{0,16},{16,0},{32,48},{48,32},{64,80},{80,64},{96,112},{112,96},{1... | collective-permute-start | bytes 196616 | tf_op jit(solution)/shard_map/ppermute | solution.py:59
  136.6 0.0 collective-permute-done.7
  136.7 0.8 collective-permute-done.11.inner
  137.5 0.0 collective-permute-done.8.far1
  137.5 0.0 collective-permute-done.9.far2
  137.5 0.0 collective-permute-done.10.far3
  137.5 0.8 grad_sum.1
  138.4 0.7 chunk_sum.1
  (30 shorter events, 0.2 us)
Async XLA Ops:
  7.2 24.3 %copy-start.15 = (bf16[1,86,128]{2,1,0:T(8,128)(2,1)S(1)}, bf16[1,86,128]{2,1,0:T(8,128)(2,1)}, u32[]{:S(2)}) copy-start(bf16[1,86,128]{2,1,0:T(8,128)(2,1)} %param.10) | copy-start | bytes 66052
  7.2 82.8 %all-gather.2.cloned.1.call-start = ((), (), s32[]{:S(2)}) async-start(), calls=%async_computation.2 | async-start | bytes 3538944 | tf_op jit(solution)/shard_map/all_gather | solution.py:213
  7.2 22.4 %collective-permute-start = (bf16[384,256]{1,0:T(8,128)(2,1)}, bf16[384,256]{1,0:T(8,128)(2,1)S(1)}, u32[]{:S(2)}, u32[]{:S(2)}) collective-permute-start(bf16[384,256]{1,0:T(8,128)(2,1)} %param.9), channel_id=1, source_target_pairs={{0,1},{1,0},{2,3},{3,2},{4,5},{5,4},{6,7},{7,6},{8,9},{9,8},{10,11... | collective-permute-start | bytes 589832 | tf_op jit(solution)/shard_map/ppermute | solution.py:63
  31.4 17.9 %copy-start.13 = (bf16[384,128]{1,0:T(8,128)(2,1)S(1)}, bf16[384,128]{1,0:T(8,128)(2,1)}, u32[]{:S(2)}) copy-start(bf16[384,128]{1,0:T(8,128)(2,1)} %param.8) | copy-start | bytes 294916
  31.4 17.9 %copy-start.14 = (bf16[384,128]{1,0:T(8,128)(2,1)S(1)}, bf16[384,128]{1,0:T(8,128)(2,1)}, u32[]{:S(2)}) copy-start(bf16[384,128]{1,0:T(8,128)(2,1)} %param.7) | copy-start | bytes 294916
  32.3 40.8 %all-to-all-start = ((bf16[24,88,128]{2,1,0:T(8,128)(2,1)}), bf16[24,88,128]{2,1,0:T(8,128)(2,1)S(1)}, u32[]{:S(2)}, u32[]{:S(2)}) async-start(bf16[24,88,128]{2,1,0:T(8,128)(2,1)} %broadcast_in_dim.16), calls=%async_computation | async-start | bytes 1081344 | tf_op jit(solution)/shard_map/all_to_all | solution.py:218
  48.1 32.3 %copy-start.16 = (s32[3,6]{1,0:T(4,128)S(1)}, s32[3,6]{1,0:T(4,128)}, u32[]{:S(2)}) copy-start(s32[3,6]{1,0:T(4,128)} %param.11) | copy-start | bytes 220
  49.3 15.6 %collective-permute-start.2 = (bf16[2,128,128]{2,1,0:T(8,128)(2,1)S(1)}, bf16[2,128,128]{2,1,0:T(8,128)(2,1)S(1)}, u32[]{:S(2)}, u32[]{:S(2)}) collective-permute-start(bf16[2,128,128]{2,1,0:T(8,128)(2,1)S(1)} %get-tuple-element.31), channel_id=1, source_target_pairs={{0,16},{16,0},{32,48},{48,32},{64,80},{80,64},{96,112},{112,96},{1... | collective-permute-start | bytes 196616 | tf_op jit(solution)/shard_map/ppermute | solution.py:59
  52.2 12.7 %collective-permute-start.1 = (bf16[2,128,128]{2,1,0:T(8,128)(2,1)S(1)}, bf16[2,128,128]{2,1,0:T(8,128)(2,1)S(1)}, u32[]{:S(2)}, u32[]{:S(2)}) collective-permute-start(bf16[2,128,128]{2,1,0:T(8,128)(2,1)S(1)} %get-tuple-element.32), channel_id=1, source_target_pairs={{0,752},{16,32},{32,16},{48,64},{64,48},{80,96},{96,80},{112,128},... | collective-permute-start | bytes 196616 | tf_op jit(solution)/shard_map/ppermute | solution.py:49
  55.6 11.8 %collective-permute-start.3 = (bf16[2,384,128]{2,1,0:T(8,128)(2,1)S(1)}, bf16[2,384,128]{2,1,0:T(8,128)(2,1)S(1)}, u32[]{:S(2)}, u32[]{:S(2)}) collective-permute-start(bf16[2,384,128]{2,1,0:T(8,128)(2,1)S(1)} %maximum_select_fusion.kv), channel_id=1, source_target_pairs={{0,576},{16,592},{32,608},{48,624},{64,640},{80,656},{96,672},{112... | collective-permute-start | bytes 589832 | tf_op jit(solution)/shard_map/ppermute | solution.py:44
  59.9 9.5 %collective-permute-start.4 = (bf16[2,384,128]{2,1,0:T(8,128)(2,1)S(1)}, bf16[2,384,128]{2,1,0:T(8,128)(2,1)S(1)}, u32[]{:S(2)}, u32[]{:S(2)}) collective-permute-start(bf16[2,384,128]{2,1,0:T(8,128)(2,1)S(1)} %maximum_select_fusion.kv), channel_id=1, source_target_pairs={{0,384},{16,400},{32,416},{48,432},{64,448},{80,464},{96,480},{112... | collective-permute-start | bytes 589832 | tf_op jit(solution)/shard_map/ppermute | solution.py:44
  62.4 9.5 %collective-permute-start.5 = (bf16[2,384,128]{2,1,0:T(8,128)(2,1)S(1)}, bf16[2,384,128]{2,1,0:T(8,128)(2,1)S(1)}, u32[]{:S(2)}, u32[]{:S(2)}) collective-permute-start(bf16[2,384,128]{2,1,0:T(8,128)(2,1)S(1)} %maximum_select_fusion.kv), channel_id=1, source_target_pairs={{0,192},{16,208},{32,224},{48,240},{64,256},{80,272},{96,288},{112... | collective-permute-start | bytes 589832 | tf_op jit(solution)/shard_map/ppermute | solution.py:44
  65.0 16.9 %copy-start = (bf16[2,128,128]{2,1,0:T(8,128)(2,1)}, bf16[2,128,128]{2,1,0:T(8,128)(2,1)S(1)}, u32[]{:S(2)}) copy-start(bf16[2,128,128]{2,1,0:T(8,128)(2,1)S(1)} %get-tuple-element.35.nxt) | copy-start | bytes 196612
  65.0 16.9 %copy-start.3 = (bf16[2,128,128]{2,1,0:T(8,128)(2,1)}, bf16[2,128,128]{2,1,0:T(8,128)(2,1)S(1)}, u32[]{:S(2)}) copy-start(bf16[2,128,128]{2,1,0:T(8,128)(2,1)S(1)} %get-tuple-element.36.prev) | copy-start | bytes 196612
  73.2 8.7 %collective-permute-start.6 = (bf16[24,88,128]{2,1,0:T(8,128)(2,1)S(1)}, bf16[24,88,128]{2,1,0:T(8,128)(2,1)S(1)}, u32[]{:S(2)}, u32[]{:S(2)}) collective-permute-start(bf16[24,88,128]{2,1,0:T(8,128)(2,1)S(1)} %broadcast_select_fusion), channel_id=1, source_target_pairs={{0,16},{16,0},{32,48},{48,32},{64,80},{80,64},{96,112},{112,96},{1... | collective-permute-start | bytes 1622024 | tf_op jit(solution)/shard_map/ppermute | solution.py:59
  84.2 0.5 copy-start.10
  84.7 0.8 copy-start.1
  85.6 0.8 copy-start.4
  86.4 0.9 copy-start.6
  87.3 0.7 copy-start.11
  89.9 9.5 %copy-start.2 = (bf16[2,128,128]{2,1,0:T(8,128)(2,1)S(1)}, bf16[2,128,128]{2,1,0:T(8,128)(2,1)}, u32[]{:S(2)}) copy-start(bf16[2,128,128]{2,1,0:T(8,128)(2,1)} %copy-done) | copy-start | bytes 196612
  89.9 9.5 %copy-start.5 = (bf16[2,128,128]{2,1,0:T(8,128)(2,1)S(1)}, bf16[2,128,128]{2,1,0:T(8,128)(2,1)}, u32[]{:S(2)}) copy-start(bf16[2,128,128]{2,1,0:T(8,128)(2,1)} %copy-done.3) | copy-start | bytes 196612
  90.0 9.5 %copy-start.7 = (bf16[384,128]{1,0:T(8,128)(2,1)S(1)}, bf16[384,128]{1,0:T(8,128)(2,1)}, u32[]{:S(2)}) copy-start(bf16[384,128]{1,0:T(8,128)(2,1)} %q.3) | copy-start | bytes 294916
  90.0 9.5 %copy-start.12 = (s32[13]{0:T(128)S(1)}, s32[13]{0:T(128)}, u32[]{:S(2)}) copy-start(s32[13]{0:T(128)} %copy-done.10) | copy-start | bytes 160
  96.4 6.0 %collective-permute-start.12 = (f32[24,88,128]{2,1,0:T(8,128)S(1)}, f32[24,88,128]{2,1,0:T(8,128)S(1)}, u32[]{:S(2)}, u32[]{:S(2)}) collective-permute-start(f32[24,88,128]{2,1,0:T(8,128)S(1)} %get-tuple-element.27), channel_id=1, source_target_pairs={{0,16},{16,0},{32,48},{48,32},{64,80},{80,64},{96,112},{112,96},{1... | collective-permute-start | bytes 3244040 | tf_op jit(solution)/shard_map/ppermute | solution.py:59
  101.8 0.7 copy-start.8
  103.3 11.0 %copy-start.9 = (bf16[2,256,128]{2,1,0:T(8,128)(2,1)S(1)}, bf16[2,256,128]{2,1,0:T(8,128)(2,1)}, u32[]{:S(2)}) copy-start(bf16[2,256,128]{2,1,0:T(8,128)(2,1)} %copy-done.8) | copy-start | bytes 393220
  103.3 35.1 %all-to-all-start.1 = ((bf16[24,88,128]{2,1,0:T(8,128)(2,1)}), bf16[24,88,128]{2,1,0:T(8,128)(2,1)S(1)}, u32[]{:S(2)}, u32[]{:S(2)}) async-start(bf16[24,88,128]{2,1,0:T(8,128)(2,1)} %pair_sum.1), calls=%async_computation.1 | async-start | bytes 1081344 | tf_op jit(solution)/shard_map/all_to_all | solution.py:298
  114.3 22.3 %collective-permute-start.7 = (bf16[2,128,128]{2,1,0:T(8,128)(2,1)S(1)}, bf16[2,128,128]{2,1,0:T(8,128)(2,1)S(1)}, u32[]{:S(2)}, u32[]{:S(2)}) collective-permute-start(bf16[2,128,128]{2,1,0:T(8,128)(2,1)S(1)} %get-tuple-element.34), channel_id=1, source_target_pairs={{0,752},{16,32},{32,16},{48,64},{64,48},{80,96},{96,80},{112,128},... | collective-permute-start | bytes 196616 | tf_op jit(solution)/shard_map/ppermute | solution.py:49
  118.0 19.5 %collective-permute-start.8 = (bf16[2,384,128]{2,1,0:T(8,128)(2,1)S(1)}, bf16[2,384,128]{2,1,0:T(8,128)(2,1)S(1)}, u32[]{:S(2)}, u32[]{:S(2)}) collective-permute-start(bf16[2,384,128]{2,1,0:T(8,128)(2,1)S(1)} %get-tuple-element.30), channel_id=1, source_target_pairs={{0,384},{16,400},{32,416},{48,432},{64,448},{80,464},{96,480},{112... | collective-permute-start | bytes 589832 | tf_op jit(solution)/shard_map/ppermute | solution.py:44
  122.6 14.9 %collective-permute-start.9 = (bf16[2,384,128]{2,1,0:T(8,128)(2,1)S(1)}, bf16[2,384,128]{2,1,0:T(8,128)(2,1)S(1)}, u32[]{:S(2)}, u32[]{:S(2)}) collective-permute-start(bf16[2,384,128]{2,1,0:T(8,128)(2,1)S(1)} %get-tuple-element.29), channel_id=1, source_target_pairs={{0,192},{16,208},{32,224},{48,240},{64,256},{80,272},{96,288},{112... | collective-permute-start | bytes 589832 | tf_op jit(solution)/shard_map/ppermute | solution.py:44
  124.8 12.7 %collective-permute-start.10 = (bf16[2,384,128]{2,1,0:T(8,128)(2,1)S(1)}, bf16[2,384,128]{2,1,0:T(8,128)(2,1)S(1)}, u32[]{:S(2)}, u32[]{:S(2)}) collective-permute-start(bf16[2,384,128]{2,1,0:T(8,128)(2,1)S(1)} %get-tuple-element.28), channel_id=1, source_target_pairs={{0,576},{16,592},{32,608},{48,624},{64,640},{80,656},{96,672},{112... | collective-permute-start | bytes 589832 | tf_op jit(solution)/shard_map/ppermute | solution.py:44
  129.1 8.4 %collective-permute-start.11 = (bf16[2,128,128]{2,1,0:T(8,128)(2,1)S(1)}, bf16[2,128,128]{2,1,0:T(8,128)(2,1)S(1)}, u32[]{:S(2)}, u32[]{:S(2)}) collective-permute-start(bf16[2,128,128]{2,1,0:T(8,128)(2,1)S(1)} %get-tuple-element.33), channel_id=1, source_target_pairs={{0,16},{16,0},{32,48},{48,32},{64,80},{80,64},{96,112},{112,96},{1... | collective-permute-start | bytes 196616 | tf_op jit(solution)/shard_map/ppermute | solution.py:59
Sparse Core Ops, SparseCore 0:
  31.5 58.1 all-gather.1

commit v12 on v9

--- a/solution.py
+++ b/solution.py
@@ -173,7 +173,7 @@
     total = parts[0].astype(F32)
     for i in range(1, CHIPS):
         total = total + parts[i].astype(F32)
-    out[0] = total[:SHARD]
+    out[...] = total[:SHARD].reshape(SHARD, 1, 128)
 
 
 def grad_sum_kernel(dkv, prev, nxt, far1, far2, far3, inner, dk, dv):
@@ -273,10 +273,10 @@
     )
     weight_grad = pl.pallas_call(
         chunk_sum_kernel,
-        out_shape=jax.ShapeDtypeStruct((1, SHARD, 128), F32),
+        out_shape=jax.ShapeDtypeStruct((SHARD, 1, 128), F32),
         compiler_params=PARAMS,
         name="chunk_sum",
-    )(spread)
+    )(spread).transpose(1, 0, 2)
     far_back = [x_shift(dfar[k], k + 1) for k in range(3)]
     from_inner = core_swap(band[:, BLK:])
     from_outer = outer_swap(band[:, :BLK])

time: 145 us -> 145 us (level)
    unnamed x37 -> x36, local copies, waits for them, and re-layouts: 6.98 us -> 6.32 us
where the time goes in v12:
time: 145 us; the launch traced here: 144 us
  starting transfers between devices  90.4 us (62%)
  between operations  18.5 us (13%)
  Pallas kernels  12 us (8%)
  waiting for transfers between devices  11.1 us (8%)
  local copies, waits for them, and re-layouts  10.6 us (7%)
  other arithmetic  1.91 us (1%)
    ppermute x4, starting transfers between devices, core_swap(): return lax.ppermute(value, 'ctx', [(s, s ^ 1) for s in range(N_CTX)])  20.5 us
    ppermute x6, starting transfers between devices, x_shift(): return lax.ppermute(value, 'ctx', pairs)  20.4 us
    all_to_all x1, starting transfers between devices, on_device(): lax.all_to_all(jnp.broadcast_to(w_pad[None], (CHIPS, SHARD_PAD, 128)), 'c...  15.7 us
    ppermute x1, starting transfers between devices, twin_swap(): return lax.ppermute(value, 'tp', [(s, s ^ 1) for s in range(N_TP)])  15.7 us
    all_to_all x1, starting transfers between devices, on_device(): lax.all_to_all(pair_sum, 'ctx', 0, 0, tiled=True, axis_index_groups=SAME_...  11 us
    ppermute x2, starting transfers between devices, outer_swap(): return lax.ppermute(value, 'ctx', pairs)  7.03 us
    ppermute x1, waiting for transfers between devices, twin_swap(): return lax.ppermute(value, 'tp', [(s, s ^ 1) for s in range(N_TP)])  6.75 us
    unnamed x36, local copies, waits for them, and re-layouts  6.32 us
  transfers between devices with their start and end apart: 16, of which 5 were waited for; matrix products, arithmetic and copies ran while one was open for 3% of the time, Pallas kernels for 5%

profile of v12, /device:TPU:1, one launch (start us, length us, event | category | flops | bytes accessed | tf_op | source)
XLA Modules:
  0.0 144.3 jit_solution(11902075072042267360)
XLA Ops:
  7.2 0.0 all-gather.2.cloned.1.call-start
  7.2 15.7 %collective-permute-start = (bf16[384,256]{1,0:T(8,128)(2,1)}, bf16[384,256]{1,0:T(8,128)(2,1)S(1)}, u32[]{:S(2)}, u32[]{:S(2)}) collective-permute-start(bf16[384,256]{1,0:T(8,128)(2,1)} %param.9), channel_id=1, source_target_pairs={{0,1},{1,0},{2,3},{3,2},{4,5},{5,4},{6,7},{7,6},{8,9},{9,8},{10,11... | collective-permute-start | bytes 589832 | tf_op jit(solution)/shard_map/ppermute | solution.py:57
  22.9 6.7 %collective-permute-done = bf16[384,256]{1,0:T(8,128)(2,1)S(1)} collective-permute-done((bf16[384,256]{1,0:T(8,128)(2,1)}, bf16[384,256]{1,0:T(8,128)(2,1)S(1)}, u32[]{:S(2)}, u32[]{:S(2)}) %collective-permute-start) | collective-permute-done | bytes 196640 | tf_op jit(solution)/shard_map/ppermute | solution.py:57
  29.7 1.7 %pad_maximum_fusion = bf16[768,256]{1,0:T(8,128)(2,1)} fusion(bf16[384,256]{1,0:T(8,128)(2,1)S(1)} %collective-permute-done, bf16[384,256]{1,0:T(8,128)(2,1)} %param.9), kind=kLoop, calls=%fused_computation.1 | loop fusion | flops 786432 | bytes 786432 | tf_op jit(solution)/shard_map/concatenate | solution.py:198
  31.4 0.0 all-gather.2.cloned.1.call-update
  31.4 0.9 broadcast_in_dim.16
  32.3 15.7 %all-to-all-start = ((bf16[24,88,128]{2,1,0:T(8,128)(2,1)}), bf16[24,88,128]{2,1,0:T(8,128)(2,1)S(1)}, u32[]{:S(2)}, u32[]{:S(2)}) async-start(bf16[24,88,128]{2,1,0:T(8,128)(2,1)} %broadcast_in_dim.16), calls=%async_computation | async-start | bytes 1081344 | tf_op jit(solution)/shard_map/all_to_all | solution.py:202
  48.1 0.0 copy-start.17
  48.1 0.5 slice.60
  49.3 0.0 copy-done.14
  49.3 0.0 copy-done.15
  49.3 2.9 %collective-permute-start.2 = (bf16[2,128,128]{2,1,0:T(8,128)(2,1)S(1)}, bf16[2,128,128]{2,1,0:T(8,128)(2,1)S(1)}, u32[]{:S(2)}, u32[]{:S(2)}) collective-permute-start(bf16[2,128,128]{2,1,0:T(8,128)(2,1)S(1)} %get-tuple-element.31), channel_id=1, source_target_pairs={{0,16},{16,0},{32,48},{48,32},{64,80},{80,64},{96,112},{112,96},{1... | collective-permute-start | bytes 196616 | tf_op jit(solution)/shard_map/ppermute | solution.py:53
  52.2 3.4 %collective-permute-start.1 = (bf16[2,128,128]{2,1,0:T(8,128)(2,1)S(1)}, bf16[2,128,128]{2,1,0:T(8,128)(2,1)S(1)}, u32[]{:S(2)}, u32[]{:S(2)}) collective-permute-start(bf16[2,128,128]{2,1,0:T(8,128)(2,1)S(1)} %get-tuple-element.32), channel_id=1, source_target_pairs={{0,752},{16,32},{32,16},{48,64},{64,48},{80,96},{96,80},{112,128},... | collective-permute-start | bytes 196616 | tf_op jit(solution)/shard_map/ppermute | solution.py:43
  55.6 4.3 %collective-permute-start.3 = (bf16[2,384,128]{2,1,0:T(8,128)(2,1)S(1)}, bf16[2,384,128]{2,1,0:T(8,128)(2,1)S(1)}, u32[]{:S(2)}, u32[]{:S(2)}) collective-permute-start(bf16[2,384,128]{2,1,0:T(8,128)(2,1)S(1)} %maximum_select_fusion.kv), channel_id=1, source_target_pairs={{0,576},{16,592},{32,608},{48,624},{64,640},{80,656},{96,672},{112... | collective-permute-start | bytes 589832 | tf_op jit(solution)/shard_map/ppermute | solution.py:38
  59.9 2.5 %collective-permute-start.4 = (bf16[2,384,128]{2,1,0:T(8,128)(2,1)S(1)}, bf16[2,384,128]{2,1,0:T(8,128)(2,1)S(1)}, u32[]{:S(2)}, u32[]{:S(2)}) collective-permute-start(bf16[2,384,128]{2,1,0:T(8,128)(2,1)S(1)} %maximum_select_fusion.kv), channel_id=1, source_target_pairs={{0,384},{16,400},{32,416},{48,432},{64,448},{80,464},{96,480},{112... | collective-permute-start | bytes 589832 | tf_op jit(solution)/shard_map/ppermute | solution.py:38
  62.4 2.5 %collective-permute-start.5 = (bf16[2,384,128]{2,1,0:T(8,128)(2,1)S(1)}, bf16[2,384,128]{2,1,0:T(8,128)(2,1)S(1)}, u32[]{:S(2)}, u32[]{:S(2)}) collective-permute-start(bf16[2,384,128]{2,1,0:T(8,128)(2,1)S(1)} %maximum_select_fusion.kv), channel_id=1, source_target_pairs={{0,192},{16,208},{32,224},{48,240},{64,256},{80,272},{96,288},{112... | collective-permute-start | bytes 589832 | tf_op jit(solution)/shard_map/ppermute | solution.py:38
  64.9 0.0 collective-permute-done.2
  64.9 0.0 collective-permute-done.1
  65.0 0.0 copy-start.1
  65.0 0.0 copy-start.4
  65.0 0.5 slice.64
  65.5 0.6 slice.65
  67.4 0.0 collective-permute-done.3.far1
  67.5 0.5 slice.66
  68.6 0.8 collective-permute-done.4.far2
  69.4 0.5 slice.67
  70.6 1.3 collective-permute-done.5.far3
  72.0 0.5 slice.68
  73.1 0.0 all-to-all-done.own
  73.2 7.1 %collective-permute-start.6 = (bf16[24,88,128]{2,1,0:T(8,128)(2,1)S(1)}, bf16[24,88,128]{2,1,0:T(8,128)(2,1)S(1)}, u32[]{:S(2)}, u32[]{:S(2)}) collective-permute-start(bf16[24,88,128]{2,1,0:T(8,128)(2,1)S(1)} %broadcast_select_fusion), channel_id=1, source_target_pairs={{0,16},{16,0},{32,48},{48,32},{64,80},{80,64},{96,112},{112,96},{1... | collective-permute-start | bytes 1622024 | tf_op jit(solution)/shard_map/ppermute | solution.py:53
  80.3 0.1 add_select_fusion
  80.4 0.1 reshape.18
  80.5 0.1 concatenate.9.meta
  80.6 1.2 collective-permute-done.6.other
  81.9 2.3 %weight_rows.1.w = bf16[16,128,256]{2,1,0:T(8,128)(2,1)S(1)} custom-call(s32[13]{0:T(128)S(1)} %concatenate.9.meta, bf16[24,88,128]{2,1,0:T(8,128)(2,1)S(1)} %all-to-all-done.own, bf16[24,88,128]{2,1,0:T(8,128)(2,1)S(1)} %collective-permute-done.6.other), custom_call_target="tpu_custom_call" | custom-call | tf_op jit(solution)/shard_map/weight_rows/pallas_call | solution.py:213
  84.2 0.0 copy-start.11
  84.2 0.5 copy-done.11
  84.7 0.8 copy-done.2
  85.6 0.8 copy-done.5
  86.4 0.9 copy-done.7
  87.3 0.7 copy-done.12
  88.0 1.9 %attention_forward.1 = (f32[3,128,768]{2,1,0:T(8,128)S(1)}, bf16[384,128]{1,0:T(8,128)(2,1)S(1)}) custom-call(s32[13]{0:T(128)S(1)} %copy-done.12, bf16[16,128,256]{2,1,0:T(8,128)(2,1)S(1)} %weight_rows.1.w, bf16[384,128]{1,0:T(8,128)(2,1)S(1)} %copy-done.7, bf16[2,384,128]{2,1,0:T(8,128)(2,1)S(1)} %maximum_select_fusion.kv, ...), custom_call_target="tpu_custom_call" | custom-call | tf_op jit(solution)/shard_map/attention_forward/pallas_call | solution.py:223
  89.9 0.0 all-gather.2.cloned.1.call-done.pieces
  89.9 1.9 %copy-done = bf16[6144,256]{1,0:T(8,128)(2,1)S(1)} copy-done((bf16[6144,256]{1,0:T(8,128)(2,1)S(1)}, bf16[6144,256]{1,0:T(8,128)(2,1)}, u32[]{:S(2)}) %copy-start) | copy-done | bytes 3145752
  91.8 2.9 %cotangent_products.1 = (f32[24,88,128]{2,1,0:T(8,128)S(1)}, f32[24,88,128]{2,1,0:T(8,128)S(1)}, bf16[384,128]{1,0:T(8,128)(2,1)S(1)}, bf16[384,128]{1,0:T(8,128)(2,1)S(1)}) custom-call(bf16[16,128,256]{2,1,0:T(8,128)(2,1)S(1)} %weight_rows.1.w, bf16[384,128]{1,0:T(8,128)(2,1)S(1)} %get-tuple-element.17.att, bf16[6144,256]{1,0:T(8,128)(2,1)S(1)} %copy-done), custom_call_target="tpu_custom_call" | custom-call | tf_op jit(solution)/shard_map/cotangent_products/pallas_call | solution.py:236
  94.8 3.0 %collective-permute-start.12 = (f32[24,88,128]{2,1,0:T(8,128)S(1)}, f32[24,88,128]{2,1,0:T(8,128)S(1)}, u32[]{:S(2)}, u32[]{:S(2)}) collective-permute-start(f32[24,88,128]{2,1,0:T(8,128)S(1)} %get-tuple-element.27), channel_id=1, source_target_pairs={{0,16},{16,0},{32,48},{48,32},{64,80},{80,64},{96,112},{112,96},{1... | collective-permute-start | bytes 3244040 | tf_op jit(solution)/shard_map/ppermute | solution.py:53
  97.8 2.3 %attention_backward.1 = (f32[384,128]{1,0:T(8,128)}, f32[2,384,128]{2,1,0:T(8,128)S(1)}, bf16[2,256,128]{2,1,0:T(8,128)(2,1)S(1)}, bf16[3,2,384,128]{3,2,1,0:T(8,128)(2,1)S(1)}) custom-call(s32[13]{0:T(128)S(1)} %copy-done.13, bf16[384,128]{1,0:T(8,128)(2,1)S(1)} %copy-done.8, bf16[2,384,128]{2,1,0:T(8,128)(2,1)S(1)} %maximum_select_fusion.kv, ...), custom_call_target="tpu_custom_call" | custom-call | tf_op jit(solution)/shard_map/attention_backward/pallas_call | solution.py:249
  100.2 0.7 copy-done.9
  100.8 0.0 collective-permute-done.12.other
  100.8 0.9 pair_sum.1
  101.7 11.0 %all-to-all-start.1 = ((bf16[24,88,128]{2,1,0:T(8,128)(2,1)}), bf16[24,88,128]{2,1,0:T(8,128)(2,1)S(1)}, u32[]{:S(2)}, u32[]{:S(2)}) async-start(bf16[24,88,128]{2,1,0:T(8,128)(2,1)} %pair_sum.1), calls=%async_computation.1 | async-start | bytes 1081344 | tf_op jit(solution)/shard_map/all_to_all | solution.py:271
  112.7 3.7 %collective-permute-start.7 = (bf16[2,128,128]{2,1,0:T(8,128)(2,1)S(1)}, bf16[2,128,128]{2,1,0:T(8,128)(2,1)S(1)}, u32[]{:S(2)}, u32[]{:S(2)}) collective-permute-start(bf16[2,128,128]{2,1,0:T(8,128)(2,1)S(1)} %get-tuple-element.34), channel_id=1, source_target_pairs={{0,752},{16,32},{32,16},{48,64},{64,48},{80,96},{96,80},{112,128},... | collective-permute-start | bytes 196616 | tf_op jit(solution)/shard_map/ppermute | solution.py:43
  116.4 4.6 %collective-permute-start.8 = (bf16[2,384,128]{2,1,0:T(8,128)(2,1)S(1)}, bf16[2,384,128]{2,1,0:T(8,128)(2,1)S(1)}, u32[]{:S(2)}, u32[]{:S(2)}) collective-permute-start(bf16[2,384,128]{2,1,0:T(8,128)(2,1)S(1)} %get-tuple-element.30), channel_id=1, source_target_pairs={{0,384},{16,400},{32,416},{48,432},{64,448},{80,464},{96,480},{112... | collective-permute-start | bytes 589832 | tf_op jit(solution)/shard_map/ppermute | solution.py:38
  121.0 2.2 %collective-permute-start.9 = (bf16[2,384,128]{2,1,0:T(8,128)(2,1)S(1)}, bf16[2,384,128]{2,1,0:T(8,128)(2,1)S(1)}, u32[]{:S(2)}, u32[]{:S(2)}) collective-permute-start(bf16[2,384,128]{2,1,0:T(8,128)(2,1)S(1)} %get-tuple-element.29), channel_id=1, source_target_pairs={{0,192},{16,208},{32,224},{48,240},{64,256},{80,272},{96,288},{112... | collective-permute-start | bytes 589832 | tf_op jit(solution)/shard_map/ppermute | solution.py:38
  123.3 4.3 %collective-permute-start.10 = (bf16[2,384,128]{2,1,0:T(8,128)(2,1)S(1)}, bf16[2,384,128]{2,1,0:T(8,128)(2,1)S(1)}, u32[]{:S(2)}, u32[]{:S(2)}) collective-permute-start(bf16[2,384,128]{2,1,0:T(8,128)(2,1)S(1)} %get-tuple-element.28), channel_id=1, source_target_pairs={{0,576},{16,592},{32,608},{48,624},{64,640},{80,656},{96,672},{112... | collective-permute-start | bytes 589832 | tf_op jit(solution)/shard_map/ppermute | solution.py:38
  127.6 7.5 %collective-permute-start.11 = (bf16[2,128,128]{2,1,0:T(8,128)(2,1)S(1)}, bf16[2,128,128]{2,1,0:T(8,128)(2,1)S(1)}, u32[]{:S(2)}, u32[]{:S(2)}) collective-permute-start(bf16[2,128,128]{2,1,0:T(8,128)(2,1)S(1)} %get-tuple-element.33), channel_id=1, source_target_pairs={{0,16},{16,0},{32,48},{48,32},{64,80},{80,64},{96,112},{112,96},{1... | collective-permute-start | bytes 196616 | tf_op jit(solution)/shard_map/ppermute | solution.py:53
  135.1 0.0 collective-permute-done.7
  135.1 0.8 collective-permute-done.11.inner
  135.9 0.0 collective-permute-done.8.far1
  135.9 0.0 collective-permute-done.9.far2
  135.9 0.0 collective-permute-done.10.far3
  135.9 0.8 grad_sum.1
  136.8 0.0 all-to-all-done.1.parts
  136.8 0.7 chunk_sum.1
  (32 shorter events, 0.2 us)
Async XLA Ops:
  7.2 24.2 %copy-start.16 = (bf16[1,86,128]{2,1,0:T(8,128)(2,1)S(1)}, bf16[1,86,128]{2,1,0:T(8,128)(2,1)}, u32[]{:S(2)}) copy-start(bf16[1,86,128]{2,1,0:T(8,128)(2,1)} %param.10) | copy-start | bytes 66052
  7.2 82.7 %all-gather.2.cloned.1.call-start = ((), (), s32[]{:S(2)}) async-start(), calls=%async_computation.2 | async-start | bytes 3538944 | tf_op jit(solution)/shard_map/all_gather | solution.py:197
  7.2 22.4 %collective-permute-start = (bf16[384,256]{1,0:T(8,128)(2,1)}, bf16[384,256]{1,0:T(8,128)(2,1)S(1)}, u32[]{:S(2)}, u32[]{:S(2)}) collective-permute-start(bf16[384,256]{1,0:T(8,128)(2,1)} %param.9), channel_id=1, source_target_pairs={{0,1},{1,0},{2,3},{3,2},{4,5},{5,4},{6,7},{7,6},{8,9},{9,8},{10,11... | collective-permute-start | bytes 589832 | tf_op jit(solution)/shard_map/ppermute | solution.py:57
  31.4 17.9 %copy-start.14 = (bf16[384,128]{1,0:T(8,128)(2,1)S(1)}, bf16[384,128]{1,0:T(8,128)(2,1)}, u32[]{:S(2)}) copy-start(bf16[384,128]{1,0:T(8,128)(2,1)} %param.8) | copy-start | bytes 294916
  31.4 17.9 %copy-start.15 = (bf16[384,128]{1,0:T(8,128)(2,1)S(1)}, bf16[384,128]{1,0:T(8,128)(2,1)}, u32[]{:S(2)}) copy-start(bf16[384,128]{1,0:T(8,128)(2,1)} %param.7) | copy-start | bytes 294916
  32.3 40.8 %all-to-all-start = ((bf16[24,88,128]{2,1,0:T(8,128)(2,1)}), bf16[24,88,128]{2,1,0:T(8,128)(2,1)S(1)}, u32[]{:S(2)}, u32[]{:S(2)}) async-start(bf16[24,88,128]{2,1,0:T(8,128)(2,1)} %broadcast_in_dim.16), calls=%async_computation | async-start | bytes 1081344 | tf_op jit(solution)/shard_map/all_to_all | solution.py:202
  48.1 32.3 %copy-start.17 = (s32[3,6]{1,0:T(4,128)S(1)}, s32[3,6]{1,0:T(4,128)}, u32[]{:S(2)}) copy-start(s32[3,6]{1,0:T(4,128)} %param.11) | copy-start | bytes 220
  49.3 15.6 %collective-permute-start.2 = (bf16[2,128,128]{2,1,0:T(8,128)(2,1)S(1)}, bf16[2,128,128]{2,1,0:T(8,128)(2,1)S(1)}, u32[]{:S(2)}, u32[]{:S(2)}) collective-permute-start(bf16[2,128,128]{2,1,0:T(8,128)(2,1)S(1)} %get-tuple-element.31), channel_id=1, source_target_pairs={{0,16},{16,0},{32,48},{48,32},{64,80},{80,64},{96,112},{112,96},{1... | collective-permute-start | bytes 196616 | tf_op jit(solution)/shard_map/ppermute | solution.py:53
  52.2 12.7 %collective-permute-start.1 = (bf16[2,128,128]{2,1,0:T(8,128)(2,1)S(1)}, bf16[2,128,128]{2,1,0:T(8,128)(2,1)S(1)}, u32[]{:S(2)}, u32[]{:S(2)}) collective-permute-start(bf16[2,128,128]{2,1,0:T(8,128)(2,1)S(1)} %get-tuple-element.32), channel_id=1, source_target_pairs={{0,752},{16,32},{32,16},{48,64},{64,48},{80,96},{96,80},{112,128},... | collective-permute-start | bytes 196616 | tf_op jit(solution)/shard_map/ppermute | solution.py:43
  55.6 11.8 %collective-permute-start.3 = (bf16[2,384,128]{2,1,0:T(8,128)(2,1)S(1)}, bf16[2,384,128]{2,1,0:T(8,128)(2,1)S(1)}, u32[]{:S(2)}, u32[]{:S(2)}) collective-permute-start(bf16[2,384,128]{2,1,0:T(8,128)(2,1)S(1)} %maximum_select_fusion.kv), channel_id=1, source_target_pairs={{0,576},{16,592},{32,608},{48,624},{64,640},{80,656},{96,672},{112... | collective-permute-start | bytes 589832 | tf_op jit(solution)/shard_map/ppermute | solution.py:38
  59.9 9.5 %collective-permute-start.4 = (bf16[2,384,128]{2,1,0:T(8,128)(2,1)S(1)}, bf16[2,384,128]{2,1,0:T(8,128)(2,1)S(1)}, u32[]{:S(2)}, u32[]{:S(2)}) collective-permute-start(bf16[2,384,128]{2,1,0:T(8,128)(2,1)S(1)} %maximum_select_fusion.kv), channel_id=1, source_target_pairs={{0,384},{16,400},{32,416},{48,432},{64,448},{80,464},{96,480},{112... | collective-permute-start | bytes 589832 | tf_op jit(solution)/shard_map/ppermute | solution.py:38
  62.4 9.5 %collective-permute-start.5 = (bf16[2,384,128]{2,1,0:T(8,128)(2,1)S(1)}, bf16[2,384,128]{2,1,0:T(8,128)(2,1)S(1)}, u32[]{:S(2)}, u32[]{:S(2)}) collective-permute-start(bf16[2,384,128]{2,1,0:T(8,128)(2,1)S(1)} %maximum_select_fusion.kv), channel_id=1, source_target_pairs={{0,192},{16,208},{32,224},{48,240},{64,256},{80,272},{96,288},{112... | collective-permute-start | bytes 589832 | tf_op jit(solution)/shard_map/ppermute | solution.py:38
  65.0 16.9 %copy-start.1 = (bf16[2,128,128]{2,1,0:T(8,128)(2,1)}, bf16[2,128,128]{2,1,0:T(8,128)(2,1)S(1)}, u32[]{:S(2)}) copy-start(bf16[2,128,128]{2,1,0:T(8,128)(2,1)S(1)} %get-tuple-element.35.nxt) | copy-start | bytes 196612
  65.0 16.9 %copy-start.4 = (bf16[2,128,128]{2,1,0:T(8,128)(2,1)}, bf16[2,128,128]{2,1,0:T(8,128)(2,1)S(1)}, u32[]{:S(2)}) copy-start(bf16[2,128,128]{2,1,0:T(8,128)(2,1)S(1)} %get-tuple-element.36.prev) | copy-start | bytes 196612
  73.2 8.7 %collective-permute-start.6 = (bf16[24,88,128]{2,1,0:T(8,128)(2,1)S(1)}, bf16[24,88,128]{2,1,0:T(8,128)(2,1)S(1)}, u32[]{:S(2)}, u32[]{:S(2)}) collective-permute-start(bf16[24,88,128]{2,1,0:T(8,128)(2,1)S(1)} %broadcast_select_fusion), channel_id=1, source_target_pairs={{0,16},{16,0},{32,48},{48,32},{64,80},{80,64},{96,112},{112,96},{1... | collective-permute-start | bytes 1622024 | tf_op jit(solution)/shard_map/ppermute | solution.py:53
  84.2 0.5 copy-start.11
  84.7 0.8 copy-start.2
  85.6 0.8 copy-start.5
  86.4 0.9 copy-start.7
  87.3 0.7 copy-start.12
  89.9 1.9 %copy-start = (bf16[6144,256]{1,0:T(8,128)(2,1)S(1)}, bf16[6144,256]{1,0:T(8,128)(2,1)}, u32[]{:S(2)}) copy-start(bf16[6144,256]{1,0:T(8,128)(2,1)} %all-gather.2.cloned.1.call-done.pieces) | copy-start | bytes 9437188
  91.8 6.0 %copy-start.3 = (bf16[2,128,128]{2,1,0:T(8,128)(2,1)S(1)}, bf16[2,128,128]{2,1,0:T(8,128)(2,1)}, u32[]{:S(2)}) copy-start(bf16[2,128,128]{2,1,0:T(8,128)(2,1)} %copy-done.1) | copy-start | bytes 196612
  91.8 6.0 %copy-start.6 = (bf16[2,128,128]{2,1,0:T(8,128)(2,1)S(1)}, bf16[2,128,128]{2,1,0:T(8,128)(2,1)}, u32[]{:S(2)}) copy-start(bf16[2,128,128]{2,1,0:T(8,128)(2,1)} %copy-done.4) | copy-start | bytes 196612
  91.8 6.0 %copy-start.8 = (bf16[384,128]{1,0:T(8,128)(2,1)S(1)}, bf16[384,128]{1,0:T(8,128)(2,1)}, u32[]{:S(2)}) copy-start(bf16[384,128]{1,0:T(8,128)(2,1)} %q.3) | copy-start | bytes 294916
  91.8 6.0 %copy-start.13 = (s32[13]{0:T(128)S(1)}, s32[13]{0:T(128)}, u32[]{:S(2)}) copy-start(s32[13]{0:T(128)} %copy-done.11) | copy-start | bytes 160
  94.8 6.1 %collective-permute-start.12 = (f32[24,88,128]{2,1,0:T(8,128)S(1)}, f32[24,88,128]{2,1,0:T(8,128)S(1)}, u32[]{:S(2)}, u32[]{:S(2)}) collective-permute-start(f32[24,88,128]{2,1,0:T(8,128)S(1)} %get-tuple-element.27), channel_id=1, source_target_pairs={{0,16},{16,0},{32,48},{48,32},{64,80},{80,64},{96,112},{112,96},{1... | collective-permute-start | bytes 3244040 | tf_op jit(solution)/shard_map/ppermute | solution.py:53
  100.2 0.7 copy-start.9
  101.7 11.0 %copy-start.10 = (bf16[2,256,128]{2,1,0:T(8,128)(2,1)S(1)}, bf16[2,256,128]{2,1,0:T(8,128)(2,1)}, u32[]{:S(2)}) copy-start(bf16[2,256,128]{2,1,0:T(8,128)(2,1)} %copy-done.9) | copy-start | bytes 393220
  101.7 35.1 %all-to-all-start.1 = ((bf16[24,88,128]{2,1,0:T(8,128)(2,1)}), bf16[24,88,128]{2,1,0:T(8,128)(2,1)S(1)}, u32[]{:S(2)}, u32[]{:S(2)}) async-start(bf16[24,88,128]{2,1,0:T(8,128)(2,1)} %pair_sum.1), calls=%async_computation.1 | async-start | bytes 1081344 | tf_op jit(solution)/shard_map/all_to_all | solution.py:271
  112.7 22.3 %collective-permute-start.7 = (bf16[2,128,128]{2,1,0:T(8,128)(2,1)S(1)}, bf16[2,128,128]{2,1,0:T(8,128)(2,1)S(1)}, u32[]{:S(2)}, u32[]{:S(2)}) collective-permute-start(bf16[2,128,128]{2,1,0:T(8,128)(2,1)S(1)} %get-tuple-element.34), channel_id=1, source_target_pairs={{0,752},{16,32},{32,16},{48,64},{64,48},{80,96},{96,80},{112,128},... | collective-permute-start | bytes 196616 | tf_op jit(solution)/shard_map/ppermute | solution.py:43
  116.4 19.5 %collective-permute-start.8 = (bf16[2,384,128]{2,1,0:T(8,128)(2,1)S(1)}, bf16[2,384,128]{2,1,0:T(8,128)(2,1)S(1)}, u32[]{:S(2)}, u32[]{:S(2)}) collective-permute-start(bf16[2,384,128]{2,1,0:T(8,128)(2,1)S(1)} %get-tuple-element.30), channel_id=1, source_target_pairs={{0,384},{16,400},{32,416},{48,432},{64,448},{80,464},{96,480},{112... | collective-permute-start | bytes 589832 | tf_op jit(solution)/shard_map/ppermute | solution.py:38
  121.0 14.9 %collective-permute-start.9 = (bf16[2,384,128]{2,1,0:T(8,128)(2,1)S(1)}, bf16[2,384,128]{2,1,0:T(8,128)(2,1)S(1)}, u32[]{:S(2)}, u32[]{:S(2)}) collective-permute-start(bf16[2,384,128]{2,1,0:T(8,128)(2,1)S(1)} %get-tuple-element.29), channel_id=1, source_target_pairs={{0,192},{16,208},{32,224},{48,240},{64,256},{80,272},{96,288},{112... | collective-permute-start | bytes 589832 | tf_op jit(solution)/shard_map/ppermute | solution.py:38
  123.3 12.7 %collective-permute-start.10 = (bf16[2,384,128]{2,1,0:T(8,128)(2,1)S(1)}, bf16[2,384,128]{2,1,0:T(8,128)(2,1)S(1)}, u32[]{:S(2)}, u32[]{:S(2)}) collective-permute-start(bf16[2,384,128]{2,1,0:T(8,128)(2,1)S(1)} %get-tuple-element.28), channel_id=1, source_target_pairs={{0,576},{16,592},{32,608},{48,624},{64,640},{80,656},{96,672},{112... | collective-permute-start | bytes 589832 | tf_op jit(solution)/shard_map/ppermute | solution.py:38
  127.6 8.4 %collective-permute-start.11 = (bf16[2,128,128]{2,1,0:T(8,128)(2,1)S(1)}, bf16[2,128,128]{2,1,0:T(8,128)(2,1)S(1)}, u32[]{:S(2)}, u32[]{:S(2)}) collective-permute-start(bf16[2,128,128]{2,1,0:T(8,128)(2,1)S(1)} %get-tuple-element.33), channel_id=1, source_target_pairs={{0,16},{16,0},{32,48},{48,32},{64,80},{80,64},{96,112},{112,96},{1... | collective-permute-start | bytes 196616 | tf_op jit(solution)/shard_map/ppermute | solution.py:53
Sparse Core Ops, SparseCore 0:
  31.5 58.1 all-gather.1
